TPU v7x, 32 devices: a whole 2x2x4 slice. The times are simulated.
32 devices in a mesh: ctx: 4 (over y, x), fsdp: 8 (over z, core).
Axes of the slice: x: 2, y: 2, z: 4, core: 2. Of those that a mesh axis runs over, the one named last changes fastest.
Arguments:
- tokens: bfloat16 [8, 768, 1536], P('fsdp', 'ctx'), may hold values from -6 to 6
- block_order: int32 [8, 8], P('fsdp'), may hold values from 0 to 7, each once within a row
- segment_ids: int32 [8, 768], P('fsdp'), may hold values from -1 to 7, as said below
- norm_gains: bfloat16 [2, 1536], P(None, 'fsdp'), may hold values from 0.5 to 1.5
- attn_in_weight: bfloat16 [1536, 6144], P('fsdp'), may hold values from -0.15625 to 0.15625
- forget_weight: bfloat16 [1536, 24], P('fsdp'), may hold values from -0.15625 to 0.15625
- forget_bias: float32 [24], replicated, may hold values from 0 to 8, as said below
- qk_gains: float32 [2, 64], replicated, may hold values from 0.5 to 1.5
- out_weight: bfloat16 [1536, 1536], P('fsdp'), may hold values from -0.625 to 0.625
- gate_up_weight: bfloat16 [1536, 8192], P('fsdp'), may hold values from -0.15625 to 0.15625
- down_weight: bfloat16 [4096, 1536], P('fsdp'), may hold values from -0.09375 to 0.09375
- out_grad: bfloat16 [8, 768, 1536], P('fsdp', 'ctx'), may hold values from -6 to 6
Outputs:
- block_out: bfloat16 [8, 768, 1536], P('fsdp', 'ctx')
- tokens_grad: bfloat16 [8, 768, 1536], P('fsdp', 'ctx')
- norm_gains_grad: float32 [2, 1536], P(None, 'fsdp')
- attn_in_grad: float32 [1536, 6144], P('fsdp')
- forget_weight_grad: float32 [1536, 24], P('fsdp')
- forget_bias_grad: float32 [24], replicated
- qk_gains_grad: float32 [2, 64], replicated
- out_weight_grad: float32 [1536, 1536], P('fsdp')
- gate_up_grad: float32 [1536, 8192], P('fsdp')
- down_grad: float32 [4096, 1536], P('fsdp')
- rms_stats: float32 [8, 2], P('fsdp')
Inputs may be any that keep to these rules, and one draw needn't show every extreme that they name: `block_order`: each row names every block of its sequence once; context index c holds storage blocks 2c and 2c + 1. `segment_ids`: in true order a sequence's non-negative ids start at 0, never fall and rise by one at each new document, so every sequence holds exactly 8 documents, ids 0 to 7, each contiguous and of uneven length; -1 marks a padding tail of 1 to 96 tokens at the end of every sequence. `forget_bias`: one bias for each head.
All inputs are finite; a program needn't handle non-finite values.
Results may differ from a plain program's by a relative error of at most 0.018.
Values may be sent and summed in bfloat16 or wider, within the bound.
A program may use at most 384 MiB of HBM per device.

v0:
```python
import jax
import jax.numpy as jnp
from jax import lax
from jax.sharding import PartitionSpec as P

EPS = 1e-06
SCALE = 0.125
PAIR = 2


def rms_scale(values):
    return lax.rsqrt(jnp.mean(values * values, axis=-1, keepdims=True) + EPS)


def norm_back(grad_normed, values, scale_values, gain_values):
    scaled = grad_normed * gain_values
    cubed = scale_values * scale_values * scale_values
    return scale_values * scaled - values * cubed * jnp.mean(
        scaled * values, axis=-1, keepdims=True
    )


def left_product(left, right):
    return lax.dot_general(
        left, right, (((0,), (0,)), ((), ())), preferred_element_type=jnp.float32
    )


def right_product(left, right):
    return lax.dot_general(
        left, right, (((1,), (1,)), ((), ())), preferred_element_type=jnp.float32
    )


def body(
    tokens,
    block_order,
    segment_ids,
    norm_gains,
    attn_in_weight,
    forget_weight,
    forget_bias,
    qk_gains,
    out_weight,
    gate_up_weight,
    down_weight,
    out_grad,
):
    inputs = tokens[0].astype(jnp.float32)
    row_count = inputs.shape[0]
    model_width = inputs.shape[1]
    head_count = forget_bias.shape[0]
    head_dim = qk_gains.shape[1]
    seq_order = block_order[0]
    block_count = seq_order.shape[0]
    block_len = row_count // 2
    seq_len = block_count * block_len
    ctx_rank = lax.axis_index("ctx")
    local_offsets = jnp.arange(row_count, dtype=jnp.int32)
    local_pos = (
        jnp.take(seq_order, 2 * ctx_rank + local_offsets // block_len) * block_len
        + local_offsets % block_len
    )
    all_offsets = jnp.arange(seq_len, dtype=jnp.int32)
    all_pos = jnp.take(seq_order, all_offsets // block_len) * block_len + all_offsets % block_len
    seg_true = segment_ids[0]
    seg_local = jnp.take(seg_true, local_pos)
    seg_all = jnp.take(seg_true, all_pos)
    block_ids = jnp.arange(block_count, dtype=jnp.int32)
    inverse = jnp.sum(
        jnp.where(seq_order[:, None] == block_ids[None, :], block_ids[:, None], 0), axis=0
    )

    def to_true(array):
        return jnp.take(array.reshape(block_count, block_len, -1), inverse, axis=0).reshape(
            seq_len, -1
        )

    def to_store(array):
        return jnp.take(array.reshape(block_count, block_len, -1), seq_order, axis=0).reshape(
            seq_len, -1
        )

    shards = (norm_gains, attn_in_weight, forget_weight, out_weight, gate_up_weight, down_weight)
    gains_full, w_in, w_forget, w_out, w_gate_up, w_down = (
        lax.all_gather(shards[0], "fsdp", axis=1, tiled=True),
        lax.all_gather(shards[1], "fsdp", axis=0, tiled=True),
        lax.all_gather(shards[2], "fsdp", axis=0, tiled=True),
        lax.all_gather(shards[3], "fsdp", axis=0, tiled=True),
        lax.all_gather(shards[4], "fsdp", axis=0, tiled=True),
        lax.all_gather(shards[5], "fsdp", axis=0, tiled=True),
    )
    gain_one = gains_full[0].astype(jnp.float32)
    gain_two = gains_full[1].astype(jnp.float32)
    scale_one = rms_scale(inputs)
    normed = (inputs * scale_one * gain_one).astype(jnp.bfloat16)
    project = jnp.dot(normed, w_in, preferred_element_type=jnp.float32)
    query_heads = project[:, :model_width].reshape(row_count, head_count, head_dim)
    key_heads = project[:, model_width : 2 * model_width].reshape(row_count, head_count, head_dim)
    values = project[:, 2 * model_width : 3 * model_width].astype(jnp.bfloat16)
    gate_logit = project[:, 3 * model_width :]
    forget_logit = jnp.dot(normed, w_forget, preferred_element_type=jnp.float32) + forget_bias
    log_forget = jax.nn.log_sigmoid(forget_logit)
    query_scale = rms_scale(query_heads)
    key_scale = rms_scale(key_heads)
    query_norm = (
        (query_heads * query_scale * qk_gains[0])
        .astype(jnp.bfloat16)
        .reshape(row_count, model_width)
    )
    key_norm = (
        (key_heads * key_scale * qk_gains[1]).astype(jnp.bfloat16).reshape(row_count, model_width)
    )
    keys_all, values_all = (
        lax.all_gather(key_norm, "ctx", axis=0, tiled=True),
        lax.all_gather(values, "ctx", axis=0, tiled=True),
    )
    forget_all = lax.all_gather(log_forget, "ctx", axis=0, tiled=True)
    prefix_all = to_store(jnp.cumsum(to_true(forget_all), axis=0))
    prefix_local = lax.dynamic_slice_in_dim(prefix_all, ctx_rank * row_count, row_count, 0)
    allowed = (all_pos[None, :] <= local_pos[:, None]) & (seg_all[None, :] == seg_local[:, None])
    group_count = head_count // PAIR
    span = PAIR * head_dim

    def group_scores(group_index):
        start = group_index * span
        query_group = lax.dynamic_slice_in_dim(query_norm, start, span, 1).reshape(
            row_count, PAIR, head_dim
        )
        key_group = lax.dynamic_slice_in_dim(keys_all, start, span, 1).reshape(
            seq_len, PAIR, head_dim
        )
        value_group = lax.dynamic_slice_in_dim(values_all, start, span, 1).reshape(
            seq_len, PAIR, head_dim
        )
        prefix_query = lax.dynamic_slice_in_dim(prefix_local, group_index * PAIR, PAIR, 1)
        prefix_key = lax.dynamic_slice_in_dim(prefix_all, group_index * PAIR, PAIR, 1)
        scores = (
            jnp.einsum("qhd,khd->hqk", query_group, key_group, preferred_element_type=jnp.float32)
            * SCALE
        )
        scores = scores + prefix_query.T[:, :, None] - prefix_key.T[:, None, :]
        return (
            jnp.where(allowed[None], scores, -jnp.inf),
            query_group,
            key_group,
            value_group,
            start,
        )

    def attend(group_index):
        scores, query_group, key_group, value_group, start = group_scores(group_index)
        row_top = jnp.max(scores, axis=-1, keepdims=True)
        expos = jnp.exp(scores - row_top)
        row_total = jnp.sum(expos, axis=-1, keepdims=True)
        probs = (expos / row_total).astype(jnp.bfloat16)
        result = jnp.einsum(
            "hqk,khd->qhd", probs, value_group, preferred_element_type=jnp.float32
        ).reshape(row_count, span)
        return (result, (row_top + jnp.log(row_total))[..., 0])

    attn_parts, log_totals = lax.map(attend, jnp.arange(group_count, dtype=jnp.int32))
    attended = attn_parts.transpose(1, 0, 2).reshape(row_count, model_width)
    gate_sig = jax.nn.sigmoid(gate_logit)
    gated = (attended * gate_sig).astype(jnp.bfloat16)
    mixed = inputs + jnp.dot(gated, w_out, preferred_element_type=jnp.float32)
    scale_two = rms_scale(mixed)
    normed_two = (mixed * scale_two * gain_two).astype(jnp.bfloat16)
    gate_up = jnp.dot(normed_two, w_gate_up, preferred_element_type=jnp.float32)
    hidden_width = gate_up.shape[1] // 2
    gate_part = gate_up[:, :hidden_width]
    up_part = gate_up[:, hidden_width:]
    hidden = (jax.nn.silu(gate_part) * up_part).astype(jnp.bfloat16)
    result = mixed + jnp.dot(hidden, w_down, preferred_element_type=jnp.float32)
    block_out = result.astype(jnp.bfloat16)[None]
    valid_rows = (seg_local >= 0).astype(jnp.float32)
    branch = result - inputs
    partial_sums = jnp.stack(
        [
            jnp.sum(valid_rows * jnp.sum(result * result, axis=-1)),
            jnp.sum(valid_rows * jnp.sum(branch * branch, axis=-1)),
        ]
    )[None]
    valid_count = jnp.sum((seg_true >= 0).astype(jnp.float32)) * model_width
    b_in, b_forget, b_out, b_gate_up, b_down = (
        lax.all_gather(attn_in_weight, "fsdp", axis=0, tiled=True),
        lax.all_gather(forget_weight, "fsdp", axis=0, tiled=True),
        lax.all_gather(out_weight, "fsdp", axis=0, tiled=True),
        lax.all_gather(gate_up_weight, "fsdp", axis=0, tiled=True),
        lax.all_gather(down_weight, "fsdp", axis=0, tiled=True),
    )
    grad_out = out_grad[0].astype(jnp.float32)
    grad_low = out_grad[0]
    grad_hidden = right_product(grad_low, b_down)
    gate_sigmoid = jax.nn.sigmoid(gate_part)
    grad_gate = grad_hidden * up_part * gate_sigmoid * (1.0 + gate_part * (1.0 - gate_sigmoid))
    grad_up = grad_hidden * gate_part * gate_sigmoid
    grad_gate_up = jnp.concatenate([grad_gate, grad_up], axis=1).astype(jnp.bfloat16)
    grad_normed_two = right_product(grad_gate_up, b_gate_up)
    gain_two_grad = jnp.sum(grad_normed_two * mixed * scale_two, axis=0)
    grad_mixed = grad_out + norm_back(grad_normed_two, mixed, scale_two, gain_two)
    grad_branch = grad_mixed.astype(jnp.bfloat16)
    out_weight_grad = left_product(gated, grad_branch)
    grad_gated = right_product(grad_branch, b_out)
    grad_attended = (grad_gated * gate_sig).astype(jnp.bfloat16)
    grad_gate_logit = grad_gated * attended * gate_sig * (1.0 - gate_sig)

    def attend_back(group_index, carry):
        query_acc, keys_acc, values_acc, prefix_query_acc, prefix_key_acc = carry
        scores, query_group, key_group, value_group, start = group_scores(group_index)
        group_lse = lax.dynamic_index_in_dim(log_totals, group_index, 0, keepdims=False)
        probs = jnp.exp(scores - group_lse[..., None])
        grad_group = lax.dynamic_slice_in_dim(grad_attended, start, span, 1).reshape(
            row_count, PAIR, head_dim
        )
        grad_probs = jnp.einsum(
            "qhd,khd->hqk", grad_group, value_group, preferred_element_type=jnp.float32
        )
        inner = jnp.sum(probs * grad_probs, axis=-1, keepdims=True)
        grad_scores = (probs * (grad_probs - inner)).astype(jnp.bfloat16)
        grad_query = (
            jnp.einsum(
                "hqk,khd->qhd", grad_scores, key_group, preferred_element_type=jnp.float32
            ).reshape(row_count, span)
            * SCALE
        )
        grad_key = (
            jnp.einsum(
                "hqk,qhd->khd", grad_scores, query_group, preferred_element_type=jnp.float32
            ).reshape(seq_len, span)
            * SCALE
        )
        grad_value = jnp.einsum(
            "hqk,qhd->khd",
            probs.astype(jnp.bfloat16),
            grad_group,
            preferred_element_type=jnp.float32,
        ).reshape(seq_len, span)
        wide_scores = grad_scores.astype(jnp.float32)
        prefix_query_piece = jnp.sum(wide_scores, axis=-1).T
        prefix_key_piece = -jnp.sum(wide_scores, axis=1).T
        head_start = group_index * PAIR
        query_acc = lax.dynamic_update_slice_in_dim(query_acc, grad_query, start, 1)
        keys_acc = lax.dynamic_update_slice_in_dim(keys_acc, grad_key, start, 1)
        values_acc = lax.dynamic_update_slice_in_dim(values_acc, grad_value, start, 1)
        prefix_query_acc = lax.dynamic_update_slice_in_dim(
            prefix_query_acc, prefix_query_piece, head_start, 1
        )
        prefix_key_acc = lax.dynamic_update_slice_in_dim(
            prefix_key_acc, prefix_key_piece, head_start, 1
        )
        return (query_acc, keys_acc, values_acc, prefix_query_acc, prefix_key_acc)

    empty_grads = (
        jnp.zeros((row_count, model_width), jnp.float32),
        jnp.zeros((seq_len, model_width), jnp.float32),
        jnp.zeros((seq_len, model_width), jnp.float32),
        jnp.zeros((row_count, head_count), jnp.float32),
        jnp.zeros((seq_len, head_count), jnp.float32),
    )
    grad_query_norm, grad_keys_all, grad_values_all, grad_prefix_local, grad_prefix_all = (
        lax.fori_loop(0, group_count, attend_back, empty_grads)
    )
    own_rows = (
        lax.dynamic_slice_in_dim(grad_prefix_all, ctx_rank * row_count, row_count, 0)
        + grad_prefix_local
    )
    grad_prefix_all = lax.dynamic_update_slice_in_dim(
        grad_prefix_all, own_rows, ctx_rank * row_count, 0
    )
    suffix_sums = jnp.flip(jnp.cumsum(jnp.flip(to_true(grad_prefix_all), 0), axis=0), 0)
    grad_forget_all = to_store(suffix_sums)
    grad_key_norm, grad_values, grad_log_forget = (
        lax.psum_scatter(grad_keys_all, "ctx", scatter_dimension=0, tiled=True),
        lax.psum_scatter(grad_values_all, "ctx", scatter_dimension=0, tiled=True),
        lax.psum_scatter(grad_forget_all, "ctx", scatter_dimension=0, tiled=True),
    )
    grad_forget_logit = (grad_log_forget * jax.nn.sigmoid(-forget_logit)).astype(jnp.bfloat16)
    bias_grad = jnp.sum(grad_forget_logit.astype(jnp.float32), axis=0)
    forget_weight_grad = left_product(normed, grad_forget_logit)
    grad_query_heads = grad_query_norm.reshape(row_count, head_count, head_dim)
    grad_key_heads = grad_key_norm.reshape(row_count, head_count, head_dim)
    query_gain_grad = jnp.sum(grad_query_heads * query_heads * query_scale, axis=(0, 1))
    key_gain_grad = jnp.sum(grad_key_heads * key_heads * key_scale, axis=(0, 1))
    grad_query_raw = norm_back(grad_query_heads, query_heads, query_scale, qk_gains[0]).reshape(
        row_count, model_width
    )
    grad_key_raw = norm_back(grad_key_heads, key_heads, key_scale, qk_gains[1]).reshape(
        row_count, model_width
    )
    grad_project = jnp.concatenate(
        [grad_query_raw, grad_key_raw, grad_values, grad_gate_logit], axis=1
    ).astype(jnp.bfloat16)
    attn_in_grad = left_product(normed, grad_project)
    grad_normed = right_product(grad_project, b_in) + right_product(grad_forget_logit, b_forget)
    gain_one_grad = jnp.sum(grad_normed * inputs * scale_one, axis=0)
    grad_inputs = grad_mixed + norm_back(grad_normed, inputs, scale_one, gain_one)
    tokens_grad = grad_inputs.astype(jnp.bfloat16)[None]
    gains_grad = jnp.stack([gain_one_grad, gain_two_grad])
    down_grad = left_product(hidden, grad_low)
    gate_up_grad = left_product(normed_two, grad_gate_up)
    gains_share, in_share, forget_share, out_share, gate_up_share, down_share = (
        lax.psum_scatter(gains_grad, "fsdp", scatter_dimension=1, tiled=True),
        lax.psum_scatter(attn_in_grad, "fsdp", scatter_dimension=0, tiled=True),
        lax.psum_scatter(forget_weight_grad, "fsdp", scatter_dimension=0, tiled=True),
        lax.psum_scatter(out_weight_grad, "fsdp", scatter_dimension=0, tiled=True),
        lax.psum_scatter(gate_up_grad, "fsdp", scatter_dimension=0, tiled=True),
        lax.psum_scatter(down_grad, "fsdp", scatter_dimension=0, tiled=True),
    )
    summed = lax.psum(
        (gains_share, in_share, forget_share, out_share, gate_up_share, down_share, partial_sums),
        "ctx",
    )
    small_grads = lax.psum(
        (bias_grad, jnp.stack([query_gain_grad, key_gain_grad])), ("ctx", "fsdp")
    )
    rms_stats = jnp.sqrt(summed[6] / valid_count)
    return (
        block_out,
        tokens_grad,
        summed[0],
        summed[1],
        summed[2],
        small_grads[0],
        small_grads[1],
        summed[3],
        summed[4],
        summed[5],
        rms_stats,
    )


def solution(mesh):
    placed = (
        P("fsdp", "ctx", None),
        P("fsdp", None),
        P("fsdp", None),
        P(None, "fsdp"),
        P("fsdp", None),
        P("fsdp", None),
        P(),
        P(),
        P("fsdp", None),
        P("fsdp", None),
        P("fsdp", None),
        P("fsdp", "ctx", None),
    )
    return jax.shard_map(
        body,
        mesh=mesh,
        in_specs=placed,
        out_specs=(
            P("fsdp", "ctx", None),
            P("fsdp", "ctx", None),
            P(None, "fsdp"),
            P("fsdp", None),
            P("fsdp", None),
            P(),
            P(),
            P("fsdp", None),
            P("fsdp", None),
            P("fsdp", None),
            P("fsdp", None),
        ),
        check_vma=False,
    )
```

profile of v0, /device:TPU:0, one launch (start us, length us, event | category | flops | bytes accessed | tf_op | source)
XLA Modules:
  0.0 2580.7 jit_solution(8462885975123148530)
XLA Ops:
  8.0 13.4 all-gather
  22.3 158.4 %all-gather.10.cloned.1.call-done = bf16[1536,6144]{1,0:T(8,128)(2,1)} async-done(((bf16[192,6144]{1,0:T(8,128)(2,1)}), bf16[1536,6144]{1,0:T(8,128)(2,1)}) %all-gather.10.cloned.1.call-update) | async-done | bytes 18874384 | tf_op jit(solution)/shard_map/all_gather | solution.py:87
  180.7 8.5 fusion.77
  222.5 13.9 all-gather.1
  237.8 9.5 all-gather.2
  263.9 4.8 all-gather.14.cloned.1.call-done
  272.9 105.4 %while.35 = (s32[]{:T(128)}, f32[12,192,128]{1,2,0:T(8,128)}, f32[12,2,192]{2,1,0:T(2,128)}, s32[12]{0:T(128)S(1)}, bf16[768,1536]{0,1:T(8,128)(2,1)S(1)}, /*ind...) while((s32[]{:T(128)}, f32[12,192,128]{1,2,0:T(8,128)}, ...), condition=%wide.region_9.11_spmd.clone, body=%wide.region_6.10_spmd.clone.sunk | while | flops 78888584 | bytes 5532469 | solution.py:162
  389.2 152.9 %all-gather.18.cloned.1.call-done = bf16[1536,8192]{1,0:T(8,128)(2,1)} async-done(((bf16[192,8192]{1,0:T(8,128)(2,1)}), bf16[1536,8192]{1,0:T(8,128)(2,1)}) %all-gather.18.cloned.1.call-update) | async-done | bytes 25165840 | tf_op jit(solution)/shard_map/all_gather | solution.py:90
  542.1 14.5 fusion.72
  556.6 102.0 %all-gather.20.cloned.1.call-done = bf16[4096,1536]{1,0:T(8,128)(2,1)} async-done(((bf16[512,1536]{1,0:T(8,128)(2,1)}), bf16[4096,1536]{1,0:T(8,128)(2,1)}) %all-gather.20.cloned.1.call-update) | async-done | bytes 12582928 | tf_op jit(solution)/shard_map/all_gather | solution.py:91
  658.6 15.0 multiply_convert_fusion.2
  673.5 15.1 multiply_reduce_fusion.8
  690.6 5.9 multiply_convert_fusion.5
  704.5 160.1 %while.36 = (s32[]{:T(128)}, f32[192,1536]{0,1:T(8,128)}, f32[768,1536]{1,0:T(8,128)}, f32[768,1536]{1,0:T(8,128)}, f32[192,24]{0,1:T(8,128)}, /*index=5*/f32[76...) while((s32[]{:T(128)}, f32[192,1536]{0,1:T(8,128)}, ...), condition=%wide.region_16.18_spmd.clone, body=%wide.region_12.17_spmd.clone.sunk | while | flops 193436928 | bytes 17747076 | solution.py:262
  882.9 5.0 fusion.42
  889.3 11.6 fusion.36
  911.4 8.7 reduce-scatter.16.cloned.1.call-done
  926.5 53.8 %reduce-scatter.18.cloned.1.call-done = f32[192,1536]{1,0:T(8,128)} async-done(((f32[768,1536]{1,0:T(8,128)}), f32[192,1536]{1,0:T(8,128)}) %reduce-scatter.18.cloned.1.call-update) | async-done | bytes 1179664 | tf_op jit(solution)/shard_map/reduce_scatter | solution.py:275
  981.7 6.4 multiply_reduce_fusion.7
  988.9 15.1 fusion.40
  1004.6 22.7 fusion.18
  1033.7 10.4 fusion.41
  1045.5 9.4 multiply_reduce_fusion.5
  1056.2 53.0 %reduce-scatter.22.cloned.1.call-done = f32[192,1536]{1,0:T(8,128)} async-done(((f32[1536,1536]{1,0:T(8,128)}), f32[192,1536]{1,0:T(8,128)}) %reduce-scatter.22.cloned.1.call-update) | async-done | bytes 1179664 | tf_op jit(solution)/shard_map/reduce_scatter | solution.py:306
  1109.2 247.9 %reduce-scatter.26.cloned.1.call-done = f32[512,1536]{1,0:T(8,128)} async-done(((f32[4096,1536]{1,0:T(8,128)}), f32[512,1536]{1,0:T(8,128)}) %reduce-scatter.26.cloned.1.call-update) | async-done | bytes 3145744 | tf_op jit(solution)/shard_map/reduce_scatter | solution.py:308
  1357.2 365.5 %reduce-scatter.20.cloned.1.call-done = f32[192,6144]{1,0:T(8,128)} async-done(((f32[1536,6144]{1,0:T(8,128)}), f32[192,6144]{1,0:T(8,128)}) %reduce-scatter.20.cloned.1.call-update) | async-done | bytes 4718608 | tf_op jit(solution)/shard_map/reduce_scatter | solution.py:304
  1722.7 484.0 %reduce-scatter.24.cloned.1.call-done = f32[192,8192]{1,0:T(8,128)} async-done(((f32[1536,8192]{1,0:T(8,128)}), f32[192,8192]{1,0:T(8,128)}) %reduce-scatter.24.cloned.1.call-update) | async-done | bytes 6291472 | tf_op jit(solution)/shard_map/reduce_scatter | solution.py:307
  2208.7 30.7 %reduce-scatter.32.cloned.1.call-done = f32[192,24]{1,0:T(8,128)} async-done(((f32[1536,24]{1,0:T(8,128)}), f32[192,24]{1,0:T(8,128)}) %reduce-scatter.32.cloned.1.call-update) | async-done | bytes 18448
  2240.5 38.1 %all-reduce = (f32[24]{0:T(128)}, f32[2,64]{1,0:T(2,128)}) all-reduce(f32[24]{0:T(128)S(1)} %copy-done.84, f32[2,64]{1,0:T(2,128)S(1)} %pad_maximum_fusion.7), channel_id=1, replica_groups=mesh['ctx'=4,'fsdp'=8] {'ctx','fsdp'}, use_global_device_ids=true, to_apply=%region_34.36 | all-reduce | flops 152 | bytes 1216 | tf_op jit(solution)/shard_map/psum | solution.py:314
  2283.5 17.9 all-reduce.1
  2301.9 259.7 %all-reduce.5.cloned.1.call-done = (f32[192,6144]{1,0:T(8,128)}, f32[192,1536]{1,0:T(8,128)}, f32[192,8192]{1,0:T(8,128)}, f32[512,1536]{1,0:T(8,128)}) async-done(((f32[192,6144]{1,0:T(8,128)}, f32[192,1536]{1,0:T(8,128)}, f32[192,8192]{1,0:T(8,128)}, f32[512,1536]{1,0:T(8,128)}), (f32[192,6144]{1,0:T(8,128)}, f32[192,1536]{1,0:T(8,128)}, f32[192,8192]{1,0:T(8,128)}, ...) | async-done | bytes 15335440 | tf_op jit(solution)/shard_map/psum | solution.py:310
  2561.6 5.2 copy.364
  (956 shorter events, 387.9 us)
Async XLA Ops:
  7.2 14.4 copy-start.3
  7.2 173.5 %all-gather.10.cloned.1.call-start = ((), (), s32[]{:S(2)}) async-start(), calls=%async_computation.9 | async-start | bytes 21233664 | tf_op jit(solution)/shard_map/all_gather | solution.py:87
  7.9 253.1 %all-gather.12.cloned.1.call-start = ((), (), s32[]{:S(2)}) async-start(), calls=%async_computation.10 | async-start | bytes 2949120 | tf_op jit(solution)/shard_map/all_gather | solution.py:116
  22.3 214.3 %copy-start.56 = (f32[192]{0:T(256)}, f32[192]{0:T(256)S(1)}, u32[]{:S(2)}) copy-start(f32[192]{0:T(256)S(1)} %get-tuple-element.704) | copy-start | bytes 2308
  192.3 76.4 %all-gather.14.cloned.1.call-start = ((), (), s32[]{:S(2)}) async-start(), calls=%async_computation.11 | async-start | bytes 2949120 | tf_op jit(solution)/shard_map/all_gather | solution.py:115
  210.7 174.3 %all-gather.16.cloned.1.call-start = ((), (), s32[]{:S(2)}) async-start(), calls=%async_computation.12 | async-start | bytes 5308416 | tf_op jit(solution)/shard_map/all_gather | solution.py:89
  211.2 330.9 %all-gather.18.cloned.1.call-start = ((), (), s32[]{:S(2)}) async-start(), calls=%async_computation.13 | async-start | bytes 28311552 | tf_op jit(solution)/shard_map/all_gather | solution.py:90
  211.8 24.7 copy-start.85
  211.9 446.7 %all-gather.20.cloned.1.call-start = ((), (), s32[]{:S(2)}) async-start(), calls=%async_computation.14 | async-start | bytes 14155776 | tf_op jit(solution)/shard_map/all_gather | solution.py:91
  212.4 707.7 %reduce-scatter.16.cloned.1.call-start = ((), (), s32[]{:S(2)}) async-start(), calls=%async_computation.15 | async-start | bytes 5898240 | tf_op jit(solution)/shard_map/reduce_scatter | solution.py:274
  212.6 35.5 %copy-start.72 = (pred[8]{0:T(512)(128)(4,1)}, pred[8]{0:T(512)(128)(4,1)S(1)}, u32[]{:S(2)}) copy-start(pred[8]{0:T(512)(128)(4,1)S(1)} %get-tuple-element.721) | copy-start | bytes 28
  212.6 38.5 %copy-start.71 = (pred[8]{0:T(512)(128)(4,1)}, pred[8]{0:T(512)(128)(4,1)S(1)}, u32[]{:S(2)}) copy-start(pred[8]{0:T(512)(128)(4,1)S(1)} %get-tuple-element.720) | copy-start | bytes 28
  389.2 167.4 %copy-start.54 = (f32[192]{0:T(256)}, f32[192]{0:T(256)S(1)}, u32[]{:S(2)}) copy-start(f32[192]{0:T(256)S(1)} %get-tuple-element.706) | copy-start | bytes 2308
  542.1 116.5 %copy-start.34 = (bf16[1,192,1536]{2,1,0:T(8,128)(2,1)S(1)}, bf16[1,192,1536]{2,1,0:T(8,128)(2,1)}, u32[]{:S(2)}) copy-start(bf16[1,192,1536]{2,1,0:T(8,128)(2,1)} %param.29) | copy-start | bytes 1769476
  864.7 115.6 %reduce-scatter.18.cloned.1.call-start = ((), (), s32[]{:S(2)}) async-start(), calls=%async_computation.16 | async-start | bytes 5898240 | tf_op jit(solution)/shard_map/reduce_scatter | solution.py:275
  865.5 163.1 %reduce-scatter.28.cloned.1.call-start = ((), (), s32[]{:S(2)}) async-start(), calls=%async_computation.21 | async-start | bytes 491520
  882.8 226.4 %reduce-scatter.22.cloned.1.call-start = ((), (), s32[]{:S(2)}) async-start(), calls=%async_computation.18 | async-start | bytes 10616832 | tf_op jit(solution)/shard_map/reduce_scatter | solution.py:306
  887.9 469.2 %reduce-scatter.26.cloned.1.call-start = ((), (), s32[]{:S(2)}) async-start(), calls=%async_computation.20 | async-start | bytes 28311552 | tf_op jit(solution)/shard_map/reduce_scatter | solution.py:308
  900.9 821.8 %reduce-scatter.20.cloned.1.call-start = ((), (), s32[]{:S(2)}) async-start(), calls=%async_computation.17 | async-start | bytes 42467328 | tf_op jit(solution)/shard_map/reduce_scatter | solution.py:304
  926.5 55.2 %copy-start.16 = (f32[192,1536]{1,0:T(8,128)S(1)}, f32[192,1536]{1,0:T(8,128)}, u32[]{:S(2)}) copy-start(f32[192,1536]{1,0:T(8,128)} %copy-done.15) | copy-start | bytes 3538948
  1004.0 1202.7 %reduce-scatter.24.cloned.1.call-start = ((), (), s32[]{:S(2)}) async-start(), calls=%async_computation.19 | async-start | bytes 56623104 | tf_op jit(solution)/shard_map/reduce_scatter | solution.py:307
  1027.3 1212.1 %reduce-scatter.32.cloned.1.call-start = ((), (), s32[]{:S(2)}) async-start(), calls=%async_computation.23 | async-start | bytes 884736
  1033.6 1248.9 %reduce-scatter.30.cloned.1.call-start = ((), (), s32[]{:S(2)}) async-start(), calls=%async_computation.22 | async-start | bytes 884736
  1056.2 1505.5 %all-reduce.5.cloned.1.call-start = ((), (), s32[]{:S(2)}) async-start(), calls=%async_computation.24 | async-start | bytes 30670848 | tf_op jit(solution)/shard_map/psum | solution.py:310
  2206.7 33.6 %copy-start.65 = (f32[1536]{0:T(1024)S(1)}, f32[1536]{0:T(1024)}, u32[]{:S(2)}) copy-start(f32[1536]{0:T(1024)} %get-tuple-element.590) | copy-start | bytes 18436
  2206.7 33.7 %copy-start.64 = (f32[1536]{0:T(1024)S(1)}, f32[1536]{0:T(1024)}, u32[]{:S(2)}) copy-start(f32[1536]{0:T(1024)} %get-tuple-element.589) | copy-start | bytes 18436
  2206.7 33.8 %copy-start.84 = (f32[24]{0:T(128)S(1)}, f32[24]{0:T(128)}, u32[]{:S(2)}) copy-start(f32[24]{0:T(128)} %get-tuple-element.673) | copy-start | bytes 292
  2206.7 72.0 %copy-start.82 = (f32[192]{0:T(256)S(1)}, f32[192]{0:T(256)}, u32[]{:S(2)}) copy-start(f32[192]{0:T(256)} %get-tuple-element.595) | copy-start | bytes 2308
  2206.7 72.0 %copy-start.83 = (f32[192]{0:T(256)S(1)}, f32[192]{0:T(256)}, u32[]{:S(2)}) copy-start(f32[192]{0:T(256)} %get-tuple-element.596) | copy-start | bytes 2308
  2206.8 74.6 %copy-start.14 = (f32[192,1536]{1,0:T(8,128)S(1)}, f32[192,1536]{1,0:T(8,128)}, u32[]{:S(2)}) copy-start(f32[192,1536]{1,0:T(8,128)} %copy-done.12) | copy-start | bytes 3538948
  2206.8 74.5 %copy-start.24 = (f32[192,1536]{1,0:T(8,128)S(1)}, f32[192,1536]{1,0:T(8,128)}, u32[]{:S(2)}) copy-start(f32[192,1536]{1,0:T(8,128)} %copy-done.23) | copy-start | bytes 3538948
  2206.8 74.5 %copy-start.78 = (f32[192]{0:T(256)S(1)}, f32[192]{0:T(256)}, u32[]{:S(2)}) copy-start(f32[192]{0:T(256)} %get-tuple-element.703) | copy-start | bytes 2308
  (180 other events, 559.2 us)
Sparse Core Ops, SparseCore 0:
  9.7 170.9 all-gather.9
  192.4 35.6 all-gather.11
  230.5 38.1 all-gather.13
  270.2 51.7 all-gather.15
  323.4 218.6 all-gather.17
  543.6 114.9 all-gather.19
  864.8 55.2 reduce-scatter.15
  923.1 57.0 reduce-scatter.17
  983.1 24.4 reduce-scatter.27
  1009.7 99.5 reduce-scatter.21
  1111.6 245.5 reduce-scatter.25
  1359.4 363.2 reduce-scatter.19
  1725.2 481.4 reduce-scatter.23
  2209.4 29.8 reduce-scatter.31
  2242.2 30.0 reduce-scatter.29
  2276.2 285.4 all-reduce.4
where the time goes:
time: 2590 us; the launch traced here: 2580 us
  waiting for transfers between devices  1920 us (74%)
  local copies, waits for them, and re-layouts  255 us (10%)
  matrix products  175 us (7%)
  other arithmetic  98.4 us (4%)
  blocking collectives  93 us (4%)
    reduce_scatter x1, waiting for transfers between devices, body(): lax.psum_scatter(gate_up_grad, 'fsdp', scatter_dimension=0, tiled=True)  484 us
    reduce_scatter x1, waiting for transfers between devices, body(): lax.psum_scatter(attn_in_grad, 'fsdp', scatter_dimension=0, tiled=True)  366 us
    psum x1, waiting for transfers between devices, body(): lax.psum((gains_share, in_share, forget_share, out_share, gate_up_share,...  260 us
    reduce_scatter x1, waiting for transfers between devices, body(): lax.psum_scatter(down_grad, 'fsdp', scatter_dimension=0, tiled=True)  248 us
    all_gather x1, waiting for transfers between devices, body(): lax.all_gather(shards[1], 'fsdp', axis=0, tiled=True)  158 us
    all_gather x1, waiting for transfers between devices, body(): lax.all_gather(shards[4], 'fsdp', axis=0, tiled=True)  153 us
    all_gather x1, waiting for transfers between devices, body(): lax.all_gather(shards[5], 'fsdp', axis=0, tiled=True)  102 us
    dot_general x4, matrix products, left_product(): lax.dot_general(left, right, (((0,), (0,)), ((), ())), preferred_element_...  54.3 us
  transfers between devices with their start and end apart: 16, of which 12 were waited for; matrix products, arithmetic and copies ran while one was open for 11% of the time, Pallas kernels for 0%

commit v1 on v0

v1 whole, which is shorter than its diff:
```python
import functools

import jax
import jax.numpy as jnp
from jax import lax
from jax.experimental import pallas as pl
from jax.experimental.pallas import tpu as pltpu
from jax.sharding import PartitionSpec as P

EPS = 1e-06
SCALE = 0.125
LANES = 128
F32 = jnp.float32
BF16 = jnp.bfloat16


def rms_scale(values):
    return lax.rsqrt(jnp.mean(values * values, axis=-1, keepdims=True) + EPS)


def norm_back(grad_normed, values, scale_values, gain_values):
    scaled = grad_normed * gain_values
    cubed = scale_values * scale_values * scale_values
    return scale_values * scaled - values * cubed * jnp.mean(
        scaled * values, axis=-1, keepdims=True
    )


def dot(left, right):
    return lax.dot_general(
        left, right, (((1,), (0,)), ((), ())), preferred_element_type=F32
    )


def left_product(left, right):
    return lax.dot_general(
        left, right, (((0,), (0,)), ((), ())), preferred_element_type=F32
    )


def right_product(left, right):
    return lax.dot_general(
        left, right, (((1,), (1,)), ((), ())), preferred_element_type=F32
    )


def split_three(values):
    high = values.astype(BF16).astype(F32)
    rest = values - high
    middle = rest.astype(BF16).astype(F32)
    return high, middle, rest - middle


def precise_left(zero_one, values):
    high, middle, low = split_three(values)
    total = dot(zero_one, high.astype(BF16))
    total = total + dot(zero_one, middle.astype(BF16))
    return total + dot(zero_one, low.astype(BF16))


def lane_ids(rows, lanes=LANES):
    return lax.broadcasted_iota(jnp.int32, (rows, lanes), 1)


def pick_lane(values, lanes, index):
    return jnp.sum(jnp.where(lanes == index, values, 0.0), axis=-1, keepdims=True)


def attend_kernel(
    head, chunk,
    pos_row, pos_col, seg_row, seg_col, bias, gains, query, key, value, gate, forget,
    gated, attended, wide_query, wide_key, wide_value,
    mask, prefix,
):
    step = pl.program_id(0)
    rows = query.shape[0]
    lanes = lane_ids(rows)
    half = lane_ids(rows, head)

    @pl.when(step == 0)
    def _():
        log_forget = jax.nn.log_sigmoid(forget[...] + bias[0:1, :])
        high, middle, low = split_three(log_forget)
        for start in range(0, rows, chunk):
            part = pl.ds(start, chunk)
            before = pos_row[0:1, :] <= pos_col[part, :]
            same = seg_row[0:1, :] == seg_col[part, :]
            mask[part, :] = jnp.where(before & same, 0.0, -jnp.inf)
            before = jnp.where(before, 1.0, 0.0).astype(BF16)
            prefix[part, :] = (
                dot(before, high.astype(BF16))
                + dot(before, middle.astype(BF16))
                + dot(before, low.astype(BF16))
            )

    for side in range(LANES // head):
        here = pl.ds(side * head, head)
        column = pick_lane(prefix[...], lanes, (LANES // head) * step + side)
        high, middle, low = split_three(column)
        wide = jnp.where(half == 1, high, 0.0)
        wide = jnp.where(half == 2, middle, wide)
        wide = jnp.where(half == 3, low, wide)
        query_rest = jnp.where((half >= 4) & (half < 7), 1.0, wide)
        wide = jnp.where(half == 4, -high, 0.0)
        wide = jnp.where(half == 5, -middle, wide)
        wide = jnp.where(half == 6, -low, wide)
        ones = ((half >= 1) & (half < 4)) | ((half >= 7) & (half < 10))
        key_rest = jnp.where(ones, 1.0, wide)
        raw = query[:, here]
        normed = (raw * rms_scale(raw) * gains[0:1, here]).astype(BF16)
        wide_query[side, :, 0:head] = (normed.astype(F32) * SCALE).astype(BF16)
        wide_query[side, :, head:LANES] = query_rest.astype(BF16)
        raw = key[:, here]
        wide_key[side, :, 0:head] = (raw * rms_scale(raw) * gains[1:2, here]).astype(BF16)
        wide_key[side, :, head:LANES] = key_rest.astype(BF16)
        wide_value[side, :, 0:head] = value[:, here].astype(BF16)
        wide_value[side, :, head:LANES] = jnp.where(half < 3, 1.0, 0.0).astype(BF16)
        for start in range(0, rows, chunk):
            part = pl.ds(start, chunk)
            scores = right_product(wide_query[side, part, :], wide_key[side]) + mask[part, :]
            expos = jnp.exp(scores)
            total = jnp.sum(expos, axis=-1, keepdims=True)
            result = dot(expos.astype(BF16), wide_value[side])[:, 0:head] / total
            attended[part, here] = result
            gated[part, here] = (result * jax.nn.sigmoid(gate[part, here])).astype(BF16)
            high, middle, low = split_three(-jnp.log(total))
            short = half[start : start + chunk]
            rest = query_rest[start : start + chunk]
            rest = jnp.where(short == 7, high, rest)
            rest = jnp.where(short == 8, middle, rest)
            rest = jnp.where(short == 9, low, rest)
            wide_query[side, part, head:LANES] = rest.astype(BF16)


def attend_back_kernel(
    head, chunk, width,
    pos_row, pos_col, seg_row, seg_col, bias, gains, query, key, gate, forget,
    attended, wide_query, wide_key, wide_value, grad_gated,
    grad_project, small,
    mask, wide_grad, grad_query, grad_key, grad_value, grad_prefix,
):
    step = pl.program_id(0)
    steps = pl.num_programs(0)
    rows = query.shape[0]
    lanes = lane_ids(rows)
    half = lane_ids(rows, head)

    @pl.when(step == 0)
    def _():
        for start in range(0, rows, chunk):
            part = pl.ds(start, chunk)
            after = pos_row[0:1, :] >= pos_col[part, :]
            same = seg_row[0:1, :] == seg_col[part, :]
            mask[part, :] = jnp.where(after & same, 0.0, -jnp.inf)
        grad_prefix[...] = jnp.zeros_like(grad_prefix)
        small[...] = jnp.zeros_like(small)

    for side in range(LANES // head):
        here = pl.ds(side * head, head)

        def column(part):
            return pl.ds(pl.multiple_of(part * width + step * LANES, LANES), LANES)

        sig = jax.nn.sigmoid(gate[:, here])
        grad_in = grad_gated[:, here]
        result = attended[:, here]
        grad_result = (grad_in * sig).astype(BF16)
        grad_gate = (grad_in * result * sig * (1.0 - sig)).astype(BF16)
        inner = -jnp.sum(grad_result.astype(F32) * result, axis=-1, keepdims=True)
        high, middle, low = split_three(inner)
        rest = jnp.where(half == 0, high, 0.0)
        rest = jnp.where(half == 1, middle, rest)
        rest = jnp.where(half == 2, low, rest)
        wide_grad[:, 0:head] = grad_result
        wide_grad[:, head:LANES] = rest.astype(BF16)
        grad_query[...] = jnp.zeros_like(grad_query)
        for start in range(0, rows, chunk):
            part = pl.ds(start, chunk)
            scores = right_product(wide_key[side, part, :], wide_query[side]) + mask[part, :]
            probs = jnp.exp(scores)
            outer = right_product(wide_value[side, part, :], wide_grad[...])
            grad_scores = (probs * outer).astype(BF16)
            grad_key[part, :] = dot(grad_scores, wide_query[side])
            grad_value[part, :] = dot(probs.astype(BF16), wide_grad[...])
            grad_query[...] += left_product(grad_scores, wide_key[side, part, :])
        from_query = grad_query[...]
        from_key = grad_key[...]
        change = pick_lane(from_query, lanes, head + 1) - pick_lane(from_key, lanes, head + 4)
        grad_prefix[...] += jnp.where(lanes == (LANES // head) * step + side, change, 0.0)

        raw = query[:, here]
        scale_raw = rms_scale(raw)
        grad_normed = from_query[:, 0:head] * SCALE
        grad_raw_query = norm_back(grad_normed, raw, scale_raw, gains[0:1, here])
        small[0:1, here] += jnp.sum(grad_normed * raw * scale_raw, axis=0, keepdims=True)
        raw = key[:, here]
        scale_raw = rms_scale(raw)
        grad_normed = from_key[:, 0:head]
        grad_raw_key = norm_back(grad_normed, raw, scale_raw, gains[1:2, here])
        small[1:2, here] += jnp.sum(grad_normed * raw * scale_raw, axis=0, keepdims=True)
        wide_grad[:, here] = grad_gate
        for part_id, piece in enumerate(
            (grad_raw_query.astype(BF16), grad_raw_key.astype(BF16), grad_value[:, 0:head].astype(BF16), grad_gate)
        ):
            if side == 0:
                grad_project[:, column(part_id)] = jnp.concatenate([piece, piece], axis=1)
            else:
                keep = grad_project[:, column(part_id)]
                both = jnp.concatenate([piece, piece], axis=1)
                grad_project[:, column(part_id)] = jnp.where(lanes < head, keep, both)

    @pl.when(step == steps - 1)
    def _():
        high, middle, low = split_three(grad_prefix[...])
        logits = forget[...] + bias[0:1, :]
        heads = steps * (LANES // head)
        for start in range(0, rows, chunk):
            part = pl.ds(start, chunk)
            after = jnp.where(pos_row[0:1, :] >= pos_col[part, :], 1.0, 0.0).astype(BF16)
            total = dot(after, high.astype(BF16)) + dot(after, middle.astype(BF16)) + dot(after, low.astype(BF16))
            grad_logit = total * jax.nn.sigmoid(-logits[start : start + chunk])
            grad_logit = jnp.where(lanes[start : start + chunk] < heads, grad_logit, 0.0).astype(BF16)
            grad_project[part, 4 * width : 4 * width + LANES] = grad_logit
            small[2:3, :] += jnp.sum(grad_logit.astype(F32), axis=0, keepdims=True)


def pick_chunk(rows):
    return 256 if rows % 256 == 0 else 192


def whole(shape):
    return pl.BlockSpec(shape, lambda step: tuple(0 for _ in shape))


def attend(project, places, bias, gains, head, width):
    rows = project.shape[0]
    steps = width // LANES
    per = LANES // head
    chunk = pick_chunk(rows)

    def part(index):
        return pl.BlockSpec((rows, LANES), lambda step: (0, index * steps + step))

    own = pl.BlockSpec((rows, LANES), lambda step: (0, step))
    wide = pl.BlockSpec((per, rows, LANES), lambda step: (step, 0, 0))
    forget = pl.BlockSpec((rows, LANES), lambda step: (0, 4 * steps))
    wide_shape = jax.ShapeDtypeStruct((per * steps, rows, LANES), BF16)
    return pl.pallas_call(
        functools.partial(attend_kernel, head, chunk),
        grid=(steps,),
        in_specs=[whole(p.shape) for p in places] + [whole(bias.shape), whole(gains.shape)]
        + [part(0), part(1), part(2), part(3), forget],
        out_specs=[own, own, wide, wide, wide],
        out_shape=[
            jax.ShapeDtypeStruct((rows, width), BF16),
            jax.ShapeDtypeStruct((rows, width), F32),
            wide_shape, wide_shape, wide_shape,
        ],
        scratch_shapes=[pltpu.VMEM((rows, rows), F32), pltpu.VMEM((rows, LANES), F32)],
        compiler_params=pltpu.CompilerParams(vmem_limit_bytes=48 << 20),
        name="attend",
    )(*places, bias, gains, project, project, project, project, project)


def attend_back(project, places, bias, gains, attended, wides, grad_gated, head, width):
    rows = project.shape[0]
    steps = width // LANES
    per = LANES // head
    chunk = pick_chunk(rows)

    def part(index):
        return pl.BlockSpec((rows, LANES), lambda step: (0, index * steps + step))

    own = pl.BlockSpec((rows, LANES), lambda step: (0, step))
    wide = pl.BlockSpec((per, rows, LANES), lambda step: (step, 0, 0))
    forget = pl.BlockSpec((rows, LANES), lambda step: (0, 4 * steps))
    total = 4 * width + LANES
    return pl.pallas_call(
        functools.partial(attend_back_kernel, head, chunk, width),
        grid=(steps,),
        in_specs=[whole(p.shape) for p in places] + [whole(bias.shape), whole(gains.shape)]
        + [part(0), part(1), part(3), forget, own, wide, wide, wide, own],
        out_specs=[whole((rows, total)), whole((8, LANES))],
        out_shape=[
            jax.ShapeDtypeStruct((rows, total), BF16),
            jax.ShapeDtypeStruct((8, LANES), F32),
        ],
        scratch_shapes=[
            pltpu.VMEM((rows, rows), F32),
            pltpu.VMEM((rows, LANES), BF16),
            pltpu.VMEM((rows, LANES), F32),
            pltpu.VMEM((rows, LANES), F32),
            pltpu.VMEM((rows, LANES), F32),
            pltpu.VMEM((rows, LANES), F32),
        ],
        compiler_params=pltpu.CompilerParams(vmem_limit_bytes=48 << 20),
        name="attend_back",
    )(*places, bias, gains, project, project, project, project, attended, *wides, grad_gated)


def body(
    tokens, block_order, segment_ids, norm_gains, attn_in_weight, forget_weight, forget_bias,
    qk_gains, out_weight, gate_up_weight, down_weight, out_grad,
):
    ranks = lax.axis_size("ctx")
    shards = lax.axis_size("fsdp")
    rank = lax.axis_index("ctx")
    row_count, model_width = tokens.shape[1], tokens.shape[2]
    head_count, head_dim = forget_bias.shape[0], qk_gains.shape[1]
    local_heads = head_count // ranks
    width = local_heads * head_dim
    seq_order = block_order[0]
    seq_len = segment_ids.shape[1]
    block_len = seq_len // seq_order.shape[0]
    hidden_all = down_weight.shape[0] * shards
    hidden_piece = down_weight.shape[0] // ranks
    hidden = hidden_piece * shards

    def slab(array, start, size, axis):
        return lax.dynamic_slice_in_dim(array, start, size, axis)

    spare = LANES - local_heads - 2
    in_piece = jnp.concatenate(
        [slab(attn_in_weight, i * model_width + rank * width, width, 1) for i in range(4)]
        + [
            slab(forget_weight, rank * local_heads, local_heads, 1),
            norm_gains.T,
            jnp.zeros((attn_in_weight.shape[0], spare), BF16),
        ],
        axis=1,
    )
    out_piece = slab(out_weight, rank * width, width, 1)
    gate_up_piece = jnp.concatenate(
        [
            slab(gate_up_weight, (i * shards + f) * hidden_piece * ranks + rank * hidden_piece, hidden_piece, 1)
            for i in range(2)
            for f in range(shards)
        ],
        axis=1,
    )
    down_piece = slab(down_weight, rank * hidden_piece, hidden_piece, 0)

    def gather_shards(array):
        return lax.all_gather(array, "fsdp", axis=0, tiled=True)

    w_in = gather_shards(in_piece)
    w_out = gather_shards(out_piece)
    w_gate_up = gather_shards(gate_up_piece)
    w_down = gather_shards(down_piece)

    inputs = lax.all_gather(tokens[0], "ctx", axis=0, tiled=True)
    grad_low = lax.all_gather(out_grad[0], "ctx", axis=0, tiled=True)

    offsets = jnp.arange(seq_len, dtype=jnp.int32)
    places = jnp.take(seq_order, offsets // block_len) * block_len + offsets % block_len
    segments = jnp.take(segment_ids[0], places)
    places_all = (places[None, :], places[:, None], segments[None, :], segments[:, None])
    valid = (segments >= 0).astype(F32)

    bias = jnp.pad(slab(forget_bias, rank * local_heads, local_heads, 0), (0, LANES - local_heads))[None]
    head_gains = jnp.tile(qk_gains, (1, LANES // head_dim))

    gain_cols = w_in[:, 4 * width : 4 * width + LANES].astype(F32).T
    gain_one = gain_cols[local_heads]
    gain_two = gain_cols[local_heads + 1]

    wide_inputs = inputs.astype(F32)
    scale_one = rms_scale(wide_inputs)
    normed = (wide_inputs * scale_one * gain_one).astype(BF16)
    project = dot(normed, w_in)
    gated, attended, wide_query, wide_key, wide_value = attend(
        project, places_all, bias, head_gains, head_dim, width
    )
    gated_all = lax.all_gather(gated, "ctx", axis=1, tiled=True)
    mixed_cols = slab(inputs, rank * width, width, 1).astype(F32) + dot(gated_all, w_out)
    mixed = lax.all_gather(mixed_cols.astype(BF16), "ctx", axis=1, tiled=True).astype(F32)
    scale_two = rms_scale(mixed)
    normed_two = (mixed * scale_two * gain_two).astype(BF16)
    gate_up = dot(normed_two, w_gate_up)
    gate_part, up_part = gate_up[:, :hidden], gate_up[:, hidden:]
    gate_sigmoid = jax.nn.sigmoid(gate_part)
    silu = gate_part * gate_sigmoid
    hidden_act = (silu * up_part).astype(BF16)
    down_sum = lax.psum_scatter(
        dot(hidden_act, w_down).astype(BF16), "ctx", scatter_dimension=0, tiled=True
    ).astype(F32)

    def own_rows(array):
        return slab(array, rank * row_count, row_count, 0)

    result = own_rows(mixed) + down_sum
    block_out = result.astype(BF16)[None]
    branch = result - own_rows(wide_inputs)
    own_valid = own_rows(valid)
    partial_sums = jnp.stack(
        [
            jnp.sum(own_valid * jnp.sum(result * result, axis=-1)),
            jnp.sum(own_valid * jnp.sum(branch * branch, axis=-1)),
        ]
    )
    valid_count = jnp.sum(valid) * model_width

    grad_hidden = right_product(grad_low, w_down)
    grad_gate = grad_hidden * up_part * gate_sigmoid * (1.0 + gate_part * (1.0 - gate_sigmoid))
    grad_gate_up = jnp.concatenate([grad_gate, grad_hidden * silu], axis=1).astype(BF16)
    grad_normed_two = right_product(grad_gate_up, w_gate_up)
    gain_two_grad = jnp.sum(grad_normed_two * mixed * scale_two, axis=0)
    grad_mixed_part = norm_back(grad_normed_two, mixed, scale_two, gain_two).astype(BF16)
    grad_mixed_cols = slab(grad_low, rank * width, width, 1).astype(F32) + lax.psum_scatter(
        grad_mixed_part, "ctx", scatter_dimension=1, tiled=True
    ).astype(F32)
    grad_branch = grad_mixed_cols.astype(BF16)
    grad_gated = lax.psum_scatter(
        right_product(grad_branch, w_out).astype(BF16), "ctx", scatter_dimension=1, tiled=True
    ).astype(F32)
    grad_project, small = attend_back(
        project, places_all, bias, head_gains, attended, (wide_query, wide_key, wide_value),
        grad_gated, head_dim, width,
    )
    grad_normed = right_product(grad_project, w_in)
    gain_one_grad = jnp.sum(grad_normed * wide_inputs * scale_one, axis=0)
    in_own = jnp.arange(model_width, dtype=jnp.int32) // width == rank
    grad_inputs = norm_back(grad_normed, wide_inputs, scale_one, gain_one) + jnp.where(
        in_own[None], jnp.tile(grad_mixed_cols, (1, ranks)), 0.0
    )
    tokens_grad = lax.psum_scatter(grad_inputs.astype(BF16), "ctx", scatter_dimension=0, tiled=True)[None]

    def reduce_shards(array):
        return lax.psum_scatter(array.astype(BF16), "fsdp", scatter_dimension=0, tiled=True)

    def gather_ranks(array):
        return lax.all_gather(array, "ctx", axis=0, tiled=False).astype(F32)

    down_own = gather_ranks(reduce_shards(left_product(hidden_act, grad_low)))
    down_out = down_own.reshape(down_weight.shape)
    gate_up_own = gather_ranks(reduce_shards(left_product(normed_two, grad_gate_up)))
    gate_up_out = jnp.concatenate(
        [
            gate_up_own[c, :, (i * shards + f) * hidden_piece : (i * shards + f + 1) * hidden_piece]
            for i in range(2)
            for f in range(shards)
            for c in range(ranks)
        ],
        axis=1,
    )
    out_own = gather_ranks(reduce_shards(left_product(gated_all, grad_branch)))
    out_out = jnp.concatenate([out_own[c] for c in range(ranks)], axis=1)
    in_own = gather_ranks(reduce_shards(left_product(normed, grad_project)))
    in_out = jnp.concatenate(
        [in_own[c, :, i * width : (i + 1) * width] for i in range(4) for c in range(ranks)], axis=1
    )
    forget_out = jnp.concatenate([in_own[c, :, 4 * width : 4 * width + local_heads] for c in range(ranks)], axis=1)
    gains_sum = lax.psum_scatter(
        jnp.stack([gain_one_grad, gain_two_grad]), "fsdp", scatter_dimension=1, tiled=True
    )
    gains_sum, partial_sums = lax.psum((gains_sum, partial_sums), "ctx")
    bias_slots = jnp.where(
        jnp.arange(ranks, dtype=jnp.int32)[:, None] == rank, small[2, :local_heads][None], 0.0
    ).reshape(-1)
    qk_sum = small[0:2].reshape(2, LANES // head_dim, head_dim).sum(axis=1)
    bias_sum, qk_sum = lax.psum((bias_slots, qk_sum), ("ctx", "fsdp"))
    return (
        block_out, tokens_grad, gains_sum, in_out, forget_out, bias_sum, qk_sum,
        out_out, gate_up_out, down_out, jnp.sqrt(partial_sums / valid_count)[None],
    )


def solution(mesh):
    rows = P("fsdp", "ctx", None)
    return jax.shard_map(
        body,
        mesh=mesh,
        in_specs=(
            rows, P("fsdp", None), P("fsdp", None), P(None, "fsdp"), P("fsdp", None), P("fsdp", None),
            P(), P(), P("fsdp", None), P("fsdp", None), P("fsdp", None), rows,
        ),
        out_specs=(
            rows, rows, P(None, "fsdp"), P("fsdp", None), P("fsdp", None), P(), P(),
            P("fsdp", None), P("fsdp", None), P("fsdp", None), P("fsdp", None),
        ),
        check_vma=False,
    )
```

time: 2590 us -> 933 us (0.36)
  waiting for transfers between devices: 1920 us -> 520 us
  local copies, waits for them, and re-layouts: 255 us -> 132 us
  matrix products: 175 us -> 93 us
  other arithmetic: 98.4 us -> 52.8 us
  Pallas kernels: 0 us -> 43.4 us
  blocking collectives: 93 us -> 63 us
    reduce_scatter x6, waiting for transfers between devices: 1210 us -> 166 us  [the longest x4 137 us: reduce_shards(): lax.psum_scatter(array.astype(BF16), 'fsdp', scatter_dimension=0, tiled=T...]
    psum x1 -> x0, waiting for transfers between devices: 260 us -> none  [body(): lax.psum((gains_share, in_share, forget_share, out_share, gate_up_share,...]
    all_gather x6 -> x11, waiting for transfers between devices: 418 us -> 294 us  [the longest x4 160 us: gather_shards(): return lax.all_gather(array, 'fsdp', axis=0, tiled=True)]
    unnamed x166 -> x161, local copies, waits for them, and re-layouts: 37.6 us -> 114 us
    dynamic_slice x97 -> x6, local copies, waits for them, and re-layouts: 75.1 us -> 4.51 us  [slab(): return lax.dynamic_slice_in_dim(array, start, size, axis)]
    pallas_call x0 -> x2, Pallas kernels: none -> 43.4 us  [the longest x1 28 us: attend_back(): pl.pallas_call(functools.partial(attend_back_kernel, head, chunk, width),...]
    dot_general x89 -> x4, matrix products: 72.5 us -> 30.2 us  [dot(): lax.dot_general(left, right, (((1,), (0,)), ((), ())), preferred_element_...]
    dynamic_update_slice x73 -> x0, local copies, waits for them, and re-layouts: 38.2 us -> none  [the longest x24 13.1 us: attend_back(): lax.dynamic_update_slice_in_dim(values_acc, grad_value, start, 1)]
  transfers between devices with their start and end apart: 16 -> 20, of which waited for: 12 -> 16; matrix products, arithmetic and copies ran while one was open for 11% -> 25% of each run, Pallas kernels for 0% -> 5%
where the time goes in v1:
time: 933 us; the launch traced here: 921 us
  waiting for transfers between devices  520 us (56%)
  local copies, waits for them, and re-layouts  132 us (14%)
  matrix products  93 us (10%)
  blocking collectives  63 us (7%)
  other arithmetic  52.8 us (6%)
  Pallas kernels  43.4 us (5%)
  between operations  15.9 us (2%)
    all_gather x4, waiting for transfers between devices, gather_shards(): return lax.all_gather(array, 'fsdp', axis=0, tiled=True)  160 us
    reduce_scatter x4, waiting for transfers between devices, reduce_shards(): lax.psum_scatter(array.astype(BF16), 'fsdp', scatter_dimension=0, tiled=T...  137 us
    unnamed x161, local copies, waits for them, and re-layouts  114 us
    unnamed x23, waiting for transfers between devices  59.2 us
    psum x1, blocking collectives, body(): bias_sum, qk_sum = lax.psum((bias_slots, qk_sum), ('ctx', 'fsdp'))  39.7 us
    all_gather x1, waiting for transfers between devices, body(): gated_all = lax.all_gather(gated, 'ctx', axis=1, tiled=True)  36 us
    dot_general x4, matrix products, right_product(): lax.dot_general(left, right, (((1,), (1,)), ((), ())), preferred_element_...  33.9 us
    all_gather x3, waiting for transfers between devices, gather_ranks(): return lax.all_gather(array, 'ctx', axis=0, tiled=False).astype(F32)  33.8 us
  transfers between devices with their start and end apart: 20, of which 16 were waited for; matrix products, arithmetic and copies ran while one was open for 25% of the time, Pallas kernels for 5%

profile of v1, /device:TPU:0, one launch (start us, length us, event | category | flops | bytes accessed | tf_op | source)
XLA Modules:
  0.0 921.3 jit_solution(10401377319169765010)
XLA Ops:
  16.2 4.9 select_reduce_fusion
  26.0 24.1 %all-gather.30.cloned.1.call-done = bf16[1,768,1536]{2,1,0:T(8,128)(2,1)} async-done(((bf16[1,192,1536]{2,1,0:T(8,128)(2,1)}), bf16[1,768,1536]{2,1,0:T(8,128)(2,1)}) %all-gather.30.cloned.1.call-update) | async-done | bytes 2359312 | tf_op jit(solution)/shard_map/all_gather | solution.py:351
  52.9 54.4 %all-gather.18.cloned.1.call-done = bf16[1536,1664]{1,0:T(8,128)(2,1)} async-done(((bf16[192,1664]{1,0:T(8,128)(2,1)}), bf16[1536,1664]{1,0:T(8,128)(2,1)}) %all-gather.18.cloned.1.call-update) | async-done | bytes 5111824 | tf_op jit(solution)/shard_map/all_gather | solution.py:344
  109.7 9.9 %fusion.36.query.key.value.gate.forget = f32[768,1664]{1,0:T(8,128)} fusion(bf16[1536,1664]{1,0:T(8,128)(2,1)} %all-gather.18.cloned.1.call-done, bf16[1,768,1536]{2,1,0:T(8,128)(2,1)} %all-gather.30.cloned.1.call-done, f32[1536]{0:T(1024)S(1)} %get-tuple-element.32, f32[768]{0:T(1024)S(1)} %get-tuple-element.60), kind=kOutput, calls=%fused_computation.71 | convolution fusion | flops 3930587136 | bytes 12592128 | tf_op jit(solution)/shard_map/dot_general | solution.py:30
  119.6 15.4 %attend.1 = (bf16[768,384]{1,0:T(8,128)(2,1)S(1)}, f32[768,384]{1,0:T(8,128)S(1)}, bf16[6,768,128]{2,1,0:T(8,128)(2,1)S(1)}, bf16[6,768,128]{2,1,0:T(8,128)(2,1)S(1)}, bf16[6,768,128]{2,1,0:T(8,128)(2,1)S(1)}) custom-call(s32[1,768]{1,0:T(1,128)S(1)} %get-tuple-element.42.pos_row, s32[768,1]{1,0:T(8,128)S(1)} %get-tuple-element.64.pos_col, ...), custom_call_target="tpu_custom_call" | custom-call | tf_op jit(solution)/shard_map/attend/pallas_call | solution.py:248
  139.2 36.0 %all-gather.20.cloned.1.call-done = bf16[768,1536]{1,0:T(8,128)(2,1)} async-done(((bf16[768,384]{1,0:T(8,128)(2,1)}), bf16[768,1536]{1,0:T(8,128)(2,1)}) %all-gather.20.cloned.1.call-update) | async-done | bytes 2359312 | tf_op jit(solution)/shard_map/all_gather | solution.py:374
  204.0 13.0 %all-gather.24.cloned.1.call-done = bf16[768,1536]{1,0:T(8,128)(2,1)} async-done(((bf16[768,384]{1,0:T(8,128)(2,1)}), bf16[768,1536]{1,0:T(8,128)(2,1)}) %all-gather.24.cloned.1.call-update) | async-done | bytes 2359312 | tf_op jit(solution)/shard_map/all_gather | solution.py:376
  219.3 64.7 %all-gather.26.cloned.1.call-done = bf16[1536,2048]{1,0:T(8,128)(2,1)} async-done(((bf16[192,2048]{1,0:T(8,128)(2,1)}), bf16[1536,2048]{1,0:T(8,128)(2,1)}) %all-gather.26.cloned.1.call-update) | async-done | bytes 6291472 | tf_op jit(solution)/shard_map/all_gather | solution.py:344
  283.9 10.3 %fusion.39 = f32[768,2048]{1,0:T(8,128)} fusion(bf16[1536,2048]{1,0:T(8,128)(2,1)} %all-gather.26.cloned.1.call-done, bf16[768,1536]{1,0:T(8,128)(2,1)} %all-gather.24.cloned.1.call-done, f32[1536]{0:T(1024)} %get-tuple-element.31, f32[768]{0:T(1024)S(1)} %get-tuple-element.62), kind=kOutput, calls=%fused_computation.72 | convolution fusion | flops 4836556800 | bytes 14951424 | tf_op jit(solution)/shard_map/dot_general | solution.py:30
  294.2 27.7 %all-gather.32.cloned.1.call-done = bf16[1,768,1536]{2,1,0:T(8,128)(2,1)} async-done(((bf16[1,192,1536]{2,1,0:T(8,128)(2,1)}), bf16[1,768,1536]{2,1,0:T(8,128)(2,1)}) %all-gather.32.cloned.1.call-update) | async-done | bytes 2359312 | tf_op jit(solution)/shard_map/all_gather | solution.py:352
  321.9 40.5 %all-gather.28.cloned.1.call-done = bf16[1024,1536]{1,0:T(8,128)(2,1)} async-done(((bf16[128,1536]{1,0:T(8,128)(2,1)}), bf16[1024,1536]{1,0:T(8,128)(2,1)}) %all-gather.28.cloned.1.call-update) | async-done | bytes 3145744 | tf_op jit(solution)/shard_map/all_gather | solution.py:344
  362.5 9.5 %fusion.21 = (bf16[768,1024]{1,0:T(8,128)(2,1)S(1)}, bf16[768,1024]{1,0:T(8,128)(2,1)S(1)}, bf16[768,1024]{1,0:T(8,128)(2,1)}) fusion(f32[768,2048]{1,0:T(8,128)} %fusion.39, bf16[1024,1536]{1,0:T(8,128)(2,1)} %all-gather.28.cloned.1.call-done, bf16[1,768,1536]{2,1,0:T(8,128)(2,1)} %all-gather.32.cloned.1.call-done), kind=kOutput, calls=%fused_computation.40 | convolution fusion | flops 2427715584 | bytes 16515072 | tf_op jit(solution)/shard_map/dot_general | solution.py:42
  371.9 9.0 fusion.8
  388.0 36.0 %reduce-scatter.28.cloned.1.call-done = bf16[384,768]{1,0:T(8,128)(2,1)} async-done(((bf16[1536,768]{1,0:T(8,128)(2,1)}), bf16[384,768]{1,0:T(8,128)(2,1)}) %reduce-scatter.28.cloned.1.call-update) | async-done | bytes 589840
  436.3 6.5 convolution_convert_fusion.2
  442.8 9.6 %convolution_convert_fusion = bf16[1536,2048]{1,0:T(8,128)(2,1)} fusion(bf16[768,1024]{1,0:T(8,128)(2,1)} %copy-done.27, bf16[768,1024]{1,0:T(8,128)(2,1)} %copy-done.26, bf16[768,1536]{1,0:T(8,128)(2,1)} %all-gather.24.cloned.1.call-done, f32[1536]{0:T(1024)S(1)} %copy-done.19, f32[768]{0:T(1024)S(1)} %get-tuple-element.62), kind=kOutput, calls=%fused_computation.1 | convolution fusion | flops 4845993984 | bytes 11805696 | tf_op jit(solution)/shard_map/dot_general | solution.py:36
  452.7 21.1 %reduce-scatter.30.cloned.1.call-done = bf16[384,768]{1,0:T(8,128)(2,1)} async-done(((bf16[1536,768]{1,0:T(8,128)(2,1)}), bf16[384,768]{1,0:T(8,128)(2,1)}) %reduce-scatter.30.cloned.1.call-update) | async-done | bytes 589840
  480.6 28.0 %attend_back.1 = (bf16[768,1664]{1,0:T(8,128)(2,1)}, f32[8,128]{1,0:T(8,128)S(1)}) custom-call(s32[1,768]{1,0:T(1,128)S(1)} %get-tuple-element.42.pos_row, s32[768,1]{1,0:T(8,128)S(1)} %get-tuple-element.64.pos_col, s32[1,768]{1,0:T(1,128)S(1)} %get-tuple-element.41.seg_row, s32[768,1]{1,0:T(8,128)S(1)} %get-tuple-element.63.seg_col, ...), custom_call_target="tpu_custom_call" | custom-call | tf_op jit(solution)/shard_map/attend_back/pallas_call | solution.py:278
  508.6 8.3 convolution_convert_fusion.1
  518.3 5.7 convolution_convert_fusion.3
  524.1 4.6 convolution_convert_fusion.5
  529.3 10.9 %fusion.18 = (f32[1536]{0:T(1024)S(1)}, f32[768]{0:T(1024)S(1)}, f32[768,1536]{1,0:T(8,128)}) fusion(bf16[1,768,1536]{2,1,0:T(8,128)(2,1)} %all-gather.30.cloned.1.call-done, f32[768]{0:T(1024)S(1)} %copy-done.22, f32[1536]{0:T(1024)S(1)} %copy-done.18, bf16[768,1664]{1,0:T(8,128)(2,1)} %get-tuple-element.23, ...), kind=kOutput, calls=%fused_computation.31 | convolution fusion | flops 3934123776 | bytes 14764032 | tf_op jit(solution)/shard_map/dot_general | solution.py:42
  541.6 47.2 %reduce-scatter.24.cloned.1.call-done = bf16[192,2048]{1,0:T(8,128)(2,1)} async-done(((bf16[1536,2048]{1,0:T(8,128)(2,1)}), bf16[192,2048]{1,0:T(8,128)(2,1)}) %reduce-scatter.24.cloned.1.call-update) | async-done | bytes 786448 | tf_op jit(solution)/shard_map/reduce_scatter | solution.py:429
  588.8 59.3 %reduce-scatter.20.cloned.1.call-done = bf16[192,1664]{1,0:T(8,128)(2,1)} async-done(((bf16[1536,1664]{1,0:T(8,128)(2,1)}), bf16[192,1664]{1,0:T(8,128)(2,1)}) %reduce-scatter.20.cloned.1.call-update) | async-done | bytes 638992 | tf_op jit(solution)/shard_map/reduce_scatter | solution.py:429
  661.8 25.3 %reduce-scatter.16.cloned.1.call-done = bf16[192,1536]{1,0:T(8,128)(2,1)} async-done(((bf16[768,1536]{1,0:T(8,128)(2,1)}), bf16[192,1536]{1,0:T(8,128)(2,1)}) %reduce-scatter.16.cloned.1.call-update) | async-done | bytes 589840 | tf_op jit(solution)/shard_map/reduce_scatter | solution.py:384
  691.9 30.8 %reduce-scatter.22.cloned.1.call-done = bf16[192,384]{1,0:T(8,128)(2,1)} async-done(((bf16[1536,384]{1,0:T(8,128)(2,1)}), bf16[192,384]{1,0:T(8,128)(2,1)}) %reduce-scatter.22.cloned.1.call-update) | async-done | bytes 147472 | tf_op jit(solution)/shard_map/reduce_scatter | solution.py:429
  722.7 11.6 %all-gather.3 = bf16[768,384]{1,0:T(8,128)(2,1)S(1)} all-gather(bf16[192,384]{1,0:T(8,128)(2,1)} %reduce-scatter.22.cloned.1.call-done), channel_id=5, replica_groups=mesh['ctx'=4,'fsdp'=8] {'ctx'}, dimensions={0}, use_global_device_ids=true | all-gather | bytes 737280 | tf_op jit(solution)/shard_map/all_gather | solution.py:432
  735.5 18.2 %all-gather.38.cloned.1.call-done = bf16[512,1536]{1,0:T(8,128)(2,1)} async-done(((bf16[128,1536]{1,0:T(8,128)(2,1)}), bf16[512,1536]{1,0:T(8,128)(2,1)}) %all-gather.38.cloned.1.call-update) | async-done | bytes 1572880 | tf_op jit(solution)/shard_map/all_gather | solution.py:432
  757.5 6.3 fusion.15
  763.8 39.7 %all-reduce.1 = (f32[24]{0:T(128)}, f32[2,64]{1,0:T(2,128)}) all-reduce(f32[24]{0:T(128)S(1)} %select_n.351, f32[2,64]{1,0:T(2,128)S(1)} %reduce_sum.114), channel_id=1, replica_groups=mesh['ctx'=4,'fsdp'=8] {'ctx','fsdp'}, use_global_device_ids=true, to_apply=%region_13.14 | all-reduce | flops 152 | bytes 1216 | tf_op jit(solution)/shard_map/psum | solution.py:461
  804.5 11.7 %all-reduce.2 = (f32[2,192]{1,0:T(2,128)}, f32[2]{0:T(128)S(1)}) all-reduce(f32[2,192]{1,0:T(2,128)S(1)} %copy.54, f32[2]{0:T(128)S(1)} %pad_maximum_fusion.6), channel_id=1, replica_groups=mesh['ctx'=4,'fsdp'=8] {'ctx'}, use_global_device_ids=true, to_apply=%region_11.12 | all-reduce | flops 386 | bytes 3088 | tf_op jit(solution)/shard_map/psum | solution.py:456
  816.6 15.6 %all-gather.36.cloned.1.call-done = bf16[768,2048]{1,0:T(8,128)(2,1)} async-done(((bf16[192,2048]{1,0:T(8,128)(2,1)}), bf16[768,2048]{1,0:T(8,128)(2,1)}) %all-gather.36.cloned.1.call-update) | async-done | bytes 3145744 | tf_op jit(solution)/shard_map/all_gather | solution.py:432
  (268 shorter events, 190.0 us)
Async XLA Ops:
  7.2 196.0 %copy-start = (bf16[512,1536]{1,0:T(8,128)(2,1)S(1)}, bf16[512,1536]{1,0:T(8,128)(2,1)}, u32[]{:S(2)}) copy-start(bf16[512,1536]{1,0:T(8,128)(2,1)} %param.22) | copy-start | bytes 4718596
  7.2 18.7 %copy-start.23 = (f32[2,64]{1,0:T(2,128)S(1)}, f32[2,64]{1,0:T(2,128)}, u32[]{:S(2)}) copy-start(f32[2,64]{1,0:T(2,128)} %param.19) | copy-start | bytes 1540
  7.2 42.9 %all-gather.30.cloned.1.call-start = ((), (), s32[]{:S(2)}) async-start(), calls=%async_computation.21 | async-start | bytes 2949120 | tf_op jit(solution)/shard_map/all_gather | solution.py:351
  7.9 99.4 %all-gather.18.cloned.1.call-start = ((), (), s32[]{:S(2)}) async-start(), calls=%async_computation.9 | async-start | bytes 5750784 | tf_op jit(solution)/shard_map/all_gather | solution.py:344
  12.0 127.2 %all-gather.22.cloned.1.call-start = ((), (), s32[]{:S(2)}) async-start(), calls=%async_computation.11 | async-start | bytes 1327104 | tf_op jit(solution)/shard_map/all_gather | solution.py:344
  13.6 161.5 %all-gather.20.cloned.1.call-start = ((), (), s32[]{:S(2)}) async-start(), calls=%async_computation.10 | async-start | bytes 2949120 | tf_op jit(solution)/shard_map/all_gather | solution.py:374
  52.9 66.7 %copy-start.21 = (f32[768]{0:T(1024)}, f32[768]{0:T(1024)S(1)}, u32[]{:S(2)}) copy-start(f32[768]{0:T(1024)S(1)} %get-tuple-element.60) | copy-start | bytes 9220
  138.9 78.2 %all-gather.24.cloned.1.call-start = ((), (), s32[]{:S(2)}) async-start(), calls=%async_computation.12 | async-start | bytes 2949120 | tf_op jit(solution)/shard_map/all_gather | solution.py:376
  179.5 104.4 %all-gather.26.cloned.1.call-start = ((), (), s32[]{:S(2)}) async-start(), calls=%async_computation.13 | async-start | bytes 7077888 | tf_op jit(solution)/shard_map/all_gather | solution.py:344
  202.4 119.6 %all-gather.32.cloned.1.call-start = ((), (), s32[]{:S(2)}) async-start(), calls=%async_computation.22 | async-start | bytes 2949120 | tf_op jit(solution)/shard_map/all_gather | solution.py:352
  203.1 159.3 %all-gather.28.cloned.1.call-start = ((), (), s32[]{:S(2)}) async-start(), calls=%async_computation.14 | async-start | bytes 3538944 | tf_op jit(solution)/shard_map/all_gather | solution.py:344
  204.0 220.0 %reduce-scatter.28.cloned.1.call-start = ((), (), s32[]{:S(2)}) async-start(), calls=%async_computation.26 | async-start | bytes 2949120
  294.2 77.7 %copy-start.19 = (f32[1536]{0:T(1024)S(1)}, f32[1536]{0:T(1024)}, u32[]{:S(2)}) copy-start(f32[1536]{0:T(1024)} %get-tuple-element.31) | copy-start | bytes 18436
  387.5 86.3 %reduce-scatter.30.cloned.1.call-start = ((), (), s32[]{:S(2)}) async-start(), calls=%async_computation.27 | async-start | bytes 2949120
  436.3 92.5 %reduce-scatter.26.cloned.1.call-start = ((), (), s32[]{:S(2)}) async-start(), calls=%async_computation.20 | async-start | bytes 3538944 | tf_op jit(solution)/shard_map/reduce_scatter | solution.py:429
  442.8 145.9 %reduce-scatter.24.cloned.1.call-start = ((), (), s32[]{:S(2)}) async-start(), calls=%async_computation.19 | async-start | bytes 7077888 | tf_op jit(solution)/shard_map/reduce_scatter | solution.py:429
  452.5 25.6 %copy-start.3 = (bf16[6,768,128]{2,1,0:T(8,128)(2,1)S(1)}, bf16[6,768,128]{2,1,0:T(8,128)(2,1)}, u32[]{:S(2)}) copy-start(bf16[6,768,128]{2,1,0:T(8,128)(2,1)} %copy-done.2) | copy-start | bytes 3538948
  452.5 195.6 %reduce-scatter.20.cloned.1.call-start = ((), (), s32[]{:S(2)}) async-start(), calls=%async_computation.17 | async-start | bytes 5750784 | tf_op jit(solution)/shard_map/reduce_scatter | solution.py:429
  480.6 28.0 %copy-start.9 = (bf16[1,768,1536]{2,1,0:T(8,128)(2,1)S(1)}, bf16[1,768,1536]{2,1,0:T(8,128)(2,1)}, u32[]{:S(2)}) copy-start(bf16[1,768,1536]{2,1,0:T(8,128)(2,1)} %all-gather.30.cloned.1.call-done) | copy-start | bytes 7077892
  480.6 28.0 %copy-start.18 = (f32[1536]{0:T(1024)S(1)}, f32[1536]{0:T(1024)}, u32[]{:S(2)}) copy-start(f32[1536]{0:T(1024)} %copy-done.17) | copy-start | bytes 18436
  480.6 28.0 %copy-start.22 = (f32[768]{0:T(1024)S(1)}, f32[768]{0:T(1024)}, u32[]{:S(2)}) copy-start(f32[768]{0:T(1024)} %copy-done.21) | copy-start | bytes 9220
  516.9 170.2 %reduce-scatter.16.cloned.1.call-start = ((), (), s32[]{:S(2)}) async-start(), calls=%async_computation.15 | async-start | bytes 2949120 | tf_op jit(solution)/shard_map/reduce_scatter | solution.py:384
  524.0 198.7 %reduce-scatter.22.cloned.1.call-start = ((), (), s32[]{:S(2)}) async-start(), calls=%async_computation.18 | async-start | bytes 1327104 | tf_op jit(solution)/shard_map/reduce_scatter | solution.py:429
  528.7 225.0 %all-gather.38.cloned.1.call-start = ((), (), s32[]{:S(2)}) async-start(), calls=%async_computation.25 | async-start | bytes 1966080 | tf_op jit(solution)/shard_map/all_gather | solution.py:432
  529.3 274.2 %reduce-scatter.32.cloned.1.call-start = ((), (), s32[]{:S(2)}) async-start(), calls=%async_computation.28 | async-start | bytes 884736
  529.3 118.9 %copy-start.14 = (s32[768]{0:T(1024)S(1)}, s32[768]{0:T(1024)}, u32[]{:S(2)}) copy-start(s32[768]{0:T(1024)} %copy-done.13) | copy-start | bytes 9220
  529.3 118.9 %copy-start.16 = (s32[768]{0:T(1024)S(1)}, s32[768]{0:T(1024)}, u32[]{:S(2)}) copy-start(s32[768]{0:T(1024)} %copy-done.15) | copy-start | bytes 9220
  541.5 290.7 %all-gather.36.cloned.1.call-start = ((), (), s32[]{:S(2)}) async-start(), calls=%async_computation.24 | async-start | bytes 3932160 | tf_op jit(solution)/shard_map/all_gather | solution.py:432
  588.8 288.0 %all-gather.34.cloned.1.call-start = ((), (), s32[]{:S(2)}) async-start(), calls=%async_computation.23 | async-start | bytes 3194880 | tf_op jit(solution)/shard_map/all_gather | solution.py:432
  648.1 265.9 %reduce-scatter.18.cloned.1.call-start = ((), (), s32[]{:S(2)}) async-start(), calls=%async_computation.16 | async-start | bytes 2949120 | tf_op jit(solution)/shard_map/reduce_scatter | solution.py:426
  690.6 66.9 %copy-start.20 = (f32[768]{0:T(1024)S(1)}, f32[768]{0:T(1024)}, u32[]{:S(2)}) copy-start(f32[768]{0:T(1024)} %get-tuple-element.59) | copy-start | bytes 9220
  881.1 32.9 %copy-start.1 = (bf16[512,1536]{1,0:T(8,128)(2,1)S(1)}, bf16[512,1536]{1,0:T(8,128)(2,1)}, u32[]{:S(2)}) copy-start(bf16[512,1536]{1,0:T(8,128)(2,1)} %param.22) | copy-start | bytes 4718596
  (16 other events, 84.4 us)
Sparse Core Ops, SparseCore 0:
  9.9 40.1 all-gather.29
  52.3 54.9 all-gather.17
  109.5 21.4 all-gather.21
  139.0 36.1 all-gather.19
  179.6 37.3 all-gather.23
  219.1 64.7 all-gather.25
  285.8 36.1 all-gather.31
  324.1 38.2 all-gather.27
  387.6 36.2 reduce-scatter.27
  436.4 37.3 reduce-scatter.29
  476.7 40.3 reduce-scatter.25
  519.8 68.8 reduce-scatter.23
  591.1 57.0 reduce-scatter.19
  651.3 35.7 reduce-scatter.15
  689.9 32.7 reduce-scatter.21
  724.5 29.1 all-gather.37
  755.9 31.5 reduce-scatter.31
  789.3 42.9 all-gather.35
  834.0 39.0 all-gather.33
  876.6 37.3 reduce-scatter.17

commit v2 on v1

--- a/solution.py
+++ b/solution.py
@@ -67,7 +67,7 @@
 
 
 def attend_kernel(
-    head, chunk,
+    head, chunk, heads,
     pos_row, pos_col, seg_row, seg_col, bias, gains, query, key, value, gate, forget,
     gated, attended, wide_query, wide_key, wide_value,
     mask, prefix,
@@ -79,10 +79,11 @@
 
     @pl.when(step == 0)
     def _():
-        log_forget = jax.nn.log_sigmoid(forget[...] + bias[0:1, :])
+        log_forget = jax.nn.log_sigmoid(jnp.where(lanes < heads, forget[...] + bias[0:1, :], 0.0))
         high, middle, low = split_three(log_forget)
-        for start in range(0, rows, chunk):
-            part = pl.ds(start, chunk)
+        @pl.loop(0, rows // chunk)
+        def _(turn):
+            part = pl.ds(pl.multiple_of(turn * chunk, chunk), chunk)
             before = pos_row[0:1, :] <= pos_col[part, :]
             same = seg_row[0:1, :] == seg_col[part, :]
             mask[part, :] = jnp.where(before & same, 0.0, -jnp.inf)
@@ -115,8 +116,11 @@
         wide_key[side, :, head:LANES] = key_rest.astype(BF16)
         wide_value[side, :, 0:head] = value[:, here].astype(BF16)
         wide_value[side, :, head:LANES] = jnp.where(half < 3, 1.0, 0.0).astype(BF16)
-        for start in range(0, rows, chunk):
-            part = pl.ds(start, chunk)
+        short = lane_ids(chunk, head)
+
+        @pl.loop(0, rows // chunk)
+        def _(turn):
+            part = pl.ds(pl.multiple_of(turn * chunk, chunk), chunk)
             scores = right_product(wide_query[side, part, :], wide_key[side]) + mask[part, :]
             expos = jnp.exp(scores)
             total = jnp.sum(expos, axis=-1, keepdims=True)
@@ -124,8 +128,7 @@
             attended[part, here] = result
             gated[part, here] = (result * jax.nn.sigmoid(gate[part, here])).astype(BF16)
             high, middle, low = split_three(-jnp.log(total))
-            short = half[start : start + chunk]
-            rest = query_rest[start : start + chunk]
+            rest = wide_query[side, part, head:LANES].astype(F32)
             rest = jnp.where(short == 7, high, rest)
             rest = jnp.where(short == 8, middle, rest)
             rest = jnp.where(short == 9, low, rest)
@@ -133,7 +136,7 @@
 
 
 def attend_back_kernel(
-    head, chunk, width,
+    head, chunk, width, heads,
     pos_row, pos_col, seg_row, seg_col, bias, gains, query, key, gate, forget,
     attended, wide_query, wide_key, wide_value, grad_gated,
     grad_project, small,
@@ -147,8 +150,9 @@
 
     @pl.when(step == 0)
     def _():
-        for start in range(0, rows, chunk):
-            part = pl.ds(start, chunk)
+        @pl.loop(0, rows // chunk)
+        def _(turn):
+            part = pl.ds(pl.multiple_of(turn * chunk, chunk), chunk)
             after = pos_row[0:1, :] >= pos_col[part, :]
             same = seg_row[0:1, :] == seg_col[part, :]
             mask[part, :] = jnp.where(after & same, 0.0, -jnp.inf)
@@ -174,8 +178,9 @@
         wide_grad[:, 0:head] = grad_result
         wide_grad[:, head:LANES] = rest.astype(BF16)
         grad_query[...] = jnp.zeros_like(grad_query)
-        for start in range(0, rows, chunk):
-            part = pl.ds(start, chunk)
+        @pl.loop(0, rows // chunk)
+        def _(turn):
+            part = pl.ds(pl.multiple_of(turn * chunk, chunk), chunk)
             scores = right_product(wide_key[side, part, :], wide_query[side]) + mask[part, :]
             probs = jnp.exp(scores)
             outer = right_product(wide_value[side, part, :], wide_grad[...])
@@ -212,27 +217,28 @@
     @pl.when(step == steps - 1)
     def _():
         high, middle, low = split_three(grad_prefix[...])
-        logits = forget[...] + bias[0:1, :]
-        heads = steps * (LANES // head)
-        for start in range(0, rows, chunk):
-            part = pl.ds(start, chunk)
+        short = lane_ids(chunk)
+
+        @pl.loop(0, rows // chunk)
+        def _(turn):
+            part = pl.ds(pl.multiple_of(turn * chunk, chunk), chunk)
             after = jnp.where(pos_row[0:1, :] >= pos_col[part, :], 1.0, 0.0).astype(BF16)
             total = dot(after, high.astype(BF16)) + dot(after, middle.astype(BF16)) + dot(after, low.astype(BF16))
-            grad_logit = total * jax.nn.sigmoid(-logits[start : start + chunk])
-            grad_logit = jnp.where(lanes[start : start + chunk] < heads, grad_logit, 0.0).astype(BF16)
+            grad_logit = total * jax.nn.sigmoid(-(forget[part, :] + bias[0:1, :]))
+            grad_logit = jnp.where(short < heads, grad_logit, 0.0).astype(BF16)
             grad_project[part, 4 * width : 4 * width + LANES] = grad_logit
             small[2:3, :] += jnp.sum(grad_logit.astype(F32), axis=0, keepdims=True)
 
 
 def pick_chunk(rows):
-    return 256 if rows % 256 == 0 else 192
+    return 256 if rows % 256 == 0 else 128
 
 
 def whole(shape):
     return pl.BlockSpec(shape, lambda step: tuple(0 for _ in shape))
 
 
-def attend(project, places, bias, gains, head, width):
+def attend(project, places, bias, gains, head, width, heads):
     rows = project.shape[0]
     steps = width // LANES
     per = LANES // head
@@ -246,7 +252,7 @@
     forget = pl.BlockSpec((rows, LANES), lambda step: (0, 4 * steps))
     wide_shape = jax.ShapeDtypeStruct((per * steps, rows, LANES), BF16)
     return pl.pallas_call(
-        functools.partial(attend_kernel, head, chunk),
+        functools.partial(attend_kernel, head, chunk, heads),
         grid=(steps,),
         in_specs=[whole(p.shape) for p in places] + [whole(bias.shape), whole(gains.shape)]
         + [part(0), part(1), part(2), part(3), forget],
@@ -262,7 +268,7 @@
     )(*places, bias, gains, project, project, project, project, project)
 
 
-def attend_back(project, places, bias, gains, attended, wides, grad_gated, head, width):
+def attend_back(project, places, bias, gains, attended, wides, grad_gated, head, width, heads):
     rows = project.shape[0]
     steps = width // LANES
     per = LANES // head
@@ -276,7 +282,7 @@
     forget = pl.BlockSpec((rows, LANES), lambda step: (0, 4 * steps))
     total = 4 * width + LANES
     return pl.pallas_call(
-        functools.partial(attend_back_kernel, head, chunk, width),
+        functools.partial(attend_back_kernel, head, chunk, width, heads),
         grid=(steps,),
         in_specs=[whole(p.shape) for p in places] + [whole(bias.shape), whole(gains.shape)]
         + [part(0), part(1), part(3), forget, own, wide, wide, wide, own],
@@ -298,6 +304,476 @@
     )(*places, bias, gains, project, project, project, project, attended, *wides, grad_gated)
 
 
+MESH = pl.DeviceIdType.MESH
+ANY = pl.BlockSpec(memory_space=pltpu.HBM)
+
+
+def greet(peers, line=None):
+    barrier = pltpu.get_barrier_semaphore()
+    if line is not None:
+        peers = peers + [line.sibling]
+    for peer in peers:
+        pl.semaphore_signal(barrier, inc=1, device_id=peer, device_id_type=MESH)
+    if line is not None:
+        for there, peer in ((line.has_above, line.above), (line.has_below, line.below)):
+
+            @pl.when(there)
+            def _():
+                pl.semaphore_signal(barrier, inc=1, device_id=peer, device_id_type=MESH)
+
+    count = len(peers)
+    if line is not None:
+        last = line.layers - 1
+        count = count + (1 - line.layer // last) + (line.layer + last) // line.layers
+    pl.semaphore_wait(barrier, count)
+
+
+class Line:
+    def __init__(self, shards, source, target, sems):
+        self.shard = lax.axis_index("fsdp")
+        self.layers = shards // 2
+        self.layer, self.core = self.shard // 2, self.shard % 2
+        self.sibling = {"fsdp": self.shard ^ 1}
+        self.above, self.below = {"fsdp": self.shard + 2}, {"fsdp": self.shard - 2}
+        self.has_above, self.has_below = self.layer < self.layers - 1, self.layer > 0
+        self.source, self.target = source, target
+        self.rows = target.shape[0] // shards
+        self.line_send, self.line_recv, self.side_send, self.side_recv, self.own_sem = sems
+
+    def block(self, owner):
+        return rows_of(self.target, owner, self.rows)
+
+    def line(self, owner_layer, peer, way, own=False):
+        here = self.block(owner_layer * 2 + self.core)
+        return pltpu.make_async_remote_copy(
+            self.source if own else here, here, self.line_send.at[way, owner_layer], self.line_recv.at[owner_layer],
+            device_id=peer, device_id_type=MESH,
+        )
+
+    def side(self, owner_layer, owner_core, own=False):
+        here = self.block(owner_layer * 2 + owner_core)
+        return pltpu.make_async_remote_copy(
+            self.source if own else here, here, self.side_send.at[owner_layer], self.side_recv.at[owner_layer],
+            device_id=self.sibling, device_id_type=MESH,
+        )
+
+    def start(self):
+        own = self.source is not None
+
+        @pl.when(self.has_above)
+        def _():
+            self.line(self.layer, self.above, 0, own).start()
+
+        @pl.when(self.has_below)
+        def _():
+            self.line(self.layer, self.below, 1, own).start()
+
+        self.side(self.layer, self.core, own).start()
+        if own:
+            self.keep = pltpu.make_async_copy(self.source, self.block(self.shard), self.own_sem)
+            self.keep.start()
+
+    def step(self, distance):
+        lower, upper = self.layer - distance, self.layer + distance
+
+        @pl.when(lower >= 0)
+        def _():
+            self.line(lower, self.below, 1).wait_recv()
+
+            @pl.when(self.has_above)
+            def _():
+                self.line(lower, self.above, 0).start()
+
+            self.side(lower, self.core).start()
+
+        @pl.when(upper < self.layers)
+        def _():
+            self.line(upper, self.above, 0).wait_recv()
+
+            @pl.when(self.has_below)
+            def _():
+                self.line(upper, self.below, 1).start()
+
+            self.side(upper, self.core).start()
+
+    def finish(self):
+        if self.source is not None:
+            self.keep.wait()
+        for owner_layer in range(self.layers):
+            self.side(owner_layer, 1 - self.core).wait_recv()
+            self.side(owner_layer, self.core).wait_send()
+
+            @pl.when(self.has_above & (owner_layer <= self.layer))
+            def _():
+                self.line(owner_layer, self.above, 0).wait_send()
+
+            @pl.when(self.has_below & (owner_layer >= self.layer))
+            def _():
+                self.line(owner_layer, self.below, 1).wait_send()
+
+
+def line_scratch(shards):
+    layers = shards // 2
+    return [
+        pltpu.SemaphoreType.DMA((2, layers)),
+        pltpu.SemaphoreType.DMA((layers,)),
+        pltpu.SemaphoreType.DMA((layers,)),
+        pltpu.SemaphoreType.DMA((layers,)),
+        pltpu.SemaphoreType.DMA,
+    ]
+
+
+class Relay:
+    def __init__(self, rank, source, place, send_sem, recv_sem, own_sem):
+        self.rank, self.source, self.place = rank, source, place
+        self.send_sem, self.recv_sem, self.own_sem = send_sem, recv_sem, own_sem
+        self.copies = []
+
+    def send(self, number, source, place, distance):
+        copy = pltpu.make_async_remote_copy(
+            source, place, self.send_sem.at[number], self.recv_sem.at[number],
+            device_id={"ctx": self.rank ^ distance}, device_id_type=MESH,
+        )
+        copy.start()
+        self.copies.append(copy)
+
+    def start(self):
+        me = self.rank
+        self.send(0, self.source(0), self.place(me, 0), 1)
+        self.send(1, self.source(1), self.place(me, 1), 2)
+        self.send(2, self.source(1), self.place(me, 1), 1)
+        self.send(3, self.source(0), self.place(me, 0), 2)
+        self.own = [
+            pltpu.make_async_copy(self.source(h), self.place(me, h), self.own_sem.at[h]) for h in range(2)
+        ]
+        for copy in self.own:
+            copy.start()
+
+    def forward(self):
+        near, below = self.rank ^ 1, self.rank ^ 2
+        self.copies[0].wait_recv()
+        self.send(4, self.place(near, 0), self.place(near, 0), 2)
+        self.copies[1].wait_recv()
+        self.send(5, self.place(below, 1), self.place(below, 1), 1)
+
+    def finish(self):
+        for copy in self.own:
+            copy.wait()
+        for number, copy in enumerate(self.copies):
+            if number >= 2:
+                copy.wait_recv()
+        for copy in self.copies:
+            copy.wait_send()
+
+
+def rows_of(ref, index, size):
+    return ref.at[pl.ds(pl.multiple_of(index * size, 16), size), :]
+
+
+def cols_of(ref, index, size):
+    return ref.at[:, pl.ds(pl.multiple_of(index * size, LANES), size)]
+
+
+def relay_ops(mode, rank, source, target, sems):
+    rows, cols = source.shape
+    half = rows // 2
+
+    def part(h):
+        return source.at[pl.ds(h * half, half), :]
+
+    def place(block, h):
+        if mode == "gather_rows":
+            return target.at[pl.ds(pl.multiple_of(block * rows + h * half, 16), half), :]
+        if mode == "gather_cols":
+            return target.at[pl.ds(h * half, half), pl.ds(pl.multiple_of(block * cols, LANES), cols)]
+        return target.at[block, pl.ds(h * half, half), :]
+
+    return Relay(rank, part, place, *sems)
+
+
+def exchange_kernel(modes, ranks, across, shards, *refs):
+    count = len(modes)
+    sources, targets = refs[:count], refs[count : 2 * count]
+    send_sem, recv_sem, own_sem = refs[2 * count : 2 * count + 3]
+    rank = lax.axis_index("ctx")
+    shard = lax.axis_index("fsdp")
+    line = None
+    if "line" in modes:
+        at = modes.index("line")
+        line = Line(shards, sources[at], targets[at], refs[2 * count + 3 :])
+    far = any(mode not in ("gather_rows", "gather_cols", "stack", "line") for mode in modes)
+    peers = [{"ctx": rank ^ distance} for distance in range(1, ranks if far else ranks - 1)]
+    if across:
+        peers += [{"fsdp": shard ^ distance} for distance in range(1, across)]
+    greet(peers, line)
+    copies, relays = [], []
+    for op, (mode, source, target) in enumerate(zip(modes, sources, targets)):
+        if mode == "line":
+            line.start()
+            continue
+        if mode in ("gather_rows", "gather_cols", "stack"):
+            relay = relay_ops(mode, rank, source, target, (send_sem.at[op], recv_sem.at[op], own_sem.at[op]))
+            relay.start()
+            relays.append(relay)
+            continue
+        axis, me, members = ("fsdp", shard, across) if mode == "shards" else ("ctx", rank, ranks)
+        for distance in range(members):
+            other = me ^ distance if distance else me
+            place = target.at[me]
+            if mode == "scatter_rows":
+                piece = rows_of(source, other, target.shape[1])
+            elif mode == "scatter_cols":
+                piece = cols_of(source, other, target.shape[2])
+            elif mode == "shards":
+                piece = source.at[other]
+            else:
+                piece = source
+            if distance == 0:
+                copy = pltpu.make_async_copy(piece, place, own_sem.at[op, 0])
+            else:
+                copy = pltpu.make_async_remote_copy(
+                    piece, place, send_sem.at[op, distance - 1], recv_sem.at[op, distance - 1],
+                    device_id={axis: other}, device_id_type=MESH,
+                )
+            copy.start()
+            copies.append(copy)
+    for index in range(max(len(relays), shards // 2 - 1 if line is not None else 0)):
+        if line is not None and 0 < index < shards // 2:
+            line.step(index)
+        if index < len(relays):
+            relays[index].forward()
+    if line is not None:
+        line.step(shards // 2 - 1)
+        line.finish()
+    for relay in relays:
+        relay.finish()
+    for copy in copies:
+        copy.wait()
+
+
+def exchange(collective_id, ranks, across, shards, *ops):
+    shapes = []
+    for mode, source in ops:
+        shape = source.shape
+        if mode == "gather_rows":
+            shape = (ranks * shape[0], shape[1])
+        elif mode == "gather_cols":
+            shape = (shape[0], ranks * shape[1])
+        elif mode == "scatter_rows":
+            shape = (ranks, shape[0] // ranks, shape[1])
+        elif mode == "scatter_cols":
+            shape = (ranks, shape[0], shape[1] // ranks)
+        elif mode in ("stack", "each"):
+            shape = (ranks,) + shape
+        elif mode == "line":
+            shape = (shards * shape[0], shape[1])
+        shapes.append(jax.ShapeDtypeStruct(shape, source.dtype))
+    count = len(ops)
+    most = max(6, across - 1)
+    moved = sum(s.size * s.dtype.itemsize for s in shapes)
+    return pl.pallas_call(
+        functools.partial(exchange_kernel, [mode for mode, _ in ops], ranks, across, shards),
+        in_specs=[ANY] * count,
+        out_specs=[ANY] * count,
+        out_shape=shapes,
+        scratch_shapes=[
+            pltpu.SemaphoreType.DMA((count, most)),
+            pltpu.SemaphoreType.DMA((count, most)),
+            pltpu.SemaphoreType.DMA((count, 2)),
+        ]
+        + (line_scratch(shards) if any(mode == "line" for mode, _ in ops) else []),
+        compiler_params=pltpu.CompilerParams(collective_id=collective_id, has_side_effects=True),
+        cost_estimate=pl.CostEstimate(flops=0, bytes_accessed=moved * 20, transcendentals=0),
+        name="exchange",
+    )(*[source for _, source in ops])
+
+
+def start_kernel(
+    shards, width, piece,
+    tokens, cotangent, weight, tail, other, inputs, grad_low, gathered, picked,
+    weight_all, other_all, own_cols, own_pick,
+    send_sem, recv_sem, own_sem, load_sem, *line_sems,
+):
+    rank = lax.axis_index("ctx")
+    ranks = lax.axis_size("ctx")
+    model = weight.shape[1] // 4
+    loads = [
+        pltpu.make_async_copy(weight, weight_all, load_sem.at[0]),
+        pltpu.make_async_copy(other, other_all, load_sem.at[1]),
+    ]
+    for copy in loads:
+        copy.start()
+    line = Line(shards, own_cols, gathered, line_sems)
+    greet([{"ctx": rank ^ 1}, {"ctx": rank ^ 2}], line)
+    first = relay_ops("gather_rows", rank, tokens, inputs, (send_sem.at[0], recv_sem.at[0], own_sem.at[0]))
+    second = relay_ops("gather_rows", rank, cotangent, grad_low, (send_sem.at[1], recv_sem.at[1], own_sem.at[1]))
+    loads[0].wait()
+    for i in range(4):
+        own_cols[:, i * width : (i + 1) * width] = weight_all[
+            :, pl.ds(pl.multiple_of(i * model + rank * width, LANES), width)
+        ]
+    own_cols[:, 4 * width : 4 * width + LANES] = tail[...]
+    line.start()
+    first.start()
+    loads[1].wait()
+    for i in range(picked.shape[1] // piece):
+        own_pick[:, i * piece : (i + 1) * piece] = other_all[
+            :, pl.ds(pl.multiple_of((i * ranks + rank) * piece, LANES), piece)
+        ]
+    keep = pltpu.make_async_copy(own_pick, picked, load_sem.at[2])
+    keep.start()
+    first.forward()
+    second.start()
+    for distance in range(1, line.layers):
+        line.step(distance)
+        if distance == 1:
+            second.forward()
+    first.finish()
+    second.finish()
+    line.finish()
+    keep.wait()
+
+
+def start_moves(collective_id, ranks, shards, width, piece, tokens, cotangent, weight, tail, other):
+    rows, model = tokens.shape
+    return pl.pallas_call(
+        functools.partial(start_kernel, shards, width, piece),
+        in_specs=[ANY] * 3 + [pl.BlockSpec(memory_space=pltpu.VMEM), ANY],
+        out_specs=[ANY] * 4,
+        out_shape=[
+            jax.ShapeDtypeStruct((ranks * rows, model), BF16),
+            jax.ShapeDtypeStruct((ranks * rows, model), BF16),
+            jax.ShapeDtypeStruct((shards * weight.shape[0], 4 * width + LANES), BF16),
+            jax.ShapeDtypeStruct((other.shape[0], other.shape[1] // ranks), BF16),
+        ],
+        scratch_shapes=[
+            pltpu.VMEM(weight.shape, BF16),
+            pltpu.VMEM(other.shape, BF16),
+            pltpu.VMEM((weight.shape[0], 4 * width + LANES), BF16),
+            pltpu.VMEM((other.shape[0], other.shape[1] // ranks), BF16),
+            pltpu.SemaphoreType.DMA((2, 6)),
+            pltpu.SemaphoreType.DMA((2, 6)),
+            pltpu.SemaphoreType.DMA((2, 2)),
+            pltpu.SemaphoreType.DMA((3,)),
+        ]
+        + line_scratch(shards),
+        compiler_params=pltpu.CompilerParams(
+            collective_id=collective_id, has_side_effects=True, vmem_limit_bytes=24 << 20
+        ),
+        cost_estimate=pl.CostEstimate(flops=0, bytes_accessed=150 << 20, transcendentals=0),
+        name="start_moves",
+    )(tokens, cotangent, weight, tail, other)
+
+
+def spread_kernel(pieces, *refs):
+    source, targets = refs[0], refs[1:]
+    ranks = source.shape[0]
+    for target, (piece, first, count) in zip(targets, pieces):
+        for block in range(count):
+            for index in range(ranks):
+                target[:, pl.ds((block * ranks + index) * piece, piece)] = source[
+                    index, :, pl.ds(first + block * piece, piece)
+                ].astype(F32)
+
+
+def spread_cols(source, *pieces):
+    ranks, rows, cols = source.shape
+    if any(piece % LANES or first % LANES for piece, first, _ in pieces):
+        return [
+            jnp.concatenate(
+                [
+                    source[c, :, first + i * piece : first + (i + 1) * piece]
+                    for i in range(count)
+                    for c in range(ranks)
+                ],
+                axis=1,
+            ).astype(F32)
+            for piece, first, count in pieces
+        ]
+    part = rows // 4 if rows % 64 == 0 else rows
+    widths = [count * ranks * piece for piece, _, count in pieces]
+    return pl.pallas_call(
+        functools.partial(spread_kernel, pieces),
+        grid=(rows // part,),
+        in_specs=[pl.BlockSpec((ranks, part, cols), lambda step: (0, step, 0))],
+        out_specs=[pl.BlockSpec((part, w), lambda step: (step, 0)) for w in widths],
+        out_shape=[jax.ShapeDtypeStruct((rows, w), F32) for w in widths],
+        compiler_params=pltpu.CompilerParams(vmem_limit_bytes=32 << 20),
+        cost_estimate=pl.CostEstimate(flops=0, bytes_accessed=rows * sum(widths) * 6, transcendentals=0),
+        name="spread_cols",
+    )(source)
+
+
+class Native:
+    def __init__(self, ranks):
+        self.ranks = ranks
+
+    def begin(self, number, tokens, cotangent, weight, tail, other, piece, width, padded):
+        rank, model = lax.axis_index("ctx"), tokens.shape[1]
+        parts = [lax.dynamic_slice_in_dim(weight, i * model + rank * width, width, 1) for i in range(4)]
+        parts = [jnp.pad(part, ((0, 0), (0, padded - width))) for part in parts]
+        cols = other.shape[1] // self.ranks
+        picks = [
+            lax.dynamic_slice_in_dim(other, (i * self.ranks + rank) * piece, piece, 1) for i in range(cols // piece)
+        ]
+        return (
+            lax.all_gather(tokens, "ctx", axis=0, tiled=True),
+            lax.all_gather(cotangent, "ctx", axis=0, tiled=True),
+            lax.all_gather(jnp.concatenate(parts + [tail], axis=1), "fsdp", axis=0, tiled=True),
+            jnp.concatenate(picks, axis=1),
+        )
+
+    def gather_cols(self, number, array, piece):
+        return lax.all_gather(array, "ctx", axis=1, tiled=True), lax.all_gather(piece, "fsdp", axis=0, tiled=True)
+
+    def scatter_cols(self, number, array):
+        return lax.psum_scatter(array, "ctx", scatter_dimension=1, tiled=True).astype(F32)
+
+    def finish_rows(self, number, first, second, sums):
+        pair = [
+            lax.psum_scatter(a, "ctx", scatter_dimension=0, tiled=True).astype(F32) for a in (first, second)
+        ]
+        return pair + [lax.psum(sums, "ctx")]
+
+    def stack(self, number, *arrays):
+        return [lax.all_gather(a, "ctx", axis=0, tiled=False) for a in arrays]
+
+    def finish(self, number, array, pieces):
+        return lax.all_gather(array, "ctx", axis=0, tiled=False), lax.psum_scatter(
+            pieces, "fsdp", scatter_dimension=0, tiled=False
+        )
+
+
+class Direct:
+    def __init__(self, ranks, shards):
+        self.ranks, self.shards = ranks, shards
+
+    def run(self, number, *ops):
+        return exchange(number, self.ranks, 0, self.shards, *ops)
+
+    def begin(self, number, tokens, cotangent, weight, tail, other, piece, width, padded):
+        return start_moves(
+            number, self.ranks, self.shards, width, piece, tokens, cotangent, weight, tail, other
+        )
+
+    def gather_cols(self, number, array, piece):
+        return self.run(number, ("gather_cols", array), ("line", piece))
+
+    def scatter_cols(self, number, array):
+        return self.run(number, ("scatter_cols", array))[0].astype(F32).sum(axis=0)
+
+    def finish_rows(self, number, first, second, sums):
+        out = self.run(number, ("scatter_rows", first), ("scatter_rows", second), ("each", sums))
+        return [a.astype(F32).sum(axis=0) for a in out]
+
+    def stack(self, number, *arrays):
+        return self.run(number, *[("stack" if a.dtype == BF16 else "each", a) for a in arrays])
+
+    def finish(self, number, array, pieces):
+        out = exchange(number, self.ranks, self.shards, self.shards, ("stack", array), ("shards", pieces))
+        return out[0], out[1].sum(axis=0)
+
+
 def body(
     tokens, block_order, segment_ids, norm_gains, attn_in_weight, forget_weight, forget_bias,
     qk_gains, out_weight, gate_up_weight, down_weight, out_grad,
@@ -309,58 +785,47 @@
     head_count, head_dim = forget_bias.shape[0], qk_gains.shape[1]
     local_heads = head_count // ranks
     width = local_heads * head_dim
+    padded = -(-width // LANES) * LANES
     seq_order = block_order[0]
     seq_len = segment_ids.shape[1]
     block_len = seq_len // seq_order.shape[0]
-    hidden_all = down_weight.shape[0] * shards
     hidden_piece = down_weight.shape[0] // ranks
     hidden = hidden_piece * shards
+    plain = ranks == 4 and shards & (shards - 1) == 0 and width == padded
+    comm = Direct(ranks, shards) if plain else Native(ranks)
 
     def slab(array, start, size, axis):
         return lax.dynamic_slice_in_dim(array, start, size, axis)
 
-    spare = LANES - local_heads - 2
-    in_piece = jnp.concatenate(
-        [slab(attn_in_weight, i * model_width + rank * width, width, 1) for i in range(4)]
-        + [
+    def widen(array):
+        return jnp.pad(array, ((0, 0), (0, padded - width))) if padded > width else array
+
+    tail = jnp.concatenate(
+        [
             slab(forget_weight, rank * local_heads, local_heads, 1),
             norm_gains.T,
-            jnp.zeros((attn_in_weight.shape[0], spare), BF16),
+            jnp.zeros((attn_in_weight.shape[0], LANES - local_heads - 2), BF16),
         ],
         axis=1,
     )
-    out_piece = slab(out_weight, rank * width, width, 1)
-    gate_up_piece = jnp.concatenate(
-        [
-            slab(gate_up_weight, (i * shards + f) * hidden_piece * ranks + rank * hidden_piece, hidden_piece, 1)
-            for i in range(2)
-            for f in range(shards)
-        ],
-        axis=1,
-    )
-    down_piece = slab(down_weight, rank * hidden_piece, hidden_piece, 0)
-
-    def gather_shards(array):
-        return lax.all_gather(array, "fsdp", axis=0, tiled=True)
-
-    w_in = gather_shards(in_piece)
-    w_out = gather_shards(out_piece)
-    w_gate_up = gather_shards(gate_up_piece)
-    w_down = gather_shards(down_piece)
-
-    inputs = lax.all_gather(tokens[0], "ctx", axis=0, tiled=True)
-    grad_low = lax.all_gather(out_grad[0], "ctx", axis=0, tiled=True)
+    inputs, grad_low, w_in, gate_up_piece = comm.begin(
+        0, tokens[0], out_grad[0], attn_in_weight, tail, gate_up_weight, hidden_piece, width, padded
+    )
+    w_gate_up = lax.all_gather(gate_up_piece, "fsdp", axis=0, tiled=True)
 
     offsets = jnp.arange(seq_len, dtype=jnp.int32)
-    places = jnp.take(seq_order, offsets // block_len) * block_len + offsets % block_len
-    segments = jnp.take(segment_ids[0], places)
+    blocks = jnp.arange(seq_order.shape[0], dtype=jnp.int32)
+    places = (seq_order[:, None] * block_len + offsets[None, :block_len]).reshape(-1)
+    by_block = segment_ids[0].reshape(-1, block_len)
+    chosen = seq_order[:, None, None] == blocks[None, :, None]
+    segments = jnp.sum(jnp.where(chosen, by_block[None], 0), axis=1).reshape(-1)
     places_all = (places[None, :], places[:, None], segments[None, :], segments[:, None])
     valid = (segments >= 0).astype(F32)
 
     bias = jnp.pad(slab(forget_bias, rank * local_heads, local_heads, 0), (0, LANES - local_heads))[None]
     head_gains = jnp.tile(qk_gains, (1, LANES // head_dim))
 
-    gain_cols = w_in[:, 4 * width : 4 * width + LANES].astype(F32).T
+    gain_cols = w_in[:, 4 * padded : 4 * padded + LANES].astype(F32).T
     gain_one = gain_cols[local_heads]
     gain_two = gain_cols[local_heads + 1]
 
@@ -369,11 +834,14 @@
     normed = (wide_inputs * scale_one * gain_one).astype(BF16)
     project = dot(normed, w_in)
     gated, attended, wide_query, wide_key, wide_value = attend(
-        project, places_all, bias, head_gains, head_dim, width
-    )
-    gated_all = lax.all_gather(gated, "ctx", axis=1, tiled=True)
+        project, places_all, bias, head_gains, head_dim, padded, local_heads
+    )
+    gated_all, w_out = comm.gather_cols(1, gated[:, :width], slab(out_weight, rank * width, width, 1))
     mixed_cols = slab(inputs, rank * width, width, 1).astype(F32) + dot(gated_all, w_out)
-    mixed = lax.all_gather(mixed_cols.astype(BF16), "ctx", axis=1, tiled=True).astype(F32)
+    mixed, w_down = comm.gather_cols(
+        2, mixed_cols.astype(BF16), slab(down_weight, rank * hidden_piece, hidden_piece, 0)
+    )
+    mixed = mixed.astype(F32)
     scale_two = rms_scale(mixed)
     normed_two = (mixed * scale_two * gain_two).astype(BF16)
     gate_up = dot(normed_two, w_gate_up)
@@ -381,13 +849,59 @@
     gate_sigmoid = jax.nn.sigmoid(gate_part)
     silu = gate_part * gate_sigmoid
     hidden_act = (silu * up_part).astype(BF16)
-    down_sum = lax.psum_scatter(
-        dot(hidden_act, w_down).astype(BF16), "ctx", scatter_dimension=0, tiled=True
-    ).astype(F32)
+    down_part = dot(hidden_act, w_down).astype(BF16)
 
     def own_rows(array):
         return slab(array, rank * row_count, row_count, 0)
 
+    grad_hidden = right_product(grad_low, w_down)
+    grad_gate = grad_hidden * up_part * gate_sigmoid * (1.0 + gate_part * (1.0 - gate_sigmoid))
+    grad_gate_up = jnp.concatenate([grad_gate, grad_hidden * silu], axis=1).astype(BF16)
+    grad_normed_two = right_product(grad_gate_up, w_gate_up)
+    gain_two_grad = jnp.sum(grad_normed_two * mixed * scale_two, axis=0)
+    grad_mixed_part = norm_back(grad_normed_two, mixed, scale_two, gain_two).astype(BF16)
+
+    def reduce_shards(array):
+        return lax.psum_scatter(array.astype(BF16), "fsdp", scatter_dimension=0, tiled=True)
+
+    down_part_grad = left_product(hidden_act, grad_low).astype(BF16)
+    grad_mixed_part, down_part_grad = lax.optimization_barrier((grad_mixed_part, down_part_grad))
+    down_share = reduce_shards(down_part_grad)
+    grad_mixed_cols = slab(grad_low, rank * width, width, 1).astype(F32) + comm.scatter_cols(3, grad_mixed_part)
+    grad_branch = grad_mixed_cols.astype(BF16)
+    gate_up_grad = left_product(normed_two, grad_gate_up).astype(BF16)
+    grad_branch, gate_up_grad = lax.optimization_barrier((grad_branch, gate_up_grad))
+    gate_up_share = reduce_shards(gate_up_grad)
+    grad_gated = widen(comm.scatter_cols(4, right_product(grad_branch, w_out).astype(BF16)))
+    grad_gated, down_share = lax.optimization_barrier((grad_gated, down_share))
+    grad_project, small = attend_back(
+        project, places_all, bias, head_gains, attended, (wide_query, wide_key, wide_value),
+        grad_gated, head_dim, padded, local_heads,
+    )
+
+    in_part = left_product(normed, grad_project).astype(BF16)
+    out_part = left_product(gated_all, grad_branch).astype(BF16)
+    late = jnp.concatenate([in_part[:, : 4 * padded], out_part, in_part[:, 4 * padded :]], axis=1)
+    late, gate_up_share = lax.optimization_barrier((late, gate_up_share))
+    late_share = reduce_shards(late)
+
+    grad_normed = right_product(grad_project, w_in)
+    gain_one_grad = jnp.sum(grad_normed * wide_inputs * scale_one, axis=0)
+    in_own = jnp.arange(model_width, dtype=jnp.int32) // width == rank
+    grad_inputs = norm_back(grad_normed, wide_inputs, scale_one, gain_one) + jnp.where(
+        in_own[None], jnp.tile(grad_mixed_cols, (1, ranks)), 0.0
+    )
+    bias_slots = jnp.where(
+        jnp.arange(ranks, dtype=jnp.int32)[:, None] == rank, small[2, :local_heads][None], 0.0
+    ).reshape(-1)
+    qk_sum = small[0:2].reshape(2, LANES // head_dim, head_dim).sum(axis=1).reshape(-1)
+    others = jnp.concatenate([bias_slots, qk_sum])
+    sums = jnp.stack(
+        [gain_one_grad, gain_two_grad, jnp.pad(others, (0, model_width - others.shape[0]))]
+        + [jnp.zeros((model_width,), F32)] * 5
+    )
+    down_sum, tokens_grad, sums = comm.finish_rows(5, down_part, grad_inputs.astype(BF16), sums)
+    tokens_grad = tokens_grad.astype(BF16)[None]
     result = own_rows(mixed) + down_sum
     block_out = result.astype(BF16)[None]
     branch = result - own_rows(wide_inputs)
@@ -400,68 +914,38 @@
     )
     valid_count = jnp.sum(valid) * model_width
 
-    grad_hidden = right_product(grad_low, w_down)
-    grad_gate = grad_hidden * up_part * gate_sigmoid * (1.0 + gate_part * (1.0 - gate_sigmoid))
-    grad_gate_up = jnp.concatenate([grad_gate, grad_hidden * silu], axis=1).astype(BF16)
-    grad_normed_two = right_product(grad_gate_up, w_gate_up)
-    gain_two_grad = jnp.sum(grad_normed_two * mixed * scale_two, axis=0)
-    grad_mixed_part = norm_back(grad_normed_two, mixed, scale_two, gain_two).astype(BF16)
-    grad_mixed_cols = slab(grad_low, rank * width, width, 1).astype(F32) + lax.psum_scatter(
-        grad_mixed_part, "ctx", scatter_dimension=1, tiled=True
-    ).astype(F32)
-    grad_branch = grad_mixed_cols.astype(BF16)
-    grad_gated = lax.psum_scatter(
-        right_product(grad_branch, w_out).astype(BF16), "ctx", scatter_dimension=1, tiled=True
-    ).astype(F32)
-    grad_project, small = attend_back(
-        project, places_all, bias, head_gains, attended, (wide_query, wide_key, wide_value),
-        grad_gated, head_dim, width,
-    )
-    grad_normed = right_product(grad_project, w_in)
-    gain_one_grad = jnp.sum(grad_normed * wide_inputs * scale_one, axis=0)
-    in_own = jnp.arange(model_width, dtype=jnp.int32) // width == rank
-    grad_inputs = norm_back(grad_normed, wide_inputs, scale_one, gain_one) + jnp.where(
-        in_own[None], jnp.tile(grad_mixed_cols, (1, ranks)), 0.0
-    )
-    tokens_grad = lax.psum_scatter(grad_inputs.astype(BF16), "ctx", scatter_dimension=0, tiled=True)[None]
-
-    def reduce_shards(array):
-        return lax.psum_scatter(array.astype(BF16), "fsdp", scatter_dimension=0, tiled=True)
-
-    def gather_ranks(array):
-        return lax.all_gather(array, "ctx", axis=0, tiled=False).astype(F32)
-
-    down_own = gather_ranks(reduce_shards(left_product(hidden_act, grad_low)))
-    down_out = down_own.reshape(down_weight.shape)
-    gate_up_own = gather_ranks(reduce_shards(left_product(normed_two, grad_gate_up)))
-    gate_up_out = jnp.concatenate(
-        [
-            gate_up_own[c, :, (i * shards + f) * hidden_piece : (i * shards + f + 1) * hidden_piece]
-            for i in range(2)
-            for f in range(shards)
-            for c in range(ranks)
-        ],
-        axis=1,
-    )
-    out_own = gather_ranks(reduce_shards(left_product(gated_all, grad_branch)))
-    out_out = jnp.concatenate([out_own[c] for c in range(ranks)], axis=1)
-    in_own = gather_ranks(reduce_shards(left_product(normed, grad_project)))
-    in_out = jnp.concatenate(
-        [in_own[c, :, i * width : (i + 1) * width] for i in range(4) for c in range(ranks)], axis=1
-    )
-    forget_out = jnp.concatenate([in_own[c, :, 4 * width : 4 * width + local_heads] for c in range(ranks)], axis=1)
-    gains_sum = lax.psum_scatter(
-        jnp.stack([gain_one_grad, gain_two_grad]), "fsdp", scatter_dimension=1, tiled=True
-    )
-    gains_sum, partial_sums = lax.psum((gains_sum, partial_sums), "ctx")
-    bias_slots = jnp.where(
-        jnp.arange(ranks, dtype=jnp.int32)[:, None] == rank, small[2, :local_heads][None], 0.0
-    ).reshape(-1)
-    qk_sum = small[0:2].reshape(2, LANES // head_dim, head_dim).sum(axis=1)
-    bias_sum, qk_sum = lax.psum((bias_slots, qk_sum), ("ctx", "fsdp"))
+    down_own, gate_up_own, stats = comm.stack(
+        6, down_share, gate_up_share, jnp.broadcast_to(jnp.pad(partial_sums, (0, LANES - 2)), (8, LANES))
+    )
+    down_out = down_own.astype(F32).reshape(down_weight.shape)
+    gate_up_out = spread_cols(gate_up_own, (hidden_piece, 0, 2 * shards))[0]
+    share = model_width // shards
+    room = -(-share // LANES) * LANES
+    gain_pieces = jnp.pad(sums[0:2].reshape(2, shards, share).transpose(1, 0, 2), ((0, 0), (0, 0), (0, room - share)))
+    tail = jnp.pad(sums[2, : others.shape[0]], (0, 2 * room - others.shape[0])).reshape(1, 2, room)
+    pieces = jnp.concatenate(
+        [gain_pieces, jnp.broadcast_to(tail, (shards, 2, room)), jnp.zeros((shards, 4, room), F32)], axis=1
+    )
+    late_own, piece_sum = comm.finish(7, late_share, pieces)
+    if plain:
+        in_out, out_out = spread_cols(late_own, (width, 0, 4), (width, 4 * width, 1))
+    else:
+        in_out = jnp.concatenate(
+            [late_own[c, :, i * padded : i * padded + width] for i in range(4) for c in range(ranks)], axis=1
+        ).astype(F32)
+        out_out = jnp.concatenate(
+            [late_own[c, :, 4 * padded : 4 * padded + width] for c in range(ranks)], axis=1
+        ).astype(F32)
+    last = 4 * padded + width
+    forget_out = jnp.concatenate([late_own[c, :, last : last + local_heads] for c in range(ranks)], axis=1).astype(F32)
+    gains_sum = piece_sum[0:2, :share]
+    tail_sum = piece_sum[2:4].reshape(-1)
+    bias_sum = tail_sum[:head_count]
+    qk_sum = tail_sum[head_count : head_count + 2 * head_dim].reshape(2, head_dim)
+    totals = stats[:, 0, :2].sum(axis=0)
     return (
         block_out, tokens_grad, gains_sum, in_out, forget_out, bias_sum, qk_sum,
-        out_out, gate_up_out, down_out, jnp.sqrt(partial_sums / valid_count)[None],
+        out_out, gate_up_out, down_out, jnp.sqrt(totals / valid_count)[None],
     )
 
 

time: 933 us -> 549 us (0.59)
  waiting for transfers between devices: 520 us -> 0.09 us
  Pallas kernels: 43.4 us -> 365 us
  local copies, waits for them, and re-layouts: 132 us -> 39.7 us
  blocking collectives: 63 us -> 0 us
  matrix products: 93 us -> 72.5 us
    pallas_call x2 -> x12, Pallas kernels: 43.4 us -> 365 us  [the longest x7 252 us: exchange(): pl.pallas_call(functools.partial(exchange_kernel, [mode for mode, _ in op...]
    all_gather x11 -> x1, waiting for transfers between devices: 294 us -> 0.02 us  [body(): w_gate_up = lax.all_gather(gate_up_piece, 'fsdp', axis=0, tiled=True)]
    reduce_scatter x4 -> x3, waiting for transfers between devices: 137 us -> 0.01 us  [reduce_shards(): lax.psum_scatter(array.astype(BF16), 'fsdp', scatter_dimension=0, tiled=T...]
    unnamed x161 -> x117, local copies, waits for them, and re-layouts: 114 us -> 29 us
    unnamed x23 -> x4, waiting for transfers between devices: 59.2 us -> 0.07 us
    psum x2 -> x0, blocking collectives: 51.4 us -> none  [the longest x1 39.7 us: body(): bias_sum, qk_sum = lax.psum((bias_slots, qk_sum), ('ctx', 'fsdp'))]
    reduce_scatter x2 -> x0, waiting for transfers between devices: 29.1 us -> none  [the longest x1 25.3 us: body(): lax.psum_scatter(dot(hidden_act, w_down).astype(BF16), 'ctx', scatter_dim...]
    reduce_sum x1 -> x9, other arithmetic: 0.02 us -> 12.5 us  [the longest x3 6.05 us: finish_rows(): return [a.astype(F32).sum(axis=0) for a in out]]
  transfers between devices with their start and end apart: 20 -> 4, of which waited for: 16 -> 0; matrix products, arithmetic and copies ran while one was open for 25% -> 19% of each run, Pallas kernels for 5% -> 52%
where the time goes in v2:
time: 549 us; the launch traced here: 544 us
  Pallas kernels  365 us (66%)
  matrix products  72.5 us (13%)
  other arithmetic  50.9 us (9%)
  local copies, waits for them, and re-layouts  39.7 us (7%)
  between operations  15.3 us (3%)
    pallas_call x7, Pallas kernels, exchange(): pl.pallas_call(functools.partial(exchange_kernel, [mode for mode, _ in op...  252 us
    pallas_call x1, Pallas kernels, start_moves(): pl.pallas_call(functools.partial(start_kernel, shards, width, piece), in_...  50.8 us
    pallas_call x1, Pallas kernels, attend_back(): pl.pallas_call(functools.partial(attend_back_kernel, head, chunk, width,...  37.6 us
    unnamed x117, local copies, waits for them, and re-layouts  29 us
    dot_general x4, matrix products, right_product(): lax.dot_general(left, right, (((1,), (1,)), ((), ())), preferred_element_...  26 us
    dot_general x4, matrix products, dot(): lax.dot_general(left, right, (((1,), (0,)), ((), ())), preferred_element_...  25.7 us
    dot_general x4, matrix products, left_product(): lax.dot_general(left, right, (((0,), (0,)), ((), ())), preferred_element_...  20.8 us
    pallas_call x1, Pallas kernels, attend(): pl.pallas_call(functools.partial(attend_kernel, head, chunk, heads), grid...  18.9 us
  transfers between devices with their start and end apart: 4, of which 0 were waited for; matrix products, arithmetic and copies ran while one was open for 19% of the time, Pallas kernels for 52%

profile of v2, /device:TPU:0, one launch (start us, length us, event | category | flops | bytes accessed | tf_op | source)
XLA Modules:
  0.0 544.1 jit_solution(2934307215309243622)
XLA Ops:
  14.9 50.8 %start_moves.1 = (bf16[768,1536]{1,0:T(8,128)(2,1)S(1)}, bf16[768,1536]{1,0:T(8,128)(2,1)S(1)}, bf16[1536,1664]{1,0:T(8,128)(2,1)S(1)}, bf16[192,2048]{1,0:T(8,128)(2,1)}) custom-call(bf16[192,1536]{1,0:T(8,128)(2,1)S(1)} %bitcast.57, bf16[192,1536]{1,0:T(8,128)(2,1)S(1)} %bitcast.58, bf16[192,6144]{1,0:T(8,128)(2,1)S(1)} %copy-done.9, ...), custom_call_target="tpu_custom_call" | custom-call | bytes 157286400 | tf_op jit(solution)/shard_map/start_moves/pallas_call | solution.py:639
  76.7 9.4 %fusion.26.query.key.value.gate.forget = f32[768,1664]{1,0:T(8,128)} fusion(bf16[1536,1664]{1,0:T(8,128)(2,1)} %copy-done.21, bf16[768,1536]{1,0:T(8,128)(2,1)S(1)} %copy-done.3, f32[1536]{0:T(1024)S(1)} %get-tuple-element.106, f32[768]{0:T(1024)S(1)} %get-tuple-element.120), kind=kOutput, calls=%fused_computation.57 | convolution fusion | flops 3930587136 | bytes 12592128 | tf_op jit(solution)/shard_map/dot_general | solution.py:30
  86.1 18.9 %attend.1 = (bf16[768,384]{1,0:T(8,128)(2,1)S(1)}, f32[768,384]{1,0:T(8,128)S(1)}, bf16[6,768,128]{2,1,0:T(8,128)(2,1)S(1)}, bf16[6,768,128]{2,1,0:T(8,128)(2,1)S(1)}, bf16[6,768,128]{2,1,0:T(8,128)(2,1)S(1)}) custom-call(s32[1,768]{1,0:T(1,128)S(1)} %add.116.pos_row, s32[768,1]{1,0:T(8,128)S(1)} %add.128.pos_col, ...), custom_call_target="tpu_custom_call" | custom-call | tf_op jit(solution)/shard_map/attend/pallas_call | solution.py:254
  110.5 33.7 %exchange.7 = (bf16[768,1536]{1,0:T(8,128)(2,1)}, bf16[1536,384]{1,0:T(8,128)(2,1)}) custom-call(bf16[768,384]{1,0:T(8,128)(2,1)} %copy-done.18, bf16[192,384]{1,0:T(8,128)(2,1)} %constant_dynamic-slice_fusion.1.refs_1_), custom_call_target="tpu_custom_call" | custom-call | bytes 70778880 | tf_op jit(solution)/shard_map/exchange/pallas_call | solution.py:574
  145.0 4.4 fusion.21.refs_0_
  149.3 33.6 %exchange.8 = (bf16[768,1536]{1,0:T(8,128)(2,1)}, bf16[1024,1536]{1,0:T(8,128)(2,1)}) custom-call(bf16[768,384]{1,0:T(8,128)(2,1)} %fusion.21.refs_0_, bf16[128,1536]{1,0:T(8,128)(2,1)} %constant_dynamic-slice_fusion.refs_1_), custom_call_target="tpu_custom_call" | custom-call | bytes 110100480 | tf_op jit(solution)/shard_map/exchange/pallas_call | solution.py:574
  185.2 8.1 %fusion.23 = f32[768,2048]{1,0:T(8,128)S(1)} fusion(bf16[1536,2048]{1,0:T(8,128)(2,1)} %all-gather.2.cloned.1.call-done, bf16[768,1536]{1,0:T(8,128)(2,1)} %get-tuple-element.49, f32[1536]{0:T(1024)S(1)} %copy-done.35, f32[768]{0:T(1024)S(1)} %get-tuple-element.122), kind=kOutput, calls=%fused_computation.56 | convolution fusion | flops 4836556800 | bytes 14951424 | tf_op jit(solution)/shard_map/dot_general | solution.py:30
  193.3 5.1 multiply_convert_fusion.1
  198.4 9.9 %fusion.18 = (f32[1536]{0:T(1024)S(1)}, f32[768]{0:T(1024)S(1)}, f32[768,1536]{1,0:T(8,128)}) fusion(bf16[768,1536]{1,0:T(8,128)(2,1)S(1)} %copy-done.22, f32[768]{0:T(1024)S(1)} %get-tuple-element.122, f32[1536]{0:T(1024)S(1)} %copy-done.35, bf16[1536,2048]{1,0:T(8,128)(2,1)S(1)} %bitcast.71, bf16[768,1024]{1,0:T(8,128)(2,1)} %get-tuple-element.113, ...), kind=kOutput, calls=%fused_computation.31 | convolution fusion | flops 4846385152 | bytes 16533504 | tf_op jit(solution)/shard_map/dot_general | solution.py:42
  208.3 4.1 convolution_convert_fusion.2
  212.4 4.7 fusion.15.refs_0_
  217.2 29.8 %exchange.9 = bf16[4,768,384]{2,1,0:T(8,128)(2,1)} custom-call(bf16[768,1536]{1,0:T(8,128)(2,1)} %fusion.15.refs_0_), custom_call_target="tpu_custom_call" | custom-call | bytes 47185920 | tf_op jit(solution)/shard_map/exchange/pallas_call | solution.py:574
  251.9 7.4 %convolution_convert_fusion = bf16[1536,2048]{1,0:T(8,128)(2,1)} fusion(bf16[768,1024]{1,0:T(8,128)(2,1)S(1)} %copy-done.51, bf16[768,1024]{1,0:T(8,128)(2,1)S(1)} %copy-done.50, bf16[768,1536]{1,0:T(8,128)(2,1)S(1)} %copy-done.23, f32[1536]{0:T(1024)S(1)} %copy-done.35, f32[768]{0:T(1024)S(1)} %get-tuple-element.122), kind=kOutput, calls=%fused_computation | convolution fusion | flops 4845993984 | bytes 11805696 | tf_op jit(solution)/shard_map/dot_general | solution.py:36
  260.4 4.1 convolution_convert_fusion.4.refs_0_
  264.5 28.8 %exchange.10 = bf16[4,768,384]{2,1,0:T(8,128)(2,1)} custom-call(bf16[768,1536]{1,0:T(8,128)(2,1)} %convolution_convert_fusion.4.refs_0_), custom_call_target="tpu_custom_call" | custom-call | bytes 47185920 | tf_op jit(solution)/shard_map/exchange/pallas_call | solution.py:574
  293.3 3.3 convert_reduce_fusion.1.grad_gated
  301.7 37.6 %attend_back.1 = (bf16[768,1664]{1,0:T(8,128)(2,1)}, f32[8,128]{1,0:T(8,128)S(1)}) custom-call(s32[1,768]{1,0:T(1,128)S(1)} %add.116.pos_row, s32[768,1]{1,0:T(8,128)S(1)} %add.128.pos_col, s32[1,768]{1,0:T(1,128)S(1)} %broadcast_in_dim_reshape.8.seg_row, s32[768,1]{1,0:T(8,128)S(1)} %broadcast_in_dim_reshape.10.seg_col, f32[1,128]{1,0:T(1,128)S(1)} %pad_bitcast_fusion.bias, ...), custom_call_target="tpu_custom_call" | custom-call | tf_op jit(solution)/shard_map/attend_back/pallas_call | solution.py:284
  339.3 6.7 %convolution_convert_fusion.1 = bf16[1536,1664]{1,0:T(8,128)(2,1)S(1)} fusion(bf16[768,1664]{1,0:T(8,128)(2,1)} %get-tuple-element.61, bf16[768,1536]{1,0:T(8,128)(2,1)S(1)} %copy-done.4, f32[1536]{0:T(1024)S(1)} %copy-done.34, f32[768]{0:T(1024)S(1)} %copy-done.38), kind=kOutput, calls=%fused_computation.1 | convolution fusion | flops 3933143040 | bytes 10036224 | tf_op jit(solution)/shard_map/dot_general | solution.py:36
  347.3 3.2 pad_maximum_fusion
  350.6 4.6 convert_element_type.91
  355.2 2.8 convert_element_type.94
  360.3 2.8 copy.62
  364.4 3.9 convolution_convert_fusion.3.refs_0_
  368.3 6.9 %fusion.9 = (f32[1536]{0:T(1024)S(1)}, f32[768]{0:T(1024)S(1)}, f32[768,1536]{1,0:T(8,128)}) fusion(bf16[768,1536]{1,0:T(8,128)(2,1)S(1)} %copy-done.5, f32[768]{0:T(1024)S(1)} %copy-done.38, f32[1536]{0:T(1024)S(1)} %copy-done.34, bf16[768,1664]{1,0:T(8,128)(2,1)S(1)} %copy-done.43, bf16[1536,1664]{1,0:T(8,128)(2,1)S(1)} %bitcast.60), kind=kOutput, calls=%fused_computation.22 | convolution fusion | flops 3934123776 | bytes 14764032 | tf_op jit(solution)/shard_map/dot_general | solution.py:42
  376.4 6.4 %fusion.6.refs_1_ = bf16[768,1536]{1,0:T(8,128)(2,1)} fusion(bf16[768,1536]{1,0:T(8,128)(2,1)} %copy-done.2, f32[768,1536]{1,0:T(8,128)} %bitcast.61, f32[768,1536]{1,0:T(8,128)} %get-tuple-element.124, f32[768]{0:T(1024)S(1)} %broadcast_multiply_fusion, f32[768]{0:T(1024)S(1)} %copy-done.36, f32[1536]{0:T(1024)S(1)} %copy-done.34, f32[768]{0:T(1024)S(1)} %copy-done.38, ...), kind=kLoop, calls=%fused_computation.19 | loop fusion | flops 10616832 | bytes 14172672 | tf_op jit(solution)/shard_map/convert_element_type | solution.py:903
  382.7 55.6 %exchange.11 = (bf16[4,192,1536]{2,1,0:T(8,128)(2,1)}, bf16[4,192,1536]{2,1,0:T(8,128)(2,1)}, f32[4,8,1536]{2,1,0:T(8,128)}) custom-call(bf16[768,1536]{1,0:T(8,128)(2,1)} %convolution_convert_fusion.3.refs_0_, bf16[768,1536]{1,0:T(8,128)(2,1)} %fusion.6.refs_1_, f32[8,1536]{1,0:T(8,128)} %stack.28.refs_2_), custom_call_target="tpu_custom_call" | custom-call | bytes 98304000 | tf_op jit(solution)/shard_map/exchange/pallas_call | solution.py:574
  439.3 3.0 reduce_sum.194
  444.5 2.6 multiply_reduce_fusion.1
  450.5 40.0 %exchange.13 = (bf16[4,128,1536]{2,1,0:T(8,128)(2,1)}, bf16[4,192,2048]{2,1,0:T(8,128)(2,1)}, f32[4,8,128]{2,1,0:T(8,128)}) custom-call(bf16[128,1536]{1,0:T(8,128)(2,1)} %reduce-scatter.4.cloned.1.call-done.refs_0_, bf16[192,2048]{1,0:T(8,128)(2,1)} %reduce-scatter.6.cloned.1.call-done.refs_1_, f32[8,128]{1,0:T(8,128)} %broadcast_in_dim.107.refs_2_), custom_call_target="tpu_custom_call" | custom-call | bytes 94699520 | tf_op jit(solution)/shard_map/exchange/pallas_call | solution.py:574
  492.4 3.2 spread_cols.3
  499.1 30.5 %exchange.12 = (bf16[4,192,2048]{2,1,0:T(8,128)(2,1)}, f32[8,8,256]{2,1,0:T(8,128)}) custom-call(bf16[192,2048]{1,0:T(8,128)(2,1)} %reduce-scatter.8.cloned.1.call-done.refs_0_, f32[8,8,256]{2,1,0:T(8,128)} %fusion.28.refs_1_), custom_call_target="tpu_custom_call" | custom-call | bytes 64225280 | tf_op jit(solution)/shard_map/exchange/pallas_call | solution.py:574
  531.4 3.0 spread_cols.2
  (214 shorter events, 60.1 us)
Async XLA Ops:
  7.2 137.0 %copy-start = (bf16[512,1536]{1,0:T(8,128)(2,1)S(1)}, bf16[512,1536]{1,0:T(8,128)(2,1)}, u32[]{:S(2)}) copy-start(bf16[512,1536]{1,0:T(8,128)(2,1)} %param.22) | copy-start | bytes 4718596
  7.2 177.9 %all-gather.2.cloned.1.call-start = ((), (), s32[]{:S(2)}) async-start(), calls=%async_computation.3 | async-start | bytes 7077888 | tf_op jit(solution)/shard_map/all_gather | solution.py:814
  14.9 56.1 %copy-start.45 = (s32[1,8]{1,0:T(1,128)S(1)}, s32[1,8]{1,0:T(1,128)}, u32[]{:S(2)}) copy-start(s32[1,8]{1,0:T(1,128)} %param.13) | copy-start | bytes 100
  14.9 56.6 %copy-start.39 = (s32[1,768]{1,0:T(1,128)S(1)}, s32[1,768]{1,0:T(1,128)}, u32[]{:S(2)}) copy-start(s32[1,768]{1,0:T(1,128)} %param.14) | copy-start | bytes 9220
  14.9 57.2 %copy-start.46 = (f32[24]{0:T(128)S(1)}, f32[24]{0:T(128)}, u32[]{:S(2)}) copy-start(f32[24]{0:T(128)} %param.18) | copy-start | bytes 292
  14.9 57.4 %copy-start.40 = (f32[2,64]{1,0:T(2,128)S(1)}, f32[2,64]{1,0:T(2,128)}, u32[]{:S(2)}) copy-start(f32[2,64]{1,0:T(2,128)} %param.19) | copy-start | bytes 1540
  71.0 228.1 %reduce-scatter.4.cloned.1.call-start = ((), (), s32[]{:S(2)}) async-start(), calls=%async_computation.4 | async-start | bytes 3538944 | tf_op jit(solution)/shard_map/reduce_scatter | solution.py:865
  149.3 35.8 %copy-start.35 = (f32[1536]{0:T(1024)S(1)}, f32[1536]{0:T(1024)}, u32[]{:S(2)}) copy-start(f32[1536]{0:T(1024)} %get-tuple-element.105) | copy-start | bytes 18436
  185.1 8.2 %copy-start.20 = (bf16[768,1536]{1,0:T(8,128)(2,1)S(1)}, bf16[768,1536]{1,0:T(8,128)(2,1)}, u32[]{:S(2)}) copy-start(bf16[768,1536]{1,0:T(8,128)(2,1)} %copy-done.19) | copy-start | bytes 7077892
  185.2 8.2 %copy-start.41 = (bf16[1024,1536]{1,0:T(8,128)(2,1)S(1)}, bf16[1024,1536]{1,0:T(8,128)(2,1)}, u32[]{:S(2)}) copy-start(bf16[1024,1536]{1,0:T(8,128)(2,1)} %get-tuple-element.51) | copy-start | bytes 9437188
  185.2 13.2 %slice-start.2 = ((s8[6291456]{0:T(1024)(128)(4,1)}), s8[4194304]{0:T(1024)(128)(4,1)S(1)}, s32[]{:S(2)}) async-start(s8[6291456]{0:T(1024)(128)(4,1)} %bitcast.70), calls=%async_computation.9 | async-start | bytes 8388608
  193.3 5.1 copy-start.22
  193.3 5.1 slice-start.3
  198.4 9.9 %copy-start.49 = (bf16[768,1024]{1,0:T(8,128)(2,1)}, bf16[768,1024]{1,0:T(8,128)(2,1)S(1)}, u32[]{:S(2)}) copy-start(bf16[768,1024]{1,0:T(8,128)(2,1)S(1)} %get-tuple-element.112) | copy-start | bytes 4718596
  198.4 9.9 %copy-start.47 = (bf16[768,1024]{1,0:T(8,128)(2,1)}, bf16[768,1024]{1,0:T(8,128)(2,1)S(1)}, u32[]{:S(2)}) copy-start(bf16[768,1024]{1,0:T(8,128)(2,1)S(1)} %get-tuple-element.114) | copy-start | bytes 4718596
  217.1 133.4 %reduce-scatter.6.cloned.1.call-start = ((), (), s32[]{:S(2)}) async-start(), calls=%async_computation.5 | async-start | bytes 7077888 | tf_op jit(solution)/shard_map/reduce_scatter | solution.py:865
  247.0 4.9 copy-start.23
  247.0 4.9 copy-start.50
  247.0 4.8 copy-start.51
  259.3 239.7 %reduce-scatter.8.cloned.1.call-start = ((), (), s32[]{:S(2)}) async-start(), calls=%async_computation.6 | async-start | bytes 7077888 | tf_op jit(solution)/shard_map/reduce_scatter | solution.py:865
  301.7 37.6 %copy-start.4 = (bf16[768,1536]{1,0:T(8,128)(2,1)S(1)}, bf16[768,1536]{1,0:T(8,128)(2,1)}, u32[]{:S(2)}) copy-start(bf16[768,1536]{1,0:T(8,128)(2,1)} %copy-done.2) | copy-start | bytes 7077892
  301.7 37.6 %copy-start.34 = (f32[1536]{0:T(1024)S(1)}, f32[1536]{0:T(1024)}, u32[]{:S(2)}) copy-start(f32[1536]{0:T(1024)} %copy-done.33) | copy-start | bytes 18436
  301.7 37.6 %copy-start.38 = (f32[768]{0:T(1024)S(1)}, f32[768]{0:T(1024)}, u32[]{:S(2)}) copy-start(f32[768]{0:T(1024)} %copy-done.37) | copy-start | bytes 9220
  350.6 4.7 copy-start.24
  355.2 4.2 copy-start.25
  360.3 4.1 copy-start.48
  360.3 8.0 %slice-start = ((s8[5111808]{0:T(1024)(128)(4,1)}), s8[4194304]{0:T(1024)(128)(4,1)S(1)}, s32[]{:S(2)}) async-start(s8[5111808]{0:T(1024)(128)(4,1)} %bitcast.59), calls=%async_computation.7 | async-start | bytes 8388608
  364.4 3.9 slice-start.1
  364.4 3.9 copy-start.43
  368.3 8.1 %copy-start.36 = (f32[768]{0:T(1024)S(1)}, f32[768]{0:T(1024)}, u32[]{:S(2)}) copy-start(f32[768]{0:T(1024)} %get-tuple-element.119) | copy-start | bytes 9220
  492.4 4.5 copy-start.26
  496.9 40.5 %copy-start.1 = (bf16[512,1536]{1,0:T(8,128)(2,1)S(1)}, bf16[512,1536]{1,0:T(8,128)(2,1)}, u32[]{:S(2)}) copy-start(bf16[512,1536]{1,0:T(8,128)(2,1)} %param.22) | copy-start | bytes 4718596
  (28 other events, 50.4 us)
Sparse Core Ops, SparseCore 0:
  71.1 69.6 all-gather.1
  217.2 40.1 reduce-scatter.3
  260.3 68.8 reduce-scatter.5
  350.7 69.3 reduce-scatter.7

commit v3 on v2

--- a/solution.py
+++ b/solution.py
@@ -10,8 +10,13 @@
 EPS = 1e-06
 SCALE = 0.125
 LANES = 128
+VMEM_LIMIT = 60 << 20
 F32 = jnp.float32
 BF16 = jnp.bfloat16
+
+
+MESH = pl.DeviceIdType.MESH
+ANY = pl.BlockSpec(memory_space=pltpu.HBM)
 
 
 def rms_scale(values):
@@ -136,14 +141,36 @@
 
 
 def attend_back_kernel(
-    head, chunk, width, heads,
+    head, chunk, width, heads, ranks,
     pos_row, pos_col, seg_row, seg_col, bias, gains, query, key, gate, forget,
-    attended, wide_query, wide_key, wide_value, grad_gated,
-    grad_project, small,
-    mask, wide_grad, grad_query, grad_key, grad_value, grad_prefix,
+    attended, wide_query, wide_key, wide_value, grad_gated, aside,
+    grad_project, small, aside_in,
+    mask, wide_grad, grad_query, grad_key, grad_value, grad_prefix, *sems,
 ):
     step = pl.program_id(0)
     steps = pl.num_programs(0)
+
+    def aside_copies():
+        send_sem, recv_sem, own_sem = sems
+        rank = lax.axis_index("ctx")
+        size = aside_in.shape[1]
+        yield pltpu.make_async_copy(rows_of(aside, rank, size), aside_in.at[rank], own_sem)
+        for distance in range(1, ranks):
+            other = rank ^ distance
+            yield to_rank(
+                rows_of(aside, other, size), aside_in.at[rank],
+                send_sem.at[distance - 1], recv_sem.at[distance - 1], other,
+            )
+
+    if ranks:
+
+        @pl.when(step == 0)
+        def _():
+            rank = lax.axis_index("ctx")
+            greet([{"ctx": rank ^ distance} for distance in range(1, ranks)])
+            for copy in aside_copies():
+                copy.start()
+
     rows = query.shape[0]
     lanes = lane_ids(rows)
     half = lane_ids(rows, head)
@@ -229,6 +256,10 @@
             grad_project[part, 4 * width : 4 * width + LANES] = grad_logit
             small[2:3, :] += jnp.sum(grad_logit.astype(F32), axis=0, keepdims=True)
 
+        if ranks:
+            for copy in aside_copies():
+                copy.wait()
+
 
 def pick_chunk(rows):
     return 256 if rows % 256 == 0 else 128
@@ -263,12 +294,12 @@
             wide_shape, wide_shape, wide_shape,
         ],
         scratch_shapes=[pltpu.VMEM((rows, rows), F32), pltpu.VMEM((rows, LANES), F32)],
-        compiler_params=pltpu.CompilerParams(vmem_limit_bytes=48 << 20),
+        compiler_params=pltpu.CompilerParams(vmem_limit_bytes=VMEM_LIMIT),
         name="attend",
     )(*places, bias, gains, project, project, project, project, project)
 
 
-def attend_back(project, places, bias, gains, attended, wides, grad_gated, head, width, heads):
+def attend_back(project, places, bias, gains, attended, wides, grad_gated, aside, ranks, head, width, heads):
     rows = project.shape[0]
     steps = width // LANES
     per = LANES // head
@@ -282,14 +313,15 @@
     forget = pl.BlockSpec((rows, LANES), lambda step: (0, 4 * steps))
     total = 4 * width + LANES
     return pl.pallas_call(
-        functools.partial(attend_back_kernel, head, chunk, width, heads),
+        functools.partial(attend_back_kernel, head, chunk, width, heads, ranks),
         grid=(steps,),
         in_specs=[whole(p.shape) for p in places] + [whole(bias.shape), whole(gains.shape)]
-        + [part(0), part(1), part(3), forget, own, wide, wide, wide, own],
-        out_specs=[whole((rows, total)), whole((8, LANES))],
+        + [part(0), part(1), part(3), forget, own, wide, wide, wide, own, ANY],
+        out_specs=[whole((rows, total)), whole((8, LANES)), ANY],
         out_shape=[
             jax.ShapeDtypeStruct((rows, total), BF16),
             jax.ShapeDtypeStruct((8, LANES), F32),
+            jax.ShapeDtypeStruct((max(ranks, 1), aside.shape[0] // max(ranks, 1), aside.shape[1]), BF16),
         ],
         scratch_shapes=[
             pltpu.VMEM((rows, rows), F32),
@@ -298,14 +330,17 @@
             pltpu.VMEM((rows, LANES), F32),
             pltpu.VMEM((rows, LANES), F32),
             pltpu.VMEM((rows, LANES), F32),
-        ],
-        compiler_params=pltpu.CompilerParams(vmem_limit_bytes=48 << 20),
+        ]
+        + (
+            [pltpu.SemaphoreType.DMA((ranks - 1,)), pltpu.SemaphoreType.DMA((ranks - 1,)), pltpu.SemaphoreType.DMA]
+            if ranks
+            else []
+        ),
+        compiler_params=pltpu.CompilerParams(
+            collective_id=5 if ranks else None, has_side_effects=ranks > 0, vmem_limit_bytes=VMEM_LIMIT
+        ),
         name="attend_back",
-    )(*places, bias, gains, project, project, project, project, attended, *wides, grad_gated)
-
-
-MESH = pl.DeviceIdType.MESH
-ANY = pl.BlockSpec(memory_space=pltpu.HBM)
+    )(*places, bias, gains, project, project, project, project, attended, *wides, grad_gated, aside)
 
 
 def greet(peers, line=None):
@@ -658,11 +693,247 @@
         ]
         + line_scratch(shards),
         compiler_params=pltpu.CompilerParams(
-            collective_id=collective_id, has_side_effects=True, vmem_limit_bytes=24 << 20
+            collective_id=collective_id, has_side_effects=True, vmem_limit_bytes=VMEM_LIMIT
         ),
         cost_estimate=pl.CostEstimate(flops=0, bytes_accessed=150 << 20, transcendentals=0),
         name="start_moves",
     )(tokens, cotangent, weight, tail, other)
+
+
+VMEM_WHOLE = pl.BlockSpec(memory_space=pltpu.VMEM)
+
+
+def to_rank(source, target, send, recv, other):
+    return pltpu.make_async_remote_copy(
+        source, target, send, recv, device_id={"ctx": other}, device_id_type=MESH
+    )
+
+
+def middle_kernel(
+    ranks,
+    grad_gate_up, w_gate_up, mixed, cotangent, w_out, gain, mixed_grad, gated_grad, gain_grad,
+    grad_in, weight_in, mixed_in, cotangent_in, out_in, wide, first_out, first_in, second_out, second_in,
+    load_sem, first_send, first_recv, second_send, second_recv,
+):
+    rank = lax.axis_index("ctx")
+    rows = mixed.shape[0] // ranks
+    model, width = w_out.shape
+    tile = 256
+    loads = [
+        pltpu.make_async_copy(a, b, load_sem.at[n])
+        for n, (a, b) in enumerate(
+            (
+                (w_gate_up, weight_in), (grad_gate_up, grad_in), (mixed, mixed_in), (cotangent, cotangent_in),
+                (w_out, out_in),
+            )
+        )
+    ]
+    for copy in loads:
+        copy.start()
+    greet([{"ctx": rank ^ distance} for distance in range(1, ranks)])
+    gain_grad[...] = jnp.zeros_like(gain_grad)
+    for copy in loads:
+        copy.wait()
+
+    def part(turn):
+        return pl.ds(pl.multiple_of(turn * rows, 16), rows)
+
+    def send(out, into, send_sem, recv_sem, turn, distance):
+        other = rank ^ distance
+        return to_rank(
+            out.at[other, part(turn), :], into.at[distance, part(turn), :],
+            send_sem.at[distance - 1, turn], recv_sem.at[distance - 1, turn], other,
+        )
+
+    def arrived(out, into, send_sem, recv_sem, turn):
+        total = out[rank, part(turn), :].astype(F32)
+        for distance in range(1, ranks):
+            send(out, into, send_sem, recv_sem, turn, distance).wait_recv()
+            total = total + into[distance, part(turn), :].astype(F32)
+        return total
+
+    first = (first_out, first_in, first_send, first_recv)
+    second = (second_out, second_in, second_send, second_recv)
+
+    def project(turn):
+        here = part(turn)
+        total = cotangent_in[here, pl.ds(pl.multiple_of(rank * width, LANES), width)].astype(F32)
+        total = total + arrived(*first, turn)
+        mixed_grad[here, :] = total
+        low = total.astype(BF16)
+        for index in range(ranks):
+            second_out[index, here, :] = right_product(low, out_in[index * width : (index + 1) * width, :]).astype(BF16)
+        for distance in range(1, ranks):
+            send(*second, turn, distance).start()
+
+    @pl.loop(0, ranks)
+    def _(turn):
+        here = part(turn)
+
+        @pl.loop(0, model // tile)
+        def _(step):
+            cols = pl.ds(pl.multiple_of(step * tile, tile), tile)
+            wide[:, cols] = right_product(grad_in[here, :], weight_in[cols, :])
+
+        values = mixed_in[here, :].astype(F32)
+        scale = rms_scale(values)
+        grad = wide[...]
+        gain_grad[0:1, :] += jnp.sum(grad * values * scale, axis=0, keepdims=True)
+        back = norm_back(grad, values, scale, gain[0:1, :]).astype(BF16)
+        for index in range(ranks):
+            first_out[index, here, :] = back[:, index * width : (index + 1) * width]
+        for distance in range(1, ranks):
+            send(*first, turn, distance).start()
+
+        @pl.when(turn > 0)
+        def _():
+            project(turn - 1)
+
+    project(ranks - 1)
+
+    @pl.loop(0, ranks)
+    def _(turn):
+        gated_grad[part(turn), :] = arrived(*second, turn)
+
+    @pl.loop(0, ranks)
+    def _(turn):
+        for distance in range(1, ranks):
+            send(*first, turn, distance).wait_send()
+            send(*second, turn, distance).wait_send()
+
+
+def middle(collective_id, ranks, grad_gate_up, w_gate_up, mixed, cotangent, w_out, gain):
+    rows, model = mixed.shape
+    width = w_out.shape[1]
+    blocks = pltpu.VMEM((ranks, rows, width), BF16)
+    sems = pltpu.SemaphoreType.DMA((ranks - 1, ranks))
+    return pl.pallas_call(
+        functools.partial(middle_kernel, ranks),
+        in_specs=[ANY] * 5 + [VMEM_WHOLE],
+        out_specs=[VMEM_WHOLE] * 3,
+        out_shape=[
+            jax.ShapeDtypeStruct((rows, width), F32),
+            jax.ShapeDtypeStruct((rows, width), F32),
+            jax.ShapeDtypeStruct((8, model), F32),
+        ],
+        scratch_shapes=[
+            pltpu.VMEM(grad_gate_up.shape, BF16),
+            pltpu.VMEM(w_gate_up.shape, BF16),
+            pltpu.VMEM(mixed.shape, BF16),
+            pltpu.VMEM(cotangent.shape, BF16),
+            pltpu.VMEM(w_out.shape, BF16),
+            pltpu.VMEM((rows // ranks, model), F32),
+            blocks, blocks, blocks, blocks,
+            pltpu.SemaphoreType.DMA((5,)),
+            sems, sems, sems, sems,
+        ],
+        compiler_params=pltpu.CompilerParams(
+            collective_id=collective_id, has_side_effects=True, vmem_limit_bytes=VMEM_LIMIT
+        ),
+        cost_estimate=pl.CostEstimate(flops=0, bytes_accessed=150 << 20, transcendentals=0),
+        name="middle",
+    )(grad_gate_up, w_gate_up, mixed, cotangent, w_out, gain)
+
+
+def last_kernel(
+    ranks,
+    grad_project, w_in, inputs, mixed_grad, gain, sums, tokens_grad, total_sums,
+    grad_in, weight_in, inputs_in, wide, out, into, sums_out, sums_in,
+    load_sem, send_sem, recv_sem, sums_send, sums_recv,
+):
+    rank = lax.axis_index("ctx")
+    rows = inputs.shape[0] // ranks
+    model, width = inputs.shape[1], mixed_grad.shape[1]
+    tile = 256
+    loads = [
+        pltpu.make_async_copy(a, b, load_sem.at[n])
+        for n, (a, b) in enumerate(((w_in, weight_in), (grad_project, grad_in), (inputs, inputs_in)))
+    ]
+    for copy in loads:
+        copy.start()
+    greet([{"ctx": rank ^ distance} for distance in range(1, ranks)])
+    sums_out[...] = sums[...]
+    for copy in loads:
+        copy.wait()
+
+    def send(distance):
+        other = rank ^ distance
+        return to_rank(out.at[other], into.at[distance], send_sem.at[distance - 1], recv_sem.at[distance - 1], other)
+
+    def send_sums(distance):
+        return to_rank(
+            sums_out, sums_in.at[distance], sums_send.at[distance - 1], sums_recv.at[distance - 1], rank ^ distance
+        )
+
+    def compute(other):
+        here = pl.ds(pl.multiple_of(other * rows, 16), rows)
+
+        @pl.loop(0, model // tile)
+        def _(step):
+            cols = pl.ds(pl.multiple_of(step * tile, tile), tile)
+            wide[:, cols] = right_product(grad_in[here, :], weight_in[cols, :])
+
+        values = inputs_in[here, :].astype(F32)
+        scale = rms_scale(values)
+        grad = wide[...]
+        sums_out[0:1, :] += jnp.sum(grad * values * scale, axis=0, keepdims=True)
+        wide[...] = norm_back(grad, values, scale, gain[0:1, :])
+        own = pl.ds(pl.multiple_of(rank * width, LANES), width)
+        wide[:, own] += mixed_grad[here, :]
+        out[other] = wide[...].astype(BF16)
+
+    @pl.loop(1, ranks)
+    def _(distance):
+        compute(rank ^ distance)
+        send(distance).start()
+
+    compute(rank)
+    for distance in range(1, ranks):
+        send_sums(distance).start()
+    total = out[rank].astype(F32)
+    for distance in range(1, ranks):
+        send(distance).wait_recv()
+        total = total + into[distance].astype(F32)
+    tokens_grad[...] = total.astype(BF16)
+    total = sums_out[...]
+    for distance in range(1, ranks):
+        send_sums(distance).wait_recv()
+        total = total + sums_in[distance]
+    total_sums[...] = total
+    for distance in range(1, ranks):
+        send(distance).wait_send()
+        send_sums(distance).wait_send()
+
+
+def last_moves(collective_id, ranks, grad_project, w_in, inputs, mixed_grad, gain, sums):
+    rows, model = inputs.shape
+    blocks = pltpu.VMEM((ranks, rows // ranks, model), BF16)
+    sems = pltpu.SemaphoreType.DMA((ranks - 1,))
+    return pl.pallas_call(
+        functools.partial(last_kernel, ranks),
+        in_specs=[ANY] * 3 + [VMEM_WHOLE] * 3,
+        out_specs=[VMEM_WHOLE] * 2,
+        out_shape=[
+            jax.ShapeDtypeStruct((rows // ranks, model), BF16),
+            jax.ShapeDtypeStruct((8, model), F32),
+        ],
+        scratch_shapes=[
+            pltpu.VMEM(grad_project.shape, BF16),
+            pltpu.VMEM(w_in.shape, BF16),
+            pltpu.VMEM(inputs.shape, BF16),
+            pltpu.VMEM((rows // ranks, model), F32),
+            blocks, blocks,
+            pltpu.VMEM((8, model), F32),
+            pltpu.VMEM((ranks, 8, model), F32),
+            pltpu.SemaphoreType.DMA((3,)),
+            sems, sems, sems, sems,
+        ],
+        compiler_params=pltpu.CompilerParams(
+            collective_id=collective_id, has_side_effects=True, vmem_limit_bytes=VMEM_LIMIT
+        ),
+        cost_estimate=pl.CostEstimate(flops=0, bytes_accessed=150 << 20, transcendentals=0),
+        name="last_moves",
+    )(grad_project, w_in, inputs, mixed_grad, gain, sums)
 
 
 def spread_kernel(pieces, *refs):
@@ -698,7 +969,7 @@
         in_specs=[pl.BlockSpec((ranks, part, cols), lambda step: (0, step, 0))],
         out_specs=[pl.BlockSpec((part, w), lambda step: (step, 0)) for w in widths],
         out_shape=[jax.ShapeDtypeStruct((rows, w), F32) for w in widths],
-        compiler_params=pltpu.CompilerParams(vmem_limit_bytes=32 << 20),
+        compiler_params=pltpu.CompilerParams(vmem_limit_bytes=VMEM_LIMIT),
         cost_estimate=pl.CostEstimate(flops=0, bytes_accessed=rows * sum(widths) * 6, transcendentals=0),
         name="spread_cols",
     )(source)
@@ -726,15 +997,6 @@
     def gather_cols(self, number, array, piece):
         return lax.all_gather(array, "ctx", axis=1, tiled=True), lax.all_gather(piece, "fsdp", axis=0, tiled=True)
 
-    def scatter_cols(self, number, array):
-        return lax.psum_scatter(array, "ctx", scatter_dimension=1, tiled=True).astype(F32)
-
-    def finish_rows(self, number, first, second, sums):
-        pair = [
-            lax.psum_scatter(a, "ctx", scatter_dimension=0, tiled=True).astype(F32) for a in (first, second)
-        ]
-        return pair + [lax.psum(sums, "ctx")]
-
     def stack(self, number, *arrays):
         return [lax.all_gather(a, "ctx", axis=0, tiled=False) for a in arrays]
 
@@ -758,13 +1020,6 @@
 
     def gather_cols(self, number, array, piece):
         return self.run(number, ("gather_cols", array), ("line", piece))
-
-    def scatter_cols(self, number, array):
-        return self.run(number, ("scatter_cols", array))[0].astype(F32).sum(axis=0)
-
-    def finish_rows(self, number, first, second, sums):
-        out = self.run(number, ("scatter_rows", first), ("scatter_rows", second), ("each", sums))
-        return [a.astype(F32).sum(axis=0) for a in out]
 
     def stack(self, number, *arrays):
         return self.run(number, *[("stack" if a.dtype == BF16 else "each", a) for a in arrays])
@@ -825,7 +1080,7 @@
     bias = jnp.pad(slab(forget_bias, rank * local_heads, local_heads, 0), (0, LANES - local_heads))[None]
     head_gains = jnp.tile(qk_gains, (1, LANES // head_dim))
 
-    gain_cols = w_in[:, 4 * padded : 4 * padded + LANES].astype(F32).T
+    gain_cols = lax.optimization_barrier(w_in[:, 4 * padded : 4 * padded + LANES]).astype(F32).T
     gain_one = gain_cols[local_heads]
     gain_two = gain_cols[local_heads + 1]
 
@@ -838,10 +1093,10 @@
     )
     gated_all, w_out = comm.gather_cols(1, gated[:, :width], slab(out_weight, rank * width, width, 1))
     mixed_cols = slab(inputs, rank * width, width, 1).astype(F32) + dot(gated_all, w_out)
-    mixed, w_down = comm.gather_cols(
+    mixed_low, w_down = comm.gather_cols(
         2, mixed_cols.astype(BF16), slab(down_weight, rank * hidden_piece, hidden_piece, 0)
     )
-    mixed = mixed.astype(F32)
+    mixed = mixed_low.astype(F32)
     scale_two = rms_scale(mixed)
     normed_two = (mixed * scale_two * gain_two).astype(BF16)
     gate_up = dot(normed_two, w_gate_up)
@@ -857,26 +1112,40 @@
     grad_hidden = right_product(grad_low, w_down)
     grad_gate = grad_hidden * up_part * gate_sigmoid * (1.0 + gate_part * (1.0 - gate_sigmoid))
     grad_gate_up = jnp.concatenate([grad_gate, grad_hidden * silu], axis=1).astype(BF16)
-    grad_normed_two = right_product(grad_gate_up, w_gate_up)
-    gain_two_grad = jnp.sum(grad_normed_two * mixed * scale_two, axis=0)
-    grad_mixed_part = norm_back(grad_normed_two, mixed, scale_two, gain_two).astype(BF16)
 
     def reduce_shards(array):
         return lax.psum_scatter(array.astype(BF16), "fsdp", scatter_dimension=0, tiled=True)
 
     down_part_grad = left_product(hidden_act, grad_low).astype(BF16)
-    grad_mixed_part, down_part_grad = lax.optimization_barrier((grad_mixed_part, down_part_grad))
+    gate_up_grad = left_product(normed_two, grad_gate_up).astype(BF16)
+    grad_gate_up, down_part_grad, gate_up_grad = lax.optimization_barrier(
+        (grad_gate_up, down_part_grad, gate_up_grad)
+    )
     down_share = reduce_shards(down_part_grad)
-    grad_mixed_cols = slab(grad_low, rank * width, width, 1).astype(F32) + comm.scatter_cols(3, grad_mixed_part)
-    grad_branch = grad_mixed_cols.astype(BF16)
-    gate_up_grad = left_product(normed_two, grad_gate_up).astype(BF16)
-    grad_branch, gate_up_grad = lax.optimization_barrier((grad_branch, gate_up_grad))
     gate_up_share = reduce_shards(gate_up_grad)
-    grad_gated = widen(comm.scatter_cols(4, right_product(grad_branch, w_out).astype(BF16)))
+    if plain:
+        grad_mixed_cols, grad_gated, gain_two_grad = middle(
+            3, ranks, grad_gate_up, w_gate_up, mixed_low, grad_low, w_out, gain_two[None]
+        )
+        gain_two_grad = gain_two_grad[0]
+        grad_branch = grad_mixed_cols.astype(BF16)
+    else:
+        grad_normed_two = right_product(grad_gate_up, w_gate_up)
+        gain_two_grad = jnp.sum(grad_normed_two * mixed * scale_two, axis=0)
+        grad_mixed_part = norm_back(grad_normed_two, mixed, scale_two, gain_two).astype(BF16)
+        grad_mixed_cols = slab(grad_low, rank * width, width, 1).astype(F32) + lax.psum_scatter(
+            grad_mixed_part, "ctx", scatter_dimension=1, tiled=True
+        ).astype(F32)
+        grad_branch = grad_mixed_cols.astype(BF16)
+        grad_gated = widen(
+            lax.psum_scatter(
+                right_product(grad_branch, w_out).astype(BF16), "ctx", scatter_dimension=1, tiled=True
+            ).astype(F32)
+        )
     grad_gated, down_share = lax.optimization_barrier((grad_gated, down_share))
-    grad_project, small = attend_back(
+    grad_project, small, down_pieces = attend_back(
         project, places_all, bias, head_gains, attended, (wide_query, wide_key, wide_value),
-        grad_gated, head_dim, padded, local_heads,
+        grad_gated, down_part, ranks if plain else 0, head_dim, padded, local_heads,
     )
 
     in_part = left_product(normed, grad_project).astype(BF16)
@@ -885,26 +1154,30 @@
     late, gate_up_share = lax.optimization_barrier((late, gate_up_share))
     late_share = reduce_shards(late)
 
-    grad_normed = right_product(grad_project, w_in)
-    gain_one_grad = jnp.sum(grad_normed * wide_inputs * scale_one, axis=0)
-    in_own = jnp.arange(model_width, dtype=jnp.int32) // width == rank
-    grad_inputs = norm_back(grad_normed, wide_inputs, scale_one, gain_one) + jnp.where(
-        in_own[None], jnp.tile(grad_mixed_cols, (1, ranks)), 0.0
-    )
     bias_slots = jnp.where(
         jnp.arange(ranks, dtype=jnp.int32)[:, None] == rank, small[2, :local_heads][None], 0.0
     ).reshape(-1)
     qk_sum = small[0:2].reshape(2, LANES // head_dim, head_dim).sum(axis=1).reshape(-1)
     others = jnp.concatenate([bias_slots, qk_sum])
-    sums = jnp.stack(
-        [gain_one_grad, gain_two_grad, jnp.pad(others, (0, model_width - others.shape[0]))]
-        + [jnp.zeros((model_width,), F32)] * 5
-    )
-    down_sum, tokens_grad, sums = comm.finish_rows(5, down_part, grad_inputs.astype(BF16), sums)
-    tokens_grad = tokens_grad.astype(BF16)[None]
-    result = own_rows(mixed) + down_sum
+    others = jnp.pad(others, (0, model_width - others.shape[0]))
+    if plain:
+        down_sum = down_pieces.astype(F32).sum(axis=0)
+        sums = jnp.stack([jnp.zeros_like(others), gain_two_grad, others] + [jnp.zeros_like(others)] * 5)
+        tokens_grad, sums = last_moves(4, ranks, grad_project, w_in, inputs, grad_mixed_cols, gain_one[None], sums)
+        tokens_grad = tokens_grad[None]
+    else:
+        grad_normed = right_product(grad_project, w_in)
+        gain_one_grad = jnp.sum(grad_normed * wide_inputs * scale_one, axis=0)
+        in_own = jnp.arange(model_width, dtype=jnp.int32) // width == rank
+        grad_inputs = norm_back(grad_normed, wide_inputs, scale_one, gain_one) + jnp.where(
+            in_own[None], jnp.tile(grad_mixed_cols, (1, ranks)), 0.0
+        )
+        down_sum = lax.psum_scatter(down_part, "ctx", scatter_dimension=0, tiled=True).astype(F32)
+        tokens_grad = lax.psum_scatter(grad_inputs.astype(BF16), "ctx", scatter_dimension=0, tiled=True)[None]
+        sums = lax.psum(jnp.stack([gain_one_grad, gain_two_grad, others]), "ctx")
+    result = own_rows(mixed_low).astype(F32) + down_sum
     block_out = result.astype(BF16)[None]
-    branch = result - own_rows(wide_inputs)
+    branch = result - own_rows(inputs).astype(F32)
     own_valid = own_rows(valid)
     partial_sums = jnp.stack(
         [
@@ -922,7 +1195,7 @@
     share = model_width // shards
     room = -(-share // LANES) * LANES
     gain_pieces = jnp.pad(sums[0:2].reshape(2, shards, share).transpose(1, 0, 2), ((0, 0), (0, 0), (0, room - share)))
-    tail = jnp.pad(sums[2, : others.shape[0]], (0, 2 * room - others.shape[0])).reshape(1, 2, room)
+    tail = sums[2, : 2 * room].reshape(1, 2, room)
     pieces = jnp.concatenate(
         [gain_pieces, jnp.broadcast_to(tail, (shards, 2, room)), jnp.zeros((shards, 4, room), F32)], axis=1
     )

time: 549 us -> 486 us (0.89)
  other arithmetic: 50.9 us -> 23.8 us
  matrix products: 72.5 us -> 51.8 us
  local copies, waits for them, and re-layouts: 39.7 us -> 28.4 us
  Pallas kernels: 365 us -> 357 us
    pallas_call x7 -> x4, Pallas kernels: 252 us -> 132 us  [exchange(): pl.pallas_call(functools.partial(exchange_kernel, [mode for mode, _ in op...]
    pallas_call x0 -> x2, Pallas kernels: none -> 107 us  [the longest x1 66.5 us: middle(): pl.pallas_call(functools.partial(middle_kernel, ranks), in_specs=[ANY] *...]
    unnamed x117 -> x39, local copies, waits for them, and re-layouts: 29 us -> 3.26 us
    dot_general x4 -> x1, matrix products: 26 us -> 3.82 us  [right_product(): lax.dot_general(left, right, (((1,), (1,)), ((), ())), preferred_element_...]
    convert_element_type x5 -> x0, other arithmetic: 21 us -> none  [the longest x1 6.35 us: body(): grad_inputs.astype(BF16)]
    reduce_sum x5 -> x1, other arithmetic: 11.6 us -> 2.12 us  [body(): down_sum = down_pieces.astype(F32).sum(axis=0)]
    pallas_call x0 -> x1, local copies, waits for them, and re-layouts: none -> 7.66 us  [start_moves(): pl.pallas_call(functools.partial(start_kernel, shards, width, piece), in_...]
  transfers between devices with their start and end apart: 4 -> 4, of which waited for: 0 -> 0; matrix products, arithmetic and copies ran while one was open for 19% -> 14% of each run, Pallas kernels for 52% -> 56%
where the time goes in v3:
time: 486 us; the launch traced here: 477 us
  Pallas kernels  357 us (73%)
  matrix products  51.8 us (11%)
  local copies, waits for them, and re-layouts  28.4 us (6%)
  other arithmetic  23.8 us (5%)
  between operations  15.3 us (3%)
    pallas_call x4, Pallas kernels, exchange(): pl.pallas_call(functools.partial(exchange_kernel, [mode for mode, _ in op...  132 us
    pallas_call x1, Pallas kernels, middle(): pl.pallas_call(functools.partial(middle_kernel, ranks), in_specs=[ANY] *...  66.5 us
    pallas_call x1, Pallas kernels, start_moves(): pl.pallas_call(functools.partial(start_kernel, shards, width, piece), in_...  53.4 us
    pallas_call x1, Pallas kernels, last_moves(): pl.pallas_call(functools.partial(last_kernel, ranks), in_specs=[ANY] * 3...  40.9 us
    pallas_call x1, Pallas kernels, attend_back(): pl.pallas_call(functools.partial(attend_back_kernel, head, chunk, width,...  33.4 us
    dot_general x4, matrix products, dot(): lax.dot_general(left, right, (((1,), (0,)), ((), ())), preferred_element_...  25.1 us
    dot_general x4, matrix products, left_product(): lax.dot_general(left, right, (((0,), (0,)), ((), ())), preferred_element_...  22.9 us
    pallas_call x1, Pallas kernels, attend(): pl.pallas_call(functools.partial(attend_kernel, head, chunk, heads), grid...  20.4 us
  transfers between devices with their start and end apart: 4, of which 0 were waited for; matrix products, arithmetic and copies ran while one was open for 14% of the time, Pallas kernels for 56%

profile of v3, /device:TPU:0, one launch (start us, length us, event | category | flops | bytes accessed | tf_op | source)
XLA Modules:
  0.0 477.4 jit_solution(529396490720174353)
XLA Ops:
  9.9 53.4 %start_moves.1 = (bf16[768,1536]{1,0:T(8,128)(2,1)}, bf16[768,1536]{1,0:T(8,128)(2,1)}, bf16[1536,1664]{1,0:T(8,128)(2,1)}, bf16[192,2048]{1,0:T(8,128)(2,1)}) custom-call(bf16[192,1536]{1,0:T(8,128)(2,1)} %bitcast.47, bf16[192,1536]{1,0:T(8,128)(2,1)} %bitcast.48, bf16[192,6144]{1,0:T(8,128)(2,1)} %weight.1, bf16[192,128]{1,0:T(8,128)(2,1)} %maximum_maximum_fusion.tail, ...), custom_call_target="tpu_custom_call" | custom-call | bytes 157286400 | tf_op jit(solution)/shard_map/start_moves/pallas_call | solution.py:674
  64.1 1.0 add.106.pos_col
  67.8 7.7 %copy.53 = bf16[1536,1664]{0,1:T(8,128)(2,1)} copy(bf16[1536,1664]{1,0:T(8,128)(2,1)} %get-tuple-element.47.w_in) | data formatting | bytes 10223616 | tf_op jit(solution)/shard_map/start_moves/pallas_call | solution.py:674
  76.0 2.5 fusion
  79.2 8.8 %fusion.12.query.key.value.gate.forget = f32[768,1664]{1,0:T(8,128)} fusion(bf16[1536,1664]{1,0:T(8,128)(2,1)} %get-tuple-element.47.w_in, bf16[768,1536]{1,0:T(8,128)(2,1)S(1)} %copy-done.2, f32[1536]{0:T(1024)S(1)} %get-tuple-element.106, f32[768]{0:T(1024)S(1)} %add_rsqrt_fusion.1), kind=kOutput, calls=%fused_computation.31 | convolution fusion | flops 3930587136 | bytes 12592128 | tf_op jit(solution)/shard_map/dot_general | solution.py:35
  88.0 20.4 %attend.1 = (bf16[768,384]{1,0:T(8,128)(2,1)}, f32[768,384]{1,0:T(8,128)}, bf16[6,768,128]{2,1,0:T(8,128)(2,1)}, bf16[6,768,128]{2,1,0:T(8,128)(2,1)}, bf16[6,768,128]{2,1,0:T(8,128)(2,1)}) custom-call(s32[1,768]{1,0:T(1,128)} %add.96.pos_row, s32[768,1]{1,0:T(8,128)} %add.106.pos_col, s32[1,768]{1,0:T(1,128)} %broadcast_in_dim_reshape.8.seg_row, ...), custom_call_target="tpu_custom_call" | custom-call | tf_op jit(solution)/shard_map/attend/pallas_call | solution.py:285
  108.3 1.6 constant_dynamic-slice_fusion.1.refs_1_
  109.9 27.9 %exchange.4 = (bf16[768,1536]{1,0:T(8,128)(2,1)}, bf16[1536,384]{1,0:T(8,128)(2,1)}) custom-call(bf16[768,384]{1,0:T(8,128)(2,1)} %get-tuple-element.48.refs_0_, bf16[192,384]{1,0:T(8,128)(2,1)} %constant_dynamic-slice_fusion.1.refs_1_), custom_call_target="tpu_custom_call" | custom-call | bytes 70778880 | tf_op jit(solution)/shard_map/exchange/pallas_call | solution.py:609
  138.7 4.3 fusion.7.refs_0_
  143.0 33.6 %exchange.5 = (bf16[768,1536]{1,0:T(8,128)(2,1)}, bf16[1024,1536]{1,0:T(8,128)(2,1)}) custom-call(bf16[768,384]{1,0:T(8,128)(2,1)} %fusion.7.refs_0_, bf16[128,1536]{1,0:T(8,128)(2,1)} %constant_dynamic-slice_fusion.refs_1_), custom_call_target="tpu_custom_call" | custom-call | bytes 110100480 | tf_op jit(solution)/shard_map/exchange/pallas_call | solution.py:609
  176.6 2.2 fusion.3
  178.8 8.1 %fusion.9 = f32[768,2048]{1,0:T(8,128)S(1)} fusion(bf16[1536,2048]{1,0:T(8,128)(2,1)} %all-gather.2.cloned.1.call-done.w_gate_up, bf16[768,1536]{1,0:T(8,128)(2,1)} %get-tuple-element.51.mixed, f32[1536]{0:T(1024)S(1)} %get-tuple-element.105, f32[768]{0:T(1024)S(1)} %add_rsqrt_fusion), kind=kOutput, calls=%fused_computation.30 | convolution fusion | flops 4836556800 | bytes 14951424 | tf_op jit(solution)/shard_map/dot_general | solution.py:35
  187.0 3.8 multiply_convert_fusion.2
  190.8 2.0 pad_maximum_fusion.1.grad_gate_up
  192.8 1.4 copy-done.4
  194.2 7.4 %convolution_convert_fusion = bf16[1536,2048]{1,0:T(8,128)(2,1)} fusion(bf16[768,1536]{1,0:T(8,128)(2,1)S(1)} %copy-done.4, f32[1536]{0:T(1024)S(1)} %get-tuple-element.105, f32[768]{0:T(1024)S(1)} %add_rsqrt_fusion, bf16[768,1024]{1,0:T(8,128)(2,1)S(1)} %get-tuple-element.110, bf16[768,1024]{1,0:T(8,128)(2,1)S(1)} %get-tuple-element.109), kind=kOutput, calls=%fused_computation | convolution fusion | flops 4845993984 | bytes 11805696 | tf_op jit(solution)/shard_map/dot_general | solution.py:41
  201.6 5.7 %convolution_convert_fusion.2 = bf16[1024,1536]{1,0:T(8,128)(2,1)} fusion(bf16[768,1024]{1,0:T(8,128)(2,1)S(1)} %get-tuple-element.111, bf16[768,1536]{1,0:T(8,128)(2,1)} %get-tuple-element.56.cotangent), kind=kOutput, calls=%fused_computation.14 | convolution fusion | flops 2417491968 | bytes 7077888 | tf_op jit(solution)/shard_map/dot_general | solution.py:41
  208.3 66.5 %middle.1 = (f32[768,384]{1,0:T(8,128)}, f32[768,384]{1,0:T(8,128)}, f32[8,1536]{1,0:T(8,128)}) custom-call(bf16[768,2048]{1,0:T(8,128)(2,1)} %pad_maximum_fusion.1.grad_gate_up, bf16[1536,2048]{1,0:T(8,128)(2,1)} %all-gather.2.cloned.1.call-done.w_gate_up, bf16[768,1536]{1,0:T(8,128)(2,1)} %get-tuple-element.51.mixed, ...), custom_call_target="tpu_custom_call" | custom-call | bytes 157286400 | tf_op jit(solution)/shard_map/middle/pallas_call | solution.py:810
  274.8 2.8 convolution_convert_fusion.4
  277.7 3.8 convolution_convert_fusion.3.aside
  281.5 33.4 %attend_back.1 = (bf16[768,1664]{1,0:T(8,128)(2,1)}, f32[8,128]{1,0:T(8,128)}, bf16[4,192,1536]{2,1,0:T(8,128)(2,1)}) custom-call(s32[1,768]{1,0:T(1,128)} %add.96.pos_row, s32[768,1]{1,0:T(8,128)} %add.106.pos_col, s32[1,768]{1,0:T(1,128)} %broadcast_in_dim_reshape.8.seg_row, s32[768,1]{1,0:T(8,128)} %broadcast_in_dim_reshape.10.seg_col, ...), custom_call_target="tpu_custom_call" | custom-call | tf_op jit(solution)/shard_map/attend_back/pallas_call | solution.py:315
  314.9 7.0 %convolution_convert_fusion.1 = bf16[1536,1664]{1,0:T(8,128)(2,1)S(1)} fusion(bf16[768,1664]{1,0:T(8,128)(2,1)} %get-tuple-element.64.grad_project, bf16[768,1536]{1,0:T(8,128)(2,1)S(1)} %copy-done.3, f32[1536]{0:T(1024)S(1)} %get-tuple-element.106, f32[768]{0:T(1024)S(1)} %add_rsqrt_fusion.1), kind=kOutput, calls=%fused_computation.1 | convolution fusion | flops 3933143040 | bytes 10036224 | tf_op jit(solution)/shard_map/dot_general | solution.py:41
  322.3 3.2 pad_maximum_fusion
  330.3 40.9 %last_moves.1 = (bf16[192,1536]{1,0:T(8,128)(2,1)}, f32[8,1536]{1,0:T(8,128)}) custom-call(bf16[768,1664]{1,0:T(8,128)(2,1)} %get-tuple-element.64.grad_project, bf16[1536,1664]{1,0:T(8,128)(2,1)} %get-tuple-element.47.w_in, bf16[768,1536]{1,0:T(8,128)(2,1)} %get-tuple-element.46.inputs, f32[768,384]{1,0:T(8,128)} %get-tuple-element.65.mixed_grad, ...), custom_call_target="tpu_custom_call" | custom-call | bytes 157286400 | tf_op jit(solution)/shard_map/last_moves/pallas_call | solution.py:912
  372.9 2.1 convert_reduce_fusion
  375.0 2.2 multiply_reduce_fusion.1
  378.0 1.4 fusion.16
  380.6 41.7 %exchange.7 = (bf16[4,128,1536]{2,1,0:T(8,128)(2,1)}, bf16[4,192,2048]{2,1,0:T(8,128)(2,1)}, f32[4,8,128]{2,1,0:T(8,128)}) custom-call(bf16[128,1536]{1,0:T(8,128)(2,1)} %reduce-scatter.4.cloned.1.call-done.refs_0_, bf16[192,2048]{1,0:T(8,128)(2,1)} %reduce-scatter.6.cloned.1.call-done.refs_1_, f32[8,128]{1,0:T(8,128)} %broadcast_in_dim.90.refs_2_), custom_call_target="tpu_custom_call" | custom-call | bytes 94699520 | tf_op jit(solution)/shard_map/exchange/pallas_call | solution.py:609
  422.3 5.2 %spread_cols.3 = f32[192,8192]{1,0:T(8,128)} custom-call(bf16[4,192,2048]{2,1,0:T(8,128)(2,1)} %get-tuple-element.78.refs_0_), custom_call_target="tpu_custom_call" | custom-call | bytes 9437184 | tf_op jit(solution)/shard_map/spread_cols/pallas_call | solution.py:966
  428.8 2.2 bitcast_convert_fusion
  431.0 29.1 %exchange.6 = (bf16[4,192,2048]{2,1,0:T(8,128)(2,1)}, f32[8,8,256]{2,1,0:T(8,128)}) custom-call(bf16[192,2048]{1,0:T(8,128)(2,1)} %reduce-scatter.8.cloned.1.call-done.refs_0_, f32[8,8,256]{2,1,0:T(8,128)} %fusion.15.refs_1_), custom_call_target="tpu_custom_call" | custom-call | bytes 64225280 | tf_op jit(solution)/shard_map/exchange/pallas_call | solution.py:609
  463.1 4.9 %spread_cols.2 = (f32[192,6144]{1,0:T(8,128)}, f32[192,1536]{1,0:T(8,128)}) custom-call(bf16[4,192,2048]{2,1,0:T(8,128)(2,1)} %get-tuple-element.73.refs_0_), custom_call_target="tpu_custom_call" | custom-call | bytes 8847360 | tf_op jit(solution)/shard_map/spread_cols/pallas_call | solution.py:966
  (119 shorter events, 23.9 us)
Async XLA Ops:
  7.2 130.7 %copy-start = (bf16[512,1536]{1,0:T(8,128)(2,1)S(1)}, bf16[512,1536]{1,0:T(8,128)(2,1)}, u32[]{:S(2)}) copy-start(bf16[512,1536]{1,0:T(8,128)(2,1)} %param.22) | copy-start | bytes 4718596
  7.2 171.6 %all-gather.2.cloned.1.call-start = ((), (), s32[]{:S(2)}) async-start(), calls=%async_computation.3 | async-start | bytes 7077888 | tf_op jit(solution)/shard_map/all_gather | solution.py:1069
  9.8 53.5 %copy-start.13 = (s32[1,8]{1,0:T(1,128)S(1)}, s32[1,8]{1,0:T(1,128)}, u32[]{:S(2)}) copy-start(s32[1,8]{1,0:T(1,128)} %param.13) | copy-start | bytes 100
  9.8 55.3 %copy-start.8 = (s32[1,768]{1,0:T(1,128)S(1)}, s32[1,768]{1,0:T(1,128)}, u32[]{:S(2)}) copy-start(s32[1,768]{1,0:T(1,128)} %param.14) | copy-start | bytes 9220
  9.8 57.2 %copy-start.14 = (f32[24]{0:T(128)S(1)}, f32[24]{0:T(128)}, u32[]{:S(2)}) copy-start(f32[24]{0:T(128)} %param.18) | copy-start | bytes 292
  9.9 57.3 %copy-start.9 = (f32[2,64]{1,0:T(2,128)S(1)}, f32[2,64]{1,0:T(2,128)}, u32[]{:S(2)}) copy-start(f32[2,64]{1,0:T(2,128)} %param.19) | copy-start | bytes 1540
  63.3 218.2 %reduce-scatter.4.cloned.1.call-start = ((), (), s32[]{:S(2)}) async-start(), calls=%async_computation.4 | async-start | bytes 3538944 | tf_op jit(solution)/shard_map/reduce_scatter | solution.py:1117
  75.4 3.0 slice-start
  75.4 3.7 copy-start.2
  178.8 8.1 %copy-start.5 = (bf16[768,1536]{1,0:T(8,128)(2,1)S(1)}, bf16[768,1536]{1,0:T(8,128)(2,1)}, u32[]{:S(2)}) copy-start(bf16[768,1536]{1,0:T(8,128)(2,1)} %get-tuple-element.56.cotangent) | copy-start | bytes 7077892
  178.8 8.1 %copy-start.10 = (bf16[1024,1536]{1,0:T(8,128)(2,1)S(1)}, bf16[1024,1536]{1,0:T(8,128)(2,1)}, u32[]{:S(2)}) copy-start(bf16[1024,1536]{1,0:T(8,128)(2,1)} %get-tuple-element.57) | copy-start | bytes 9437188
  190.8 10.8 %copy-start.15 = (bf16[768,1024]{1,0:T(8,128)(2,1)}, bf16[768,1024]{1,0:T(8,128)(2,1)S(1)}, u32[]{:S(2)}) copy-start(bf16[768,1024]{1,0:T(8,128)(2,1)S(1)} %get-tuple-element.111) | copy-start | bytes 4718596
  190.8 3.4 copy-start.4
  207.3 118.3 %reduce-scatter.6.cloned.1.call-start = ((), (), s32[]{:S(2)}) async-start(), calls=%async_computation.5 | async-start | bytes 7077888 | tf_op jit(solution)/shard_map/reduce_scatter | solution.py:1117
  208.0 223.0 %reduce-scatter.8.cloned.1.call-start = ((), (), s32[]{:S(2)}) async-start(), calls=%async_computation.6 | async-start | bytes 7077888 | tf_op jit(solution)/shard_map/reduce_scatter | solution.py:1117
  208.3 66.5 %copy-start.12 = (bf16[768,1536]{1,0:T(8,128)(2,1)S(1)}, bf16[768,1536]{1,0:T(8,128)(2,1)}, u32[]{:S(2)}) copy-start(bf16[768,1536]{1,0:T(8,128)(2,1)} %get-tuple-element.49) | copy-start | bytes 7077892
  274.8 2.9 copy-start.11
  274.8 2.9 copy-start.16
  281.5 33.4 %copy-start.3 = (bf16[768,1536]{1,0:T(8,128)(2,1)S(1)}, bf16[768,1536]{1,0:T(8,128)(2,1)}, u32[]{:S(2)}) copy-start(bf16[768,1536]{1,0:T(8,128)(2,1)} %get-tuple-element.46.inputs) | copy-start | bytes 7077892
  422.3 6.5 %copy-start.6 = (bf16[4,128,1536]{2,1,0:T(8,128)(2,1)S(1)}, bf16[4,128,1536]{2,1,0:T(8,128)(2,1)}, u32[]{:S(2)}) copy-start(bf16[4,128,1536]{2,1,0:T(8,128)(2,1)} %get-tuple-element.79) | copy-start | bytes 4718596
  428.8 41.6 %copy-start.1 = (bf16[512,1536]{1,0:T(8,128)(2,1)S(1)}, bf16[512,1536]{1,0:T(8,128)(2,1)}, u32[]{:S(2)}) copy-start(bf16[512,1536]{1,0:T(8,128)(2,1)} %param.22) | copy-start | bytes 4718596
  431.0 38.6 %copy-start.7 = (bf16[192,1536]{1,0:T(8,128)(2,1)S(1)}, bf16[192,1536]{1,0:T(8,128)(2,1)}, u32[]{:S(2)}) copy-start(bf16[192,1536]{1,0:T(8,128)(2,1)} %get-tuple-element.68) | copy-start | bytes 1769476
Sparse Core Ops, SparseCore 0:
  63.4 68.0 all-gather.1
  207.4 39.3 reduce-scatter.3
  249.7 68.9 reduce-scatter.5
  325.7 67.8 reduce-scatter.7

commit v4 on v3

--- a/solution.py
+++ b/solution.py
@@ -56,13 +56,6 @@
     return high, middle, rest - middle
 
 
-def precise_left(zero_one, values):
-    high, middle, low = split_three(values)
-    total = dot(zero_one, high.astype(BF16))
-    total = total + dot(zero_one, middle.astype(BF16))
-    return total + dot(zero_one, low.astype(BF16))
-
-
 def lane_ids(rows, lanes=LANES):
     return lax.broadcasted_iota(jnp.int32, (rows, lanes), 1)
 
@@ -71,37 +64,46 @@
     return jnp.sum(jnp.where(lanes == index, values, 0.0), axis=-1, keepdims=True)
 
 
-def attend_kernel(
-    head, chunk, heads,
-    pos_row, pos_col, seg_row, seg_col, bias, gains, query, key, value, gate, forget,
+def turns(rows, chunk, unroll=False):
+    def decorate(body):
+        @pl.loop(0, rows // chunk, unroll=rows // chunk if unroll else None)
+        def _(turn):
+            body(pl.ds(pl.multiple_of(turn * chunk, chunk), chunk))
+
+    return decorate
+
+
+def fill_mask(chunk, pos_row, pos_col, seg_row, seg_col, mask):
+    @turns(mask.shape[0], chunk)
+    def _(part):
+        allowed = (pos_row[0:1, :] <= pos_col[part, :]) & (seg_row[0:1, :] == seg_col[part, :])
+        mask[part, :] = jnp.where(allowed, 0.0, -jnp.inf)
+
+
+def fill_prefix(chunk, heads, pos_row, pos_col, logits, prefix):
+    rows = prefix.shape[0]
+    log_forget = jax.nn.log_sigmoid(jnp.where(lane_ids(rows) < heads, logits, 0.0))
+    high, middle, low = split_three(log_forget)
+
+    @turns(rows, chunk)
+    def _(part):
+        before = jnp.where(pos_row[0:1, :] <= pos_col[part, :], 1.0, 0.0).astype(BF16)
+        prefix[part, :] = (
+            dot(before, high.astype(BF16)) + dot(before, middle.astype(BF16)) + dot(before, low.astype(BF16))
+        )
+
+
+def attend_block(
+    head, chunk, index, query, key, value, gate, gains, mask, prefix,
     gated, attended, wide_query, wide_key, wide_value,
-    mask, prefix,
 ):
-    step = pl.program_id(0)
-    rows = query.shape[0]
+    rows = mask.shape[0]
     lanes = lane_ids(rows)
     half = lane_ids(rows, head)
-
-    @pl.when(step == 0)
-    def _():
-        log_forget = jax.nn.log_sigmoid(jnp.where(lanes < heads, forget[...] + bias[0:1, :], 0.0))
-        high, middle, low = split_three(log_forget)
-        @pl.loop(0, rows // chunk)
-        def _(turn):
-            part = pl.ds(pl.multiple_of(turn * chunk, chunk), chunk)
-            before = pos_row[0:1, :] <= pos_col[part, :]
-            same = seg_row[0:1, :] == seg_col[part, :]
-            mask[part, :] = jnp.where(before & same, 0.0, -jnp.inf)
-            before = jnp.where(before, 1.0, 0.0).astype(BF16)
-            prefix[part, :] = (
-                dot(before, high.astype(BF16))
-                + dot(before, middle.astype(BF16))
-                + dot(before, low.astype(BF16))
-            )
-
+    short = lane_ids(chunk, head)
     for side in range(LANES // head):
-        here = pl.ds(side * head, head)
-        column = pick_lane(prefix[...], lanes, (LANES // head) * step + side)
+        here = slice(side * head, (side + 1) * head)
+        column = pick_lane(prefix[...], lanes, (LANES // head) * index + side)
         high, middle, low = split_three(column)
         wide = jnp.where(half == 1, high, 0.0)
         wide = jnp.where(half == 2, middle, wide)
@@ -121,17 +123,15 @@
         wide_key[side, :, head:LANES] = key_rest.astype(BF16)
         wide_value[side, :, 0:head] = value[:, here].astype(BF16)
         wide_value[side, :, head:LANES] = jnp.where(half < 3, 1.0, 0.0).astype(BF16)
-        short = lane_ids(chunk, head)
-
-        @pl.loop(0, rows // chunk)
-        def _(turn):
-            part = pl.ds(pl.multiple_of(turn * chunk, chunk), chunk)
+
+        @turns(rows, chunk, unroll=True)
+        def _(part):
             scores = right_product(wide_query[side, part, :], wide_key[side]) + mask[part, :]
             expos = jnp.exp(scores)
             total = jnp.sum(expos, axis=-1, keepdims=True)
             result = dot(expos.astype(BF16), wide_value[side])[:, 0:head] / total
             attended[part, here] = result
-            gated[part, here] = (result * jax.nn.sigmoid(gate[part, here])).astype(BF16)
+            gated[part, here] = (result * jax.nn.sigmoid(gate(part)[:, here])).astype(BF16)
             high, middle, low = split_three(-jnp.log(total))
             rest = wide_query[side, part, head:LANES].astype(F32)
             rest = jnp.where(short == 7, high, rest)
@@ -140,13 +140,35 @@
             wide_query[side, part, head:LANES] = rest.astype(BF16)
 
 
+def attend_kernel(
+    head, chunk, heads,
+    pos_row, pos_col, seg_row, seg_col, bias, gains, query, key, value, gate, forget,
+    gated, attended, wide_query, wide_key, wide_value,
+    mask, prefix,
+):
+    @pl.when(pl.program_id(0) == 0)
+    def _():
+        fill_mask(chunk, pos_row, pos_col, seg_row, seg_col, mask)
+        fill_prefix(chunk, heads, pos_row, pos_col, forget[...] + bias[0:1, :], prefix)
+
+    attend_block(
+        head, chunk, pl.program_id(0), query, key, value, lambda part: gate[part, :], gains, mask, prefix,
+        gated, attended.at[0], wide_query, wide_key, wide_value,
+    )
+
+
 def attend_back_kernel(
     head, chunk, width, heads, ranks,
     pos_row, pos_col, seg_row, seg_col, bias, gains, query, key, gate, forget,
-    attended, wide_query, wide_key, wide_value, grad_gated, aside,
-    grad_project, small, aside_in,
-    mask, wide_grad, grad_query, grad_key, grad_value, grad_prefix, *sems,
+    attended, wide_query, wide_key, wide_value, grad_gated, *rest,
 ):
+    if ranks:
+        aside, normed, out_grad, grad_project, small, aside_in, late = rest[:7]
+        mask, wide_grad, grad_query, grad_key, grad_value, grad_prefix = rest[7:13]
+        normed_in, out_in, late_all, load_sem, save_sem = rest[13:18]
+        sems = rest[18:]
+    else:
+        grad_project, small, mask, wide_grad, grad_query, grad_key, grad_value, grad_prefix = rest
     step = pl.program_id(0)
     steps = pl.num_programs(0)
 
@@ -170,6 +192,8 @@
             greet([{"ctx": rank ^ distance} for distance in range(1, ranks)])
             for copy in aside_copies():
                 copy.start()
+            pltpu.make_async_copy(normed, normed_in, load_sem.at[0]).start()
+            pltpu.make_async_copy(out_grad, out_in, load_sem.at[1]).start()
 
     rows = query.shape[0]
     lanes = lane_ids(rows)
@@ -194,7 +218,7 @@
 
         sig = jax.nn.sigmoid(gate[:, here])
         grad_in = grad_gated[:, here]
-        result = attended[:, here]
+        result = attended[0, :, here]
         grad_result = (grad_in * sig).astype(BF16)
         grad_gate = (grad_in * result * sig * (1.0 - sig)).astype(BF16)
         inner = -jnp.sum(grad_result.astype(F32) * result, axis=-1, keepdims=True)
@@ -257,8 +281,29 @@
             small[2:3, :] += jnp.sum(grad_logit.astype(F32), axis=0, keepdims=True)
 
         if ranks:
+            pltpu.make_async_copy(normed, normed_in, load_sem.at[0]).wait()
+            pltpu.make_async_copy(out_grad, out_in, load_sem.at[1]).wait()
+            ends = 4 * width, 4 * width + out_grad.shape[1]
+
+            def save(turn):
+                part = pl.ds(pl.multiple_of(turn * chunk, chunk), chunk)
+                return pltpu.make_async_copy(late_all.at[part, :], late.at[part, :], save_sem.at[turn])
+
+            @pl.loop(0, late.shape[0] // chunk)
+            def _(turn):
+                part = pl.ds(pl.multiple_of(turn * chunk, chunk), chunk)
+                product = left_product(normed_in[:, part], grad_project[...]).astype(BF16)
+                late_all[part, 0 : ends[0]] = product[:, 0 : ends[0]]
+                late_all[part, ends[0] : ends[1]] = out_in[part, :]
+                late_all[part, ends[1] : ends[1] + LANES] = product[:, ends[0] :]
+                save(turn).start()
+
             for copy in aside_copies():
                 copy.wait()
+
+            @pl.loop(0, late.shape[0] // chunk)
+            def _(turn):
+                save(turn).wait()
 
 
 def pick_chunk(rows):
@@ -287,10 +332,10 @@
         grid=(steps,),
         in_specs=[whole(p.shape) for p in places] + [whole(bias.shape), whole(gains.shape)]
         + [part(0), part(1), part(2), part(3), forget],
-        out_specs=[own, own, wide, wide, wide],
+        out_specs=[own, pl.BlockSpec((1, rows, LANES), lambda step: (step, 0, 0)), wide, wide, wide],
         out_shape=[
             jax.ShapeDtypeStruct((rows, width), BF16),
-            jax.ShapeDtypeStruct((rows, width), F32),
+            jax.ShapeDtypeStruct((steps, rows, LANES), F32),
             wide_shape, wide_shape, wide_shape,
         ],
         scratch_shapes=[pltpu.VMEM((rows, rows), F32), pltpu.VMEM((rows, LANES), F32)],
@@ -299,7 +344,7 @@
     )(*places, bias, gains, project, project, project, project, project)
 
 
-def attend_back(project, places, bias, gains, attended, wides, grad_gated, aside, ranks, head, width, heads):
+def attend_back(project, places, bias, gains, attended, wides, grad_gated, beside, ranks, head, width, heads):
     rows = project.shape[0]
     steps = width // LANES
     per = LANES // head
@@ -309,38 +354,51 @@
         return pl.BlockSpec((rows, LANES), lambda step: (0, index * steps + step))
 
     own = pl.BlockSpec((rows, LANES), lambda step: (0, step))
+    block = pl.BlockSpec((1, rows, LANES), lambda step: (step, 0, 0))
     wide = pl.BlockSpec((per, rows, LANES), lambda step: (step, 0, 0))
     forget = pl.BlockSpec((rows, LANES), lambda step: (0, 4 * steps))
     total = 4 * width + LANES
+    out_specs = [whole((rows, total)), whole((8, LANES))]
+    out_shape = [jax.ShapeDtypeStruct((rows, total), BF16), jax.ShapeDtypeStruct((8, LANES), F32)]
+    scratch = [
+        pltpu.VMEM((rows, rows), F32),
+        pltpu.VMEM((rows, LANES), BF16),
+        pltpu.VMEM((rows, LANES), F32),
+        pltpu.VMEM((rows, LANES), F32),
+        pltpu.VMEM((rows, LANES), F32),
+        pltpu.VMEM((rows, LANES), F32),
+    ]
+    if ranks:
+        aside, normed, out_grad = beside
+        model, late_cols = normed.shape[1], total + out_grad.shape[1]
+        out_specs += [ANY, ANY]
+        out_shape += [
+            jax.ShapeDtypeStruct((ranks, aside.shape[0] // ranks, aside.shape[1]), BF16),
+            jax.ShapeDtypeStruct((model, late_cols), BF16),
+        ]
+        scratch += [
+            pltpu.VMEM(normed.shape, BF16),
+            pltpu.VMEM(out_grad.shape, BF16),
+            pltpu.VMEM((model, late_cols), BF16),
+            pltpu.SemaphoreType.DMA((2,)),
+            pltpu.SemaphoreType.DMA((model // chunk,)),
+            pltpu.SemaphoreType.DMA((ranks - 1,)),
+            pltpu.SemaphoreType.DMA((ranks - 1,)),
+            pltpu.SemaphoreType.DMA,
+        ]
     return pl.pallas_call(
         functools.partial(attend_back_kernel, head, chunk, width, heads, ranks),
         grid=(steps,),
         in_specs=[whole(p.shape) for p in places] + [whole(bias.shape), whole(gains.shape)]
-        + [part(0), part(1), part(3), forget, own, wide, wide, wide, own, ANY],
-        out_specs=[whole((rows, total)), whole((8, LANES)), ANY],
-        out_shape=[
-            jax.ShapeDtypeStruct((rows, total), BF16),
-            jax.ShapeDtypeStruct((8, LANES), F32),
-            jax.ShapeDtypeStruct((max(ranks, 1), aside.shape[0] // max(ranks, 1), aside.shape[1]), BF16),
-        ],
-        scratch_shapes=[
-            pltpu.VMEM((rows, rows), F32),
-            pltpu.VMEM((rows, LANES), BF16),
-            pltpu.VMEM((rows, LANES), F32),
-            pltpu.VMEM((rows, LANES), F32),
-            pltpu.VMEM((rows, LANES), F32),
-            pltpu.VMEM((rows, LANES), F32),
-        ]
-        + (
-            [pltpu.SemaphoreType.DMA((ranks - 1,)), pltpu.SemaphoreType.DMA((ranks - 1,)), pltpu.SemaphoreType.DMA]
-            if ranks
-            else []
-        ),
+        + [part(0), part(1), part(3), forget, block, wide, wide, wide, own] + [ANY] * len(beside),
+        out_specs=out_specs,
+        out_shape=out_shape,
+        scratch_shapes=scratch,
         compiler_params=pltpu.CompilerParams(
             collective_id=5 if ranks else None, has_side_effects=ranks > 0, vmem_limit_bytes=VMEM_LIMIT
         ),
         name="attend_back",
-    )(*places, bias, gains, project, project, project, project, attended, *wides, grad_gated, aside)
+    )(*places, bias, gains, project, project, project, project, attended, *wides, grad_gated, *beside)
 
 
 def greet(peers, line=None):
@@ -431,11 +489,17 @@
 
             self.side(upper, self.core).start()
 
+    def from_side(self, owner_layer):
+        self.side(owner_layer, 1 - self.core).wait_recv()
+
     def finish(self):
-        if self.source is not None:
-            self.keep.wait()
+        self.keep.wait()
         for owner_layer in range(self.layers):
-            self.side(owner_layer, 1 - self.core).wait_recv()
+            self.from_side(owner_layer)
+        self.sent()
+
+    def sent(self):
+        for owner_layer in range(self.layers):
             self.side(owner_layer, self.core).wait_send()
 
             @pl.when(self.has_above & (owner_layer <= self.layer))
@@ -462,43 +526,49 @@
     def __init__(self, rank, source, place, send_sem, recv_sem, own_sem):
         self.rank, self.source, self.place = rank, source, place
         self.send_sem, self.recv_sem, self.own_sem = send_sem, recv_sem, own_sem
-        self.copies = []
-
-    def send(self, number, source, place, distance):
-        copy = pltpu.make_async_remote_copy(
+
+    def copy(self, number):
+        me = self.rank
+        source, place, distance = (
+            lambda: (self.source(0), self.place(me, 0), 1),
+            lambda: (self.source(1), self.place(me, 1), 2),
+            lambda: (self.source(1), self.place(me, 1), 1),
+            lambda: (self.source(0), self.place(me, 0), 2),
+            lambda: (self.place(me ^ 1, 0), self.place(me ^ 1, 0), 2),
+            lambda: (self.place(me ^ 2, 1), self.place(me ^ 2, 1), 1),
+        )[number]()
+        return pltpu.make_async_remote_copy(
             source, place, self.send_sem.at[number], self.recv_sem.at[number],
-            device_id={"ctx": self.rank ^ distance}, device_id_type=MESH,
-        )
-        copy.start()
-        self.copies.append(copy)
-
-    def start(self):
-        me = self.rank
-        self.send(0, self.source(0), self.place(me, 0), 1)
-        self.send(1, self.source(1), self.place(me, 1), 2)
-        self.send(2, self.source(1), self.place(me, 1), 1)
-        self.send(3, self.source(0), self.place(me, 0), 2)
-        self.own = [
-            pltpu.make_async_copy(self.source(h), self.place(me, h), self.own_sem.at[h]) for h in range(2)
-        ]
-        for copy in self.own:
-            copy.start()
+            device_id={"ctx": me ^ distance}, device_id_type=MESH,
+        )
+
+    def own(self, h):
+        return pltpu.make_async_copy(self.source(h), self.place(self.rank, h), self.own_sem.at[h])
+
+    def start(self, keep=True):
+        for number in range(4):
+            self.copy(number).start()
+        if keep:
+            for h in range(2):
+                self.own(h).start()
 
     def forward(self):
-        near, below = self.rank ^ 1, self.rank ^ 2
-        self.copies[0].wait_recv()
-        self.send(4, self.place(near, 0), self.place(near, 0), 2)
-        self.copies[1].wait_recv()
-        self.send(5, self.place(below, 1), self.place(below, 1), 1)
-
-    def finish(self):
-        for copy in self.own:
-            copy.wait()
-        for number, copy in enumerate(self.copies):
-            if number >= 2:
-                copy.wait_recv()
-        for copy in self.copies:
-            copy.wait_send()
+        for number in range(2):
+            self.copy(number).wait_recv()
+            self.copy(number + 4).start()
+
+    def arrive(self):
+        for number in range(2, 6):
+            self.copy(number).wait_recv()
+
+    def finish(self, arrive=True, keep=True):
+        if keep:
+            for h in range(2):
+                self.own(h).wait()
+        if arrive:
+            self.arrive()
+        for number in range(6):
+            self.copy(number).wait_send()
 
 
 def rows_of(ref, index, size):
@@ -623,97 +693,471 @@
     )(*[source for _, source in ops])
 
 
-def start_kernel(
-    shards, width, piece,
-    tokens, cotangent, weight, tail, other, inputs, grad_low, gathered, picked,
-    weight_all, other_all, own_cols, own_pick,
-    send_sem, recv_sem, own_sem, load_sem, *line_sems,
+VMEM_WHOLE = pl.BlockSpec(memory_space=pltpu.VMEM)
+
+
+def to_rank(source, target, send, recv, other):
+    return pltpu.make_async_remote_copy(
+        source, target, send, recv, device_id={"ctx": other}, device_id_type=MESH
+    )
+
+
+FRONT_LOADS = 3
+FRONT_SAVES = 9
+
+
+def front_kernel(
+    shards, head, heads, width, piece, chunk,
+    tokens, cotangent, weight, weight_out, other, forget_weight, norm_gains, qk_gains, segments, order, forget_bias,
+    inputs, grad_low, w_in, w_out, w_gate_up, normed, project, gated, attended, wide_query, wide_key, wide_value,
+    mixed, gain_rows, pos_row, pos_col, seg_row, seg_col, bias, gains,
+    weight_all, other_all, out_all, own_in, own_pick, own_out, x_all, in_all, hn_all, proj_all, mask, prefix,
+    gated_all, attended_all, query_all, key_all, value_all, out_cols, scale_one, y_own,
+    send_sem, recv_sem, own_sem, load_sem, save_sem, *line_sems,
 ):
     rank = lax.axis_index("ctx")
     ranks = lax.axis_size("ctx")
     model = weight.shape[1] // 4
+    rows = x_all.shape[0]
+    steps = width // LANES
+    tail_at = 4 * width
     loads = [
-        pltpu.make_async_copy(weight, weight_all, load_sem.at[0]),
-        pltpu.make_async_copy(other, other_all, load_sem.at[1]),
+        pltpu.make_async_copy(a, b, load_sem.at[n])
+        for n, (a, b) in enumerate(((weight, weight_all), (other, other_all), (weight_out, out_all)))
+    ]
+    saves = [
+        pltpu.make_async_copy(a, b, save_sem.at[n])
+        for n, (a, b) in enumerate(
+            (
+                (x_all, inputs), (in_all, w_in), (hn_all, normed), (proj_all, project), (query_all, wide_query),
+                (key_all, wide_key), (value_all, wide_value), (attended_all, attended), (gated_all, gated),
+            )
+        )
     ]
     for copy in loads:
         copy.start()
-    line = Line(shards, own_cols, gathered, line_sems)
-    greet([{"ctx": rank ^ 1}, {"ctx": rank ^ 2}], line)
-    first = relay_ops("gather_rows", rank, tokens, inputs, (send_sem.at[0], recv_sem.at[0], own_sem.at[0]))
-    second = relay_ops("gather_rows", rank, cotangent, grad_low, (send_sem.at[1], recv_sem.at[1], own_sem.at[1]))
+    per = len(line_sems) // 3
+    in_line = Line(shards, own_in, in_all, line_sems[:per])
+    out_line = Line(shards, own_out, out_cols, line_sems[per : 2 * per])
+    up_line = Line(shards, own_pick, w_gate_up, line_sems[2 * per :])
+    greet([{"ctx": rank ^ 1}, {"ctx": rank ^ 2}], in_line)
+
+    def sems(n):
+        return send_sem.at[n], recv_sem.at[n], own_sem.at[n]
+
+    first = relay_ops("gather_rows", rank, tokens, x_all, sems(0))
+    second = relay_ops("gather_rows", rank, cotangent, grad_low, sems(1))
+
+    def cols(start, size):
+        return pl.ds(pl.multiple_of(start, LANES), size)
+
     loads[0].wait()
     for i in range(4):
-        own_cols[:, i * width : (i + 1) * width] = weight_all[
-            :, pl.ds(pl.multiple_of(i * model + rank * width, LANES), width)
-        ]
-    own_cols[:, 4 * width : 4 * width + LANES] = tail[...]
-    line.start()
+        own_in[:, i * width : (i + 1) * width] = weight_all[:, cols(i * model + rank * width, width)]
+    total_heads = forget_weight.shape[1]
+    from_head = lax.broadcasted_iota(jnp.int32, (total_heads, LANES), 0)
+    to_lane = lax.broadcasted_iota(jnp.int32, (total_heads, LANES), 1)
+    chosen = jnp.where((to_lane < heads) & (from_head == rank * heads + to_lane), 1.0, 0.0).astype(BF16)
+    from_gain = lax.broadcasted_iota(jnp.int32, (2, LANES), 0)
+    to_lane = lax.broadcasted_iota(jnp.int32, (2, LANES), 1)
+    chosen_gain = jnp.where(to_lane == heads + from_gain, 1.0, 0.0).astype(BF16)
+    tail = dot(forget_weight[...], chosen) + left_product(norm_gains[...], chosen_gain)
+    own_in[:, tail_at : tail_at + LANES] = tail.astype(BF16)
+    in_line.start()
     first.start()
     loads[1].wait()
-    for i in range(picked.shape[1] // piece):
-        own_pick[:, i * piece : (i + 1) * piece] = other_all[
-            :, pl.ds(pl.multiple_of((i * ranks + rank) * piece, LANES), piece)
-        ]
-    keep = pltpu.make_async_copy(own_pick, picked, load_sem.at[2])
-    keep.start()
+    for i in range(own_pick.shape[1] // piece):
+        own_pick[:, i * piece : (i + 1) * piece] = other_all[:, cols((i * ranks + rank) * piece, piece)]
+    loads[2].wait()
+    own_out[...] = out_all[:, cols(rank * width, width)]
+    count = order.shape[1]
+    length = rows // count
+    row_ids = lax.broadcasted_iota(jnp.int32, (rows, LANES), 0)
+    lane_id = lax.broadcasted_iota(jnp.int32, (8, rows), 1)
+    tall = jnp.zeros((rows, LANES), jnp.int32)
+    flat = jnp.zeros((8, rows), jnp.int32)
+    for block in range(count):
+        start = order[0, block] * length - block * length
+        tall = jnp.where((row_ids >= block * length) & (row_ids < (block + 1) * length), row_ids + start, tall)
+        flat = jnp.where((lane_id >= block * length) & (lane_id < (block + 1) * length), lane_id + start, flat)
+    pos_col[...] = tall[:, 0:1].astype(F32)
+    pos_row[...] = flat[0:1, :].astype(F32)
+    true_segments = segments[0:1, :].astype(F32)
+
+    @turns(rows, chunk)
+    def _(part):
+        true_place = lax.broadcasted_iota(jnp.int32, (chunk, rows), 1).astype(F32)
+        own_place = true_place == pos_col[part, :]
+        seg_col[part, :] = jnp.sum(jnp.where(own_place, true_segments, 0.0), axis=-1, keepdims=True)
+
+    seg_row[...] = jnp.broadcast_to(seg_col[...], (rows, LANES)).T[0:1, :]
+    lane = lax.broadcasted_iota(jnp.int32, (1, LANES), 1)
+    bias_row = jnp.zeros((1, LANES), F32)
+    for index in range(heads):
+        bias_row = jnp.where(lane == index, forget_bias[0, rank * heads + index], bias_row)
+    bias[...] = bias_row
+    for side in range(LANES // head):
+        gains[:, side * head : (side + 1) * head] = qk_gains[...]
+    fill_mask(chunk, pos_row, pos_col, seg_row, seg_col, mask)
+    proj_all[...] = jnp.zeros_like(proj_all)
+    gain_rows[...] = jnp.zeros_like(gain_rows)
     first.forward()
     second.start()
-    for distance in range(1, line.layers):
-        line.step(distance)
-        if distance == 1:
-            second.forward()
+    in_line.step(1)
     first.finish()
+    saves[0].start()
+
+    @turns(rows, chunk)
+    def _(part):
+        values = x_all[part, :].astype(F32)
+        scale_one[part, :] = jnp.broadcast_to(rms_scale(values), (chunk, LANES))
+
+    def consume(layer):
+        in_line.from_side(layer)
+        size = 2 * in_line.rows
+        here = cols(layer * size, size)
+        tail_block = in_all[here, tail_at : tail_at + LANES].astype(F32).T
+        gain_rows[0:1, here] = tail_block[heads : heads + 1, :]
+        gain_rows[1:2, here] = tail_block[heads + 1 : heads + 2, :]
+
+        @turns(rows, chunk)
+        def _(part):
+            values = x_all[part, here].astype(F32) * scale_one[part, 0:1] * gain_rows[0:1, here]
+            hn_all[part, here] = values.astype(BF16)
+            proj_all[part, :] += dot(values.astype(BF16), in_all[here, :])
+
+    def consume_at(distance):
+        lower, upper = in_line.layer - distance, in_line.layer + distance
+
+        @pl.when(lower >= 0)
+        def _():
+            consume(lower)
+
+        @pl.when(upper < in_line.layers)
+        def _():
+            consume(upper)
+
+    in_line.keep.wait()
+    consume(in_line.layer)
+    consume_at(1)
+    second.forward()
+    for distance in range(2, in_line.layers):
+        in_line.step(distance)
+        if distance == in_line.layers - 1:
+            out_line.start()
+        consume_at(distance)
+
+    for n in (1, 2, 3):
+        saves[n].start()
+    up_line.start()
+    out_line.step(1)
+    fill_prefix(chunk, heads, pos_row, pos_col, proj_all[:, tail_at : tail_at + LANES] + bias[0:1, :], prefix)
+
+    def share(index):
+        block = rank * steps + index
+        half = rows // 2
+
+        def source(h):
+            return gated_all.at[block, pl.ds(h * half, half), :]
+
+        def place(owner, h):
+            return gated_all.at[owner * steps + index, pl.ds(h * half, half), :]
+
+        return Relay(rank, source, place, send_sem.at[2 + index], recv_sem.at[2 + index], None)
+
+    per_block = LANES // head
+
+    @pl.loop(0, steps)
+    def _(index):
+        def lanes_of(part_id):
+            return proj_all[:, cols(part_id * width + index * LANES, LANES)]
+
+        def gate(part):
+            return proj_all[part, cols(3 * width + index * LANES, LANES)]
+
+        group = pl.ds(index * per_block, per_block)
+        attend_block(
+            head, chunk, index, lanes_of(0), lanes_of(1), lanes_of(2), gate, gains, mask, prefix,
+            gated_all.at[rank * steps + index], attended_all.at[index],
+            query_all.at[group], key_all.at[group], value_all.at[group],
+        )
+        share(index).start(keep=False)
+
+        @pl.when(index == 0)
+        def _():
+            out_line.step(2)
+
+        @pl.when(index > 0)
+        def _():
+            share(index - 1).forward()
+
+    up_line.step(1)
+    out_line.step(3)
+    share(steps - 1).forward()
+    for n in (4, 5, 6, 7):
+        saves[n].start()
+    for index in range(steps):
+        share(index).arrive()
+    saves[8].start()
+    out_line.keep.wait()
+    for layer in range(out_line.layers):
+        out_line.from_side(layer)
+    save_out = pltpu.make_async_copy(out_cols, w_out, save_sem.at[len(saves)])
+    save_out.start()
+
+    third = relay_ops("gather_cols", rank, y_own, mixed, sems(2 + steps))
+
+    @turns(rows, chunk)
+    def _(part):
+        total = x_all[part, cols(rank * width, width)].astype(F32)
+        for block in range(gated_all.shape[0]):
+            total = total + dot(gated_all[block, part, :], out_cols[block * LANES : (block + 1) * LANES, :])
+        y_own[part, :] = total.astype(BF16)
+
+    third.start()
+    third.forward()
+    up_line.step(2)
+    up_line.step(3)
+    third.finish()
+    up_line.finish()
+    out_line.sent()
+    in_line.sent()
     second.finish()
-    line.finish()
-    keep.wait()
-
-
-def start_moves(collective_id, ranks, shards, width, piece, tokens, cotangent, weight, tail, other):
-    rows, model = tokens.shape
+    for index in range(steps):
+        share(index).finish(arrive=False, keep=False)
+    for copy in saves:
+        copy.wait()
+    save_out.wait()
+
+
+def front(
+    collective_id, ranks, shards, head, heads, width, piece,
+    tokens, cotangent, weight, weight_out, other, forget_weight, norm_gains, qk_gains, segments, order, forget_bias,
+):
+    own_rows, model = tokens.shape
+    rows = ranks * own_rows
+    chunk = pick_chunk(rows)
+    steps, shard_rows = width // LANES, weight.shape[0]
+    wide_in = 4 * width + LANES
+    other_cols = other.shape[1] // ranks
+    wide = (heads, rows, LANES)
+    shape, vmem = jax.ShapeDtypeStruct, pltpu.VMEM
     return pl.pallas_call(
-        functools.partial(start_kernel, shards, width, piece),
-        in_specs=[ANY] * 3 + [pl.BlockSpec(memory_space=pltpu.VMEM), ANY],
-        out_specs=[ANY] * 4,
+        functools.partial(front_kernel, shards, head, heads, width, piece, chunk),
+        in_specs=[ANY] * 5 + [VMEM_WHOLE] * 4 + [pl.BlockSpec(memory_space=pltpu.SMEM)] * 2,
+        out_specs=[ANY] * 13 + [VMEM_WHOLE] * 7,
         out_shape=[
-            jax.ShapeDtypeStruct((ranks * rows, model), BF16),
-            jax.ShapeDtypeStruct((ranks * rows, model), BF16),
-            jax.ShapeDtypeStruct((shards * weight.shape[0], 4 * width + LANES), BF16),
-            jax.ShapeDtypeStruct((other.shape[0], other.shape[1] // ranks), BF16),
+            shape((rows, model), BF16),
+            shape((rows, model), BF16),
+            shape((model, wide_in), BF16),
+            shape((model, width), BF16),
+            shape((model, other_cols), BF16),
+            shape((rows, model), BF16),
+            shape((rows, wide_in), F32),
+            shape((ranks * steps, rows, LANES), BF16),
+            shape((steps, rows, LANES), F32),
+            shape(wide, BF16), shape(wide, BF16), shape(wide, BF16),
+            shape((rows, model), BF16),
+            shape((8, model), F32),
+            shape((1, rows), F32), shape((rows, 1), F32), shape((1, rows), F32), shape((rows, 1), F32),
+            shape((1, LANES), F32),
+            shape((2, LANES), F32),
         ],
         scratch_shapes=[
-            pltpu.VMEM(weight.shape, BF16),
-            pltpu.VMEM(other.shape, BF16),
-            pltpu.VMEM((weight.shape[0], 4 * width + LANES), BF16),
-            pltpu.VMEM((other.shape[0], other.shape[1] // ranks), BF16),
-            pltpu.SemaphoreType.DMA((2, 6)),
-            pltpu.SemaphoreType.DMA((2, 6)),
-            pltpu.SemaphoreType.DMA((2, 2)),
-            pltpu.SemaphoreType.DMA((3,)),
+            vmem(weight.shape, BF16),
+            vmem(other.shape, BF16),
+            vmem(weight_out.shape, BF16),
+            vmem((shard_rows, wide_in), BF16),
+            vmem((shard_rows, other_cols), BF16),
+            vmem((shard_rows, width), BF16),
+            vmem((rows, model), BF16),
+            vmem((model, wide_in), BF16),
+            vmem((rows, model), BF16),
+            vmem((rows, wide_in), F32),
+            vmem((rows, rows), F32),
+            vmem((rows, LANES), F32),
+            vmem((ranks * steps, rows, LANES), BF16),
+            vmem((steps, rows, LANES), F32),
+            vmem(wide, BF16), vmem(wide, BF16), vmem(wide, BF16),
+            vmem((model, width), BF16),
+            vmem((rows, LANES), F32),
+            vmem((rows, width), BF16),
+            pltpu.SemaphoreType.DMA((3 + steps, 6)),
+            pltpu.SemaphoreType.DMA((3 + steps, 6)),
+            pltpu.SemaphoreType.DMA((3 + steps, 2)),
+            pltpu.SemaphoreType.DMA((FRONT_LOADS,)),
+            pltpu.SemaphoreType.DMA((FRONT_SAVES + 1,)),
+        ]
+        + 3 * line_scratch(shards),
+        compiler_params=pltpu.CompilerParams(
+            collective_id=collective_id, has_side_effects=True, vmem_limit_bytes=VMEM_LIMIT
+        ),
+        cost_estimate=pl.CostEstimate(flops=0, bytes_accessed=300 << 20, transcendentals=0),
+        name="front",
+    )(
+        tokens, cotangent, weight, weight_out, other, forget_weight, norm_gains, qk_gains, segments, order, forget_bias
+    )
+
+
+def ffn_kernel(
+    shards, chunk,
+    mixed, w_gate_up, cotangent, down_weight, gain,
+    w_down, normed, hidden, grad_gate_up, grad_down, grad_weight,
+    mixed_in, weight_in, cotangent_in, own_in, gates, ups, hn, turned, acts, grads, down_out, weight_out,
+    load_sem, save_sem, *line_sems,
+):
+    size = gates.shape[1]
+    rows, model = mixed.shape
+    tile = 2 * own_in.shape[0]
+    rank = lax.axis_index("ctx")
+    loads = [
+        pltpu.make_async_copy(a, b, load_sem.at[n])
+        for n, (a, b) in enumerate(
+            (
+                (rows_of(down_weight, rank, own_in.shape[0]), own_in), (mixed, mixed_in), (w_gate_up, weight_in),
+                (cotangent, cotangent_in),
+            )
+        )
+    ]
+    saves = [
+        pltpu.make_async_copy(a, b, save_sem.at[n])
+        for n, (a, b) in enumerate(
+            ((hn, normed), (acts, hidden), (down_out, grad_down), (grads, grad_gate_up), (weight_out, grad_weight))
+        )
+    ]
+    for copy in loads:
+        copy.start()
+    line = Line(shards, own_in, w_down, line_sems)
+    greet([], line)
+    loads[0].wait()
+    line.start()
+    loads[1].wait()
+
+    @turns(rows, chunk)
+    def _(part):
+        values = mixed_in[part, :].astype(F32)
+        low = values * rms_scale(values) * gain[1:2, :]
+        hn[part, :] = low.astype(BF16)
+        turned[:, part] = low.T.astype(BF16)
+
+    saves[0].start()
+    loads[2].wait()
+
+    def span(turn, start=0):
+        return pl.ds(pl.multiple_of(start + turn * tile, LANES), tile)
+
+    @pl.loop(0, size // tile)
+    def _(turn):
+        @turns(rows, chunk)
+        def _(part):
+            gate = dot(hn[part, :], weight_in[:, span(turn)])
+            up = dot(hn[part, :], weight_in[:, span(turn, size)])
+            gates[part, span(turn)] = gate
+            ups[part, span(turn)] = up
+            acts[part, span(turn)] = (jax.nn.silu(gate) * up).astype(BF16)
+
+    saves[1].start()
+    line.step(1)
+    loads[3].wait()
+
+    def consume(turn):
+        line.from_side(turn)
+
+        @turns(rows, chunk)
+        def _(part):
+            grad = right_product(cotangent_in[part, :], w_down[span(turn), :])
+            gate, up = gates[part, span(turn)], ups[part, span(turn)]
+            sig = jax.nn.sigmoid(gate)
+            grads[part, span(turn)] = (grad * up * sig * (1.0 + gate * (1.0 - sig))).astype(BF16)
+            grads[part, span(turn, size)] = (grad * gate * sig).astype(BF16)
+
+        for start in (0, size):
+            here = span(turn, start)
+
+            @turns(model, 3 * chunk if model % (3 * chunk) == 0 else chunk)
+            def _(part):
+                weight_out[part, here] = dot(turned[part, :], grads[:, here]).astype(BF16)
+
+    def consume_at(distance):
+        lower, upper = line.layer - distance, line.layer + distance
+
+        @pl.when(lower >= 0)
+        def _():
+            consume(lower)
+
+        @pl.when(upper < line.layers)
+        def _():
+            consume(upper)
+
+    line.keep.wait()
+    consume(line.layer)
+    consume_at(1)
+    line.step(2)
+
+    @pl.loop(0, size // tile)
+    def _(turn):
+        down_out[span(turn), :] = left_product(acts[:, span(turn)], cotangent_in[...]).astype(BF16)
+
+    saves[2].start()
+    consume_at(2)
+    for distance in range(3, line.layers):
+        line.step(distance)
+        consume_at(distance)
+    saves[3].start()
+    saves[4].start()
+    line.sent()
+    for copy in saves:
+        copy.wait()
+
+
+def ffn(collective_id, ranks, shards, mixed, w_gate_up, cotangent, down_weight, gain):
+    rows, model = mixed.shape
+    size = w_gate_up.shape[1] // 2
+    shape, vmem = jax.ShapeDtypeStruct, pltpu.VMEM
+    return pl.pallas_call(
+        functools.partial(ffn_kernel, shards, pick_chunk(rows)),
+        in_specs=[ANY] * 4 + [VMEM_WHOLE],
+        out_specs=[VMEM_WHOLE] + [ANY] * 5,
+        out_shape=[
+            shape((size, model), BF16),
+            shape((rows, model), BF16),
+            shape((rows, size), BF16),
+            shape((rows, 2 * size), BF16),
+            shape((size, model), BF16),
+            shape((model, 2 * size), BF16),
+        ],
+        scratch_shapes=[
+            vmem((rows, model), BF16),
+            vmem(w_gate_up.shape, BF16),
+            vmem((rows, model), BF16),
+            vmem((down_weight.shape[0] // ranks, model), BF16),
+            vmem((rows, size), F32),
+            vmem((rows, size), F32),
+            vmem((rows, model), BF16),
+            vmem((model, rows), BF16),
+            vmem((rows, size), BF16),
+            vmem((rows, 2 * size), BF16),
+            vmem((size, model), BF16),
+            vmem((model, 2 * size), BF16),
+            pltpu.SemaphoreType.DMA((4,)),
+            pltpu.SemaphoreType.DMA((5,)),
         ]
         + line_scratch(shards),
         compiler_params=pltpu.CompilerParams(
             collective_id=collective_id, has_side_effects=True, vmem_limit_bytes=VMEM_LIMIT
         ),
-        cost_estimate=pl.CostEstimate(flops=0, bytes_accessed=150 << 20, transcendentals=0),
-        name="start_moves",
-    )(tokens, cotangent, weight, tail, other)
-
-
-VMEM_WHOLE = pl.BlockSpec(memory_space=pltpu.VMEM)
-
-
-def to_rank(source, target, send, recv, other):
-    return pltpu.make_async_remote_copy(
-        source, target, send, recv, device_id={"ctx": other}, device_id_type=MESH
-    )
+        cost_estimate=pl.CostEstimate(flops=0, bytes_accessed=100 << 20, transcendentals=0),
+        name="ffn",
+    )(mixed, w_gate_up, cotangent, down_weight, gain)
 
 
 def middle_kernel(
     ranks,
-    grad_gate_up, w_gate_up, mixed, cotangent, w_out, gain, mixed_grad, gated_grad, gain_grad,
-    grad_in, weight_in, mixed_in, cotangent_in, out_in, wide, first_out, first_in, second_out, second_in,
-    load_sem, first_send, first_recv, second_send, second_recv,
+    grad_gate_up, w_gate_up, mixed, cotangent, w_out, hidden, w_down, gated, gain,
+    mixed_grad, gated_grad, gain_grad, down_part, out_grad,
+    grad_in, weight_in, mixed_in, cotangent_in, out_in, hidden_in, down_in, gated_in, low_grad, down_all, out_all,
+    wide, first_out, first_in, second_out, second_in,
+    load_sem, save_sem, first_send, first_recv, second_send, second_recv,
 ):
     rank = lax.axis_index("ctx")
     rows = mixed.shape[0] // ranks
@@ -724,15 +1168,19 @@
         for n, (a, b) in enumerate(
             (
                 (w_gate_up, weight_in), (grad_gate_up, grad_in), (mixed, mixed_in), (cotangent, cotangent_in),
-                (w_out, out_in),
+                (w_out, out_in), (hidden, hidden_in), (w_down, down_in), (gated, gated_in),
             )
         )
+    ]
+    saves = [
+        pltpu.make_async_copy(down_all, down_part, save_sem.at[0]),
+        pltpu.make_async_copy(out_all, out_grad, save_sem.at[1]),
     ]
     for copy in loads:
         copy.start()
     greet([{"ctx": rank ^ distance} for distance in range(1, ranks)])
     gain_grad[...] = jnp.zeros_like(gain_grad)
-    for copy in loads:
+    for copy in loads[:5]:
         copy.wait()
 
     def part(turn):
@@ -761,6 +1209,7 @@
         total = total + arrived(*first, turn)
         mixed_grad[here, :] = total
         low = total.astype(BF16)
+        low_grad[here, :] = low
         for index in range(ranks):
             second_out[index, here, :] = right_product(low, out_in[index * width : (index + 1) * width, :]).astype(BF16)
         for distance in range(1, ranks):
@@ -789,7 +1238,24 @@
         def _():
             project(turn - 1)
 
+    for copy in loads[5:]:
+        copy.wait()
+
+    @pl.loop(0, model // tile)
+    def _(step):
+        cols = pl.ds(pl.multiple_of(step * tile, tile), tile)
+        down_all[:, cols] = dot(hidden_in[...], down_in[:, cols]).astype(BF16)
+
+    saves[0].start()
     project(ranks - 1)
+
+    @pl.loop(0, gated_in.shape[0])
+    def _(block):
+        out_all[pl.ds(pl.multiple_of(block * LANES, LANES), LANES), :] = left_product(
+            gated_in[block], low_grad[...]
+        ).astype(BF16)
+
+    saves[1].start()
 
     @pl.loop(0, ranks)
     def _(turn):
@@ -801,20 +1267,25 @@
             send(*first, turn, distance).wait_send()
             send(*second, turn, distance).wait_send()
 
-
-def middle(collective_id, ranks, grad_gate_up, w_gate_up, mixed, cotangent, w_out, gain):
+    for copy in saves:
+        copy.wait()
+
+
+def middle(collective_id, ranks, grad_gate_up, w_gate_up, mixed, cotangent, w_out, hidden, w_down, gated, gain):
     rows, model = mixed.shape
     width = w_out.shape[1]
     blocks = pltpu.VMEM((ranks, rows, width), BF16)
     sems = pltpu.SemaphoreType.DMA((ranks - 1, ranks))
     return pl.pallas_call(
         functools.partial(middle_kernel, ranks),
-        in_specs=[ANY] * 5 + [VMEM_WHOLE],
-        out_specs=[VMEM_WHOLE] * 3,
+        in_specs=[ANY] * 8 + [VMEM_WHOLE],
+        out_specs=[VMEM_WHOLE] * 3 + [ANY] * 2,
         out_shape=[
             jax.ShapeDtypeStruct((rows, width), F32),
             jax.ShapeDtypeStruct((rows, width), F32),
             jax.ShapeDtypeStruct((8, model), F32),
+            jax.ShapeDtypeStruct((rows, model), BF16),
+            jax.ShapeDtypeStruct((model, width), BF16),
         ],
         scratch_shapes=[
             pltpu.VMEM(grad_gate_up.shape, BF16),
@@ -822,9 +1293,16 @@
             pltpu.VMEM(mixed.shape, BF16),
             pltpu.VMEM(cotangent.shape, BF16),
             pltpu.VMEM(w_out.shape, BF16),
+            pltpu.VMEM(hidden.shape, BF16),
+            pltpu.VMEM(w_down.shape, BF16),
+            pltpu.VMEM(gated.shape, BF16),
+            pltpu.VMEM((rows, width), BF16),
+            pltpu.VMEM((rows, model), BF16),
+            pltpu.VMEM((model, width), BF16),
             pltpu.VMEM((rows // ranks, model), F32),
             blocks, blocks, blocks, blocks,
-            pltpu.SemaphoreType.DMA((5,)),
+            pltpu.SemaphoreType.DMA((8,)),
+            pltpu.SemaphoreType.DMA((2,)),
             sems, sems, sems, sems,
         ],
         compiler_params=pltpu.CompilerParams(
@@ -832,14 +1310,15 @@
         ),
         cost_estimate=pl.CostEstimate(flops=0, bytes_accessed=150 << 20, transcendentals=0),
         name="middle",
-    )(grad_gate_up, w_gate_up, mixed, cotangent, w_out, gain)
+    )(grad_gate_up, w_gate_up, mixed, cotangent, w_out, hidden, w_down, gated, gain)
 
 
 def last_kernel(
     ranks,
-    grad_project, w_in, inputs, mixed_grad, gain, sums, tokens_grad, total_sums,
+    grad_project, w_in, inputs, aside, other, mixed_grad, gain, gain_two_grad, small,
+    tokens_grad, total_sums, aside_all, other_all,
     grad_in, weight_in, inputs_in, wide, out, into, sums_out, sums_in,
-    load_sem, send_sem, recv_sem, sums_send, sums_recv,
+    load_sem, send_sem, recv_sem, sums_send, sums_recv, aside_send, aside_recv, aside_own,
 ):
     rank = lax.axis_index("ctx")
     rows = inputs.shape[0] // ranks
@@ -852,7 +1331,17 @@
     for copy in loads:
         copy.start()
     greet([{"ctx": rank ^ distance} for distance in range(1, ranks)])
-    sums_out[...] = sums[...]
+    relays = [
+        relay_ops("stack", rank, a, b, (aside_send.at[n], aside_recv.at[n], aside_own.at[n]))
+        for n, (a, b) in enumerate(((aside, aside_all), (other, other_all)))
+    ]
+    relays[0].start()
+    sums_out[...] = jnp.zeros_like(sums_out)
+    sums_out[1:2, :] = gain_two_grad[0:1, :]
+    sums_out[2:3, 0:LANES] = small[0:1, :]
+    sums_out[2:3, LANES : 2 * LANES] = small[1:2, :]
+    for index in range(ranks):
+        sums_out[3 + index : 4 + index, 0:LANES] = jnp.where(rank == index, small[2:3, :], 0.0)
     for copy in loads:
         copy.wait()
 
@@ -887,6 +1376,14 @@
         compute(rank ^ distance)
         send(distance).start()
 
+        @pl.when(distance == 1)
+        def _():
+            relays[0].forward()
+
+        @pl.when(distance == 2)
+        def _():
+            relays[1].start()
+
     compute(rank)
     for distance in range(1, ranks):
         send_sums(distance).start()
@@ -895,6 +1392,7 @@
         send(distance).wait_recv()
         total = total + into[distance].astype(F32)
     tokens_grad[...] = total.astype(BF16)
+    relays[1].forward()
     total = sums_out[...]
     for distance in range(1, ranks):
         send_sums(distance).wait_recv()
@@ -903,19 +1401,25 @@
     for distance in range(1, ranks):
         send(distance).wait_send()
         send_sums(distance).wait_send()
-
-
-def last_moves(collective_id, ranks, grad_project, w_in, inputs, mixed_grad, gain, sums):
+    for relay in relays:
+        relay.finish()
+
+
+def last_moves(
+    collective_id, ranks, grad_project, w_in, inputs, aside, other, mixed_grad, gain, gain_two_grad, small
+):
     rows, model = inputs.shape
     blocks = pltpu.VMEM((ranks, rows // ranks, model), BF16)
     sems = pltpu.SemaphoreType.DMA((ranks - 1,))
     return pl.pallas_call(
         functools.partial(last_kernel, ranks),
-        in_specs=[ANY] * 3 + [VMEM_WHOLE] * 3,
-        out_specs=[VMEM_WHOLE] * 2,
+        in_specs=[ANY] * 5 + [VMEM_WHOLE] * 4,
+        out_specs=[VMEM_WHOLE] * 2 + [ANY] * 2,
         out_shape=[
             jax.ShapeDtypeStruct((rows // ranks, model), BF16),
             jax.ShapeDtypeStruct((8, model), F32),
+            jax.ShapeDtypeStruct((ranks,) + aside.shape, BF16),
+            jax.ShapeDtypeStruct((ranks,) + other.shape, BF16),
         ],
         scratch_shapes=[
             pltpu.VMEM(grad_project.shape, BF16),
@@ -927,13 +1431,16 @@
             pltpu.VMEM((ranks, 8, model), F32),
             pltpu.SemaphoreType.DMA((3,)),
             sems, sems, sems, sems,
+            pltpu.SemaphoreType.DMA((2, 6)),
+            pltpu.SemaphoreType.DMA((2, 6)),
+            pltpu.SemaphoreType.DMA((2, 2)),
         ],
         compiler_params=pltpu.CompilerParams(
             collective_id=collective_id, has_side_effects=True, vmem_limit_bytes=VMEM_LIMIT
         ),
         cost_estimate=pl.CostEstimate(flops=0, bytes_accessed=150 << 20, transcendentals=0),
         name="last_moves",
-    )(grad_project, w_in, inputs, mixed_grad, gain, sums)
+    )(grad_project, w_in, inputs, aside, other, mixed_grad, gain, gain_two_grad, small)
 
 
 def spread_kernel(pieces, *refs):
@@ -979,7 +1486,7 @@
     def __init__(self, ranks):
         self.ranks = ranks
 
-    def begin(self, number, tokens, cotangent, weight, tail, other, piece, width, padded):
+    def begin(self, tokens, cotangent, weight, tail, other, piece, width, padded):
         rank, model = lax.axis_index("ctx"), tokens.shape[1]
         parts = [lax.dynamic_slice_in_dim(weight, i * model + rank * width, width, 1) for i in range(4)]
         parts = [jnp.pad(part, ((0, 0), (0, padded - width))) for part in parts]
@@ -994,15 +1501,17 @@
             jnp.concatenate(picks, axis=1),
         )
 
-    def gather_cols(self, number, array, piece):
+    def gather_cols(self, array, piece):
         return lax.all_gather(array, "ctx", axis=1, tiled=True), lax.all_gather(piece, "fsdp", axis=0, tiled=True)
 
     def stack(self, number, *arrays):
         return [lax.all_gather(a, "ctx", axis=0, tiled=False) for a in arrays]
 
-    def finish(self, number, array, pieces):
-        return lax.all_gather(array, "ctx", axis=0, tiled=False), lax.psum_scatter(
-            pieces, "fsdp", scatter_dimension=0, tiled=False
+    def finish(self, number, array, pieces, stats):
+        return (
+            lax.all_gather(array, "ctx", axis=0, tiled=False),
+            lax.psum_scatter(pieces, "fsdp", scatter_dimension=0, tiled=False),
+            lax.psum(stats, "ctx"),
         )
 
 
@@ -1013,20 +1522,14 @@
     def run(self, number, *ops):
         return exchange(number, self.ranks, 0, self.shards, *ops)
 
-    def begin(self, number, tokens, cotangent, weight, tail, other, piece, width, padded):
-        return start_moves(
-            number, self.ranks, self.shards, width, piece, tokens, cotangent, weight, tail, other
-        )
-
-    def gather_cols(self, number, array, piece):
-        return self.run(number, ("gather_cols", array), ("line", piece))
-
     def stack(self, number, *arrays):
         return self.run(number, *[("stack" if a.dtype == BF16 else "each", a) for a in arrays])
 
-    def finish(self, number, array, pieces):
-        out = exchange(number, self.ranks, self.shards, self.shards, ("stack", array), ("shards", pieces))
-        return out[0], out[1].sum(axis=0)
+    def finish(self, number, array, pieces, stats):
+        out = exchange(
+            number, self.ranks, self.shards, self.shards, ("stack", array), ("shards", pieces), ("each", stats)
+        )
+        return out[0], out[1].sum(axis=0), out[2].sum(axis=0)
 
 
 def body(
@@ -1055,80 +1558,86 @@
     def widen(array):
         return jnp.pad(array, ((0, 0), (0, padded - width))) if padded > width else array
 
-    tail = jnp.concatenate(
-        [
-            slab(forget_weight, rank * local_heads, local_heads, 1),
-            norm_gains.T,
-            jnp.zeros((attn_in_weight.shape[0], LANES - local_heads - 2), BF16),
-        ],
-        axis=1,
-    )
-    inputs, grad_low, w_in, gate_up_piece = comm.begin(
-        0, tokens[0], out_grad[0], attn_in_weight, tail, gate_up_weight, hidden_piece, width, padded
-    )
-    w_gate_up = lax.all_gather(gate_up_piece, "fsdp", axis=0, tiled=True)
-
-    offsets = jnp.arange(seq_len, dtype=jnp.int32)
-    blocks = jnp.arange(seq_order.shape[0], dtype=jnp.int32)
-    places = (seq_order[:, None] * block_len + offsets[None, :block_len]).reshape(-1)
-    by_block = segment_ids[0].reshape(-1, block_len)
-    chosen = seq_order[:, None, None] == blocks[None, :, None]
-    segments = jnp.sum(jnp.where(chosen, by_block[None], 0), axis=1).reshape(-1)
-    places_all = (places[None, :], places[:, None], segments[None, :], segments[:, None])
-    valid = (segments >= 0).astype(F32)
-
-    bias = jnp.pad(slab(forget_bias, rank * local_heads, local_heads, 0), (0, LANES - local_heads))[None]
-    head_gains = jnp.tile(qk_gains, (1, LANES // head_dim))
-
-    gain_cols = lax.optimization_barrier(w_in[:, 4 * padded : 4 * padded + LANES]).astype(F32).T
-    gain_one = gain_cols[local_heads]
-    gain_two = gain_cols[local_heads + 1]
-
-    wide_inputs = inputs.astype(F32)
-    scale_one = rms_scale(wide_inputs)
-    normed = (wide_inputs * scale_one * gain_one).astype(BF16)
-    project = dot(normed, w_in)
-    gated, attended, wide_query, wide_key, wide_value = attend(
-        project, places_all, bias, head_gains, head_dim, padded, local_heads
-    )
-    gated_all, w_out = comm.gather_cols(1, gated[:, :width], slab(out_weight, rank * width, width, 1))
-    mixed_cols = slab(inputs, rank * width, width, 1).astype(F32) + dot(gated_all, w_out)
-    mixed_low, w_down = comm.gather_cols(
-        2, mixed_cols.astype(BF16), slab(down_weight, rank * hidden_piece, hidden_piece, 0)
-    )
-    mixed = mixed_low.astype(F32)
-    scale_two = rms_scale(mixed)
-    normed_two = (mixed * scale_two * gain_two).astype(BF16)
-    gate_up = dot(normed_two, w_gate_up)
-    gate_part, up_part = gate_up[:, :hidden], gate_up[:, hidden:]
-    gate_sigmoid = jax.nn.sigmoid(gate_part)
-    silu = gate_part * gate_sigmoid
-    hidden_act = (silu * up_part).astype(BF16)
-    down_part = dot(hidden_act, w_down).astype(BF16)
+    if plain:
+        (
+            inputs, grad_low, w_in, w_out, w_gate_up, normed, project, gated_all, attended,
+            wide_query, wide_key, wide_value, mixed_low, gain_rows, *places_all, bias, head_gains,
+        ) = front(
+            0, ranks, shards, head_dim, local_heads, width, hidden_piece,
+            tokens[0], out_grad[0], attn_in_weight, out_weight, gate_up_weight, forget_weight, norm_gains, qk_gains,
+            segment_ids, block_order, forget_bias[None],
+        )
+        gain_one, gain_two = gain_rows[0], gain_rows[1]
+        w_down, normed_two, hidden_act, grad_gate_up, down_part_grad, gate_up_grad = ffn(
+            1, ranks, shards, mixed_low, w_gate_up, grad_low, down_weight, gain_rows
+        )
+    else:
+        tail = jnp.concatenate(
+            [
+                slab(forget_weight, rank * local_heads, local_heads, 1),
+                norm_gains.T,
+                jnp.zeros((attn_in_weight.shape[0], LANES - local_heads - 2), BF16),
+            ],
+            axis=1,
+        )
+        offsets = jnp.arange(block_len, dtype=jnp.int32)
+        blocks = jnp.arange(seq_order.shape[0], dtype=jnp.int32)
+        places = (seq_order[:, None] * block_len + offsets[None]).reshape(-1)
+        by_block = segment_ids[0].reshape(-1, block_len)
+        chosen = seq_order[:, None, None] == blocks[None, :, None]
+        segments = jnp.sum(jnp.where(chosen, by_block[None], 0), axis=1).reshape(-1)
+        places, segments = places.astype(F32), segments.astype(F32)
+        places_all = (places[None, :], places[:, None], segments[None, :], segments[:, None])
+        bias = jnp.pad(slab(forget_bias, rank * local_heads, local_heads, 0), (0, LANES - local_heads))[None]
+        head_gains = jnp.tile(qk_gains, (1, LANES // head_dim))
+        down_piece = slab(down_weight, rank * hidden_piece, hidden_piece, 0)
+        inputs, grad_low, w_in, gate_up_piece = comm.begin(
+            tokens[0], out_grad[0], attn_in_weight, tail, gate_up_weight, hidden_piece, width, padded
+        )
+        w_gate_up = lax.all_gather(gate_up_piece, "fsdp", axis=0, tiled=True)
+        gain_cols = w_in[:, 4 * padded : 4 * padded + LANES].astype(F32).T
+        gain_one = gain_cols[local_heads]
+        gain_two = gain_cols[local_heads + 1]
+        wide_inputs = inputs.astype(F32)
+        scale_one = rms_scale(wide_inputs)
+        normed = (wide_inputs * scale_one * gain_one).astype(BF16)
+        project = dot(normed, w_in)
+        gated, attended, wide_query, wide_key, wide_value = attend(
+            project, places_all, bias, head_gains, head_dim, padded, local_heads
+        )
+        gated_all, w_out = comm.gather_cols(gated[:, :width], slab(out_weight, rank * width, width, 1))
+        mixed_cols = slab(inputs, rank * width, width, 1).astype(F32) + dot(gated_all, w_out)
+        mixed_low, w_down = comm.gather_cols(mixed_cols.astype(BF16), down_piece)
+        mixed = mixed_low.astype(F32)
+        scale_two = rms_scale(mixed)
+        normed_two = (mixed * scale_two * gain_two).astype(BF16)
+        gate_up = dot(normed_two, w_gate_up)
+        gate_part, up_part = gate_up[:, :hidden], gate_up[:, hidden:]
+        gate_sigmoid = jax.nn.sigmoid(gate_part)
+        silu = gate_part * gate_sigmoid
+        hidden_act = (silu * up_part).astype(BF16)
+        grad_hidden = right_product(grad_low, w_down)
+        grad_gate = grad_hidden * up_part * gate_sigmoid * (1.0 + gate_part * (1.0 - gate_sigmoid))
+        grad_gate_up = jnp.concatenate([grad_gate, grad_hidden * silu], axis=1).astype(BF16)
+        down_part_grad = left_product(hidden_act, grad_low).astype(BF16)
+        gate_up_grad = left_product(normed_two, grad_gate_up).astype(BF16)
+        down_part = dot(hidden_act, w_down).astype(BF16)
 
     def own_rows(array):
         return slab(array, rank * row_count, row_count, 0)
 
-    grad_hidden = right_product(grad_low, w_down)
-    grad_gate = grad_hidden * up_part * gate_sigmoid * (1.0 + gate_part * (1.0 - gate_sigmoid))
-    grad_gate_up = jnp.concatenate([grad_gate, grad_hidden * silu], axis=1).astype(BF16)
-
     def reduce_shards(array):
         return lax.psum_scatter(array.astype(BF16), "fsdp", scatter_dimension=0, tiled=True)
 
-    down_part_grad = left_product(hidden_act, grad_low).astype(BF16)
-    gate_up_grad = left_product(normed_two, grad_gate_up).astype(BF16)
     grad_gate_up, down_part_grad, gate_up_grad = lax.optimization_barrier(
         (grad_gate_up, down_part_grad, gate_up_grad)
     )
     down_share = reduce_shards(down_part_grad)
     gate_up_share = reduce_shards(gate_up_grad)
     if plain:
-        grad_mixed_cols, grad_gated, gain_two_grad = middle(
-            3, ranks, grad_gate_up, w_gate_up, mixed_low, grad_low, w_out, gain_two[None]
-        )
-        gain_two_grad = gain_two_grad[0]
-        grad_branch = grad_mixed_cols.astype(BF16)
+        grad_mixed_cols, grad_gated, gain_two_grad, down_part, out_part = middle(
+            3, ranks, grad_gate_up, w_gate_up, mixed_low, grad_low, w_out, hidden_act, w_down, gated_all, gain_two[None]
+        )
     else:
         grad_normed_two = right_product(grad_gate_up, w_gate_up)
         gain_two_grad = jnp.sum(grad_normed_two * mixed * scale_two, axis=0)
@@ -1143,27 +1652,25 @@
             ).astype(F32)
         )
     grad_gated, down_share = lax.optimization_barrier((grad_gated, down_share))
-    grad_project, small, down_pieces = attend_back(
+    grad_project, small, *rest = attend_back(
         project, places_all, bias, head_gains, attended, (wide_query, wide_key, wide_value),
-        grad_gated, down_part, ranks if plain else 0, head_dim, padded, local_heads,
+        grad_gated, (down_part, normed, out_part) if plain else (), ranks if plain else 0, head_dim, padded, local_heads,
     )
-
-    in_part = left_product(normed, grad_project).astype(BF16)
-    out_part = left_product(gated_all, grad_branch).astype(BF16)
-    late = jnp.concatenate([in_part[:, : 4 * padded], out_part, in_part[:, 4 * padded :]], axis=1)
+    if plain:
+        down_pieces, late = rest
+    else:
+        in_part = left_product(normed, grad_project).astype(BF16)
+        out_part = left_product(gated_all, grad_branch).astype(BF16)
+        late = jnp.concatenate([in_part[:, : 4 * padded], out_part, in_part[:, 4 * padded :]], axis=1)
     late, gate_up_share = lax.optimization_barrier((late, gate_up_share))
     late_share = reduce_shards(late)
 
-    bias_slots = jnp.where(
-        jnp.arange(ranks, dtype=jnp.int32)[:, None] == rank, small[2, :local_heads][None], 0.0
-    ).reshape(-1)
-    qk_sum = small[0:2].reshape(2, LANES // head_dim, head_dim).sum(axis=1).reshape(-1)
-    others = jnp.concatenate([bias_slots, qk_sum])
-    others = jnp.pad(others, (0, model_width - others.shape[0]))
     if plain:
         down_sum = down_pieces.astype(F32).sum(axis=0)
-        sums = jnp.stack([jnp.zeros_like(others), gain_two_grad, others] + [jnp.zeros_like(others)] * 5)
-        tokens_grad, sums = last_moves(4, ranks, grad_project, w_in, inputs, grad_mixed_cols, gain_one[None], sums)
+        tokens_grad, sums, down_own, gate_up_own = last_moves(
+            4, ranks, grad_project, w_in, inputs, down_share, gate_up_share, grad_mixed_cols, gain_one[None],
+            gain_two_grad, small,
+        )
         tokens_grad = tokens_grad[None]
     else:
         grad_normed = right_product(grad_project, w_in)
@@ -1174,32 +1681,42 @@
         )
         down_sum = lax.psum_scatter(down_part, "ctx", scatter_dimension=0, tiled=True).astype(F32)
         tokens_grad = lax.psum_scatter(grad_inputs.astype(BF16), "ctx", scatter_dimension=0, tiled=True)[None]
-        sums = lax.psum(jnp.stack([gain_one_grad, gain_two_grad, others]), "ctx")
+        own_bias = jnp.where(jnp.arange(ranks, dtype=jnp.int32)[:, None] == rank, small[2:3], 0.0)
+        small_rows = jnp.concatenate([small[0:2].reshape(1, -1), jnp.pad(own_bias, ((0, 0), (0, LANES)))], axis=0)
+        sums = jnp.concatenate(
+            [
+                jnp.stack([gain_one_grad, gain_two_grad]),
+                jnp.pad(small_rows, ((0, 0), (0, model_width - 2 * LANES))),
+            ],
+            axis=0,
+        )
+        sums = lax.psum(sums, "ctx")
+        down_own = lax.all_gather(down_share, "ctx", axis=0, tiled=False)
+        gate_up_own = lax.all_gather(gate_up_share, "ctx", axis=0, tiled=False)
     result = own_rows(mixed_low).astype(F32) + down_sum
     block_out = result.astype(BF16)[None]
     branch = result - own_rows(inputs).astype(F32)
-    own_valid = own_rows(valid)
+    own_valid = own_rows(places_all[3][:, 0] >= 0).astype(F32)
     partial_sums = jnp.stack(
         [
             jnp.sum(own_valid * jnp.sum(result * result, axis=-1)),
             jnp.sum(own_valid * jnp.sum(branch * branch, axis=-1)),
         ]
     )
-    valid_count = jnp.sum(valid) * model_width
-
-    down_own, gate_up_own, stats = comm.stack(
-        6, down_share, gate_up_share, jnp.broadcast_to(jnp.pad(partial_sums, (0, LANES - 2)), (8, LANES))
-    )
+    valid_count = jnp.sum((segment_ids[0] >= 0).astype(F32)) * model_width
+
     down_out = down_own.astype(F32).reshape(down_weight.shape)
     gate_up_out = spread_cols(gate_up_own, (hidden_piece, 0, 2 * shards))[0]
     share = model_width // shards
     room = -(-share // LANES) * LANES
     gain_pieces = jnp.pad(sums[0:2].reshape(2, shards, share).transpose(1, 0, 2), ((0, 0), (0, 0), (0, room - share)))
-    tail = sums[2, : 2 * room].reshape(1, 2, room)
-    pieces = jnp.concatenate(
-        [gain_pieces, jnp.broadcast_to(tail, (shards, 2, room)), jnp.zeros((shards, 4, room), F32)], axis=1
-    )
-    late_own, piece_sum = comm.finish(7, late_share, pieces)
+    tail = jnp.broadcast_to(sums[None, 2 : 3 + ranks, : 2 * LANES], (shards, 1 + ranks, 2 * LANES))
+    tail = jnp.pad(tail, ((0, 0), (0, 0), (0, max(room - 2 * LANES, 0))))
+    gain_pieces = jnp.pad(gain_pieces, ((0, 0), (0, 0), (0, max(2 * LANES - room, 0))))
+    pieces = jnp.concatenate([gain_pieces, tail], axis=1)
+    pieces = jnp.pad(pieces, ((0, 0), (0, -pieces.shape[1] % 8), (0, 0)))
+    stats = jnp.broadcast_to(jnp.pad(partial_sums, (0, LANES - 2)), (8, LANES))
+    late_own, piece_sum, stats = comm.finish(7, late_share, pieces, stats)
     if plain:
         in_out, out_out = spread_cols(late_own, (width, 0, 4), (width, 4 * width, 1))
     else:
@@ -1212,10 +1729,9 @@
     last = 4 * padded + width
     forget_out = jnp.concatenate([late_own[c, :, last : last + local_heads] for c in range(ranks)], axis=1).astype(F32)
     gains_sum = piece_sum[0:2, :share]
-    tail_sum = piece_sum[2:4].reshape(-1)
-    bias_sum = tail_sum[:head_count]
-    qk_sum = tail_sum[head_count : head_count + 2 * head_dim].reshape(2, head_dim)
-    totals = stats[:, 0, :2].sum(axis=0)
+    bias_sum = piece_sum[3 : 3 + ranks, :local_heads].reshape(-1)
+    qk_sum = piece_sum[2, : 2 * LANES].reshape(2, LANES // head_dim, head_dim).sum(axis=1)
+    totals = stats[0, :2]
     return (
         block_out, tokens_grad, gains_sum, in_out, forget_out, bias_sum, qk_sum,
         out_out, gate_up_out, down_out, jnp.sqrt(totals / valid_count)[None],

time: 486 us -> 427 us (0.88)
  matrix products: 51.8 us -> 0 us
  Pallas kernels: 357 us -> 377 us
  local copies, waits for them, and re-layouts: 28.4 us -> 9.79 us
  other arithmetic: 23.8 us -> 10.1 us
  waiting for transfers between devices: 0.76 us -> 6.81 us
    pallas_call x3, Pallas kernels: 115 us -> 231 us  [the longest x1 118 us: front(): pl.pallas_call(functools.partial(front_kernel, shards, head, heads, width...]
    pallas_call x4 -> x1, Pallas kernels: 132 us -> 32.1 us  [exchange(): pl.pallas_call(functools.partial(exchange_kernel, [mode for mode, _ in op...]
    dot_general x9 -> x0, matrix products: 51.8 us -> none  [the longest x4 25.1 us: dot(): lax.dot_general(left, right, (((1,), (0,)), ((), ())), preferred_element_...]
    pallas_call x1 -> x0, local copies, waits for them, and re-layouts: 7.66 us -> none  [start_moves(): pl.pallas_call(functools.partial(start_kernel, shards, width, piece), in_...]
    concatenate x5 -> x1, other arithmetic: 6.7 us -> 0.02 us  [body(): pieces = jnp.concatenate([gain_pieces, tail], axis=1)]
    reduce_scatter x3, waiting for transfers between devices: 0.01 us -> 6.08 us  [reduce_shards(): lax.psum_scatter(array.astype(BF16), 'fsdp', scatter_dimension=0, tiled=T...]
    reduce_sum x7 -> x4, other arithmetic: 7 us -> 1.23 us  [the longest x1 0.61 us: body(): piece_sum[2, :2 * LANES].reshape(2, LANES // head_dim, head_dim).sum(axis=1)]
    pallas_call x1, Pallas kernels: 33.4 us -> 39 us  [attend_back(): pl.pallas_call(functools.partial(attend_back_kernel, head, chunk, width,...]
  transfers between devices with their start and end apart: 4 -> 3, of which waited for: 0 -> 1; matrix products, arithmetic and copies ran while one was open for 14% -> 3% of each run, Pallas kernels for 56% -> 43%
where the time goes in v4:
time: 427 us; the launch traced here: 419 us
  Pallas kernels  377 us (88%)
  between operations  15 us (4%)
  other arithmetic  10.1 us (2%)
  local copies, waits for them, and re-layouts  9.79 us (2%)
  waiting for transfers between devices  6.81 us (2%)
    pallas_call x1, Pallas kernels, front(): pl.pallas_call(functools.partial(front_kernel, shards, head, heads, width...  118 us
    pallas_call x1, Pallas kernels, last_moves(): pl.pallas_call(functools.partial(last_kernel, ranks), in_specs=[ANY] * 5...  69.4 us
    pallas_call x1, Pallas kernels, middle(): pl.pallas_call(functools.partial(middle_kernel, ranks), in_specs=[ANY] *...  64.7 us
    pallas_call x1, Pallas kernels, ffn(): pl.pallas_call(functools.partial(ffn_kernel, shards, pick_chunk(rows)), i...  43.8 us
    pallas_call x1, Pallas kernels, attend_back(): pl.pallas_call(functools.partial(attend_back_kernel, head, chunk, width,...  39 us
    pallas_call x1, Pallas kernels, exchange(): pl.pallas_call(functools.partial(exchange_kernel, [mode for mode, _ in op...  32.1 us
    pallas_call x2, Pallas kernels, spread_cols(): pl.pallas_call(functools.partial(spread_kernel, pieces), grid=(rows // pa...  10.1 us
  transfers between devices with their start and end apart: 3, of which 1 were waited for; matrix products, arithmetic and copies ran while one was open for 3% of the time, Pallas kernels for 43%

profile of v4, /device:TPU:0, one launch (start us, length us, event | category | flops | bytes accessed | tf_op | source)
XLA Modules:
  0.0 418.9 jit_solution(9938831841600127509)
XLA Ops:
  7.2 1.4 copy.28.forget_weight
  8.7 117.8 %front.1 = (bf16[768,1536]{1,0:T(8,128)(2,1)}, bf16[768,1536]{1,0:T(8,128)(2,1)}, bf16[1536,1664]{1,0:T(8,128)(2,1)}, bf16[1536,384]{1,0:T(8,128)(2,1)}, bf16[15...) custom-call(bf16[192,1536]{1,0:T(8,128)(2,1)} %bitcast.23, ...), custom_call_target="tpu_custom_call" | custom-call | bytes 314572800 | tf_op jit(solution)/shard_map/front/pallas_call | solution.py:945
  126.5 43.8 %ffn.1 = (bf16[1024,1536]{1,0:T(8,128)(2,1)}, bf16[768,1536]{1,0:T(8,128)(2,1)}, bf16[768,1024]{1,0:T(8,128)(2,1)}, bf16[768,2048]{1,0:T(8,128)(2,1)}, bf16[1024...) custom-call(bf16[768,1536]{1,0:T(8,128)(2,1)} %get-tuple-element.61.mixed, bf16[1536,2048]{1,0:T(8,128)(2,1)} %get-tuple-element.73.w_gate_up, ...), custom_call_target="tpu_custom_call" | custom-call | bytes 104857600 | tf_op jit(solution)/shard_map/ffn/pallas_call | solution.py:1117
  170.4 0.7 reduce-scatter.6.cloned.1.call-update
  171.1 1.5 fusion.3
  172.6 64.7 %middle.1 = (f32[768,384]{1,0:T(8,128)}, f32[768,384]{1,0:T(8,128)}, f32[8,1536]{1,0:T(8,128)}, bf16[768,1536]{1,0:T(8,128)(2,1)}, bf16[1536,384]{1,0:T(8,128)(2,1)}) custom-call(bf16[768,2048]{1,0:T(8,128)(2,1)} %get-tuple-element.79.grad_gate_up, bf16[1536,2048]{1,0:T(8,128)(2,1)} %get-tuple-element.73.w_gate_up, ...), custom_call_target="tpu_custom_call" | custom-call | bytes 157286400 | tf_op jit(solution)/shard_map/middle/pallas_call | solution.py:1279
  237.4 39.0 %attend_back.1 = (bf16[768,1664]{1,0:T(8,128)(2,1)}, f32[8,128]{1,0:T(8,128)}, bf16[4,192,1536]{2,1,0:T(8,128)(2,1)}, bf16[1536,2048]{1,0:T(8,128)(2,1)}) custom-call(f32[1,768]{1,0:T(1,128)} %get-tuple-element.62.pos_row, f32[768,1]{1,0:T(8,128)} %get-tuple-element.63.pos_col, f32[1,768]{1,0:T(1,128)} %get-tuple-element.64.seg_row, ...), custom_call_target="tpu_custom_call" | custom-call | tf_op jit(solution)/shard_map/attend_back/pallas_call | solution.py:389
  276.4 6.1 %reduce-scatter.6.cloned.1.call-done.other = bf16[192,2048]{1,0:T(8,128)(2,1)} async-done(((bf16[1536,2048]{1,0:T(8,128)(2,1)}), bf16[192,2048]{1,0:T(8,128)(2,1)}) %reduce-scatter.6.cloned.1.call-update) | async-done | bytes 786448 | tf_op jit(solution)/shard_map/reduce_scatter | solution.py:1630
  282.5 0.7 copy-done.5
  283.1 0.6 fusion.1
  284.4 1.0 fusion
  285.4 0.3 convert_reduce_fusion
  285.8 2.3 multiply_reduce_fusion.1
  288.0 0.6 select_reduce_fusion.1
  288.6 1.4 fusion.2
  290.0 69.4 %last_moves.1 = (bf16[192,1536]{1,0:T(8,128)(2,1)}, f32[8,1536]{1,0:T(8,128)}, bf16[4,128,1536]{2,1,0:T(8,128)(2,1)}, bf16[4,192,2048]{2,1,0:T(8,128)(2,1)}) custom-call(bf16[768,1664]{1,0:T(8,128)(2,1)} %get-tuple-element.91.grad_project, bf16[1536,1664]{1,0:T(8,128)(2,1)} %get-tuple-element.92.w_in, bf16[768,1536]{1,0:T(8,128)(2,1)} %get-tuple-element.93.inputs, ...), custom_call_target="tpu_custom_call" | custom-call | bytes 157286400 | tf_op jit(solution)/shard_map/last_moves/pallas_call | solution.py:1414
  359.4 0.7 slice.39
  360.1 0.8 slice.38
  361.0 5.2 %spread_cols.3 = f32[192,8192]{1,0:T(8,128)} custom-call(bf16[4,192,2048]{2,1,0:T(8,128)(2,1)} %get-tuple-element.108.refs_0_), custom_call_target="tpu_custom_call" | custom-call | bytes 9437184 | tf_op jit(solution)/shard_map/spread_cols/pallas_call | solution.py:1473
  366.3 0.6 pad.13.refs_1_
  366.9 2.2 bitcast_convert_fusion
  369.1 0.6 broadcast_in_dim.23.refs_2_
  369.7 32.1 %exchange.1 = (bf16[4,192,2048]{2,1,0:T(8,128)(2,1)}, f32[8,8,256]{2,1,0:T(8,128)}, f32[4,8,128]{2,1,0:T(8,128)}) custom-call(bf16[192,2048]{1,0:T(8,128)(2,1)} %reduce-scatter.8.cloned.1.call-done.refs_0_, f32[8,8,256]{2,1,0:T(8,128)} %pad.13.refs_1_, f32[8,128]{1,0:T(8,128)} %broadcast_in_dim.23.refs_2_), custom_call_target="tpu_custom_call" | custom-call | bytes 64552960 | tf_op jit(solution)/shard_map/exchange/pallas_call | solution.py:679
  401.8 0.9 slice_bitcast_fusion.3
  402.7 4.9 %spread_cols.2 = (f32[192,6144]{1,0:T(8,128)}, f32[192,1536]{1,0:T(8,128)}) custom-call(bf16[4,192,2048]{2,1,0:T(8,128)(2,1)} %get-tuple-element.105.refs_0_), custom_call_target="tpu_custom_call" | custom-call | bytes 8847360 | tf_op jit(solution)/shard_map/spread_cols/pallas_call | solution.py:1473
  407.7 0.6 slice.48
  408.6 0.1 copy.33
  408.7 0.6 reduce_sum.87
  409.3 0.6 reshape.42
  409.9 0.5 divide_sqrt_fusion
  410.5 0.6 maximum_convert_fusion
  411.1 0.8 copy.37
  (30 shorter events, 0.7 us)
Async XLA Ops:
  7.2 230.2 %reduce-scatter.4.cloned.1.call-start = ((), (), s32[]{:S(2)}) async-start(), calls=%async_computation.3 | async-start | bytes 3538944 | tf_op jit(solution)/shard_map/reduce_scatter | solution.py:1630
  170.3 112.1 %reduce-scatter.6.cloned.1.call-start = ((), (), s32[]{:S(2)}) async-start(), calls=%async_computation.4 | async-start | bytes 7077888 | tf_op jit(solution)/shard_map/reduce_scatter | solution.py:1630
  171.1 198.0 %reduce-scatter.8.cloned.1.call-start = ((), (), s32[]{:S(2)}) async-start(), calls=%async_computation.5 | async-start | bytes 7077888 | tf_op jit(solution)/shard_map/reduce_scatter | solution.py:1630
  282.5 0.7 copy-start.5
  282.5 3.0 copy-start
  361.0 5.9 %copy-start.1 = (bf16[4,128,1536]{2,1,0:T(8,128)(2,1)S(1)}, bf16[4,128,1536]{2,1,0:T(8,128)(2,1)}, u32[]{:S(2)}) copy-start(bf16[4,128,1536]{2,1,0:T(8,128)(2,1)} %get-tuple-element.109) | copy-start | bytes 4718596
  369.7 41.4 %copy-start.2 = (bf16[192,1536]{1,0:T(8,128)(2,1)S(1)}, bf16[192,1536]{1,0:T(8,128)(2,1)}, u32[]{:S(2)}) copy-start(bf16[192,1536]{1,0:T(8,128)(2,1)} %get-tuple-element.101) | copy-start | bytes 1769476
  401.8 5.9 %copy-start.3 = (f32[8,8,256]{2,1,0:T(8,128)S(1)}, f32[8,8,256]{2,1,0:T(8,128)}, u32[]{:S(2)}) copy-start(f32[8,8,256]{2,1,0:T(8,128)} %get-tuple-element.104) | copy-start | bytes 196612
  401.8 8.1 %copy-start.4 = (f32[4,8,128]{2,1,0:T(8,128)S(1)}, f32[4,8,128]{2,1,0:T(8,128)}, u32[]{:S(2)}) copy-start(f32[4,8,128]{2,1,0:T(8,128)} %get-tuple-element.110) | copy-start | bytes 49156
Sparse Core Ops, SparseCore 0:
  170.5 40.6 reduce-scatter.3
  213.5 68.9 reduce-scatter.5
  284.8 68.1 reduce-scatter.7

commit v5 on v4

--- a/solution.py
+++ b/solution.py
@@ -1,4 +1,5 @@
 import functools
+import math
 
 import jax
 import jax.numpy as jnp
@@ -165,18 +166,23 @@
     if ranks:
         aside, normed, out_grad, grad_project, small, aside_in, late = rest[:7]
         mask, wide_grad, grad_query, grad_key, grad_value, grad_prefix = rest[7:13]
-        normed_in, out_in, late_all, load_sem, save_sem = rest[13:18]
-        sems = rest[18:]
+        normed_in, out_in, aside_own, late_all, load_sem, save_sem = rest[13:19]
+        sems = rest[19:]
+
+        def loads():
+            own = rows_of(aside, lax.axis_index("ctx"), aside_in.shape[1])
+            for n, pair in enumerate(((normed, normed_in), (out_grad, out_in), (own, aside_own))):
+                yield pltpu.make_async_copy(*pair, load_sem.at[n])
+
     else:
         grad_project, small, mask, wide_grad, grad_query, grad_key, grad_value, grad_prefix = rest
     step = pl.program_id(0)
     steps = pl.num_programs(0)
 
     def aside_copies():
-        send_sem, recv_sem, own_sem = sems
+        send_sem, recv_sem = sems
         rank = lax.axis_index("ctx")
         size = aside_in.shape[1]
-        yield pltpu.make_async_copy(rows_of(aside, rank, size), aside_in.at[rank], own_sem)
         for distance in range(1, ranks):
             other = rank ^ distance
             yield to_rank(
@@ -192,8 +198,8 @@
             greet([{"ctx": rank ^ distance} for distance in range(1, ranks)])
             for copy in aside_copies():
                 copy.start()
-            pltpu.make_async_copy(normed, normed_in, load_sem.at[0]).start()
-            pltpu.make_async_copy(out_grad, out_in, load_sem.at[1]).start()
+            for copy in loads():
+                copy.start()
 
     rows = query.shape[0]
     lanes = lane_ids(rows)
@@ -229,9 +235,8 @@
         wide_grad[:, 0:head] = grad_result
         wide_grad[:, head:LANES] = rest.astype(BF16)
         grad_query[...] = jnp.zeros_like(grad_query)
-        @pl.loop(0, rows // chunk)
-        def _(turn):
-            part = pl.ds(pl.multiple_of(turn * chunk, chunk), chunk)
+        @turns(rows, chunk, unroll=True)
+        def _(part):
             scores = right_product(wide_key[side, part, :], wide_query[side]) + mask[part, :]
             probs = jnp.exp(scores)
             outer = right_product(wide_value[side, part, :], wide_grad[...])
@@ -281,27 +286,45 @@
             small[2:3, :] += jnp.sum(grad_logit.astype(F32), axis=0, keepdims=True)
 
         if ranks:
-            pltpu.make_async_copy(normed, normed_in, load_sem.at[0]).wait()
-            pltpu.make_async_copy(out_grad, out_in, load_sem.at[1]).wait()
+            for copy in loads():
+                copy.wait()
+            keep = pltpu.make_async_copy(aside_own, aside_in.at[lax.axis_index("ctx")], load_sem.at[3])
+            keep.start()
             ends = 4 * width, 4 * width + out_grad.shape[1]
-
-            def save(turn):
-                part = pl.ds(pl.multiple_of(turn * chunk, chunk), chunk)
-                return pltpu.make_async_copy(late_all.at[part, :], late.at[part, :], save_sem.at[turn])
-
-            @pl.loop(0, late.shape[0] // chunk)
+            late_all[:, ends[0] : ends[1]] = out_in[...]
+            piece = 2 * LANES
+
+            def save(turn, size=piece):
+                cols = pl.ds(pl.multiple_of(turn * piece, LANES), size)
+                return pltpu.make_async_copy(late_all.at[:, cols], late.at[:, cols], save_sem.at[turn])
+
+            count = 4 * width // piece
+            rest_save = pltpu.make_async_copy(
+                late_all.at[:, pl.ds(ends[0], late.shape[1] - ends[0])],
+                late.at[:, pl.ds(ends[0], late.shape[1] - ends[0])],
+                save_sem.at[count],
+            )
+
+            def product(into, cols):
+                @turns(late.shape[0], 3 * chunk if late.shape[0] % (3 * chunk) == 0 else chunk)
+                def _(part):
+                    late_all[part, into] = dot(normed_in[part, :], grad_project[:, cols]).astype(BF16)
+
+            product(slice(ends[1], ends[1] + LANES), slice(ends[0], ends[0] + LANES))
+            rest_save.start()
+
+            @pl.loop(0, count)
             def _(turn):
-                part = pl.ds(pl.multiple_of(turn * chunk, chunk), chunk)
-                product = left_product(normed_in[:, part], grad_project[...]).astype(BF16)
-                late_all[part, 0 : ends[0]] = product[:, 0 : ends[0]]
-                late_all[part, ends[0] : ends[1]] = out_in[part, :]
-                late_all[part, ends[1] : ends[1] + LANES] = product[:, ends[0] :]
+                cols = pl.ds(pl.multiple_of(turn * piece, LANES), piece)
+                product(cols, cols)
                 save(turn).start()
 
             for copy in aside_copies():
                 copy.wait()
-
-            @pl.loop(0, late.shape[0] // chunk)
+            keep.wait()
+            rest_save.wait()
+
+            @pl.loop(0, count)
             def _(turn):
                 save(turn).wait()
 
@@ -370,7 +393,7 @@
     ]
     if ranks:
         aside, normed, out_grad = beside
-        model, late_cols = normed.shape[1], total + out_grad.shape[1]
+        model, late_cols = normed.shape[0], total + out_grad.shape[1]
         out_specs += [ANY, ANY]
         out_shape += [
             jax.ShapeDtypeStruct((ranks, aside.shape[0] // ranks, aside.shape[1]), BF16),
@@ -379,12 +402,12 @@
         scratch += [
             pltpu.VMEM(normed.shape, BF16),
             pltpu.VMEM(out_grad.shape, BF16),
+            pltpu.VMEM((aside.shape[0] // ranks, aside.shape[1]), BF16),
             pltpu.VMEM((model, late_cols), BF16),
-            pltpu.SemaphoreType.DMA((2,)),
-            pltpu.SemaphoreType.DMA((model // chunk,)),
+            pltpu.SemaphoreType.DMA((4,)),
+            pltpu.SemaphoreType.DMA((4 * width // (2 * LANES) + 1,)),
             pltpu.SemaphoreType.DMA((ranks - 1,)),
             pltpu.SemaphoreType.DMA((ranks - 1,)),
-            pltpu.SemaphoreType.DMA,
         ]
     return pl.pallas_call(
         functools.partial(attend_back_kernel, head, chunk, width, heads, ranks),
@@ -510,6 +533,77 @@
             def _():
                 self.line(owner_layer, self.below, 1).wait_send()
 
+    def near_finish(self):
+        self.keep.wait()
+        self.from_side(self.layer)
+        self.side(self.layer, self.core).wait_send()
+
+        @pl.when(self.has_below)
+        def _():
+            self.line(self.layer - 1, self.below, 1).wait_recv()
+            self.line(self.layer, self.below, 1).wait_send()
+
+        @pl.when(self.has_above)
+        def _():
+            self.line(self.layer + 1, self.above, 0).wait_recv()
+            self.line(self.layer, self.above, 0).wait_send()
+
+    def near_load(self, near, sems, number):
+        if number == 0:
+            chip = 2 * self.rows
+            source, target = rows_of(near, self.layer, chip), rows_of(self.target, self.layer, chip)
+        else:
+            owner = self.shard + (-2, 2)[number - 1]
+            source, target = rows_of(near, owner, self.rows), self.block(owner)
+        return pltpu.make_async_copy(source, target, sems.at[number])
+
+    def near_start(self, near, sems):
+        self.near_load(near, sems, 0).start()
+
+        @pl.when(self.has_below)
+        def _():
+            self.near_load(near, sems, 1).start()
+
+        @pl.when(self.has_above)
+        def _():
+            self.near_load(near, sems, 2).start()
+
+    def resume(self, near, sems):
+        @pl.when(self.has_below)
+        def _():
+            self.near_load(near, sems, 1).wait()
+
+            @pl.when(self.has_above)
+            def _():
+                self.line(self.layer - 1, self.above, 0).start()
+
+            self.side(self.layer - 1, self.core).start()
+
+        @pl.when(self.has_above)
+        def _():
+            self.near_load(near, sems, 2).wait()
+
+            @pl.when(self.has_below)
+            def _():
+                self.line(self.layer + 1, self.below, 1).start()
+
+            self.side(self.layer + 1, self.core).start()
+
+    def resumed_sent(self):
+        for owner_layer in range(self.layers):
+
+            @pl.when(owner_layer != self.layer)
+            def _():
+                self.side(owner_layer, self.core).wait_send()
+
+            @pl.when(self.has_above & (owner_layer < self.layer))
+            def _():
+                self.line(owner_layer, self.above, 0).wait_send()
+
+            @pl.when(self.has_below & (owner_layer > self.layer))
+            def _():
+                self.line(owner_layer, self.below, 1).wait_send()
+
 
 def line_scratch(shards):
     layers = shards // 2
@@ -596,103 +690,6 @@
     return Relay(rank, part, place, *sems)
 
 
-def exchange_kernel(modes, ranks, across, shards, *refs):
-    count = len(modes)
-    sources, targets = refs[:count], refs[count : 2 * count]
-    send_sem, recv_sem, own_sem = refs[2 * count : 2 * count + 3]
-    rank = lax.axis_index("ctx")
-    shard = lax.axis_index("fsdp")
-    line = None
-    if "line" in modes:
-        at = modes.index("line")
-        line = Line(shards, sources[at], targets[at], refs[2 * count + 3 :])
-    far = any(mode not in ("gather_rows", "gather_cols", "stack", "line") for mode in modes)
-    peers = [{"ctx": rank ^ distance} for distance in range(1, ranks if far else ranks - 1)]
-    if across:
-        peers += [{"fsdp": shard ^ distance} for distance in range(1, across)]
-    greet(peers, line)
-    copies, relays = [], []
-    for op, (mode, source, target) in enumerate(zip(modes, sources, targets)):
-        if mode == "line":
-            line.start()
-            continue
-        if mode in ("gather_rows", "gather_cols", "stack"):
-            relay = relay_ops(mode, rank, source, target, (send_sem.at[op], recv_sem.at[op], own_sem.at[op]))
-            relay.start()
-            relays.append(relay)
-            continue
-        axis, me, members = ("fsdp", shard, across) if mode == "shards" else ("ctx", rank, ranks)
-        for distance in range(members):
-            other = me ^ distance if distance else me
-            place = target.at[me]
-            if mode == "scatter_rows":
-                piece = rows_of(source, other, target.shape[1])
-            elif mode == "scatter_cols":
-                piece = cols_of(source, other, target.shape[2])
-            elif mode == "shards":
-                piece = source.at[other]
-            else:
-                piece = source
-            if distance == 0:
-                copy = pltpu.make_async_copy(piece, place, own_sem.at[op, 0])
-            else:
-                copy = pltpu.make_async_remote_copy(
-                    piece, place, send_sem.at[op, distance - 1], recv_sem.at[op, distance - 1],
-                    device_id={axis: other}, device_id_type=MESH,
-                )
-            copy.start()
-            copies.append(copy)
-    for index in range(max(len(relays), shards // 2 - 1 if line is not None else 0)):
-        if line is not None and 0 < index < shards // 2:
-            line.step(index)
-        if index < len(relays):
-            relays[index].forward()
-    if line is not None:
-        line.step(shards // 2 - 1)
-        line.finish()
-    for relay in relays:
-        relay.finish()
-    for copy in copies:
-        copy.wait()
-
-
-def exchange(collective_id, ranks, across, shards, *ops):
-    shapes = []
-    for mode, source in ops:
-        shape = source.shape
-        if mode == "gather_rows":
-            shape = (ranks * shape[0], shape[1])
-        elif mode == "gather_cols":
-            shape = (shape[0], ranks * shape[1])
-        elif mode == "scatter_rows":
-            shape = (ranks, shape[0] // ranks, shape[1])
-        elif mode == "scatter_cols":
-            shape = (ranks, shape[0], shape[1] // ranks)
-        elif mode in ("stack", "each"):
-            shape = (ranks,) + shape
-        elif mode == "line":
-            shape = (shards * shape[0], shape[1])
-        shapes.append(jax.ShapeDtypeStruct(shape, source.dtype))
-    count = len(ops)
-    most = max(6, across - 1)
-    moved = sum(s.size * s.dtype.itemsize for s in shapes)
-    return pl.pallas_call(
-        functools.partial(exchange_kernel, [mode for mode, _ in ops], ranks, across, shards),
-        in_specs=[ANY] * count,
-        out_specs=[ANY] * count,
-        out_shape=shapes,
-        scratch_shapes=[
-            pltpu.SemaphoreType.DMA((count, most)),
-            pltpu.SemaphoreType.DMA((count, most)),
-            pltpu.SemaphoreType.DMA((count, 2)),
-        ]
-        + (line_scratch(shards) if any(mode == "line" for mode, _ in ops) else []),
-        compiler_params=pltpu.CompilerParams(collective_id=collective_id, has_side_effects=True),
-        cost_estimate=pl.CostEstimate(flops=0, bytes_accessed=moved * 20, transcendentals=0),
-        name="exchange",
-    )(*[source for _, source in ops])
-
-
 VMEM_WHOLE = pl.BlockSpec(memory_space=pltpu.VMEM)
 
 
@@ -702,17 +699,18 @@
     )
 
 
-FRONT_LOADS = 3
-FRONT_SAVES = 9
+FRONT_LOADS = 6
+FRONT_SAVES = 12
 
 
 def front_kernel(
     shards, head, heads, width, piece, chunk,
-    tokens, cotangent, weight, weight_out, other, forget_weight, norm_gains, qk_gains, segments, order, forget_bias,
+    tokens, cotangent, weight, weight_out, other, down, forget_weight, norm_gains, qk_gains, segments, order, forget_bias,
     inputs, grad_low, w_in, w_out, w_gate_up, normed, project, gated, attended, wide_query, wide_key, wide_value,
-    mixed, gain_rows, pos_row, pos_col, seg_row, seg_col, bias, gains,
-    weight_all, other_all, out_all, own_in, own_pick, own_out, x_all, in_all, hn_all, proj_all, mask, prefix,
-    gated_all, attended_all, query_all, key_all, value_all, out_cols, scale_one, y_own,
+    mixed, down_near, normed_two, turned, gain_rows, pos_row, pos_col, seg_row, seg_col, bias, gains,
+    weight_all, other_all, out_all, own_x, own_g, own_in, own_pick, own_out, x_all, in_all, hn_all, proj_all, mask, prefix,
+    gated_all, attended_all, query_all, key_all, value_all, out_cols, scale_one, y_own, own_down,
+    mixed_all, h2_all, turned_all,
     send_sem, recv_sem, own_sem, load_sem, save_sem, *line_sems,
 ):
     rank = lax.axis_index("ctx")
@@ -723,7 +721,12 @@
     tail_at = 4 * width
     loads = [
         pltpu.make_async_copy(a, b, load_sem.at[n])
-        for n, (a, b) in enumerate(((weight, weight_all), (other, other_all), (weight_out, out_all)))
+        for n, (a, b) in enumerate(
+            (
+                (weight, weight_all), (other, other_all), (weight_out, out_all), (tokens, own_x), (cotangent, own_g),
+                (rows_of(down, rank, own_down.shape[0]), own_down),
+            )
+        )
     ]
     saves = [
         pltpu.make_async_copy(a, b, save_sem.at[n])
@@ -731,22 +734,24 @@
             (
                 (x_all, inputs), (in_all, w_in), (hn_all, normed), (proj_all, project), (query_all, wide_query),
                 (key_all, wide_key), (value_all, wide_value), (attended_all, attended), (gated_all, gated),
+                (mixed_all, mixed), (h2_all, normed_two), (turned_all, turned),
             )
         )
     ]
     for copy in loads:
         copy.start()
-    per = len(line_sems) // 3
+    per = len(line_sems) // 4
     in_line = Line(shards, own_in, in_all, line_sems[:per])
     out_line = Line(shards, own_out, out_cols, line_sems[per : 2 * per])
-    up_line = Line(shards, own_pick, w_gate_up, line_sems[2 * per :])
+    up_line = Line(shards, own_pick, w_gate_up, line_sems[2 * per : 3 * per])
+    down_line = Line(shards, own_down, down_near, line_sems[3 * per :])
     greet([{"ctx": rank ^ 1}, {"ctx": rank ^ 2}], in_line)
 
     def sems(n):
         return send_sem.at[n], recv_sem.at[n], own_sem.at[n]
 
-    first = relay_ops("gather_rows", rank, tokens, x_all, sems(0))
-    second = relay_ops("gather_rows", rank, cotangent, grad_low, sems(1))
+    first = relay_ops("gather_rows", rank, own_x, x_all, sems(0))
+    second = relay_ops("gather_rows", rank, own_g, grad_low, sems(1))
 
     def cols(start, size):
         return pl.ds(pl.multiple_of(start, LANES), size)
@@ -754,16 +759,17 @@
     loads[0].wait()
     for i in range(4):
         own_in[:, i * width : (i + 1) * width] = weight_all[:, cols(i * model + rank * width, width)]
-    total_heads = forget_weight.shape[1]
+    total_heads = forget_weight.shape[0]
     from_head = lax.broadcasted_iota(jnp.int32, (total_heads, LANES), 0)
     to_lane = lax.broadcasted_iota(jnp.int32, (total_heads, LANES), 1)
     chosen = jnp.where((to_lane < heads) & (from_head == rank * heads + to_lane), 1.0, 0.0).astype(BF16)
     from_gain = lax.broadcasted_iota(jnp.int32, (2, LANES), 0)
     to_lane = lax.broadcasted_iota(jnp.int32, (2, LANES), 1)
     chosen_gain = jnp.where(to_lane == heads + from_gain, 1.0, 0.0).astype(BF16)
-    tail = dot(forget_weight[...], chosen) + left_product(norm_gains[...], chosen_gain)
+    tail = left_product(forget_weight[...], chosen) + left_product(norm_gains[...], chosen_gain)
     own_in[:, tail_at : tail_at + LANES] = tail.astype(BF16)
     in_line.start()
+    loads[3].wait()
     first.start()
     loads[1].wait()
     for i in range(own_pick.shape[1] // piece):
@@ -802,6 +808,7 @@
     proj_all[...] = jnp.zeros_like(proj_all)
     gain_rows[...] = jnp.zeros_like(gain_rows)
     first.forward()
+    loads[4].wait()
     second.start()
     in_line.step(1)
     first.finish()
@@ -823,7 +830,7 @@
         @turns(rows, chunk)
         def _(part):
             values = x_all[part, here].astype(F32) * scale_one[part, 0:1] * gain_rows[0:1, here]
-            hn_all[part, here] = values.astype(BF16)
+            hn_all[here, part] = values.T.astype(BF16)
             proj_all[part, :] += dot(values.astype(BF16), in_all[here, :])
 
     def consume_at(distance):
@@ -845,11 +852,11 @@
         in_line.step(distance)
         if distance == in_line.layers - 1:
             out_line.start()
+            up_line.start()
         consume_at(distance)
 
     for n in (1, 2, 3):
         saves[n].start()
-    up_line.start()
     out_line.step(1)
     fill_prefix(chunk, heads, pos_row, pos_col, proj_all[:, tail_at : tail_at + LANES] + bias[0:1, :], prefix)
 
@@ -905,7 +912,7 @@
     save_out = pltpu.make_async_copy(out_cols, w_out, save_sem.at[len(saves)])
     save_out.start()
 
-    third = relay_ops("gather_cols", rank, y_own, mixed, sems(2 + steps))
+    third = relay_ops("gather_cols", rank, y_own, mixed_all, sems(2 + steps))
 
     @turns(rows, chunk)
     def _(part):
@@ -917,9 +924,24 @@
     third.start()
     third.forward()
     up_line.step(2)
-    up_line.step(3)
+    loads[5].wait()
+    down_line.start()
     third.finish()
+    saves[9].start()
+
+    @turns(rows, chunk)
+    def _(part):
+        values = mixed_all[part, :].astype(F32)
+        low = values * rms_scale(values) * gain_rows[1:2, :]
+        h2_all[part, :] = low.astype(BF16)
+        turned_all[:, part] = low.T.astype(BF16)
+
+    saves[10].start()
+    saves[11].start()
+    for distance in range(3, up_line.layers):
+        up_line.step(distance)
     up_line.finish()
+    down_line.near_finish()
     out_line.sent()
     in_line.sent()
     second.finish()
@@ -932,7 +954,7 @@
 
 def front(
     collective_id, ranks, shards, head, heads, width, piece,
-    tokens, cotangent, weight, weight_out, other, forget_weight, norm_gains, qk_gains, segments, order, forget_bias,
+    tokens, cotangent, weight, weight_out, other, down, forget_weight, norm_gains, qk_gains, segments, order, forget_bias,
 ):
     own_rows, model = tokens.shape
     rows = ranks * own_rows
@@ -944,20 +966,23 @@
     shape, vmem = jax.ShapeDtypeStruct, pltpu.VMEM
     return pl.pallas_call(
         functools.partial(front_kernel, shards, head, heads, width, piece, chunk),
-        in_specs=[ANY] * 5 + [VMEM_WHOLE] * 4 + [pl.BlockSpec(memory_space=pltpu.SMEM)] * 2,
-        out_specs=[ANY] * 13 + [VMEM_WHOLE] * 7,
+        in_specs=[ANY] * 6 + [VMEM_WHOLE] * 4 + [pl.BlockSpec(memory_space=pltpu.SMEM)] * 2,
+        out_specs=[ANY] * 16 + [VMEM_WHOLE] * 7,
         out_shape=[
             shape((rows, model), BF16),
             shape((rows, model), BF16),
             shape((model, wide_in), BF16),
             shape((model, width), BF16),
             shape((model, other_cols), BF16),
-            shape((rows, model), BF16),
+            shape((model, rows), BF16),
             shape((rows, wide_in), F32),
             shape((ranks * steps, rows, LANES), BF16),
             shape((steps, rows, LANES), F32),
             shape(wide, BF16), shape(wide, BF16), shape(wide, BF16),
             shape((rows, model), BF16),
+            shape((shards * (down.shape[0] // ranks), model), BF16),
+            shape((rows, model), BF16),
+            shape((model, rows), BF16),
             shape((8, model), F32),
             shape((1, rows), F32), shape((rows, 1), F32), shape((1, rows), F32), shape((rows, 1), F32),
             shape((1, LANES), F32),
@@ -967,12 +992,14 @@
             vmem(weight.shape, BF16),
             vmem(other.shape, BF16),
             vmem(weight_out.shape, BF16),
+            vmem(tokens.shape, BF16),
+            vmem(cotangent.shape, BF16),
             vmem((shard_rows, wide_in), BF16),
             vmem((shard_rows, other_cols), BF16),
             vmem((shard_rows, width), BF16),
             vmem((rows, model), BF16),
             vmem((model, wide_in), BF16),
-            vmem((rows, model), BF16),
+            vmem((model, rows), BF16),
             vmem((rows, wide_in), F32),
             vmem((rows, rows), F32),
             vmem((rows, LANES), F32),
@@ -982,94 +1009,104 @@
             vmem((model, width), BF16),
             vmem((rows, LANES), F32),
             vmem((rows, width), BF16),
+            vmem((down.shape[0] // ranks, model), BF16),
+            vmem((rows, model), BF16),
+            vmem((rows, model), BF16),
+            vmem((model, rows), BF16),
             pltpu.SemaphoreType.DMA((3 + steps, 6)),
             pltpu.SemaphoreType.DMA((3 + steps, 6)),
             pltpu.SemaphoreType.DMA((3 + steps, 2)),
             pltpu.SemaphoreType.DMA((FRONT_LOADS,)),
             pltpu.SemaphoreType.DMA((FRONT_SAVES + 1,)),
         ]
-        + 3 * line_scratch(shards),
+        + 4 * line_scratch(shards),
         compiler_params=pltpu.CompilerParams(
             collective_id=collective_id, has_side_effects=True, vmem_limit_bytes=VMEM_LIMIT
         ),
         cost_estimate=pl.CostEstimate(flops=0, bytes_accessed=300 << 20, transcendentals=0),
         name="front",
     )(
-        tokens, cotangent, weight, weight_out, other, forget_weight, norm_gains, qk_gains, segments, order, forget_bias
+        tokens, cotangent, weight, weight_out, other, down, forget_weight, norm_gains, qk_gains, segments, order, forget_bias
     )
+
+
+def fold_tiles(rows, cols, share_rows):
+    extra = rows * cols // share_rows
+    high, wide = math.gcd(rows, share_rows), math.gcd(cols, extra)
+    tiles = []
+    for row in range(rows // high):
+        for col in range(cols // wide):
+            k = row * (cols // wide) + col
+            tiles.append((row * high, col * wide, k // (extra // wide) * high, k % (extra // wide) * wide))
+    return tiles, high, wide, extra
 
 
 def ffn_kernel(
     shards, chunk,
-    mixed, w_gate_up, cotangent, down_weight, gain,
-    w_down, normed, hidden, grad_gate_up, grad_down, grad_weight,
-    mixed_in, weight_in, cotangent_in, own_in, gates, ups, hn, turned, acts, grads, down_out, weight_out,
-    load_sem, save_sem, *line_sems,
+    normed, turned_from, w_gate_up, cotangent, down_near,
+    w_down, hidden, grad_gate_up, grad_weight,
+    weight_in, cotangent_in, gates, ups, hn, turned, acts, grads, weight_out,
+    load_sem, save_sem, tile_sem, near_sem, *line_sems,
 ):
     size = gates.shape[1]
-    rows, model = mixed.shape
-    tile = 2 * own_in.shape[0]
-    rank = lax.axis_index("ctx")
+    rows, model = normed.shape
+    tile = 2 * w_down.shape[0] // shards
     loads = [
         pltpu.make_async_copy(a, b, load_sem.at[n])
         for n, (a, b) in enumerate(
-            (
-                (rows_of(down_weight, rank, own_in.shape[0]), own_in), (mixed, mixed_in), (w_gate_up, weight_in),
-                (cotangent, cotangent_in),
-            )
+            ((normed, hn), (w_gate_up, weight_in), (cotangent, cotangent_in), (turned_from, turned))
         )
     ]
     saves = [
         pltpu.make_async_copy(a, b, save_sem.at[n])
         for n, (a, b) in enumerate(
-            ((hn, normed), (acts, hidden), (down_out, grad_down), (grads, grad_gate_up), (weight_out, grad_weight))
+            ((acts, hidden), (weight_out.at[:, pl.ds(2 * size, size)], grad_weight.at[:, pl.ds(2 * size, size)]))
         )
     ]
+    line = Line(shards, None, w_down, line_sems)
+    line.near_start(down_near, near_sem)
     for copy in loads:
         copy.start()
-    line = Line(shards, own_in, w_down, line_sems)
     greet([], line)
+    line.resume(down_near, near_sem)
     loads[0].wait()
-    line.start()
     loads[1].wait()
 
-    @turns(rows, chunk)
-    def _(part):
-        values = mixed_in[part, :].astype(F32)
-        low = values * rms_scale(values) * gain[1:2, :]
-        hn[part, :] = low.astype(BF16)
-        turned[:, part] = low.T.astype(BF16)
-
+    def span(turn, start=0):
+        return pl.ds(pl.multiple_of(start + turn * tile, LANES), tile)
+
+    def activate(turn):
+        gate = dot(hn[...], weight_in[:, span(turn)])
+        up = dot(hn[...], weight_in[:, span(turn, size)])
+        gates[:, span(turn)] = gate
+        ups[:, span(turn)] = up
+        acts[:, span(turn)] = (jax.nn.silu(gate) * up).astype(BF16)
+
+    tiles, high, wide, _ = fold_tiles(tile // 2, model, model // shards)
+
+    def down_grad(turn):
+        product = left_product(acts[:, span(turn)], cotangent_in[...]).astype(BF16)
+        for half in range(2):
+            base = (2 * turn + half) * (model // shards)
+            for row, col, new_row, new_col in tiles:
+                row = row + half * (tile // 2)
+                weight_out[
+                    pl.ds(pl.multiple_of(base + new_row, high), high), 2 * size + new_col : 2 * size + new_col + wide
+                ] = product[row : row + high, col : col + wide]
+
+    count = size // tile
+    pl.loop(0, count)(activate)
     saves[0].start()
     loads[2].wait()
-
-    def span(turn, start=0):
-        return pl.ds(pl.multiple_of(start + turn * tile, LANES), tile)
-
-    @pl.loop(0, size // tile)
-    def _(turn):
-        @turns(rows, chunk)
-        def _(part):
-            gate = dot(hn[part, :], weight_in[:, span(turn)])
-            up = dot(hn[part, :], weight_in[:, span(turn, size)])
-            gates[part, span(turn)] = gate
-            ups[part, span(turn)] = up
-            acts[part, span(turn)] = (jax.nn.silu(gate) * up).astype(BF16)
-
-    saves[1].start()
-    line.step(1)
     loads[3].wait()
+    line.near_load(down_near, near_sem, 0).wait()
 
     def consume(turn):
-        line.from_side(turn)
-
-        @turns(rows, chunk)
-        def _(part):
-            grad = right_product(cotangent_in[part, :], w_down[span(turn), :])
-            gate, up = gates[part, span(turn)], ups[part, span(turn)]
-            sig = jax.nn.sigmoid(gate)
-            grads[part, span(turn)] = (grad * up * sig * (1.0 + gate * (1.0 - sig))).astype(BF16)
-            grads[part, span(turn, size)] = (grad * gate * sig).astype(BF16)
+        grad = right_product(cotangent_in[...], w_down[span(turn), :])
+        gate, up = gates[:, span(turn)], ups[:, span(turn)]
+        sig = jax.nn.sigmoid(gate)
+        grads[:, span(turn)] = (grad * up * sig * (1.0 + gate * (1.0 - sig))).astype(BF16)
+        grads[:, span(turn, size)] = (grad * gate * sig).astype(BF16)
 
         for start in (0, size):
             here = span(turn, start)
@@ -1078,69 +1115,75 @@
             def _(part):
                 weight_out[part, here] = dot(turned[part, :], grads[:, here]).astype(BF16)
 
+        for copy in tile_saves(turn):
+            copy.start()
+
+    def tile_saves(turn):
+        for n, start in enumerate((0, size)):
+            here = span(turn, start)
+            yield pltpu.make_async_copy(grads.at[:, here], grad_gate_up.at[:, here], tile_sem.at[turn, 2 * n])
+            yield pltpu.make_async_copy(weight_out.at[:, here], grad_weight.at[:, here], tile_sem.at[turn, 2 * n + 1])
+
     def consume_at(distance):
         lower, upper = line.layer - distance, line.layer + distance
 
         @pl.when(lower >= 0)
         def _():
+            line.from_side(lower)
             consume(lower)
 
         @pl.when(upper < line.layers)
         def _():
+            line.from_side(upper)
             consume(upper)
 
-    line.keep.wait()
+    line.step(2)
     consume(line.layer)
     consume_at(1)
-    line.step(2)
-
-    @pl.loop(0, size // tile)
-    def _(turn):
-        down_out[span(turn), :] = left_product(acts[:, span(turn)], cotangent_in[...]).astype(BF16)
-
-    saves[2].start()
-    consume_at(2)
+    pl.loop(0, count)(down_grad)
+    saves[1].start()
     for distance in range(3, line.layers):
         line.step(distance)
+    for distance in range(2, line.layers):
         consume_at(distance)
-    saves[3].start()
-    saves[4].start()
-    line.sent()
+    line.resumed_sent()
     for copy in saves:
         copy.wait()
 
-
-def ffn(collective_id, ranks, shards, mixed, w_gate_up, cotangent, down_weight, gain):
-    rows, model = mixed.shape
+    @pl.loop(0, count)
+    def _(turn):
+        for copy in tile_saves(turn):
+            copy.wait()
+
+
+def ffn(collective_id, shards, normed, turned, w_gate_up, cotangent, down_near):
+    rows, model = normed.shape
     size = w_gate_up.shape[1] // 2
     shape, vmem = jax.ShapeDtypeStruct, pltpu.VMEM
     return pl.pallas_call(
         functools.partial(ffn_kernel, shards, pick_chunk(rows)),
-        in_specs=[ANY] * 4 + [VMEM_WHOLE],
-        out_specs=[VMEM_WHOLE] + [ANY] * 5,
+        in_specs=[ANY] * 5,
+        out_specs=[VMEM_WHOLE] + [ANY] * 3,
         out_shape=[
             shape((size, model), BF16),
-            shape((rows, model), BF16),
             shape((rows, size), BF16),
             shape((rows, 2 * size), BF16),
-            shape((size, model), BF16),
-            shape((model, 2 * size), BF16),
+            shape((model, 3 * size), BF16),
         ],
         scratch_shapes=[
-            vmem((rows, model), BF16),
             vmem(w_gate_up.shape, BF16),
             vmem((rows, model), BF16),
-            vmem((down_weight.shape[0] // ranks, model), BF16),
             vmem((rows, size), F32),
             vmem((rows, size), F32),
             vmem((rows, model), BF16),
             vmem((model, rows), BF16),
             vmem((rows, size), BF16),
             vmem((rows, 2 * size), BF16),
-            vmem((size, model), BF16),
-            vmem((model, 2 * size), BF16),
+            vmem((model, 3 * size), BF16),
             pltpu.SemaphoreType.DMA((4,)),
-            pltpu.SemaphoreType.DMA((5,)),
+            pltpu.SemaphoreType.DMA((2,)),
+            pltpu.SemaphoreType.DMA((shards // 2, 4)),
+            pltpu.SemaphoreType.DMA((3,)),
         ]
         + line_scratch(shards),
         compiler_params=pltpu.CompilerParams(
@@ -1148,7 +1191,46 @@
         ),
         cost_estimate=pl.CostEstimate(flops=0, bytes_accessed=100 << 20, transcendentals=0),
         name="ffn",
-    )(mixed, w_gate_up, cotangent, down_weight, gain)
+    )(normed, turned, w_gate_up, cotangent, down_near)
+
+
+class Fold:
+    def __init__(self, rank, piece, first, between, second, send_sem, recv_sem):
+        self.rank, self.piece, self.first, self.between, self.second = rank, piece, first, between, second
+        self.send_sem, self.recv_sem = send_sem, recv_sem
+
+    def copy(self, number):
+        me = self.rank
+        source, target, distance = (
+            lambda: (self.piece(me ^ 1, 0), self.first(0, 0), 1),
+            lambda: (self.piece(me ^ 3, 0), self.first(1, 0), 1),
+            lambda: (self.piece(me ^ 2, 1), self.first(0, 1), 2),
+            lambda: (self.piece(me ^ 3, 1), self.first(1, 1), 2),
+            lambda: (self.between(0), self.second(0), 2),
+            lambda: (self.between(1), self.second(1), 1),
+        )[number]()
+        return to_rank(source, target, self.send_sem.at[number], self.recv_sem.at[number], me ^ distance)
+
+    def start(self):
+        for number in range(4):
+            self.copy(number).start()
+
+    def pass_on(self):
+        for h, distance in ((0, 2), (1, 1)):
+            self.copy(2 * h).wait_recv()
+            self.copy(2 * h + 1).wait_recv()
+            own = self.piece(self.rank ^ distance, h)[...].astype(F32)
+            self.between(h)[...] = (own + self.first(1, h)[...].astype(F32)).astype(BF16)
+            self.copy(4 + h).start()
+
+    def total(self, h):
+        self.copy(4 + h).wait_recv()
+        own = self.piece(self.rank, h)[...].astype(F32)
+        return own + self.first(0, h)[...].astype(F32) + self.second(h)[...].astype(F32)
+
+    def sent(self):
+        for number in range(6):
+            self.copy(number).wait_send()
 
 
 def middle_kernel(
@@ -1156,7 +1238,7 @@
     grad_gate_up, w_gate_up, mixed, cotangent, w_out, hidden, w_down, gated, gain,
     mixed_grad, gated_grad, gain_grad, down_part, out_grad,
     grad_in, weight_in, mixed_in, cotangent_in, out_in, hidden_in, down_in, gated_in, low_grad, down_all, out_all,
-    wide, first_out, first_in, second_out, second_in,
+    wide, first_out, first_in, first_between, first_end, second_out, second_in, second_between, second_end,
     load_sem, save_sem, first_send, first_recv, second_send, second_recv,
 ):
     rank = lax.axis_index("ctx")
@@ -1180,49 +1262,46 @@
         copy.start()
     greet([{"ctx": rank ^ distance} for distance in range(1, ranks)])
     gain_grad[...] = jnp.zeros_like(gain_grad)
-    for copy in loads[:5]:
+    for copy in loads[:2]:
         copy.wait()
 
     def part(turn):
         return pl.ds(pl.multiple_of(turn * rows, 16), rows)
 
-    def send(out, into, send_sem, recv_sem, turn, distance):
-        other = rank ^ distance
-        return to_rank(
-            out.at[other, part(turn), :], into.at[distance, part(turn), :],
-            send_sem.at[distance - 1, turn], recv_sem.at[distance - 1, turn], other,
-        )
-
-    def arrived(out, into, send_sem, recv_sem, turn):
-        total = out[rank, part(turn), :].astype(F32)
-        for distance in range(1, ranks):
-            send(out, into, send_sem, recv_sem, turn, distance).wait_recv()
-            total = total + into[distance, part(turn), :].astype(F32)
-        return total
-
-    first = (first_out, first_in, first_send, first_recv)
-    second = (second_out, second_in, second_send, second_recv)
-
-    def project(turn):
-        here = part(turn)
-        total = cotangent_in[here, pl.ds(pl.multiple_of(rank * width, LANES), width)].astype(F32)
-        total = total + arrived(*first, turn)
-        mixed_grad[here, :] = total
-        low = total.astype(BF16)
-        low_grad[here, :] = low
-        for index in range(ranks):
-            second_out[index, here, :] = right_product(low, out_in[index * width : (index + 1) * width, :]).astype(BF16)
-        for distance in range(1, ranks):
-            send(*second, turn, distance).start()
-
-    @pl.loop(0, ranks)
-    def _(turn):
+    half = rows // 2
+
+    def fold(out, into, between, end, send_sem, recv_sem):
+        def make(turn):
+            def at(h):
+                return pl.ds(pl.multiple_of(turn * rows + h * half, 16), half)
+
+            return Fold(
+                rank,
+                lambda index, h: out.at[index, at(h), :],
+                lambda slot, h: into.at[slot, at(h), :],
+                lambda h: between.at[at(h), :],
+                lambda h: end.at[at(h), :],
+                send_sem.at[turn],
+                recv_sem.at[turn],
+            )
+
+        return make
+
+    first = fold(first_out, first_in, first_between, first_end, first_send, first_recv)
+    second = fold(second_out, second_in, second_between, second_end, second_send, second_recv)
+
+    def compute(turn):
         here = part(turn)
 
         @pl.loop(0, model // tile)
         def _(step):
             cols = pl.ds(pl.multiple_of(step * tile, tile), tile)
             wide[:, cols] = right_product(grad_in[here, :], weight_in[cols, :])
+
+        @pl.when(turn == 0)
+        def _():
+            for copy in loads[2:5]:
+                copy.wait()
 
         values = mixed_in[here, :].astype(F32)
         scale = rms_scale(values)
@@ -1231,41 +1310,67 @@
         back = norm_back(grad, values, scale, gain[0:1, :]).astype(BF16)
         for index in range(ranks):
             first_out[index, here, :] = back[:, index * width : (index + 1) * width]
-        for distance in range(1, ranks):
-            send(*first, turn, distance).start()
-
-        @pl.when(turn > 0)
-        def _():
-            project(turn - 1)
-
-    for copy in loads[5:]:
-        copy.wait()
-
-    @pl.loop(0, model // tile)
-    def _(step):
-        cols = pl.ds(pl.multiple_of(step * tile, tile), tile)
-        down_all[:, cols] = dot(hidden_in[...], down_in[:, cols]).astype(BF16)
-
-    saves[0].start()
-    project(ranks - 1)
-
-    @pl.loop(0, gated_in.shape[0])
-    def _(block):
-        out_all[pl.ds(pl.multiple_of(block * LANES, LANES), LANES), :] = left_product(
-            gated_in[block], low_grad[...]
-        ).astype(BF16)
-
-    saves[1].start()
+        first(turn).start()
+
+    def project(turn):
+        here = part(turn)
+        for h in range(2):
+            at = pl.ds(pl.multiple_of(turn * rows + h * half, 16), half)
+            total = cotangent_in[at, pl.ds(pl.multiple_of(rank * width, LANES), width)].astype(F32)
+            total = total + first(turn).total(h)
+            mixed_grad[at, :] = total
+            low_grad[at, :] = total.astype(BF16)
+        for index in range(ranks):
+            second_out[index, here, :] = right_product(
+                low_grad[here, :], out_in[index * width : (index + 1) * width, :]
+            ).astype(BF16)
+        second(turn).start()
+
+    def collect(turn):
+        for h in range(2):
+            at = pl.ds(pl.multiple_of(turn * rows + h * half, 16), half)
+            gated_grad[at, :] = second(turn).total(h)
+
+    def aside(turn):
+        @pl.when(turn == ranks)
+        def _():
+            for copy in loads[5:]:
+                copy.wait()
+
+            @pl.loop(0, model // tile)
+            def _(step):
+                cols = pl.ds(pl.multiple_of(step * tile, tile), tile)
+                down_all[:, cols] = dot(hidden_in[...], down_in[:, cols]).astype(BF16)
+
+            saves[0].start()
+
+        @pl.when(turn == ranks + 2)
+        def _():
+            @pl.loop(0, gated_in.shape[0])
+            def _(block):
+                out_all[pl.ds(pl.multiple_of(block * LANES, LANES), LANES), :] = left_product(
+                    gated_in[block], low_grad[...]
+                ).astype(BF16)
+
+            saves[1].start()
+
+    @pl.loop(0, ranks + 4)
+    def _(turn):
+        stages = (
+            compute, lambda t: first(t).pass_on(), project, lambda t: second(t).pass_on(), collect,
+        )
+        for lag, stage in enumerate(stages):
+            if lag == 4:
+                aside(turn)
+
+            @pl.when((turn >= lag) & (turn < ranks + lag))
+            def _():
+                stage(turn - lag)
 
     @pl.loop(0, ranks)
     def _(turn):
-        gated_grad[part(turn), :] = arrived(*second, turn)
-
-    @pl.loop(0, ranks)
-    def _(turn):
-        for distance in range(1, ranks):
-            send(*first, turn, distance).wait_send()
-            send(*second, turn, distance).wait_send()
+        first(turn).sent()
+        second(turn).sent()
 
     for copy in saves:
         copy.wait()
@@ -1274,8 +1379,9 @@
 def middle(collective_id, ranks, grad_gate_up, w_gate_up, mixed, cotangent, w_out, hidden, w_down, gated, gain):
     rows, model = mixed.shape
     width = w_out.shape[1]
-    blocks = pltpu.VMEM((ranks, rows, width), BF16)
-    sems = pltpu.SemaphoreType.DMA((ranks - 1, ranks))
+    flat = pltpu.VMEM((rows, width), BF16)
+    blocks = [pltpu.VMEM((ranks, rows, width), BF16), pltpu.VMEM((2, rows, width), BF16), flat, flat]
+    sems = pltpu.SemaphoreType.DMA((ranks, 6))
     return pl.pallas_call(
         functools.partial(middle_kernel, ranks),
         in_specs=[ANY] * 8 + [VMEM_WHOLE],
@@ -1300,7 +1406,7 @@
             pltpu.VMEM((rows, model), BF16),
             pltpu.VMEM((model, width), BF16),
             pltpu.VMEM((rows // ranks, model), F32),
-            blocks, blocks, blocks, blocks,
+            *blocks, *blocks,
             pltpu.SemaphoreType.DMA((8,)),
             pltpu.SemaphoreType.DMA((2,)),
             sems, sems, sems, sems,
@@ -1314,10 +1420,10 @@
 
 
 def last_kernel(
-    ranks,
-    grad_project, w_in, inputs, aside, other, mixed_grad, gain, gain_two_grad, small,
-    tokens_grad, total_sums, aside_all, other_all,
-    grad_in, weight_in, inputs_in, wide, out, into, sums_out, sums_in,
+    ranks, shards,
+    grad_project, w_in, inputs, aside, pieces, mixed, mixed_grad, gain, gain_two_grad, small, segments,
+    tokens_grad, block_out, total_sums, parts, aside_all,
+    grad_in, weight_in, inputs_in, aside_in, pieces_in, mixed_in, wide, out, into, between, end, sums_out, sums_in,
     load_sem, send_sem, recv_sem, sums_send, sums_recv, aside_send, aside_recv, aside_own,
 ):
     rank = lax.axis_index("ctx")
@@ -1326,28 +1432,42 @@
     tile = 256
     loads = [
         pltpu.make_async_copy(a, b, load_sem.at[n])
-        for n, (a, b) in enumerate(((w_in, weight_in), (grad_project, grad_in), (inputs, inputs_in)))
+        for n, (a, b) in enumerate(
+            (
+                (aside, aside_in), (w_in, weight_in), (grad_project, grad_in), (inputs, inputs_in),
+                (pieces, pieces_in), (rows_of(mixed, rank, rows), mixed_in),
+            )
+        )
     ]
     for copy in loads:
         copy.start()
     greet([{"ctx": rank ^ distance} for distance in range(1, ranks)])
-    relays = [
-        relay_ops("stack", rank, a, b, (aside_send.at[n], aside_recv.at[n], aside_own.at[n]))
-        for n, (a, b) in enumerate(((aside, aside_all), (other, other_all)))
-    ]
-    relays[0].start()
+    relay = relay_ops("stack", rank, aside_in, aside_all, (aside_send, aside_recv, aside_own))
+    loads[0].wait()
+    relay.start()
     sums_out[...] = jnp.zeros_like(sums_out)
     sums_out[1:2, :] = gain_two_grad[0:1, :]
     sums_out[2:3, 0:LANES] = small[0:1, :]
     sums_out[2:3, LANES : 2 * LANES] = small[1:2, :]
     for index in range(ranks):
         sums_out[3 + index : 4 + index, 0:LANES] = jnp.where(rank == index, small[2:3, :], 0.0)
-    for copy in loads:
+    for copy in loads[1:4]:
         copy.wait()
 
-    def send(distance):
-        other = rank ^ distance
-        return to_rank(out.at[other], into.at[distance], send_sem.at[distance - 1], recv_sem.at[distance - 1], other)
+    half = rows // 2
+
+    def at(h):
+        return pl.ds(h * half, half)
+
+    fold = Fold(
+        rank,
+        lambda index, h: out.at[index, at(h), :],
+        lambda slot, h: into.at[slot, at(h), :],
+        lambda h: between.at[at(h), :],
+        lambda h: end.at[at(h), :],
+        send_sem,
+        recv_sem,
+    )
 
     def send_sums(distance):
         return to_rank(
@@ -1372,75 +1492,160 @@
         out[other] = wide[...].astype(BF16)
 
     @pl.loop(1, ranks)
-    def _(distance):
-        compute(rank ^ distance)
-        send(distance).start()
-
-        @pl.when(distance == 1)
-        def _():
-            relays[0].forward()
-
-        @pl.when(distance == 2)
-        def _():
-            relays[1].start()
-
+    def _(turn):
+        compute(rank ^ (ranks - turn))
+
+        @pl.when(turn == 2)
+        def _():
+            for number in (2, 3):
+                fold.copy(number).start()
+
+        @pl.when(turn == 3)
+        def _():
+            for number in (0, 1):
+                fold.copy(number).start()
+
+    for copy in loads[4:]:
+        copy.wait()
+    own = pl.ds(pl.multiple_of(rank * rows, 16), rows)
+    result = mixed_in[...].astype(F32)
+    for index in range(ranks):
+        result = result + pieces_in[index].astype(F32)
+    block_out[...] = result.astype(BF16)
+    branch = result - inputs_in[own, :].astype(F32)
+    valid = jnp.where(segments[own, :] >= 0.0, 1.0, 0.0)
+    lane = lax.broadcasted_iota(jnp.int32, (1, LANES), 1)
+    stats = jnp.zeros((1, LANES), F32)
+    for index, values in enumerate((result, branch)):
+        total = jnp.sum(valid * jnp.sum(values * values, axis=-1, keepdims=True), axis=0, keepdims=True)
+        stats = jnp.where(lane == index, total, stats)
+    sums_out[7:8, 0:LANES] = stats
     compute(rank)
     for distance in range(1, ranks):
         send_sums(distance).start()
-    total = out[rank].astype(F32)
-    for distance in range(1, ranks):
-        send(distance).wait_recv()
-        total = total + into[distance].astype(F32)
-    tokens_grad[...] = total.astype(BF16)
-    relays[1].forward()
+    relay.forward()
+    fold.pass_on()
+    for h in range(2):
+        tokens_grad[at(h), :] = fold.total(h).astype(BF16)
     total = sums_out[...]
     for distance in range(1, ranks):
         send_sums(distance).wait_recv()
         total = total + sums_in[distance]
     total_sums[...] = total
+    share = model // shards
+    parts[...] = jnp.zeros_like(parts)
+    for index in range(shards):
+        parts[index, 0:2, 0:share] = total[0:2, index * share : (index + 1) * share]
+        parts[index, 2:8, :] = total[2:8, 0 : parts.shape[2]]
+    fold.sent()
     for distance in range(1, ranks):
-        send(distance).wait_send()
         send_sums(distance).wait_send()
-    for relay in relays:
-        relay.finish()
+    relay.finish()
 
 
 def last_moves(
-    collective_id, ranks, grad_project, w_in, inputs, aside, other, mixed_grad, gain, gain_two_grad, small
+    collective_id, ranks, shards,
+    grad_project, w_in, inputs, aside, pieces, mixed, mixed_grad, gain, gain_two_grad, small, segments,
 ):
     rows, model = inputs.shape
-    blocks = pltpu.VMEM((ranks, rows // ranks, model), BF16)
+    own = (rows // ranks, model)
+    flat = pltpu.VMEM(own, BF16)
+    blocks = [pltpu.VMEM((ranks,) + own, BF16), pltpu.VMEM((2,) + own, BF16), flat, flat]
     sems = pltpu.SemaphoreType.DMA((ranks - 1,))
     return pl.pallas_call(
-        functools.partial(last_kernel, ranks),
-        in_specs=[ANY] * 5 + [VMEM_WHOLE] * 4,
-        out_specs=[VMEM_WHOLE] * 2 + [ANY] * 2,
+        functools.partial(last_kernel, ranks, shards),
+        in_specs=[ANY] * 6 + [VMEM_WHOLE] * 5,
+        out_specs=[VMEM_WHOLE] * 4 + [ANY],
         out_shape=[
-            jax.ShapeDtypeStruct((rows // ranks, model), BF16),
+            jax.ShapeDtypeStruct(own, BF16),
+            jax.ShapeDtypeStruct(own, BF16),
             jax.ShapeDtypeStruct((8, model), F32),
+            jax.ShapeDtypeStruct((shards, 8, max(2 * LANES, -(-model // shards // LANES) * LANES)), F32),
             jax.ShapeDtypeStruct((ranks,) + aside.shape, BF16),
-            jax.ShapeDtypeStruct((ranks,) + other.shape, BF16),
         ],
         scratch_shapes=[
             pltpu.VMEM(grad_project.shape, BF16),
             pltpu.VMEM(w_in.shape, BF16),
             pltpu.VMEM(inputs.shape, BF16),
-            pltpu.VMEM((rows // ranks, model), F32),
-            blocks, blocks,
+            pltpu.VMEM(aside.shape, BF16),
+            pltpu.VMEM(pieces.shape, BF16),
+            pltpu.VMEM(own, BF16),
+            pltpu.VMEM(own, F32),
+            *blocks,
             pltpu.VMEM((8, model), F32),
             pltpu.VMEM((ranks, 8, model), F32),
-            pltpu.SemaphoreType.DMA((3,)),
-            sems, sems, sems, sems,
-            pltpu.SemaphoreType.DMA((2, 6)),
-            pltpu.SemaphoreType.DMA((2, 6)),
-            pltpu.SemaphoreType.DMA((2, 2)),
+            pltpu.SemaphoreType.DMA((6,)),
+            pltpu.SemaphoreType.DMA((6,)),
+            pltpu.SemaphoreType.DMA((6,)),
+            sems, sems,
+            pltpu.SemaphoreType.DMA((6,)),
+            pltpu.SemaphoreType.DMA((6,)),
+            pltpu.SemaphoreType.DMA((2,)),
         ],
         compiler_params=pltpu.CompilerParams(
             collective_id=collective_id, has_side_effects=True, vmem_limit_bytes=VMEM_LIMIT
         ),
         cost_estimate=pl.CostEstimate(flops=0, bytes_accessed=150 << 20, transcendentals=0),
         name="last_moves",
-    )(grad_project, w_in, inputs, aside, other, mixed_grad, gain, gain_two_grad, small)
+    )(grad_project, w_in, inputs, aside, pieces, mixed, mixed_grad, gain, gain_two_grad, small, segments)
+
+
+def finish_kernel(ranks, shards, late, parts, late_all, part_sum, late_in, into, load_sem, send_sem, recv_sem, own_sem,
+                  part_send, part_recv):
+    rank = lax.axis_index("ctx")
+    shard = lax.axis_index("fsdp")
+    load = pltpu.make_async_copy(late, late_in, load_sem.at[0])
+    load.start()
+    relay = relay_ops("stack", rank, late_in, late_all, (send_sem, recv_sem, own_sem))
+    greet([{"ctx": rank ^ 1}, {"ctx": rank ^ 2}] + [{"fsdp": shard ^ distance} for distance in range(1, shards)])
+    load.wait()
+    relay.start()
+
+    def send(distance):
+        other = shard ^ distance
+        return pltpu.make_async_remote_copy(
+            parts.at[other], into.at[distance], part_send.at[distance - 1], part_recv.at[distance - 1],
+            device_id={"fsdp": other}, device_id_type=MESH,
+        )
+
+    for distance in range(1, shards):
+        send(distance).start()
+    relay.forward()
+    total = parts[shard]
+    for distance in range(1, shards):
+        send(distance).wait_recv()
+        total = total + into[distance]
+    part_sum[...] = total
+    for distance in range(1, shards):
+        send(distance).wait_send()
+    relay.finish()
+
+
+def finish_moves(collective_id, ranks, shards, late, parts):
+    sems = pltpu.SemaphoreType.DMA((shards - 1,))
+    return pl.pallas_call(
+        functools.partial(finish_kernel, ranks, shards),
+        in_specs=[ANY, VMEM_WHOLE],
+        out_specs=[ANY, VMEM_WHOLE],
+        out_shape=[
+            jax.ShapeDtypeStruct((ranks,) + late.shape, BF16),
+            jax.ShapeDtypeStruct(parts.shape[1:], F32),
+        ],
+        scratch_shapes=[
+            pltpu.VMEM(late.shape, BF16),
+            pltpu.VMEM(parts.shape, F32),
+            pltpu.SemaphoreType.DMA((1,)),
+            pltpu.SemaphoreType.DMA((6,)),
+            pltpu.SemaphoreType.DMA((6,)),
+            pltpu.SemaphoreType.DMA((2,)),
+            sems, sems,
+        ],
+        compiler_params=pltpu.CompilerParams(
+            collective_id=collective_id, has_side_effects=True, vmem_limit_bytes=VMEM_LIMIT
+        ),
+        cost_estimate=pl.CostEstimate(flops=0, bytes_accessed=50 << 20, transcendentals=0),
+        name="finish_moves",
+    )(late, parts)
 
 
 def spread_kernel(pieces, *refs):
@@ -1482,6 +1687,103 @@
     )(source)
 
 
+def unfold_kernel(tiles, high, wide, source, target):
+    for row, col, new_row, new_col in tiles:
+        target[row : row + high, col : col + wide] = source[
+            0, new_row : new_row + high, new_col : new_col + wide
+        ].astype(F32)
+
+
+def unfold_rows(source, rows, cols, first):
+    ranks, share_rows, _ = source.shape
+    tiles, high, wide, extra = fold_tiles(rows, cols, share_rows)
+    return pl.pallas_call(
+        functools.partial(unfold_kernel, tiles, high, wide),
+        grid=(ranks,),
+        in_specs=[pl.BlockSpec((1, share_rows, extra), lambda step: (step, 0, first // extra))],
+        out_specs=pl.BlockSpec((rows, cols), lambda step: (step, 0)),
+        out_shape=jax.ShapeDtypeStruct((ranks * rows, cols), F32),
+        compiler_params=pltpu.CompilerParams(vmem_limit_bytes=VMEM_LIMIT),
+        cost_estimate=pl.CostEstimate(flops=0, bytes_accessed=ranks * rows * cols * 6, transcendentals=0),
+        name="unfold_rows",
+    )(source)
+
+
+def unpack_kernel(
+    width, heads, head, late, late_tail, sums, totals, segments, first_rows, second_rows,
+    in_out, out_out, first_out, second_out, forget_out, gains, bias, qk, rms,
+):
+    ranks = late.shape[0]
+    first = 4 * width
+    for block in range(4):
+        for index in range(ranks):
+            in_out[:, (block * ranks + index) * width : (block * ranks + index + 1) * width] = late[
+                index, :, block * width : (block + 1) * width
+            ].astype(F32)
+    first_out[...] = first_rows[...]
+    second_out[...] = second_rows[...]
+    lane = lax.broadcasted_iota(jnp.int32, (LANES, ranks * heads), 0)
+    place = lax.broadcasted_iota(jnp.int32, (LANES, ranks * heads), 1)
+    lane_t = lax.broadcasted_iota(jnp.int32, (ranks * heads, LANES), 1)
+    place_t = lax.broadcasted_iota(jnp.int32, (ranks * heads, LANES), 0)
+    forget = jnp.zeros(forget_out.shape, F32)
+    biases = jnp.zeros((8, ranks * heads), F32)
+    for index in range(ranks):
+        chosen = (lane < heads) & (place == index * heads + lane)
+        out_out[:, index * width : (index + 1) * width] = late[index, :, first : first + width].astype(F32)
+        chosen_t = (lane_t < heads) & (place_t == index * heads + lane_t)
+        forget = forget + right_product(jnp.where(chosen_t, 1.0, 0.0).astype(BF16), late_tail[index])
+        row = jnp.broadcast_to(sums[3 + index : 4 + index, 0:LANES], (8, LANES))
+        for part in split_three(row):
+            biases = biases + dot(part.astype(BF16), jnp.where(chosen, 1.0, 0.0).astype(BF16))
+    forget_out[...] = forget
+    gains[...] = sums[0:2, 0 : gains.shape[1]]
+    bias[...] = biases[0:1, :]
+    for row in range(2):
+        qk[row : row + 1, :] = sum(
+            sums[2:3, row * LANES + side * head : row * LANES + (side + 1) * head] for side in range(LANES // head)
+        )
+    count = jnp.sum(jnp.where(segments[...] >= 0, 1.0, 0.0), axis=-1, keepdims=True)
+    rms[...] = jnp.sqrt(totals[7:8, 0:2] / (count * totals.shape[1]))
+
+
+def unpack(late, sums, totals, segments, first_rows, second_rows, width, heads, head):
+    ranks, rows, cols = late.shape
+    part = rows // 4
+
+    def block(lanes):
+        return pl.BlockSpec((part, lanes), lambda step: (step, 0))
+
+    share = rows
+    shape = jax.ShapeDtypeStruct
+    return pl.pallas_call(
+        functools.partial(unpack_kernel, width, heads, head),
+        grid=(rows // part,),
+        in_specs=[
+            pl.BlockSpec((ranks, part, cols), lambda step: (0, step, 0)),
+            pl.BlockSpec((ranks, rows, LANES), lambda step: (0, 0, 5 * width // LANES)),
+        ]
+        + [whole(a.shape) for a in (sums, totals, segments)]
+        + [block(first_rows.shape[1])] * 2,
+        out_specs=[block(4 * ranks * width), block(ranks * width)] + [block(first_rows.shape[1])] * 2
+        + [whole(a) for a in ((ranks * heads, rows), (2, share), (1, ranks * heads), (2, head), (1, 2))],
+        out_shape=[
+            shape((rows, 4 * ranks * width), F32),
+            shape((rows, ranks * width), F32),
+            shape(first_rows.shape, BF16),
+            shape(second_rows.shape, BF16),
+            shape((ranks * heads, rows), F32),
+            shape((2, share), F32),
+            shape((1, ranks * heads), F32),
+            shape((2, head), F32),
+            shape((1, 2), F32),
+        ],
+        compiler_params=pltpu.CompilerParams(vmem_limit_bytes=VMEM_LIMIT),
+        cost_estimate=pl.CostEstimate(flops=0, bytes_accessed=ranks * rows * cols * 6, transcendentals=0),
+        name="unpack",
+    )(late, late, sums, totals, segments, first_rows, second_rows)
+
+
 class Native:
     def __init__(self, ranks):
         self.ranks = ranks
@@ -1503,33 +1805,6 @@
 
     def gather_cols(self, array, piece):
         return lax.all_gather(array, "ctx", axis=1, tiled=True), lax.all_gather(piece, "fsdp", axis=0, tiled=True)
-
-    def stack(self, number, *arrays):
-        return [lax.all_gather(a, "ctx", axis=0, tiled=False) for a in arrays]
-
-    def finish(self, number, array, pieces, stats):
-        return (
-            lax.all_gather(array, "ctx", axis=0, tiled=False),
-            lax.psum_scatter(pieces, "fsdp", scatter_dimension=0, tiled=False),
-            lax.psum(stats, "ctx"),
-        )
-
-
-class Direct:
-    def __init__(self, ranks, shards):
-        self.ranks, self.shards = ranks, shards
-
-    def run(self, number, *ops):
-        return exchange(number, self.ranks, 0, self.shards, *ops)
-
-    def stack(self, number, *arrays):
-        return self.run(number, *[("stack" if a.dtype == BF16 else "each", a) for a in arrays])
-
-    def finish(self, number, array, pieces, stats):
-        out = exchange(
-            number, self.ranks, self.shards, self.shards, ("stack", array), ("shards", pieces), ("each", stats)
-        )
-        return out[0], out[1].sum(axis=0), out[2].sum(axis=0)
 
 
 def body(
@@ -1550,7 +1825,7 @@
     hidden_piece = down_weight.shape[0] // ranks
     hidden = hidden_piece * shards
     plain = ranks == 4 and shards & (shards - 1) == 0 and width == padded
-    comm = Direct(ranks, shards) if plain else Native(ranks)
+    comm = Native(ranks)
 
     def slab(array, start, size, axis):
         return lax.dynamic_slice_in_dim(array, start, size, axis)
@@ -1561,15 +1836,16 @@
     if plain:
         (
             inputs, grad_low, w_in, w_out, w_gate_up, normed, project, gated_all, attended,
-            wide_query, wide_key, wide_value, mixed_low, gain_rows, *places_all, bias, head_gains,
+            wide_query, wide_key, wide_value, mixed_low, down_near, normed_two, turned, gain_rows, *places_all,
+            bias, head_gains,
         ) = front(
             0, ranks, shards, head_dim, local_heads, width, hidden_piece,
-            tokens[0], out_grad[0], attn_in_weight, out_weight, gate_up_weight, forget_weight, norm_gains, qk_gains,
-            segment_ids, block_order, forget_bias[None],
+            tokens[0], out_grad[0], attn_in_weight, out_weight, gate_up_weight, down_weight, forget_weight.T,
+            norm_gains, qk_gains, segment_ids, block_order, forget_bias[None],
         )
         gain_one, gain_two = gain_rows[0], gain_rows[1]
-        w_down, normed_two, hidden_act, grad_gate_up, down_part_grad, gate_up_grad = ffn(
-            1, ranks, shards, mixed_low, w_gate_up, grad_low, down_weight, gain_rows
+        w_down, hidden_act, grad_gate_up, early_grad = ffn(
+            1, shards, normed_two, turned, w_gate_up, grad_low, down_near
         )
     else:
         tail = jnp.concatenate(
@@ -1629,11 +1905,10 @@
     def reduce_shards(array):
         return lax.psum_scatter(array.astype(BF16), "fsdp", scatter_dimension=0, tiled=True)
 
-    grad_gate_up, down_part_grad, gate_up_grad = lax.optimization_barrier(
-        (grad_gate_up, down_part_grad, gate_up_grad)
-    )
-    down_share = reduce_shards(down_part_grad)
-    gate_up_share = reduce_shards(gate_up_grad)
+    if plain:
+        early_share = (reduce_shards(early_grad),)
+    else:
+        early_share = (reduce_shards(down_part_grad), reduce_shards(gate_up_grad))
     if plain:
         grad_mixed_cols, grad_gated, gain_two_grad, down_part, out_part = middle(
             3, ranks, grad_gate_up, w_gate_up, mixed_low, grad_low, w_out, hidden_act, w_down, gated_all, gain_two[None]
@@ -1651,7 +1926,6 @@
                 right_product(grad_branch, w_out).astype(BF16), "ctx", scatter_dimension=1, tiled=True
             ).astype(F32)
         )
-    grad_gated, down_share = lax.optimization_barrier((grad_gated, down_share))
     grad_project, small, *rest = attend_back(
         project, places_all, bias, head_gains, attended, (wide_query, wide_key, wide_value),
         grad_gated, (down_part, normed, out_part) if plain else (), ranks if plain else 0, head_dim, padded, local_heads,
@@ -1662,16 +1936,17 @@
         in_part = left_product(normed, grad_project).astype(BF16)
         out_part = left_product(gated_all, grad_branch).astype(BF16)
         late = jnp.concatenate([in_part[:, : 4 * padded], out_part, in_part[:, 4 * padded :]], axis=1)
-    late, gate_up_share = lax.optimization_barrier((late, gate_up_share))
+    late, early_share = lax.optimization_barrier((late, early_share))
     late_share = reduce_shards(late)
 
     if plain:
-        down_sum = down_pieces.astype(F32).sum(axis=0)
-        tokens_grad, sums, down_own, gate_up_own = last_moves(
-            4, ranks, grad_project, w_in, inputs, down_share, gate_up_share, grad_mixed_cols, gain_one[None],
-            gain_two_grad, small,
-        )
-        tokens_grad = tokens_grad[None]
+        tokens_grad, block_out, sums, parts, early_own = last_moves(
+            4, ranks, shards, grad_project, w_in, inputs, early_share[0], down_pieces, mixed_low, grad_mixed_cols,
+            gain_one[None], gain_two_grad, small, places_all[3],
+        )
+        late_own, piece_sum = finish_moves(6, ranks, shards, late_share, parts)
+        gate_up_out = spread_cols(early_own, (hidden_piece, 0, 2 * shards))[0]
+        down_out = unfold_rows(early_own, hidden_piece, model_width, 2 * hidden)
     else:
         grad_normed = right_product(grad_project, w_in)
         gain_one_grad = jnp.sum(grad_normed * wide_inputs * scale_one, axis=0)
@@ -1691,50 +1966,57 @@
             axis=0,
         )
         sums = lax.psum(sums, "ctx")
-        down_own = lax.all_gather(down_share, "ctx", axis=0, tiled=False)
-        gate_up_own = lax.all_gather(gate_up_share, "ctx", axis=0, tiled=False)
-    result = own_rows(mixed_low).astype(F32) + down_sum
-    block_out = result.astype(BF16)[None]
-    branch = result - own_rows(inputs).astype(F32)
-    own_valid = own_rows(places_all[3][:, 0] >= 0).astype(F32)
-    partial_sums = jnp.stack(
-        [
-            jnp.sum(own_valid * jnp.sum(result * result, axis=-1)),
-            jnp.sum(own_valid * jnp.sum(branch * branch, axis=-1)),
-        ]
-    )
-    valid_count = jnp.sum((segment_ids[0] >= 0).astype(F32)) * model_width
-
-    down_out = down_own.astype(F32).reshape(down_weight.shape)
-    gate_up_out = spread_cols(gate_up_own, (hidden_piece, 0, 2 * shards))[0]
-    share = model_width // shards
-    room = -(-share // LANES) * LANES
-    gain_pieces = jnp.pad(sums[0:2].reshape(2, shards, share).transpose(1, 0, 2), ((0, 0), (0, 0), (0, room - share)))
-    tail = jnp.broadcast_to(sums[None, 2 : 3 + ranks, : 2 * LANES], (shards, 1 + ranks, 2 * LANES))
-    tail = jnp.pad(tail, ((0, 0), (0, 0), (0, max(room - 2 * LANES, 0))))
-    gain_pieces = jnp.pad(gain_pieces, ((0, 0), (0, 0), (0, max(2 * LANES - room, 0))))
-    pieces = jnp.concatenate([gain_pieces, tail], axis=1)
-    pieces = jnp.pad(pieces, ((0, 0), (0, -pieces.shape[1] % 8), (0, 0)))
-    stats = jnp.broadcast_to(jnp.pad(partial_sums, (0, LANES - 2)), (8, LANES))
-    late_own, piece_sum, stats = comm.finish(7, late_share, pieces, stats)
+        down_own, gate_up_own = [lax.all_gather(a, "ctx", axis=0, tiled=False) for a in early_share]
+        down_out = down_own.astype(F32).reshape(down_weight.shape)
+        gate_up_out = spread_cols(gate_up_own, (hidden_piece, 0, 2 * shards))[0]
+        result = own_rows(mixed_low).astype(F32) + down_sum
+        block_out = result.astype(BF16)[None]
+        branch = result - own_rows(inputs).astype(F32)
+        own_valid = own_rows(places_all[3][:, 0] >= 0).astype(F32)
+        totals = lax.psum(
+            jnp.stack(
+                [
+                    jnp.sum(own_valid * jnp.sum(result * result, axis=-1)),
+                    jnp.sum(own_valid * jnp.sum(branch * branch, axis=-1)),
+                ]
+            ),
+            "ctx",
+        )
+        share = model_width // shards
+        room = 2 * LANES
+        gain_pieces = sums[0:2].reshape(2, shards, share).transpose(1, 0, 2)
+        gain_pieces = jnp.pad(gain_pieces, ((0, 0), (0, 0), (0, room - share)))
+        others = jnp.broadcast_to(sums[None, 2 : 3 + ranks, :room], (shards, 1 + ranks, room))
+        piece_sum = lax.psum_scatter(
+            jnp.concatenate([gain_pieces, others], axis=1), "fsdp", scatter_dimension=0, tiled=False
+        )
+        late_own = lax.all_gather(late_share, "ctx", axis=0, tiled=False)
     if plain:
-        in_out, out_out = spread_cols(late_own, (width, 0, 4), (width, 4 * width, 1))
+        in_out, out_out, tokens_grad, block_out, forget_out, gains_sum, bias_sum, qk_sum, rms = unpack(
+            late_own, piece_sum, sums, segment_ids, tokens_grad, block_out, width, local_heads, head_dim
+        )
+        tokens_grad, block_out = tokens_grad[None], block_out[None]
+        bias_sum, forget_out = bias_sum[0], forget_out.T
     else:
+        share = model_width // shards
+        valid_count = jnp.sum((segment_ids[0] >= 0).astype(F32)) * model_width
         in_out = jnp.concatenate(
             [late_own[c, :, i * padded : i * padded + width] for i in range(4) for c in range(ranks)], axis=1
         ).astype(F32)
         out_out = jnp.concatenate(
             [late_own[c, :, 4 * padded : 4 * padded + width] for c in range(ranks)], axis=1
         ).astype(F32)
-    last = 4 * padded + width
-    forget_out = jnp.concatenate([late_own[c, :, last : last + local_heads] for c in range(ranks)], axis=1).astype(F32)
-    gains_sum = piece_sum[0:2, :share]
-    bias_sum = piece_sum[3 : 3 + ranks, :local_heads].reshape(-1)
-    qk_sum = piece_sum[2, : 2 * LANES].reshape(2, LANES // head_dim, head_dim).sum(axis=1)
-    totals = stats[0, :2]
+        last = 4 * padded + width
+        forget_out = jnp.concatenate(
+            [late_own[c, :, last : last + local_heads] for c in range(ranks)], axis=1
+        ).astype(F32)
+        gains_sum = piece_sum[0:2, :share]
+        bias_sum = piece_sum[3 : 3 + ranks, :local_heads].reshape(-1)
+        qk_sum = piece_sum[2, : 2 * LANES].reshape(2, LANES // head_dim, head_dim).sum(axis=1)
+        rms = jnp.sqrt(totals / valid_count)[None]
     return (
         block_out, tokens_grad, gains_sum, in_out, forget_out, bias_sum, qk_sum,
-        out_out, gate_up_out, down_out, jnp.sqrt(totals / valid_count)[None],
+        out_out, gate_up_out, down_out, rms,
     )
 
 

time: 427 us -> 394 us (0.923); the launches traced: 419 us -> 394 us
  other arithmetic: 10.1 us -> 0 us
  Pallas kernels: 377 us -> 368 us
  local copies, waits for them, and re-layouts: 9.79 us -> 1.48 us
    pallas_call x1, Pallas kernels: 64.7 us -> 51 us  [middle(): pl.pallas_call(functools.partial(middle_kernel, ranks), in_specs=[ANY] *...]
    pallas_call x2 -> x1, Pallas kernels: 10.1 us -> 5.48 us  [spread_cols(): pl.pallas_call(functools.partial(spread_kernel, pieces), grid=(rows // pa...]
    reduce_sum x7 -> x0, other arithmetic: 4.42 us -> none  [the longest x1 2.26 us: body(): jnp.sum(result * result, axis=-1)]
    pallas_call x1, Pallas kernels: 118 us -> 122 us  [front(): pl.pallas_call(functools.partial(front_kernel, shards, head, heads, width...]
    reduce_scatter x3 -> x2, waiting for transfers between devices: 6.08 us -> 10.4 us  [reduce_shards(): lax.psum_scatter(array.astype(BF16), 'fsdp', scatter_dimension=0, tiled=T...]
    pallas_call x2 -> x4, Pallas kernels: 102 us -> 105 us  [the longest x1 63.4 us: last_moves(): pl.pallas_call(functools.partial(last_kernel, ranks, shards), in_specs=[A...]
  transfers between devices with their start and end apart: 3 -> 2, of which waited for: 1 -> 1; matrix products, arithmetic and copies ran while one was open for 3% -> 0% of each run, Pallas kernels for 43% -> 42%
where the time goes in v5:
time: 394 us
  Pallas kernels  368 us (93%)
  between operations  14.3 us (4%)
  waiting for transfers between devices  10.5 us (3%)
    pallas_call x1, Pallas kernels, front(): pl.pallas_call(functools.partial(front_kernel, shards, head, heads, width...  122 us
    pallas_call x1, Pallas kernels, last_moves(): pl.pallas_call(functools.partial(last_kernel, ranks, shards), in_specs=[A...  63.4 us
    pallas_call x1, Pallas kernels, middle(): pl.pallas_call(functools.partial(middle_kernel, ranks), in_specs=[ANY] *...  51 us
    pallas_call x1, Pallas kernels, ffn(): pl.pallas_call(functools.partial(ffn_kernel, shards, pick_chunk(rows)), i...  43.7 us
    pallas_call x1, Pallas kernels, attend_back(): pl.pallas_call(functools.partial(attend_back_kernel, head, chunk, width,...  40.3 us
    pallas_call x1, Pallas kernels, finish_moves(): pl.pallas_call(functools.partial(finish_kernel, ranks, shards), in_specs=...  32.4 us
    reduce_scatter x2, waiting for transfers between devices, reduce_shards(): lax.psum_scatter(array.astype(BF16), 'fsdp', scatter_dimension=0, tiled=T...  10.4 us
  transfers between devices with their start and end apart: 2, of which 1 were waited for; matrix products, arithmetic and copies ran while one was open for 0% of the time, Pallas kernels for 42%

profile of v5, /device:TPU:0, one launch (start us, length us, event | category | flops | bytes accessed | tf_op | source)
XLA Modules:
  0.0 394.4 jit_solution(16769812878229608362)
XLA Ops:
  7.2 0.0 reduce-scatter.3.cloned.1.call-start
  7.2 122.2 %front.1 = (bf16[768,1536]{1,0:T(8,128)(2,1)}, bf16[768,1536]{1,0:T(8,128)(2,1)}, bf16[1536,1664]{1,0:T(8,128)(2,1)}, bf16[1536,384]{1,0:T(8,128)(2,1)}, bf16[15...) custom-call(bf16[192,1536]{1,0:T(8,128)(2,1)} %bitcast.8, ...), custom_call_target="tpu_custom_call" | custom-call | bytes 314572800 | tf_op jit(solution)/shard_map/front/pallas_call | solution.py:967
  129.5 43.7 %ffn.1 = (bf16[1024,1536]{1,0:T(8,128)(2,1)}, bf16[768,1024]{1,0:T(8,128)(2,1)}, bf16[768,2048]{1,0:T(8,128)(2,1)}, bf16[1536,3072]{1,0:T(8,128)(2,1)}) custom-call(bf16[768,1536]{1,0:T(8,128)(2,1)} %get-tuple-element.76.normed, bf16[1536,768]{1,0:T(8,128)(2,1)} %get-tuple-element.77.turned_from, bf16[1536,2048]{1,0:T(8,128)(2,1)} %get-tuple-element.78.w_gate_up, ...), custom_call_target="tpu_custom_call" | custom-call | bytes 104857600 | tf_op jit(solution)/shard_map/ffn/pallas_call | solution.py:1163
  173.1 0.0 reduce-scatter.3.cloned.1.call-update
  173.1 0.0 reduce-scatter.5.cloned.1.call-start
  173.2 1.5 fusion
  174.7 51.0 %middle.1 = (f32[768,384]{1,0:T(8,128)}, f32[768,384]{1,0:T(8,128)}, f32[8,1536]{1,0:T(8,128)}, bf16[768,1536]{1,0:T(8,128)(2,1)}, bf16[1536,384]{1,0:T(8,128)(2,1)}) custom-call(bf16[768,2048]{1,0:T(8,128)(2,1)} %get-tuple-element.81.grad_gate_up, bf16[1536,2048]{1,0:T(8,128)(2,1)} %get-tuple-element.78.w_gate_up, ...), custom_call_target="tpu_custom_call" | custom-call | bytes 157286400 | tf_op jit(solution)/shard_map/middle/pallas_call | solution.py:1385
  225.6 40.3 %attend_back.1 = (bf16[768,1664]{1,0:T(8,128)(2,1)}, f32[8,128]{1,0:T(8,128)}, bf16[4,192,1536]{2,1,0:T(8,128)(2,1)}, bf16[1536,2048]{1,0:T(8,128)(2,1)}) custom-call(f32[1,768]{1,0:T(1,128)} %get-tuple-element.65.pos_row, f32[768,1]{1,0:T(8,128)} %get-tuple-element.66.pos_col, f32[1,768]{1,0:T(1,128)} %get-tuple-element.67.seg_row, ...), custom_call_target="tpu_custom_call" | custom-call | tf_op jit(solution)/shard_map/attend_back/pallas_call | solution.py:412
  265.9 10.4 %reduce-scatter.3.cloned.1.call-done.aside = bf16[192,3072]{1,0:T(8,128)(2,1)} async-done(((bf16[1536,3072]{1,0:T(8,128)(2,1)}), bf16[192,3072]{1,0:T(8,128)(2,1)}) %reduce-scatter.3.cloned.1.call-update) | async-done | bytes 1179664 | tf_op jit(solution)/shard_map/reduce_scatter | solution.py:1906
  276.4 0.0 reduce-scatter.5.cloned.1.call-update
  276.4 63.4 %last_moves.1 = (bf16[192,1536]{1,0:T(8,128)(2,1)}, bf16[192,1536]{1,0:T(8,128)(2,1)}, f32[8,1536]{1,0:T(8,128)}, f32[8,8,256]{2,1,0:T(8,128)}, bf16[4,192,3072]{2,1,0:T(8,128)(2,1)}) custom-call(bf16[768,1664]{1,0:T(8,128)(2,1)} %get-tuple-element.95.grad_project, bf16[1536,1664]{1,0:T(8,128)(2,1)} %get-tuple-element.96.w_in, ...), custom_call_target="tpu_custom_call" | custom-call | bytes 157286400 | tf_op jit(solution)/shard_map/last_moves/pallas_call | solution.py:1555
  339.8 3.9 unfold_rows.1
  343.7 5.5 %spread_cols.1 = f32[192,8192]{1,0:T(8,128)} custom-call(bf16[4,192,3072]{2,1,0:T(8,128)(2,1)} %get-tuple-element.117.refs_0_.source), custom_call_target="tpu_custom_call" | custom-call | bytes 9437184 | tf_op jit(solution)/shard_map/spread_cols/pallas_call | solution.py:1678
  349.2 0.0 reduce-scatter.5.cloned.1.call-done.late
  349.2 32.4 %finish_moves.1 = (bf16[4,192,2048]{2,1,0:T(8,128)(2,1)}, f32[8,256]{1,0:T(8,128)}) custom-call(bf16[192,2048]{1,0:T(8,128)(2,1)} %reduce-scatter.5.cloned.1.call-done.late, f32[8,8,256]{2,1,0:T(8,128)} %get-tuple-element.103.parts), custom_call_target="tpu_custom_call" | custom-call | bytes 52428800 | tf_op jit(solution)/shard_map/finish_moves/pallas_call | solution.py:1626
  381.6 5.7 %unpack.1 = (f32[192,6144]{1,0:T(8,128)}, f32[192,1536]{1,0:T(8,128)}, bf16[192,1536]{1,0:T(8,128)(2,1)}, bf16[192,1536]{1,0:T(8,128)(2,1)}, f32[24,192]{1,0:T(8...) custom-call(bf16[4,192,2048]{2,1,0:T(8,128)(2,1)} %get-tuple-element.104.late.late_tail, ...), custom_call_target="tpu_custom_call" | custom-call | bytes 9437184 | tf_op jit(solution)/shard_map/unpack/pallas_call | solution.py:1759
Async XLA Ops:
  7.2 269.2 %reduce-scatter.3.cloned.1.call-start = ((), (), s32[]{:S(2)}) async-start(), calls=%async_computation.2 | async-start | bytes 10616832 | tf_op jit(solution)/shard_map/reduce_scatter | solution.py:1906
  173.1 176.0 %reduce-scatter.5.cloned.1.call-start = ((), (), s32[]{:S(2)}) async-start(), calls=%async_computation.3 | async-start | bytes 7077888 | tf_op jit(solution)/shard_map/reduce_scatter | solution.py:1906
Sparse Core Ops, SparseCore 0:
  173.3 103.0 reduce-scatter.2
  278.7 68.1 reduce-scatter.4

commit v6 on v5

--- a/solution.py
+++ b/solution.py
@@ -1,5 +1,4 @@
 import functools
-import math
 
 import jax
 import jax.numpy as jnp
@@ -159,15 +158,17 @@
 
 
 def attend_back_kernel(
-    head, chunk, width, heads, ranks,
+    head, chunk, width, heads, ranks, shards,
     pos_row, pos_col, seg_row, seg_col, bias, gains, query, key, gate, forget,
     attended, wide_query, wide_key, wide_value, grad_gated, *rest,
 ):
     if ranks:
-        aside, normed, out_grad, grad_project, small, aside_in, late = rest[:7]
-        mask, wide_grad, grad_query, grad_key, grad_value, grad_prefix = rest[7:13]
-        normed_in, out_in, aside_own, late_all, load_sem, save_sem = rest[13:19]
-        sems = rest[19:]
+        aside, normed, out_grad, blocks, grad_project, small, aside_in, late, share, forget_grad = rest[:10]
+        mask, wide_grad, grad_query, grad_key, grad_value, grad_prefix = rest[10:16]
+        normed_in, out_in, aside_own, blocks_in, side_in, kept, from_below, from_above = rest[16:24]
+        late_all, load_sem, save_sem = rest[24:27]
+        sems = rest[27:29]
+        over_shards = ShardSum(shards, blocks_in, side_in, kept, from_below, from_above, rest[29:])
 
         def loads():
             own = rows_of(aside, lax.axis_index("ctx"), aside_in.shape[1])
@@ -190,16 +191,34 @@
                 send_sem.at[distance - 1], recv_sem.at[distance - 1], other,
             )
 
+    def sum_stage(hook):
+        if not ranks:
+            return
+        now = (LANES // head) * step + hook
+        for stage in range(over_shards.layers - 1):
+
+            @pl.when(now == 2 + 2 * stage)
+            def _():
+                if stage == 0:
+                    over_shards.presum()
+                else:
+                    over_shards.receive(stage - 1)
+                over_shards.send(stage)
+
     if ranks:
 
         @pl.when(step == 0)
         def _():
             rank = lax.axis_index("ctx")
-            greet([{"ctx": rank ^ distance} for distance in range(1, ranks)])
+            greet([{"ctx": rank ^ distance} for distance in range(1, ranks)], over_shards)
+            early = pltpu.make_async_copy(blocks, blocks_in, load_sem.at[4])
+            early.start()
             for copy in aside_copies():
                 copy.start()
             for copy in loads():
                 copy.start()
+            early.wait()
+            over_shards.start()
 
     rows = query.shape[0]
     lanes = lane_ids(rows)
@@ -217,6 +236,7 @@
         small[...] = jnp.zeros_like(small)
 
     for side in range(LANES // head):
+        sum_stage(side)
         here = pl.ds(side * head, head)
 
         def column(part):
@@ -243,8 +263,8 @@
             grad_scores = (probs * outer).astype(BF16)
             grad_key[part, :] = dot(grad_scores, wide_query[side])
             grad_value[part, :] = dot(probs.astype(BF16), wide_grad[...])
-            grad_query[...] += left_product(grad_scores, wide_key[side, part, :])
-        from_query = grad_query[...]
+            grad_query[...] += left_product(wide_key[side, part, :], grad_scores)
+        from_query = grad_query[...].T
         from_key = grad_key[...]
         change = pick_lane(from_query, lanes, head + 1) - pick_lane(from_key, lanes, head + 4)
         grad_prefix[...] += jnp.where(lanes == (LANES // head) * step + side, change, 0.0)
@@ -290,6 +310,10 @@
                 copy.wait()
             keep = pltpu.make_async_copy(aside_own, aside_in.at[lax.axis_index("ctx")], load_sem.at[3])
             keep.start()
+            late_stages = [n for n in range(over_shards.layers - 1) if 2 + 2 * n >= heads]
+            for stage in late_stages:
+                over_shards.receive(stage - 1)
+                over_shards.send(stage)
             ends = 4 * width, 4 * width + out_grad.shape[1]
             late_all[:, ends[0] : ends[1]] = out_in[...]
             piece = 2 * LANES
@@ -310,8 +334,9 @@
                 def _(part):
                     late_all[part, into] = dot(normed_in[part, :], grad_project[:, cols]).astype(BF16)
 
-            product(slice(ends[1], ends[1] + LANES), slice(ends[0], ends[0] + LANES))
             rest_save.start()
+            turned = grad_project[:, ends[0] : ends[0] + LANES].astype(F32).T[0:8, :]
+            forget_grad[...] = right_product(turned.astype(BF16), normed_in[...])
 
             @pl.loop(0, count)
             def _(turn):
@@ -322,6 +347,9 @@
             for copy in aside_copies():
                 copy.wait()
             keep.wait()
+            over_shards.receive(over_shards.layers - 2)
+            share[...] = kept[over_shards.layer]
+            over_shards.sent()
             rest_save.wait()
 
             @pl.loop(0, count)
@@ -367,7 +395,7 @@
     )(*places, bias, gains, project, project, project, project, project)
 
 
-def attend_back(project, places, bias, gains, attended, wides, grad_gated, beside, ranks, head, width, heads):
+def attend_back(project, places, bias, gains, attended, wides, grad_gated, beside, ranks, shards, head, width, heads):
     rows = project.shape[0]
     steps = width // LANES
     per = LANES // head
@@ -386,31 +414,38 @@
     scratch = [
         pltpu.VMEM((rows, rows), F32),
         pltpu.VMEM((rows, LANES), BF16),
-        pltpu.VMEM((rows, LANES), F32),
+        pltpu.VMEM((LANES, rows), F32),
         pltpu.VMEM((rows, LANES), F32),
         pltpu.VMEM((rows, LANES), F32),
         pltpu.VMEM((rows, LANES), F32),
     ]
     if ranks:
-        aside, normed, out_grad = beside
-        model, late_cols = normed.shape[0], total + out_grad.shape[1]
-        out_specs += [ANY, ANY]
+        aside, normed, out_grad, blocks = beside
+        share = (blocks.shape[0] // shards, blocks.shape[1])
+        sum_blocks, sum_sems = shard_sum_scratch(shards, *share)
+        model, late_cols = normed.shape[0], 4 * width + out_grad.shape[1]
+        out_specs += [ANY, ANY, whole(share), whole((8, model))]
         out_shape += [
             jax.ShapeDtypeStruct((ranks, aside.shape[0] // ranks, aside.shape[1]), BF16),
             jax.ShapeDtypeStruct((model, late_cols), BF16),
+            jax.ShapeDtypeStruct(share, BF16),
+            jax.ShapeDtypeStruct((8, model), F32),
         ]
         scratch += [
             pltpu.VMEM(normed.shape, BF16),
             pltpu.VMEM(out_grad.shape, BF16),
             pltpu.VMEM((aside.shape[0] // ranks, aside.shape[1]), BF16),
+            pltpu.VMEM(blocks.shape, BF16),
+            *sum_blocks,
             pltpu.VMEM((model, late_cols), BF16),
-            pltpu.SemaphoreType.DMA((4,)),
+            pltpu.SemaphoreType.DMA((5,)),
             pltpu.SemaphoreType.DMA((4 * width // (2 * LANES) + 1,)),
             pltpu.SemaphoreType.DMA((ranks - 1,)),
             pltpu.SemaphoreType.DMA((ranks - 1,)),
+            *sum_sems,
         ]
     return pl.pallas_call(
-        functools.partial(attend_back_kernel, head, chunk, width, heads, ranks),
+        functools.partial(attend_back_kernel, head, chunk, width, heads, ranks, shards),
         grid=(steps,),
         in_specs=[whole(p.shape) for p in places] + [whole(bias.shape), whole(gains.shape)]
         + [part(0), part(1), part(3), forget, block, wide, wide, wide, own] + [ANY] * len(beside),
@@ -1030,22 +1065,11 @@
     )
 
 
-def fold_tiles(rows, cols, share_rows):
-    extra = rows * cols // share_rows
-    high, wide = math.gcd(rows, share_rows), math.gcd(cols, extra)
-    tiles = []
-    for row in range(rows // high):
-        for col in range(cols // wide):
-            k = row * (cols // wide) + col
-            tiles.append((row * high, col * wide, k // (extra // wide) * high, k % (extra // wide) * wide))
-    return tiles, high, wide, extra
-
-
 def ffn_kernel(
     shards, chunk,
     normed, turned_from, w_gate_up, cotangent, down_near,
-    w_down, hidden, grad_gate_up, grad_weight,
-    weight_in, cotangent_in, gates, ups, hn, turned, acts, grads, weight_out,
+    w_down, hidden, grad_gate_up, grad_weight, grad_down,
+    weight_in, cotangent_in, gates, ups, hn, turned, acts, grads, weight_out, down_out,
     load_sem, save_sem, tile_sem, near_sem, *line_sems,
 ):
     size = gates.shape[1]
@@ -1060,7 +1084,7 @@
     saves = [
         pltpu.make_async_copy(a, b, save_sem.at[n])
         for n, (a, b) in enumerate(
-            ((acts, hidden), (weight_out.at[:, pl.ds(2 * size, size)], grad_weight.at[:, pl.ds(2 * size, size)]))
+            ((acts, hidden), (down_out, grad_down))
         )
     ]
     line = Line(shards, None, w_down, line_sems)
@@ -1082,17 +1106,8 @@
         ups[:, span(turn)] = up
         acts[:, span(turn)] = (jax.nn.silu(gate) * up).astype(BF16)
 
-    tiles, high, wide, _ = fold_tiles(tile // 2, model, model // shards)
-
     def down_grad(turn):
-        product = left_product(acts[:, span(turn)], cotangent_in[...]).astype(BF16)
-        for half in range(2):
-            base = (2 * turn + half) * (model // shards)
-            for row, col, new_row, new_col in tiles:
-                row = row + half * (tile // 2)
-                weight_out[
-                    pl.ds(pl.multiple_of(base + new_row, high), high), 2 * size + new_col : 2 * size + new_col + wide
-                ] = product[row : row + high, col : col + wide]
+        down_out[span(turn), :] = left_product(acts[:, span(turn)], cotangent_in[...]).astype(BF16)
 
     count = size // tile
     pl.loop(0, count)(activate)
@@ -1163,12 +1178,13 @@
     return pl.pallas_call(
         functools.partial(ffn_kernel, shards, pick_chunk(rows)),
         in_specs=[ANY] * 5,
-        out_specs=[VMEM_WHOLE] + [ANY] * 3,
+        out_specs=[VMEM_WHOLE] + [ANY] * 4,
         out_shape=[
             shape((size, model), BF16),
             shape((rows, size), BF16),
             shape((rows, 2 * size), BF16),
-            shape((model, 3 * size), BF16),
+            shape((model, 2 * size), BF16),
+            shape((size, model), BF16),
         ],
         scratch_shapes=[
             vmem(w_gate_up.shape, BF16),
@@ -1179,7 +1195,8 @@
             vmem((model, rows), BF16),
             vmem((rows, size), BF16),
             vmem((rows, 2 * size), BF16),
-            vmem((model, 3 * size), BF16),
+            vmem((model, 2 * size), BF16),
+            vmem((size, model), BF16),
             pltpu.SemaphoreType.DMA((4,)),
             pltpu.SemaphoreType.DMA((2,)),
             pltpu.SemaphoreType.DMA((shards // 2, 4)),
@@ -1192,6 +1209,94 @@
         cost_estimate=pl.CostEstimate(flops=0, bytes_accessed=100 << 20, transcendentals=0),
         name="ffn",
     )(normed, turned, w_gate_up, cotangent, down_near)
+
+
+class ShardSum:
+    def __init__(self, shards, blocks, side_in, kept, from_below, from_above, sems):
+        self.shard = lax.axis_index("fsdp")
+        self.layers = shards // 2
+        self.layer, self.core = self.shard // 2, self.shard % 2
+        self.sibling = {"fsdp": self.shard ^ 1}
+        self.above, self.below = {"fsdp": self.shard + 2}, {"fsdp": self.shard - 2}
+        self.has_above, self.has_below = self.layer < self.layers - 1, self.layer > 0
+        self.blocks, self.side_in, self.kept = blocks, side_in, kept
+        self.from_below, self.from_above = from_below, from_above
+        self.rows = kept.shape[1]
+        self.side_send, self.side_recv, self.up_send, self.up_recv, self.down_send, self.down_recv = sems
+
+    def side(self, layer):
+        return pltpu.make_async_remote_copy(
+            rows_of(self.blocks, 2 * layer + 1 - self.core, self.rows), self.side_in.at[layer],
+            self.side_send.at[layer], self.side_recv.at[layer], device_id=self.sibling, device_id_type=MESH,
+        )
+
+    def start(self):
+        for layer in range(self.layers):
+            self.side(layer).start()
+
+    def presum(self):
+        for layer in range(self.layers):
+            self.side(layer).wait_recv()
+            own = rows_of(self.blocks, 2 * layer + self.core, self.rows)[...].astype(F32)
+            self.kept[layer] = (own + self.side_in[layer].astype(F32)).astype(BF16)
+
+    def up(self, stage):
+        return pltpu.make_async_remote_copy(
+            self.kept.at[self.layers - 1 - stage + self.layer], self.from_below.at[stage],
+            self.up_send.at[stage], self.up_recv.at[stage], device_id=self.above, device_id_type=MESH,
+        )
+
+    def down(self, stage):
+        return pltpu.make_async_remote_copy(
+            self.kept.at[stage - self.layers + 1 + self.layer], self.from_above.at[stage],
+            self.down_send.at[stage], self.down_recv.at[stage], device_id=self.below, device_id_type=MESH,
+        )
+
+    def each_sent(self, stage, what):
+        @pl.when(self.has_above & (self.layer <= stage))
+        def _():
+            what(self.up(stage))
+
+        @pl.when(self.has_below & (self.layers - 1 - self.layer <= stage))
+        def _():
+            what(self.down(stage))
+
+    def send(self, stage):
+        self.each_sent(stage, lambda copy: copy.start())
+
+    def receive(self, stage):
+        def add(target, arrived):
+            self.kept[target] = (self.kept[target].astype(F32) + arrived[stage].astype(F32)).astype(BF16)
+
+        @pl.when(self.has_below & (self.layer - 1 <= stage))
+        def _():
+            pltpu.make_async_remote_copy(
+                self.from_below.at[stage], self.from_below.at[stage], self.up_send.at[stage], self.up_recv.at[stage],
+                device_id=self.below, device_id_type=MESH,
+            ).wait_recv()
+            add(self.layers - 2 - stage + self.layer, self.from_below)
+
+        @pl.when(self.has_above & (self.layers - 2 - self.layer <= stage))
+        def _():
+            pltpu.make_async_remote_copy(
+                self.from_above.at[stage], self.from_above.at[stage], self.down_send.at[stage],
+                self.down_recv.at[stage], device_id=self.above, device_id_type=MESH,
+            ).wait_recv()
+            add(stage - self.layers + 2 + self.layer, self.from_above)
+
+    def sent(self):
+        for layer in range(self.layers):
+            self.side(layer).wait_send()
+        for stage in range(self.layers - 1):
+            self.each_sent(stage, lambda copy: copy.wait_send())
+
+
+def shard_sum_scratch(shards, rows, cols):
+    layers = shards // 2
+    few, all_layers = pltpu.SemaphoreType.DMA((layers - 1,)), pltpu.SemaphoreType.DMA((layers,))
+    block = pltpu.VMEM((layers, rows, cols), BF16)
+    part = pltpu.VMEM((layers - 1, rows, cols), BF16)
+    return [block, block, part, part], [all_layers, all_layers, few, few, few, few]
 
 
 class Fold:
@@ -1307,7 +1412,7 @@
         scale = rms_scale(values)
         grad = wide[...]
         gain_grad[0:1, :] += jnp.sum(grad * values * scale, axis=0, keepdims=True)
-        back = norm_back(grad, values, scale, gain[0:1, :]).astype(BF16)
+        back = norm_back(grad, values, scale, gain[1:2, :]).astype(BF16)
         for index in range(ranks):
             first_out[index, here, :] = back[:, index * width : (index + 1) * width]
         first(turn).start()
@@ -1334,7 +1439,7 @@
     def aside(turn):
         @pl.when(turn == ranks)
         def _():
-            for copy in loads[5:]:
+            for copy in loads[5:8]:
                 copy.wait()
 
             @pl.loop(0, model // tile)
@@ -1376,7 +1481,9 @@
         copy.wait()
 
 
-def middle(collective_id, ranks, grad_gate_up, w_gate_up, mixed, cotangent, w_out, hidden, w_down, gated, gain):
+def middle(
+    collective_id, ranks, grad_gate_up, w_gate_up, mixed, cotangent, w_out, hidden, w_down, gated, gain
+):
     rows, model = mixed.shape
     width = w_out.shape[1]
     flat = pltpu.VMEM((rows, width), BF16)
@@ -1421,10 +1528,10 @@
 
 def last_kernel(
     ranks, shards,
-    grad_project, w_in, inputs, aside, pieces, mixed, mixed_grad, gain, gain_two_grad, small, segments,
-    tokens_grad, block_out, total_sums, parts, aside_all,
+    grad_project, w_in, inputs, aside, pieces, mixed, share, mixed_grad, gain, gain_two_grad, small, segments, forget_grad,
+    tokens_grad, block_out, total_sums, parts, aside_all, share_all,
     grad_in, weight_in, inputs_in, aside_in, pieces_in, mixed_in, wide, out, into, between, end, sums_out, sums_in,
-    load_sem, send_sem, recv_sem, sums_send, sums_recv, aside_send, aside_recv, aside_own,
+    share_in, load_sem, send_sem, recv_sem, sums_send, sums_recv, aside_send, aside_recv, aside_own,
 ):
     rank = lax.axis_index("ctx")
     rows = inputs.shape[0] // ranks
@@ -1435,14 +1542,19 @@
         for n, (a, b) in enumerate(
             (
                 (aside, aside_in), (w_in, weight_in), (grad_project, grad_in), (inputs, inputs_in),
-                (pieces, pieces_in), (rows_of(mixed, rank, rows), mixed_in),
+                (pieces, pieces_in), (rows_of(mixed, rank, rows), mixed_in), (share, share_in),
             )
         )
     ]
     for copy in loads:
         copy.start()
     greet([{"ctx": rank ^ distance} for distance in range(1, ranks)])
-    relay = relay_ops("stack", rank, aside_in, aside_all, (aside_send, aside_recv, aside_own))
+    relay, share_relay = [
+        relay_ops("stack", rank, a, b, (aside_send.at[n], aside_recv.at[n], aside_own.at[n]))
+        for n, (a, b) in enumerate(((aside_in, aside_all), (share_in, share_all)))
+    ]
+    loads[6].wait()
+    share_relay.start()
     loads[0].wait()
     relay.start()
     sums_out[...] = jnp.zeros_like(sums_out)
@@ -1505,7 +1617,8 @@
             for number in (0, 1):
                 fold.copy(number).start()
 
-    for copy in loads[4:]:
+    share_relay.forward()
+    for copy in loads[4:6]:
         copy.wait()
     own = pl.ds(pl.multiple_of(rank * rows, 16), rows)
     result = mixed_in[...].astype(F32)
@@ -1537,15 +1650,18 @@
     for index in range(shards):
         parts[index, 0:2, 0:share] = total[0:2, index * share : (index + 1) * share]
         parts[index, 2:8, :] = total[2:8, 0 : parts.shape[2]]
+        parts[index, 8:16, 0:share] = forget_grad[:, index * share : (index + 1) * share]
     fold.sent()
     for distance in range(1, ranks):
         send_sums(distance).wait_send()
     relay.finish()
+    share_relay.finish()
 
 
 def last_moves(
     collective_id, ranks, shards,
-    grad_project, w_in, inputs, aside, pieces, mixed, mixed_grad, gain, gain_two_grad, small, segments,
+    grad_project, w_in, inputs, aside, pieces, mixed, share, mixed_grad, gain, gain_two_grad, small, segments,
+    forget_grad,
 ):
     rows, model = inputs.shape
     own = (rows // ranks, model)
@@ -1554,14 +1670,15 @@
     sems = pltpu.SemaphoreType.DMA((ranks - 1,))
     return pl.pallas_call(
         functools.partial(last_kernel, ranks, shards),
-        in_specs=[ANY] * 6 + [VMEM_WHOLE] * 5,
-        out_specs=[VMEM_WHOLE] * 4 + [ANY],
+        in_specs=[ANY] * 7 + [VMEM_WHOLE] * 6,
+        out_specs=[VMEM_WHOLE] * 4 + [ANY] * 2,
         out_shape=[
             jax.ShapeDtypeStruct(own, BF16),
             jax.ShapeDtypeStruct(own, BF16),
             jax.ShapeDtypeStruct((8, model), F32),
-            jax.ShapeDtypeStruct((shards, 8, max(2 * LANES, -(-model // shards // LANES) * LANES)), F32),
+            jax.ShapeDtypeStruct((shards, 16, max(2 * LANES, -(-model // shards // LANES) * LANES)), F32),
             jax.ShapeDtypeStruct((ranks,) + aside.shape, BF16),
+            jax.ShapeDtypeStruct((ranks,) + share.shape, BF16),
         ],
         scratch_shapes=[
             pltpu.VMEM(grad_project.shape, BF16),
@@ -1574,30 +1691,36 @@
             *blocks,
             pltpu.VMEM((8, model), F32),
             pltpu.VMEM((ranks, 8, model), F32),
-            pltpu.SemaphoreType.DMA((6,)),
+            pltpu.VMEM(share.shape, BF16),
+            pltpu.SemaphoreType.DMA((7,)),
             pltpu.SemaphoreType.DMA((6,)),
             pltpu.SemaphoreType.DMA((6,)),
             sems, sems,
-            pltpu.SemaphoreType.DMA((6,)),
-            pltpu.SemaphoreType.DMA((6,)),
-            pltpu.SemaphoreType.DMA((2,)),
+            pltpu.SemaphoreType.DMA((2, 6)),
+            pltpu.SemaphoreType.DMA((2, 6)),
+            pltpu.SemaphoreType.DMA((2, 2)),
         ],
         compiler_params=pltpu.CompilerParams(
             collective_id=collective_id, has_side_effects=True, vmem_limit_bytes=VMEM_LIMIT
         ),
         cost_estimate=pl.CostEstimate(flops=0, bytes_accessed=150 << 20, transcendentals=0),
         name="last_moves",
-    )(grad_project, w_in, inputs, aside, pieces, mixed, mixed_grad, gain, gain_two_grad, small, segments)
-
-
-def finish_kernel(ranks, shards, late, parts, late_all, part_sum, late_in, into, load_sem, send_sem, recv_sem, own_sem,
-                  part_send, part_recv):
+    )(grad_project, w_in, inputs, aside, pieces, mixed, share, mixed_grad, gain, gain_two_grad, small, segments, forget_grad)
+
+
+def finish_kernel(
+    ranks, shards, late, parts, late_all, part_sum, forget_all,
+    late_in, into, load_sem, send_sem, recv_sem, own_sem, part_send, part_recv, forget_send, forget_recv,
+):
     rank = lax.axis_index("ctx")
     shard = lax.axis_index("fsdp")
     load = pltpu.make_async_copy(late, late_in, load_sem.at[0])
     load.start()
     relay = relay_ops("stack", rank, late_in, late_all, (send_sem, recv_sem, own_sem))
-    greet([{"ctx": rank ^ 1}, {"ctx": rank ^ 2}] + [{"fsdp": shard ^ distance} for distance in range(1, shards)])
+    greet(
+        [{"ctx": rank ^ distance} for distance in range(1, ranks)]
+        + [{"fsdp": shard ^ distance} for distance in range(1, shards)]
+    )
     load.wait()
     relay.start()
 
@@ -1608,14 +1731,25 @@
             device_id={"fsdp": other}, device_id_type=MESH,
         )
 
+    def send_forget(distance):
+        return to_rank(
+            forget_all.at[rank], forget_all.at[rank], forget_send.at[distance - 1], forget_recv.at[distance - 1],
+            rank ^ distance,
+        )
+
     for distance in range(1, shards):
         send(distance).start()
-    relay.forward()
     total = parts[shard]
     for distance in range(1, shards):
         send(distance).wait_recv()
         total = total + into[distance]
     part_sum[...] = total
+    forget_all[rank] = total[8:16, :]
+    for distance in range(1, ranks):
+        send_forget(distance).start()
+    relay.forward()
+    for distance in range(1, ranks):
+        send_forget(distance).wait()
     for distance in range(1, shards):
         send(distance).wait_send()
     relay.finish()
@@ -1626,10 +1760,11 @@
     return pl.pallas_call(
         functools.partial(finish_kernel, ranks, shards),
         in_specs=[ANY, VMEM_WHOLE],
-        out_specs=[ANY, VMEM_WHOLE],
+        out_specs=[ANY, VMEM_WHOLE, VMEM_WHOLE],
         out_shape=[
             jax.ShapeDtypeStruct((ranks,) + late.shape, BF16),
             jax.ShapeDtypeStruct(parts.shape[1:], F32),
+            jax.ShapeDtypeStruct((ranks, 8, parts.shape[2]), F32),
         ],
         scratch_shapes=[
             pltpu.VMEM(late.shape, BF16),
@@ -1639,6 +1774,8 @@
             pltpu.SemaphoreType.DMA((6,)),
             pltpu.SemaphoreType.DMA((2,)),
             sems, sems,
+            pltpu.SemaphoreType.DMA((ranks - 1,)),
+            pltpu.SemaphoreType.DMA((ranks - 1,)),
         ],
         compiler_params=pltpu.CompilerParams(
             collective_id=collective_id, has_side_effects=True, vmem_limit_bytes=VMEM_LIMIT
@@ -1687,30 +1824,8 @@
     )(source)
 
 
-def unfold_kernel(tiles, high, wide, source, target):
-    for row, col, new_row, new_col in tiles:
-        target[row : row + high, col : col + wide] = source[
-            0, new_row : new_row + high, new_col : new_col + wide
-        ].astype(F32)
-
-
-def unfold_rows(source, rows, cols, first):
-    ranks, share_rows, _ = source.shape
-    tiles, high, wide, extra = fold_tiles(rows, cols, share_rows)
-    return pl.pallas_call(
-        functools.partial(unfold_kernel, tiles, high, wide),
-        grid=(ranks,),
-        in_specs=[pl.BlockSpec((1, share_rows, extra), lambda step: (step, 0, first // extra))],
-        out_specs=pl.BlockSpec((rows, cols), lambda step: (step, 0)),
-        out_shape=jax.ShapeDtypeStruct((ranks * rows, cols), F32),
-        compiler_params=pltpu.CompilerParams(vmem_limit_bytes=VMEM_LIMIT),
-        cost_estimate=pl.CostEstimate(flops=0, bytes_accessed=ranks * rows * cols * 6, transcendentals=0),
-        name="unfold_rows",
-    )(source)
-
-
 def unpack_kernel(
-    width, heads, head, late, late_tail, sums, totals, segments, first_rows, second_rows,
+    width, heads, head, late, forget_all, sums, totals, segments, first_rows, second_rows,
     in_out, out_out, first_out, second_out, forget_out, gains, bias, qk, rms,
 ):
     ranks = late.shape[0]
@@ -1724,19 +1839,14 @@
     second_out[...] = second_rows[...]
     lane = lax.broadcasted_iota(jnp.int32, (LANES, ranks * heads), 0)
     place = lax.broadcasted_iota(jnp.int32, (LANES, ranks * heads), 1)
-    lane_t = lax.broadcasted_iota(jnp.int32, (ranks * heads, LANES), 1)
-    place_t = lax.broadcasted_iota(jnp.int32, (ranks * heads, LANES), 0)
-    forget = jnp.zeros(forget_out.shape, F32)
     biases = jnp.zeros((8, ranks * heads), F32)
     for index in range(ranks):
         chosen = (lane < heads) & (place == index * heads + lane)
         out_out[:, index * width : (index + 1) * width] = late[index, :, first : first + width].astype(F32)
-        chosen_t = (lane_t < heads) & (place_t == index * heads + lane_t)
-        forget = forget + right_product(jnp.where(chosen_t, 1.0, 0.0).astype(BF16), late_tail[index])
+        forget_out[index * heads : (index + 1) * heads, :] = forget_all[index, 0:heads, 0 : forget_out.shape[1]]
         row = jnp.broadcast_to(sums[3 + index : 4 + index, 0:LANES], (8, LANES))
         for part in split_three(row):
             biases = biases + dot(part.astype(BF16), jnp.where(chosen, 1.0, 0.0).astype(BF16))
-    forget_out[...] = forget
     gains[...] = sums[0:2, 0 : gains.shape[1]]
     bias[...] = biases[0:1, :]
     for row in range(2):
@@ -1747,7 +1857,7 @@
     rms[...] = jnp.sqrt(totals[7:8, 0:2] / (count * totals.shape[1]))
 
 
-def unpack(late, sums, totals, segments, first_rows, second_rows, width, heads, head):
+def unpack(late, forget_all, sums, totals, segments, first_rows, second_rows, width, heads, head):
     ranks, rows, cols = late.shape
     part = rows // 4
 
@@ -1761,9 +1871,8 @@
         grid=(rows // part,),
         in_specs=[
             pl.BlockSpec((ranks, part, cols), lambda step: (0, step, 0)),
-            pl.BlockSpec((ranks, rows, LANES), lambda step: (0, 0, 5 * width // LANES)),
         ]
-        + [whole(a.shape) for a in (sums, totals, segments)]
+        + [whole(a.shape) for a in (forget_all, sums, totals, segments)]
         + [block(first_rows.shape[1])] * 2,
         out_specs=[block(4 * ranks * width), block(ranks * width)] + [block(first_rows.shape[1])] * 2
         + [whole(a) for a in ((ranks * heads, rows), (2, share), (1, ranks * heads), (2, head), (1, 2))],
@@ -1781,7 +1890,7 @@
         compiler_params=pltpu.CompilerParams(vmem_limit_bytes=VMEM_LIMIT),
         cost_estimate=pl.CostEstimate(flops=0, bytes_accessed=ranks * rows * cols * 6, transcendentals=0),
         name="unpack",
-    )(late, late, sums, totals, segments, first_rows, second_rows)
+    )(late, forget_all, sums, totals, segments, first_rows, second_rows)
 
 
 class Native:
@@ -1843,8 +1952,7 @@
             tokens[0], out_grad[0], attn_in_weight, out_weight, gate_up_weight, down_weight, forget_weight.T,
             norm_gains, qk_gains, segment_ids, block_order, forget_bias[None],
         )
-        gain_one, gain_two = gain_rows[0], gain_rows[1]
-        w_down, hidden_act, grad_gate_up, early_grad = ffn(
+        w_down, hidden_act, grad_gate_up, early_grad, down_part_grad = ffn(
             1, shards, normed_two, turned, w_gate_up, grad_low, down_near
         )
     else:
@@ -1911,7 +2019,8 @@
         early_share = (reduce_shards(down_part_grad), reduce_shards(gate_up_grad))
     if plain:
         grad_mixed_cols, grad_gated, gain_two_grad, down_part, out_part = middle(
-            3, ranks, grad_gate_up, w_gate_up, mixed_low, grad_low, w_out, hidden_act, w_down, gated_all, gain_two[None]
+            3, ranks, grad_gate_up, w_gate_up, mixed_low, grad_low, w_out, hidden_act, w_down, gated_all,
+            gain_rows,
         )
     else:
         grad_normed_two = right_product(grad_gate_up, w_gate_up)
@@ -1928,10 +2037,10 @@
         )
     grad_project, small, *rest = attend_back(
         project, places_all, bias, head_gains, attended, (wide_query, wide_key, wide_value),
-        grad_gated, (down_part, normed, out_part) if plain else (), ranks if plain else 0, head_dim, padded, local_heads,
+        grad_gated, (down_part, normed, out_part, down_part_grad) if plain else (), ranks if plain else 0, shards, head_dim, padded, local_heads,
     )
     if plain:
-        down_pieces, late = rest
+        down_pieces, late, down_share, forget_grad = rest
     else:
         in_part = left_product(normed, grad_project).astype(BF16)
         out_part = left_product(gated_all, grad_branch).astype(BF16)
@@ -1940,13 +2049,13 @@
     late_share = reduce_shards(late)
 
     if plain:
-        tokens_grad, block_out, sums, parts, early_own = last_moves(
-            4, ranks, shards, grad_project, w_in, inputs, early_share[0], down_pieces, mixed_low, grad_mixed_cols,
-            gain_one[None], gain_two_grad, small, places_all[3],
-        )
-        late_own, piece_sum = finish_moves(6, ranks, shards, late_share, parts)
+        tokens_grad, block_out, sums, parts, early_own, down_own = last_moves(
+            4, ranks, shards, grad_project, w_in, inputs, early_share[0], down_pieces, mixed_low, down_share,
+            grad_mixed_cols,             gain_rows, gain_two_grad, small, places_all[3], forget_grad,
+        )
+        late_own, piece_sum, forget_all = finish_moves(6, ranks, shards, late_share, parts)
         gate_up_out = spread_cols(early_own, (hidden_piece, 0, 2 * shards))[0]
-        down_out = unfold_rows(early_own, hidden_piece, model_width, 2 * hidden)
+        down_out = down_own.astype(F32).reshape(down_weight.shape)
     else:
         grad_normed = right_product(grad_project, w_in)
         gain_one_grad = jnp.sum(grad_normed * wide_inputs * scale_one, axis=0)
@@ -1993,7 +2102,7 @@
         late_own = lax.all_gather(late_share, "ctx", axis=0, tiled=False)
     if plain:
         in_out, out_out, tokens_grad, block_out, forget_out, gains_sum, bias_sum, qk_sum, rms = unpack(
-            late_own, piece_sum, sums, segment_ids, tokens_grad, block_out, width, local_heads, head_dim
+            late_own, forget_all, piece_sum, sums, segment_ids, tokens_grad, block_out, width, local_heads, head_dim
         )
         tokens_grad, block_out = tokens_grad[None], block_out[None]
         bias_sum, forget_out = bias_sum[0], forget_out.T

time: 394 us -> 385 us (0.977); the launches traced: 394 us -> 379 us
  waiting for transfers between devices: 10.5 us -> 0.06 us
  Pallas kernels: 368 us -> 362 us
    reduce_scatter x2, waiting for transfers between devices: 10.4 us -> 0.02 us  [reduce_shards(): lax.psum_scatter(array.astype(BF16), 'fsdp', scatter_dimension=0, tiled=T...]
    pallas_call x1, Pallas kernels: 43.7 us -> 34.1 us  [ffn(): pl.pallas_call(functools.partial(ffn_kernel, shards, pick_chunk(rows)), i...]
    pallas_call x1, Pallas kernels: 40.3 us -> 44.6 us  [attend_back(): pl.pallas_call(functools.partial(attend_back_kernel, head, chunk, width,...]
  transfers between devices with their start and end apart: 2 -> 2, of which waited for: 1 -> 0; matrix products, arithmetic and copies ran while one was open for 0% -> 1% of each run, Pallas kernels for 42% -> 44%
where the time goes in v6:
time: 385 us; the launch traced here: 379 us
  Pallas kernels  362 us (94%)
  between operations  14.6 us (4%)
    pallas_call x1, Pallas kernels, front(): pl.pallas_call(functools.partial(front_kernel, shards, head, heads, width...  122 us
    pallas_call x1, Pallas kernels, last_moves(): pl.pallas_call(functools.partial(last_kernel, ranks, shards), in_specs=[A...  65.7 us
    pallas_call x1, Pallas kernels, middle(): pl.pallas_call(functools.partial(middle_kernel, ranks), in_specs=[ANY] *...  51 us
    pallas_call x1, Pallas kernels, attend_back(): pl.pallas_call(functools.partial(attend_back_kernel, head, chunk, width,...  44.6 us
    pallas_call x1, Pallas kernels, finish_moves(): pl.pallas_call(functools.partial(finish_kernel, ranks, shards), in_specs=...  34.2 us
    pallas_call x1, Pallas kernels, ffn(): pl.pallas_call(functools.partial(ffn_kernel, shards, pick_chunk(rows)), i...  34.1 us
  transfers between devices with their start and end apart: 2, of which 0 were waited for; matrix products, arithmetic and copies ran while one was open for 1% of the time, Pallas kernels for 44%

profile of v6, /device:TPU:0, one launch (start us, length us, event | category | flops | bytes accessed | tf_op | source)
XLA Modules:
  0.0 379.3 jit_solution(4917946476669642326)
XLA Ops:
  7.2 0.0 reduce-scatter.3.cloned.1.call-start
  7.2 122.2 %front.1 = (bf16[768,1536]{1,0:T(8,128)(2,1)}, bf16[768,1536]{1,0:T(8,128)(2,1)}, bf16[1536,1664]{1,0:T(8,128)(2,1)}, bf16[1536,384]{1,0:T(8,128)(2,1)}, bf16[15...) custom-call(bf16[192,1536]{1,0:T(8,128)(2,1)} %bitcast.11, ...), custom_call_target="tpu_custom_call" | custom-call | bytes 314572800 | tf_op jit(solution)/shard_map/front/pallas_call | solution.py:1002
  129.4 34.1 %ffn.1 = (bf16[1024,1536]{1,0:T(8,128)(2,1)}, bf16[768,1024]{1,0:T(8,128)(2,1)}, bf16[768,2048]{1,0:T(8,128)(2,1)}, bf16[1536,2048]{1,0:T(8,128)(2,1)}, bf16[1024,1536]{1,0:T(8,128)(2,1)}) custom-call(bf16[768,1536]{1,0:T(8,128)(2,1)} %get-tuple-element.81.normed, bf16[1536,768]{1,0:T(8,128)(2,1)} %get-tuple-element.82.turned_from, ...), custom_call_target="tpu_custom_call" | custom-call | bytes 104857600 | tf_op jit(solution)/shard_map/ffn/pallas_call | solution.py:1178
  163.6 0.0 reduce-scatter.3.cloned.1.call-update
  163.6 0.0 reduce-scatter.5.cloned.1.call-start
  163.6 51.0 %middle.1 = (f32[768,384]{1,0:T(8,128)}, f32[768,384]{1,0:T(8,128)}, f32[8,1536]{1,0:T(8,128)}, bf16[768,1536]{1,0:T(8,128)(2,1)}, bf16[1536,384]{1,0:T(8,128)(2,1)}) custom-call(bf16[768,2048]{1,0:T(8,128)(2,1)} %get-tuple-element.86.grad_gate_up, bf16[1536,2048]{1,0:T(8,128)(2,1)} %get-tuple-element.83.w_gate_up, ...), custom_call_target="tpu_custom_call" | custom-call | bytes 157286400 | tf_op jit(solution)/shard_map/middle/pallas_call | solution.py:1492
  214.6 44.6 %attend_back.1 = (bf16[768,1664]{1,0:T(8,128)(2,1)}, f32[8,128]{1,0:T(8,128)}, bf16[4,192,1536]{2,1,0:T(8,128)(2,1)}, bf16[1536,1920]{1,0:T(8,128)(2,1)}, bf16[128,1536]{1,0:T(8,128)(2,1)}, /*index=5*/f32[8,1536]{1,0:T(8,128)}) custom-call(f32[1,768]{1,0:T(1,128)} %get-tuple-element.70.pos_row, f32[768,1]{1,0:T(8,128)} %get-tuple-element.71.pos_col, ...), custom_call_target="tpu_custom_call" | custom-call | tf_op jit(solution)/shard_map/attend_back/pallas_call | solution.py:447
  259.2 0.0 reduce-scatter.3.cloned.1.call-done.aside
  259.2 0.0 reduce-scatter.5.cloned.1.call-update
  259.3 65.7 %last_moves.1 = (bf16[192,1536]{1,0:T(8,128)(2,1)}, bf16[192,1536]{1,0:T(8,128)(2,1)}, f32[8,1536]{1,0:T(8,128)}, f32[8,16,256]{2,1,0:T(8,128)}, bf16[4,192,2048...) custom-call(bf16[768,1664]{1,0:T(8,128)(2,1)} %get-tuple-element.101.grad_project, ...), custom_call_target="tpu_custom_call" | custom-call | bytes 157286400 | tf_op jit(solution)/shard_map/last_moves/pallas_call | solution.py:1671
  324.9 0.0 copy-start
  324.9 5.2 %spread_cols.1 = f32[192,8192]{1,0:T(8,128)} custom-call(bf16[4,192,2048]{2,1,0:T(8,128)(2,1)} %get-tuple-element.126.refs_0_), custom_call_target="tpu_custom_call" | custom-call | bytes 9437184 | tf_op jit(solution)/shard_map/spread_cols/pallas_call | solution.py:1815
  330.2 0.0 copy-done
  330.2 2.2 bitcast_convert_fusion
  332.3 0.0 reduce-scatter.5.cloned.1.call-done.late
  332.3 34.2 %finish_moves.1 = (bf16[4,192,1920]{2,1,0:T(8,128)(2,1)}, f32[16,256]{1,0:T(8,128)}, f32[4,8,256]{2,1,0:T(8,128)}) custom-call(bf16[192,1920]{1,0:T(8,128)(2,1)} %reduce-scatter.5.cloned.1.call-done.late, f32[8,16,256]{2,1,0:T(8,128)} %get-tuple-element.111.parts), custom_call_target="tpu_custom_call" | custom-call | bytes 52428800 | tf_op jit(solution)/shard_map/finish_moves/pallas_call | solution.py:1760
  366.5 5.4 %unpack.1 = (f32[192,6144]{1,0:T(8,128)}, f32[192,1536]{1,0:T(8,128)}, bf16[192,1536]{1,0:T(8,128)(2,1)}, bf16[192,1536]{1,0:T(8,128)(2,1)}, f32[24,192]{1,0:T(8...) custom-call(bf16[4,192,1920]{2,1,0:T(8,128)(2,1)} %get-tuple-element.112.late, ...), custom_call_target="tpu_custom_call" | custom-call | bytes 8847360 | tf_op jit(solution)/shard_map/unpack/pallas_call | solution.py:1869
Async XLA Ops:
  7.2 252.1 %reduce-scatter.3.cloned.1.call-start = ((), (), s32[]{:S(2)}) async-start(), calls=%async_computation.2 | async-start | bytes 7077888 | tf_op jit(solution)/shard_map/reduce_scatter | solution.py:2014
  163.6 168.8 %reduce-scatter.5.cloned.1.call-start = ((), (), s32[]{:S(2)}) async-start(), calls=%async_computation.3 | async-start | bytes 6635520 | tf_op jit(solution)/shard_map/reduce_scatter | solution.py:2014
  324.9 5.2 %copy-start = (bf16[4,128,1536]{2,1,0:T(8,128)(2,1)S(1)}, bf16[4,128,1536]{2,1,0:T(8,128)(2,1)}, u32[]{:S(2)}) copy-start(bf16[4,128,1536]{2,1,0:T(8,128)(2,1)} %get-tuple-element.127) | copy-start | bytes 4718596
Sparse Core Ops, SparseCore 0:
  163.7 70.9 reduce-scatter.2
  259.4 67.5 reduce-scatter.4

commit v7 on v6

--- a/solution.py
+++ b/solution.py
@@ -1824,6 +1824,46 @@
     )(source)
 
 
+def spread_early_kernel(piece, gate_up, down, gate_up_out, down_out):
+    ranks = gate_up.shape[0]
+    for block in range(gate_up.shape[2] // piece):
+        for index in range(ranks):
+            gate_up_out[:, (block * ranks + index) * piece : (block * ranks + index + 1) * piece] = gate_up[
+                index, :, block * piece : (block + 1) * piece
+            ].astype(F32)
+    size = down.shape[1]
+    for index in range(down.shape[0]):
+        down_out[index * size : (index + 1) * size, :] = down[index].astype(F32)
+
+
+def spread_early(gate_up, down, piece):
+    ranks, rows, cols = gate_up.shape
+    _, down_rows, model = down.shape
+    steps = 2
+    part, each = rows // steps, ranks // steps
+    return pl.pallas_call(
+        functools.partial(spread_early_kernel, piece),
+        grid=(steps,),
+        in_specs=[
+            pl.BlockSpec((ranks, part, cols), lambda step: (0, step, 0)),
+            pl.BlockSpec((each, down_rows, model), lambda step: (step, 0, 0)),
+        ],
+        out_specs=[
+            pl.BlockSpec((part, ranks * cols), lambda step: (step, 0)),
+            pl.BlockSpec((each * down_rows, model), lambda step: (step, 0)),
+        ],
+        out_shape=[
+            jax.ShapeDtypeStruct((rows, ranks * cols), F32),
+            jax.ShapeDtypeStruct((ranks * down_rows, model), F32),
+        ],
+        compiler_params=pltpu.CompilerParams(vmem_limit_bytes=VMEM_LIMIT),
+        cost_estimate=pl.CostEstimate(
+            flops=0, bytes_accessed=6 * ranks * (rows * cols + down_rows * model), transcendentals=0
+        ),
+        name="spread_early",
+    )(gate_up, down)
+
+
 def unpack_kernel(
     width, heads, head, late, forget_all, sums, totals, segments, first_rows, second_rows,
     in_out, out_out, first_out, second_out, forget_out, gains, bias, qk, rms,
@@ -1859,7 +1899,7 @@
 
 def unpack(late, forget_all, sums, totals, segments, first_rows, second_rows, width, heads, head):
     ranks, rows, cols = late.shape
-    part = rows // 4
+    part = rows // 2
 
     def block(lanes):
         return pl.BlockSpec((part, lanes), lambda step: (step, 0))
@@ -2054,8 +2094,7 @@
             grad_mixed_cols,             gain_rows, gain_two_grad, small, places_all[3], forget_grad,
         )
         late_own, piece_sum, forget_all = finish_moves(6, ranks, shards, late_share, parts)
-        gate_up_out = spread_cols(early_own, (hidden_piece, 0, 2 * shards))[0]
-        down_out = down_own.astype(F32).reshape(down_weight.shape)
+        gate_up_out, down_out = spread_early(early_own, down_own, hidden_piece)
     else:
         grad_normed = right_product(grad_project, w_in)
         gain_one_grad = jnp.sum(grad_normed * wide_inputs * scale_one, axis=0)

time: 385 us -> 382 us (level)
  transfers between devices with their start and end apart: 2 -> 2, of which waited for: 0 -> 0; matrix products, arithmetic and copies ran while one was open for 1% -> 0% of each run, Pallas kernels for 44% -> 44%
where the time goes in v7:
time: 382 us; the launch traced here: 377 us
  Pallas kernels  362 us (95%)
  between operations  14.6 us (4%)
    pallas_call x1, Pallas kernels, front(): pl.pallas_call(functools.partial(front_kernel, shards, head, heads, width...  122 us
    pallas_call x1, Pallas kernels, last_moves(): pl.pallas_call(functools.partial(last_kernel, ranks, shards), in_specs=[A...  65.7 us
    pallas_call x1, Pallas kernels, middle(): pl.pallas_call(functools.partial(middle_kernel, ranks), in_specs=[ANY] *...  51 us
    pallas_call x1, Pallas kernels, attend_back(): pl.pallas_call(functools.partial(attend_back_kernel, head, chunk, width,...  44.6 us
    pallas_call x1, Pallas kernels, finish_moves(): pl.pallas_call(functools.partial(finish_kernel, ranks, shards), in_specs=...  34.2 us
    pallas_call x1, Pallas kernels, ffn(): pl.pallas_call(functools.partial(ffn_kernel, shards, pick_chunk(rows)), i...  34.1 us
  transfers between devices with their start and end apart: 2, of which 0 were waited for; matrix products, arithmetic and copies ran while one was open for 0% of the time, Pallas kernels for 44%

profile of v7, /device:TPU:0, one launch (start us, length us, event | category | flops | bytes accessed | tf_op | source)
XLA Modules:
  0.0 376.6 jit_solution(11309817230760381841)
XLA Ops:
  7.2 0.0 reduce-scatter.3.cloned.1.call-start
  7.2 122.2 %front.1 = (bf16[768,1536]{1,0:T(8,128)(2,1)}, bf16[768,1536]{1,0:T(8,128)(2,1)}, bf16[1536,1664]{1,0:T(8,128)(2,1)}, bf16[1536,384]{1,0:T(8,128)(2,1)}, bf16[15...) custom-call(bf16[192,1536]{1,0:T(8,128)(2,1)} %bitcast.8, ...), custom_call_target="tpu_custom_call" | custom-call | bytes 314572800 | tf_op jit(solution)/shard_map/front/pallas_call | solution.py:1002
  129.4 34.1 %ffn.1 = (bf16[1024,1536]{1,0:T(8,128)(2,1)}, bf16[768,1024]{1,0:T(8,128)(2,1)}, bf16[768,2048]{1,0:T(8,128)(2,1)}, bf16[1536,2048]{1,0:T(8,128)(2,1)}, bf16[1024,1536]{1,0:T(8,128)(2,1)}) custom-call(bf16[768,1536]{1,0:T(8,128)(2,1)} %get-tuple-element.83.normed, bf16[1536,768]{1,0:T(8,128)(2,1)} %get-tuple-element.84.turned_from, ...), custom_call_target="tpu_custom_call" | custom-call | bytes 104857600 | tf_op jit(solution)/shard_map/ffn/pallas_call | solution.py:1178
  163.6 0.0 reduce-scatter.3.cloned.1.call-update
  163.6 0.0 reduce-scatter.5.cloned.1.call-start
  163.6 51.0 %middle.1 = (f32[768,384]{1,0:T(8,128)}, f32[768,384]{1,0:T(8,128)}, f32[8,1536]{1,0:T(8,128)}, bf16[768,1536]{1,0:T(8,128)(2,1)}, bf16[1536,384]{1,0:T(8,128)(2,1)}) custom-call(bf16[768,2048]{1,0:T(8,128)(2,1)} %get-tuple-element.88.grad_gate_up, bf16[1536,2048]{1,0:T(8,128)(2,1)} %get-tuple-element.85.w_gate_up, ...), custom_call_target="tpu_custom_call" | custom-call | bytes 157286400 | tf_op jit(solution)/shard_map/middle/pallas_call | solution.py:1492
  214.6 44.6 %attend_back.1 = (bf16[768,1664]{1,0:T(8,128)(2,1)}, f32[8,128]{1,0:T(8,128)}, bf16[4,192,1536]{2,1,0:T(8,128)(2,1)}, bf16[1536,1920]{1,0:T(8,128)(2,1)}, bf16[128,1536]{1,0:T(8,128)(2,1)}, /*index=5*/f32[8,1536]{1,0:T(8,128)}) custom-call(f32[1,768]{1,0:T(1,128)} %get-tuple-element.72.pos_row, f32[768,1]{1,0:T(8,128)} %get-tuple-element.73.pos_col, ...), custom_call_target="tpu_custom_call" | custom-call | tf_op jit(solution)/shard_map/attend_back/pallas_call | solution.py:447
  259.2 0.0 reduce-scatter.3.cloned.1.call-done.aside
  259.2 0.0 reduce-scatter.5.cloned.1.call-update
  259.3 65.7 %last_moves.1 = (bf16[192,1536]{1,0:T(8,128)(2,1)}, bf16[192,1536]{1,0:T(8,128)(2,1)}, f32[8,1536]{1,0:T(8,128)}, f32[8,16,256]{2,1,0:T(8,128)}, bf16[4,192,2048...) custom-call(bf16[768,1664]{1,0:T(8,128)(2,1)} %get-tuple-element.103.grad_project, ...), custom_call_target="tpu_custom_call" | custom-call | bytes 157286400 | tf_op jit(solution)/shard_map/last_moves/pallas_call | solution.py:1671
  324.9 5.6 %spread_early.1 = (f32[192,8192]{1,0:T(8,128)}, f32[512,1536]{1,0:T(8,128)}) custom-call(bf16[4,192,2048]{2,1,0:T(8,128)(2,1)} %get-tuple-element.128.gate_up, bf16[4,128,1536]{2,1,0:T(8,128)(2,1)} %get-tuple-element.129.down), custom_call_target="tpu_custom_call" | custom-call | bytes 14155776 | tf_op jit(solution)/shard_map/spread_early/pallas_call | solution.py:1844
  330.5 0.0 reduce-scatter.5.cloned.1.call-done.late
  330.5 34.2 %finish_moves.1 = (bf16[4,192,1920]{2,1,0:T(8,128)(2,1)}, f32[16,256]{1,0:T(8,128)}, f32[4,8,256]{2,1,0:T(8,128)}) custom-call(bf16[192,1920]{1,0:T(8,128)(2,1)} %reduce-scatter.5.cloned.1.call-done.late, f32[8,16,256]{2,1,0:T(8,128)} %get-tuple-element.113.parts), custom_call_target="tpu_custom_call" | custom-call | bytes 52428800 | tf_op jit(solution)/shard_map/finish_moves/pallas_call | solution.py:1760
  364.7 4.6 %unpack.1 = (f32[192,6144]{1,0:T(8,128)}, f32[192,1536]{1,0:T(8,128)}, bf16[192,1536]{1,0:T(8,128)(2,1)}, bf16[192,1536]{1,0:T(8,128)(2,1)}, f32[24,192]{1,0:T(8...) custom-call(bf16[4,192,1920]{2,1,0:T(8,128)(2,1)} %get-tuple-element.114.late, ...), custom_call_target="tpu_custom_call" | custom-call | bytes 8847360 | tf_op jit(solution)/shard_map/unpack/pallas_call | solution.py:1909
Async XLA Ops:
  7.2 252.1 %reduce-scatter.3.cloned.1.call-start = ((), (), s32[]{:S(2)}) async-start(), calls=%async_computation.2 | async-start | bytes 7077888 | tf_op jit(solution)/shard_map/reduce_scatter | solution.py:2054
  163.6 166.9 %reduce-scatter.5.cloned.1.call-start = ((), (), s32[]{:S(2)}) async-start(), calls=%async_computation.3 | async-start | bytes 6635520 | tf_op jit(solution)/shard_map/reduce_scatter | solution.py:2054
Sparse Core Ops, SparseCore 0:
  163.7 70.9 reduce-scatter.2
  259.4 67.5 reduce-scatter.4

commit v8 on v7

--- a/solution.py
+++ b/solution.py
@@ -163,12 +163,12 @@
     attended, wide_query, wide_key, wide_value, grad_gated, *rest,
 ):
     if ranks:
-        aside, normed, out_grad, blocks, grad_project, small, aside_in, late, share, forget_grad = rest[:10]
-        mask, wide_grad, grad_query, grad_key, grad_value, grad_prefix = rest[10:16]
-        normed_in, out_in, aside_own, blocks_in, side_in, kept, from_below, from_above = rest[16:24]
-        late_all, load_sem, save_sem = rest[24:27]
-        sems = rest[27:29]
-        over_shards = ShardSum(shards, blocks_in, side_in, kept, from_below, from_above, rest[29:])
+        aside, normed, out_grad, blocks, grad_project, small, aside_in, late, share = rest[:9]
+        mask, wide_grad, grad_query, grad_key, grad_value, grad_prefix = rest[9:15]
+        normed_in, out_in, aside_own, blocks_in, side_in, kept, from_below, from_above = rest[15:23]
+        late_all, load_sem, save_sem = rest[23:26]
+        sems = rest[26:28]
+        over_shards = ShardSum(shards, blocks_in, side_in, kept, from_below, from_above, rest[28:])
 
         def loads():
             own = rows_of(aside, lax.axis_index("ctx"), aside_in.shape[1])
@@ -195,6 +195,12 @@
         if not ranks:
             return
         now = (LANES // head) * step + hook
+
+        @pl.when(now == 1)
+        def _():
+            pltpu.make_async_copy(blocks, blocks_in, load_sem.at[4]).wait()
+            over_shards.start()
+
         for stage in range(over_shards.layers - 1):
 
             @pl.when(now == 2 + 2 * stage)
@@ -217,8 +223,6 @@
                 copy.start()
             for copy in loads():
                 copy.start()
-            early.wait()
-            over_shards.start()
 
     rows = query.shape[0]
     lanes = lane_ids(rows)
@@ -335,8 +339,6 @@
                     late_all[part, into] = dot(normed_in[part, :], grad_project[:, cols]).astype(BF16)
 
             rest_save.start()
-            turned = grad_project[:, ends[0] : ends[0] + LANES].astype(F32).T[0:8, :]
-            forget_grad[...] = right_product(turned.astype(BF16), normed_in[...])
 
             @pl.loop(0, count)
             def _(turn):
@@ -424,12 +426,11 @@
         share = (blocks.shape[0] // shards, blocks.shape[1])
         sum_blocks, sum_sems = shard_sum_scratch(shards, *share)
         model, late_cols = normed.shape[0], 4 * width + out_grad.shape[1]
-        out_specs += [ANY, ANY, whole(share), whole((8, model))]
+        out_specs += [ANY, ANY, whole(share)]
         out_shape += [
             jax.ShapeDtypeStruct((ranks, aside.shape[0] // ranks, aside.shape[1]), BF16),
             jax.ShapeDtypeStruct((model, late_cols), BF16),
             jax.ShapeDtypeStruct(share, BF16),
-            jax.ShapeDtypeStruct((8, model), F32),
         ]
         scratch += [
             pltpu.VMEM(normed.shape, BF16),
@@ -1528,10 +1529,10 @@
 
 def last_kernel(
     ranks, shards,
-    grad_project, w_in, inputs, aside, pieces, mixed, share, mixed_grad, gain, gain_two_grad, small, segments, forget_grad,
+    grad_project, w_in, inputs, aside, pieces, mixed, share, normed, mixed_grad, gain, gain_two_grad, small, segments,
     tokens_grad, block_out, total_sums, parts, aside_all, share_all,
     grad_in, weight_in, inputs_in, aside_in, pieces_in, mixed_in, wide, out, into, between, end, sums_out, sums_in,
-    share_in, load_sem, send_sem, recv_sem, sums_send, sums_recv, aside_send, aside_recv, aside_own,
+    share_in, normed_in, load_sem, send_sem, recv_sem, sums_send, sums_recv, aside_send, aside_recv, aside_own,
 ):
     rank = lax.axis_index("ctx")
     rows = inputs.shape[0] // ranks
@@ -1543,6 +1544,7 @@
             (
                 (aside, aside_in), (w_in, weight_in), (grad_project, grad_in), (inputs, inputs_in),
                 (pieces, pieces_in), (rows_of(mixed, rank, rows), mixed_in), (share, share_in),
+                (normed, normed_in),
             )
         )
     ]
@@ -1634,6 +1636,9 @@
         stats = jnp.where(lane == index, total, stats)
     sums_out[7:8, 0:LANES] = stats
     compute(rank)
+    loads[7].wait()
+    turned = grad_in[:, 4 * width : 4 * width + LANES].astype(F32).T[0:8, :]
+    forget_grad = right_product(turned.astype(BF16), normed_in[...])
     for distance in range(1, ranks):
         send_sums(distance).start()
     relay.forward()
@@ -1660,8 +1665,8 @@
 
 def last_moves(
     collective_id, ranks, shards,
-    grad_project, w_in, inputs, aside, pieces, mixed, share, mixed_grad, gain, gain_two_grad, small, segments,
-    forget_grad,
+    grad_project, w_in, inputs, aside, pieces, mixed, share, normed, mixed_grad, gain, gain_two_grad, small,
+    segments,
 ):
     rows, model = inputs.shape
     own = (rows // ranks, model)
@@ -1670,7 +1675,7 @@
     sems = pltpu.SemaphoreType.DMA((ranks - 1,))
     return pl.pallas_call(
         functools.partial(last_kernel, ranks, shards),
-        in_specs=[ANY] * 7 + [VMEM_WHOLE] * 6,
+        in_specs=[ANY] * 8 + [VMEM_WHOLE] * 5,
         out_specs=[VMEM_WHOLE] * 4 + [ANY] * 2,
         out_shape=[
             jax.ShapeDtypeStruct(own, BF16),
@@ -1692,7 +1697,8 @@
             pltpu.VMEM((8, model), F32),
             pltpu.VMEM((ranks, 8, model), F32),
             pltpu.VMEM(share.shape, BF16),
-            pltpu.SemaphoreType.DMA((7,)),
+            pltpu.VMEM(normed.shape, BF16),
+            pltpu.SemaphoreType.DMA((8,)),
             pltpu.SemaphoreType.DMA((6,)),
             pltpu.SemaphoreType.DMA((6,)),
             sems, sems,
@@ -1705,7 +1711,7 @@
         ),
         cost_estimate=pl.CostEstimate(flops=0, bytes_accessed=150 << 20, transcendentals=0),
         name="last_moves",
-    )(grad_project, w_in, inputs, aside, pieces, mixed, share, mixed_grad, gain, gain_two_grad, small, segments, forget_grad)
+    )(grad_project, w_in, inputs, aside, pieces, mixed, share, normed, mixed_grad, gain, gain_two_grad, small, segments)
 
 
 def finish_kernel(
@@ -2080,7 +2086,7 @@
         grad_gated, (down_part, normed, out_part, down_part_grad) if plain else (), ranks if plain else 0, shards, head_dim, padded, local_heads,
     )
     if plain:
-        down_pieces, late, down_share, forget_grad = rest
+        down_pieces, late, down_share = rest
     else:
         in_part = left_product(normed, grad_project).astype(BF16)
         out_part = left_product(gated_all, grad_branch).astype(BF16)
@@ -2091,7 +2097,7 @@
     if plain:
         tokens_grad, block_out, sums, parts, early_own, down_own = last_moves(
             4, ranks, shards, grad_project, w_in, inputs, early_share[0], down_pieces, mixed_low, down_share,
-            grad_mixed_cols,             gain_rows, gain_two_grad, small, places_all[3], forget_grad,
+            normed, grad_mixed_cols,             gain_rows, gain_two_grad, small, places_all[3],
         )
         late_own, piece_sum, forget_all = finish_moves(6, ranks, shards, late_share, parts)
         gate_up_out, down_out = spread_early(early_own, down_own, hidden_piece)

time: 382 us -> 383 us (level)
    pallas_call x1, Pallas kernels: 34.2 us -> 30 us  [finish_moves(): pl.pallas_call(functools.partial(finish_kernel, ranks, shards), in_specs=...]
  transfers between devices with their start and end apart: 2 -> 2, of which waited for: 0 -> 0; matrix products, arithmetic and copies ran while one was open for 0% -> 0% of each run, Pallas kernels for 44% -> 46%
where the time goes in v8:
time: 383 us; the launch traced here: 378 us
  Pallas kernels  363 us (95%)
  between operations  14.6 us (4%)
    pallas_call x1, Pallas kernels, front(): pl.pallas_call(functools.partial(front_kernel, shards, head, heads, width...  122 us
    pallas_call x1, Pallas kernels, last_moves(): pl.pallas_call(functools.partial(last_kernel, ranks, shards), in_specs=[A...  67.9 us
    pallas_call x1, Pallas kernels, middle(): pl.pallas_call(functools.partial(middle_kernel, ranks), in_specs=[ANY] *...  51 us
    pallas_call x1, Pallas kernels, attend_back(): pl.pallas_call(functools.partial(attend_back_kernel, head, chunk, width,...  47.9 us
    pallas_call x1, Pallas kernels, ffn(): pl.pallas_call(functools.partial(ffn_kernel, shards, pick_chunk(rows)), i...  34.1 us
    pallas_call x1, Pallas kernels, finish_moves(): pl.pallas_call(functools.partial(finish_kernel, ranks, shards), in_specs=...  30 us
  transfers between devices with their start and end apart: 2, of which 0 were waited for; matrix products, arithmetic and copies ran while one was open for 0% of the time, Pallas kernels for 46%

profile of v8, /device:TPU:0, one launch (start us, length us, event | category | flops | bytes accessed | tf_op | source)
XLA Modules:
  0.0 378.0 jit_solution(1567764078842316581)
XLA Ops:
  7.2 0.0 reduce-scatter.3.cloned.1.call-start
  7.2 122.2 %front.1 = (bf16[768,1536]{1,0:T(8,128)(2,1)}, bf16[768,1536]{1,0:T(8,128)(2,1)}, bf16[1536,1664]{1,0:T(8,128)(2,1)}, bf16[1536,384]{1,0:T(8,128)(2,1)}, bf16[15...) custom-call(bf16[192,1536]{1,0:T(8,128)(2,1)} %bitcast.8, ...), custom_call_target="tpu_custom_call" | custom-call | bytes 314572800 | tf_op jit(solution)/shard_map/front/pallas_call | solution.py:1003
  129.4 34.1 %ffn.1 = (bf16[1024,1536]{1,0:T(8,128)(2,1)}, bf16[768,1024]{1,0:T(8,128)(2,1)}, bf16[768,2048]{1,0:T(8,128)(2,1)}, bf16[1536,2048]{1,0:T(8,128)(2,1)}, bf16[1024,1536]{1,0:T(8,128)(2,1)}) custom-call(bf16[768,1536]{1,0:T(8,128)(2,1)} %get-tuple-element.82.normed, bf16[1536,768]{1,0:T(8,128)(2,1)} %get-tuple-element.83.turned_from, ...), custom_call_target="tpu_custom_call" | custom-call | bytes 104857600 | tf_op jit(solution)/shard_map/ffn/pallas_call | solution.py:1179
  163.6 0.0 reduce-scatter.3.cloned.1.call-update
  163.6 0.0 reduce-scatter.5.cloned.1.call-start
  163.6 51.0 %middle.1 = (f32[768,384]{1,0:T(8,128)}, f32[768,384]{1,0:T(8,128)}, f32[8,1536]{1,0:T(8,128)}, bf16[768,1536]{1,0:T(8,128)(2,1)}, bf16[1536,384]{1,0:T(8,128)(2,1)}) custom-call(bf16[768,2048]{1,0:T(8,128)(2,1)} %get-tuple-element.87.grad_gate_up, bf16[1536,2048]{1,0:T(8,128)(2,1)} %get-tuple-element.84.w_gate_up, ...), custom_call_target="tpu_custom_call" | custom-call | bytes 157286400 | tf_op jit(solution)/shard_map/middle/pallas_call | solution.py:1493
  214.6 47.9 %attend_back.1 = (bf16[768,1664]{1,0:T(8,128)(2,1)}, f32[8,128]{1,0:T(8,128)}, bf16[4,192,1536]{2,1,0:T(8,128)(2,1)}, bf16[1536,1920]{1,0:T(8,128)(2,1)}, bf16[128,1536]{1,0:T(8,128)(2,1)}) custom-call(f32[1,768]{1,0:T(1,128)} %get-tuple-element.71.pos_row, f32[768,1]{1,0:T(8,128)} %get-tuple-element.72.pos_col, f32[1,768]{1,0:T(1,128)} %get-tuple-element.73.seg_row, ...), custom_call_target="tpu_custom_call" | custom-call | tf_op jit(solution)/shard_map/attend_back/pallas_call | solution.py:448
  262.5 0.0 reduce-scatter.3.cloned.1.call-done.aside
  262.5 0.0 reduce-scatter.5.cloned.1.call-update
  262.6 67.9 %last_moves.1 = (bf16[192,1536]{1,0:T(8,128)(2,1)}, bf16[192,1536]{1,0:T(8,128)(2,1)}, f32[8,1536]{1,0:T(8,128)}, f32[8,16,256]{2,1,0:T(8,128)}, bf16[4,192,2048...) custom-call(bf16[768,1664]{1,0:T(8,128)(2,1)} %get-tuple-element.102.grad_project, ...), custom_call_target="tpu_custom_call" | custom-call | bytes 157286400 | tf_op jit(solution)/shard_map/last_moves/pallas_call | solution.py:1676
  330.5 5.6 %spread_early.1 = (f32[192,8192]{1,0:T(8,128)}, f32[512,1536]{1,0:T(8,128)}) custom-call(bf16[4,192,2048]{2,1,0:T(8,128)(2,1)} %get-tuple-element.126.gate_up, bf16[4,128,1536]{2,1,0:T(8,128)(2,1)} %get-tuple-element.127.down), custom_call_target="tpu_custom_call" | custom-call | bytes 14155776 | tf_op jit(solution)/shard_map/spread_early/pallas_call | solution.py:1850
  336.0 0.0 reduce-scatter.5.cloned.1.call-done.late
  336.0 30.0 %finish_moves.1 = (bf16[4,192,1920]{2,1,0:T(8,128)(2,1)}, f32[16,256]{1,0:T(8,128)}, f32[4,8,256]{2,1,0:T(8,128)}) custom-call(bf16[192,1920]{1,0:T(8,128)(2,1)} %reduce-scatter.5.cloned.1.call-done.late, f32[8,16,256]{2,1,0:T(8,128)} %get-tuple-element.111.parts), custom_call_target="tpu_custom_call" | custom-call | bytes 52428800 | tf_op jit(solution)/shard_map/finish_moves/pallas_call | solution.py:1766
  366.0 4.6 %unpack.1 = (f32[192,6144]{1,0:T(8,128)}, f32[192,1536]{1,0:T(8,128)}, bf16[192,1536]{1,0:T(8,128)(2,1)}, bf16[192,1536]{1,0:T(8,128)(2,1)}, f32[24,192]{1,0:T(8...) custom-call(bf16[4,192,1920]{2,1,0:T(8,128)(2,1)} %get-tuple-element.112.late, ...), custom_call_target="tpu_custom_call" | custom-call | bytes 8847360 | tf_op jit(solution)/shard_map/unpack/pallas_call | solution.py:1915
Async XLA Ops:
  7.2 255.4 %reduce-scatter.3.cloned.1.call-start = ((), (), s32[]{:S(2)}) async-start(), calls=%async_computation.2 | async-start | bytes 7077888 | tf_op jit(solution)/shard_map/reduce_scatter | solution.py:2060
  163.6 172.5 %reduce-scatter.5.cloned.1.call-start = ((), (), s32[]{:S(2)}) async-start(), calls=%async_computation.3 | async-start | bytes 6635520 | tf_op jit(solution)/shard_map/reduce_scatter | solution.py:2060
Sparse Core Ops, SparseCore 0:
  163.7 71.4 reduce-scatter.2
  262.7 65.2 reduce-scatter.4

commit v9 on v7

--- a/solution.py
+++ b/solution.py
@@ -1349,7 +1349,7 @@
     rank = lax.axis_index("ctx")
     rows = mixed.shape[0] // ranks
     model, width = w_out.shape
-    tile = 256
+    tile = 512
     loads = [
         pltpu.make_async_copy(a, b, load_sem.at[n])
         for n, (a, b) in enumerate(
@@ -1536,7 +1536,7 @@
     rank = lax.axis_index("ctx")
     rows = inputs.shape[0] // ranks
     model, width = inputs.shape[1], mixed_grad.shape[1]
-    tile = 256
+    tile = 512
     loads = [
         pltpu.make_async_copy(a, b, load_sem.at[n])
         for n, (a, b) in enumerate(

time: 382 us -> 382 us (level)
  no operation moved by 1% of the time
where the time goes in v9:
time: 382 us; the launch traced here: 377 us
  Pallas kernels  362 us (95%)
  between operations  14.6 us (4%)
    pallas_call x1, Pallas kernels, front(): pl.pallas_call(functools.partial(front_kernel, shards, head, heads, width...  122 us
    pallas_call x1, Pallas kernels, last_moves(): pl.pallas_call(functools.partial(last_kernel, ranks, shards), in_specs=[A...  65.7 us
    pallas_call x1, Pallas kernels, middle(): pl.pallas_call(functools.partial(middle_kernel, ranks), in_specs=[ANY] *...  50.9 us
    pallas_call x1, Pallas kernels, attend_back(): pl.pallas_call(functools.partial(attend_back_kernel, head, chunk, width,...  45.2 us
    pallas_call x1, Pallas kernels, ffn(): pl.pallas_call(functools.partial(ffn_kernel, shards, pick_chunk(rows)), i...  34.1 us
    pallas_call x1, Pallas kernels, finish_moves(): pl.pallas_call(functools.partial(finish_kernel, ranks, shards), in_specs=...  33.6 us
  transfers between devices with their start and end apart: 2, of which 0 were waited for; matrix products, arithmetic and copies ran while one was open for 0% of the time, Pallas kernels for 44%

profile of v9, /device:TPU:0, one launch (start us, length us, event | category | flops | bytes accessed | tf_op | source)
XLA Modules:
  0.0 376.6 jit_solution(10849424823864055724)
XLA Ops:
  7.2 0.0 reduce-scatter.3.cloned.1.call-start
  7.2 122.2 %front.1 = (bf16[768,1536]{1,0:T(8,128)(2,1)}, bf16[768,1536]{1,0:T(8,128)(2,1)}, bf16[1536,1664]{1,0:T(8,128)(2,1)}, bf16[1536,384]{1,0:T(8,128)(2,1)}, bf16[15...) custom-call(bf16[192,1536]{1,0:T(8,128)(2,1)} %bitcast.8, ...), custom_call_target="tpu_custom_call" | custom-call | bytes 314572800 | tf_op jit(solution)/shard_map/front/pallas_call | solution.py:1002
  129.4 34.1 %ffn.1 = (bf16[1024,1536]{1,0:T(8,128)(2,1)}, bf16[768,1024]{1,0:T(8,128)(2,1)}, bf16[768,2048]{1,0:T(8,128)(2,1)}, bf16[1536,2048]{1,0:T(8,128)(2,1)}, bf16[1024,1536]{1,0:T(8,128)(2,1)}) custom-call(bf16[768,1536]{1,0:T(8,128)(2,1)} %get-tuple-element.83.normed, bf16[1536,768]{1,0:T(8,128)(2,1)} %get-tuple-element.84.turned_from, ...), custom_call_target="tpu_custom_call" | custom-call | bytes 104857600 | tf_op jit(solution)/shard_map/ffn/pallas_call | solution.py:1178
  163.6 0.0 reduce-scatter.3.cloned.1.call-update
  163.6 0.0 reduce-scatter.5.cloned.1.call-start
  163.6 50.9 %middle.1 = (f32[768,384]{1,0:T(8,128)}, f32[768,384]{1,0:T(8,128)}, f32[8,1536]{1,0:T(8,128)}, bf16[768,1536]{1,0:T(8,128)(2,1)}, bf16[1536,384]{1,0:T(8,128)(2,1)}) custom-call(bf16[768,2048]{1,0:T(8,128)(2,1)} %get-tuple-element.88.grad_gate_up, bf16[1536,2048]{1,0:T(8,128)(2,1)} %get-tuple-element.85.w_gate_up, ...), custom_call_target="tpu_custom_call" | custom-call | bytes 157286400 | tf_op jit(solution)/shard_map/middle/pallas_call | solution.py:1492
  214.5 45.2 %attend_back.1 = (bf16[768,1664]{1,0:T(8,128)(2,1)}, f32[8,128]{1,0:T(8,128)}, bf16[4,192,1536]{2,1,0:T(8,128)(2,1)}, bf16[1536,1920]{1,0:T(8,128)(2,1)}, bf16[128,1536]{1,0:T(8,128)(2,1)}, /*index=5*/f32[8,1536]{1,0:T(8,128)}) custom-call(f32[1,768]{1,0:T(1,128)} %get-tuple-element.72.pos_row, f32[768,1]{1,0:T(8,128)} %get-tuple-element.73.pos_col, ...), custom_call_target="tpu_custom_call" | custom-call | tf_op jit(solution)/shard_map/attend_back/pallas_call | solution.py:447
  259.7 0.0 reduce-scatter.3.cloned.1.call-done.aside
  259.7 0.0 reduce-scatter.5.cloned.1.call-update
  259.8 65.7 %last_moves.1 = (bf16[192,1536]{1,0:T(8,128)(2,1)}, bf16[192,1536]{1,0:T(8,128)(2,1)}, f32[8,1536]{1,0:T(8,128)}, f32[8,16,256]{2,1,0:T(8,128)}, bf16[4,192,2048...) custom-call(bf16[768,1664]{1,0:T(8,128)(2,1)} %get-tuple-element.103.grad_project, ...), custom_call_target="tpu_custom_call" | custom-call | bytes 157286400 | tf_op jit(solution)/shard_map/last_moves/pallas_call | solution.py:1671
  325.5 5.6 %spread_early.1 = (f32[192,8192]{1,0:T(8,128)}, f32[512,1536]{1,0:T(8,128)}) custom-call(bf16[4,192,2048]{2,1,0:T(8,128)(2,1)} %get-tuple-element.128.gate_up, bf16[4,128,1536]{2,1,0:T(8,128)(2,1)} %get-tuple-element.129.down), custom_call_target="tpu_custom_call" | custom-call | bytes 14155776 | tf_op jit(solution)/shard_map/spread_early/pallas_call | solution.py:1844
  331.0 0.0 reduce-scatter.5.cloned.1.call-done.late
  331.0 33.6 %finish_moves.1 = (bf16[4,192,1920]{2,1,0:T(8,128)(2,1)}, f32[16,256]{1,0:T(8,128)}, f32[4,8,256]{2,1,0:T(8,128)}) custom-call(bf16[192,1920]{1,0:T(8,128)(2,1)} %reduce-scatter.5.cloned.1.call-done.late, f32[8,16,256]{2,1,0:T(8,128)} %get-tuple-element.113.parts), custom_call_target="tpu_custom_call" | custom-call | bytes 52428800 | tf_op jit(solution)/shard_map/finish_moves/pallas_call | solution.py:1760
  364.7 4.6 %unpack.1 = (f32[192,6144]{1,0:T(8,128)}, f32[192,1536]{1,0:T(8,128)}, bf16[192,1536]{1,0:T(8,128)(2,1)}, bf16[192,1536]{1,0:T(8,128)(2,1)}, f32[24,192]{1,0:T(8...) custom-call(bf16[4,192,1920]{2,1,0:T(8,128)(2,1)} %get-tuple-element.114.late, ...), custom_call_target="tpu_custom_call" | custom-call | bytes 8847360 | tf_op jit(solution)/shard_map/unpack/pallas_call | solution.py:1909
Async XLA Ops:
  7.2 252.6 %reduce-scatter.3.cloned.1.call-start = ((), (), s32[]{:S(2)}) async-start(), calls=%async_computation.2 | async-start | bytes 7077888 | tf_op jit(solution)/shard_map/reduce_scatter | solution.py:2054
  163.6 167.5 %reduce-scatter.5.cloned.1.call-start = ((), (), s32[]{:S(2)}) async-start(), calls=%async_computation.3 | async-start | bytes 6635520 | tf_op jit(solution)/shard_map/reduce_scatter | solution.py:2054
Sparse Core Ops, SparseCore 0:
  163.7 70.9 reduce-scatter.2
  259.9 67.0 reduce-scatter.4
